TPU v7x, 32 devices: a whole 2x2x4 slice. The times are simulated.
32 devices in a mesh: clips: 2 (over x), lon: 16 (over z, y, core).
Axes of the slice: x: 2, y: 2, z: 4, core: 2. Of those that a mesh axis runs over, the one named last changes fastest.
Arguments:
- video_span: bfloat16 [2, 180, 128, 192], P(None, 'clips', 'lon'), parts along dimension 1, may hold values from -6 to 6
- caches: bfloat16 [3, 2, 180, 128, 192], P(None, None, 'clips', 'lon'), parts along dimension 2, may hold values from -0.25 to 1.5
- norm_gains: float32 [3, 192], replicated, may hold values from 0.5 to 1.5
- shifts: float32 [3, 192], replicated, may hold values from -0.5 to 0.5
- weights: bfloat16 [3, 5184, 192], replicated, may hold values from -0.078125 to 0.078125
- biases: float32 [3, 192], replicated, may hold values from -0.5 to 0.5
Outputs:
- encoded: bfloat16 [2, 180, 128, 192], P(None, 'clips', 'lon'), parts along dimension 1
- carried_frames: bfloat16 [3, 2, 180, 128, 192], P(None, None, 'clips', 'lon'), parts along dimension 2
There are 2 independent parts, one for each index of `clips`. A program takes and returns all parts, laid end to end along the dimension named above; an argument that names none is the same for every part. Nothing has to cross between parts.
All inputs are finite; a program needn't handle non-finite values.
Results may differ from a plain program's by a relative error of at most 0.0031.
Values may be sent and summed in bfloat16 or wider, within the bound.
No kernel may reach another device: no remote copies, remote signals or barrier semaphores. Data moves between devices by JAX's collectives and lax.ppermute only.
A program may use at most 192 MiB of HBM per device.

v0:
```python
import functools

import jax
import jax.numpy as jnp
from jax import lax
from jax.experimental import pallas as pl
from jax.experimental.pallas import tpu as pltpu
from jax.sharding import PartitionSpec as P

GROUPS = 32
EPSILON = 1e-06
LANES = 128
COLS = 8
SLABS = 10
VMEM = pl.BlockSpec(memory_space=pltpu.VMEM)
ANY = pl.BlockSpec(memory_space=pl.ANY)


def silu(u):
    return u * (0.5 + 0.5 * jnp.tanh(0.5 * u))


def twice(v):
    return jnp.concatenate([v, v], axis=-1)


def pair(a, b):
    return jnp.concatenate([a, b], axis=0).astype(jnp.bfloat16)


def build_slabs(rows, row_of, edge_of, slab):
    lane = lax.broadcasted_iota(jnp.int32, (COLS, LANES), 1)
    low = lane < LANES // 2
    column = lax.broadcasted_iota(jnp.int32, (COLS, LANES), 0)
    first, last = column == 0, column == COLS - 1
    zero = jnp.zeros((COLS, LANES), jnp.float32)

    def shifted(h):
        out = []
        for part, value in enumerate(row_of(h)):
            left, right = edge_of(h, part)
            out.append(
                (
                    jnp.where(first, left, pltpu.roll(value, 1, 0)),
                    value,
                    jnp.where(last, right, pltpu.roll(value, COLS - 1, 0)),
                )
            )
        main, rest = out
        return main + (jnp.where(low, rest[0], rest[1]), rest[2])

    def put(index, k, value):
        start = k * 16 if isinstance(k, int) else pl.multiple_of(k * 16, 16)
        slab[index, pl.ds(start, 16), :] = value

    def step(k, carry):
        before, older, oldest = carry
        one, two = shifted(2 * k), shifted(2 * k + 1)
        for r in range(3):
            put(r, k, pair(one[r], two[r]))
            put(3 + r, k, pair(before[r], one[r]))
        put(6, k, pair(one[3], two[3]))
        put(7, k, pair(before[3], one[3]))
        put(9, k, pair(one[4], two[4]))

        if older is not None:
            put(8, k - 1, pair(jnp.where(low, oldest, before[4]), jnp.where(low, older, one[4])))

        return two, one[4], before[4]

    count = rows // 2
    begun = step(0, ((zero,) * 5, None, None))
    before, older, oldest = lax.fori_loop(1, count, step, begun, unroll=4)
    for r in range(3):
        put(3 + r, count, pair(before[r], zero))
    put(7, count, pair(before[3], zero))
    put(8, count - 1, pair(jnp.where(low, oldest, before[4]), jnp.where(low, older, zero)))


def slab_rows(slab, start, size):
    def at(index, step=0):
        return slab[index, pl.ds(start + step, size), :]

    tiles = [at(3 + r) for r in range(3)] + [at(r) for r in range(3)]
    tiles += [at(3 + r, 16) for r in range(3)]
    tiles += [at(7), at(6), at(7, 16), at(8), at(9)]
    return jnp.concatenate(tiles, axis=1)


def tap_rows(weight, layer, tap_t, channels):
    def at(q, r, start, size):
        return weight[layer, pl.ds(((tap_t * 3 + q) * 3 + r) * channels + start, size), :]

    half = LANES // 2
    tiles = [at(q, r, 0, LANES) for q in range(3) for r in range(3)]
    for q in range(3):
        tiles += [at(q, 0, LANES, half), at(q, 1, LANES, half)]
    tiles += [at(0, 2, LANES, half), at(2, 2, LANES, half), at(1, 2, LANES, half)]
    tiles.append(jnp.zeros((half, weight.shape[2]), weight.dtype))
    return jnp.concatenate(tiles, axis=0)


def product(slab, start, size, weight):
    return jnp.dot(slab_rows(slab, start, size), weight, preferred_element_type=jnp.float32)


def cached_kernel(chunk, cache, before, after, weight, bias, out, edges, slab):
    layers, frames, rows, cols, channels = cache.shape
    for layer in range(layers):
        for frame in range(frames):
            for side, ref in enumerate((before, after)):
                value = ref[layer, frame].astype(jnp.float32)
                edges[side, 0, frame] = value[:, :LANES]
                edges[side, 1, frame] = twice(value[:, LANES:])

            def row_of(h, frame=frame):
                value = cache[layer, frame, h].astype(jnp.float32)
                return value[:, :LANES], twice(value[:, LANES:])

            def edge_of(h, part, frame=frame):
                return [edges[side, part, frame, pl.ds(h, COLS, stride=0), :] for side in (0, 1)]

            build_slabs(rows, row_of, edge_of, slab.at[frame])
        taps = [tap_rows(weight, layer, p, channels) for p in range(2)]
        for i in range(rows * cols // chunk):
            start = i * chunk
            here = pl.ds(start, chunk)
            out[layer, 0, here, :] = (
                product(slab.at[0], start, chunk, taps[0])
                + product(slab.at[1], start, chunk, taps[1])
                + bias[layer : layer + 1, :]
            )
            out[layer, 1, here, :] = (
                product(slab.at[1], start, chunk, taps[0]) + bias[layer : layer + 1, :]
            )


def halves(value):
    return value[..., :LANES], value[..., LANES:]


def active_kernel(layer, chunk, entries, final, *refs):
    x, before, after, stats, gain, shift, weight, part = refs[:8]
    rest = refs[8:]
    residual = None
    if layer == 1:
        residual, *rest = rest
    if layer > 0:
        _, *rest = rest
    if final:
        y, carried, edges, slab, kept, sem = rest
    else:
        y, carried, sums, first, last, edges, slab, kept, sem = rest
    frames, rows, cols, channels = kept.shape
    places = rows * cols
    members = channels // GROUPS

    total = jnp.sum(stats[...], axis=0)
    own = lax.broadcasted_iota(jnp.int32, (channels, channels), 0) // members
    other = lax.broadcasted_iota(jnp.int32, (channels, channels), 1) // members
    same = jnp.where(own == other, 1.0, 0.0)
    means = (
        jnp.dot(
            total, same, precision=lax.Precision.HIGHEST, preferred_element_type=jnp.float32
        )
        / entries
    )
    average = means[0:1]
    variance = means[1:2] - average * average
    scale = lax.rsqrt(variance + EPSILON) * gain[layer : layer + 1, :]
    offset = shift[layer : layer + 1, :] - average * scale
    scales = (scale[:, :LANES], twice(scale[:, LANES:]))
    offsets = (offset[:, :LANES], twice(offset[:, LANES:]))

    def act(part, value):
        return silu(value * scales[part] + offsets[part])

    for frame in range(frames):
        for side, ref in enumerate((before, after)):
            for part_index in range(2):
                if layer:
                    value = ref[part_index, frame]
                else:
                    value = halves(ref[frame].astype(jnp.float32))[part_index]
                    value = twice(value) if part_index else value
                edges[side, part_index, frame] = act(part_index, value)

        def row_of(h, frame=frame):
            if layer:
                start = h * COLS if isinstance(h, int) else pl.multiple_of(h * COLS, COLS)
                main, other = (x[i, frame, pl.ds(start, COLS), :] for i in range(2))
            else:
                main, other = halves(x[frame, h].astype(jnp.float32))
                other = twice(other)
            main, other = act(0, main), act(1, other)
            whole = jnp.concatenate([main, other[:, : channels - LANES]], axis=1)
            kept[frame, h] = whole.astype(jnp.bfloat16)
            return main, other

        def edge_of(h, part, frame=frame):
            return [edges[side, part, frame, pl.ds(h, COLS, stride=0), :] for side in (0, 1)]

        build_slabs(rows, row_of, edge_of, slab.at[frame])
    copy = pltpu.make_async_copy(kept, carried.at[layer], sem)
    copy.start()
    taps = [tap_rows(weight, layer, p, channels) for p in (1, 2)]
    sum_rows = jnp.zeros((COLS, channels), jnp.float32)
    square_rows = jnp.zeros((COLS, channels), jnp.float32)
    for i in range(places // chunk):
        start = i * chunk
        here = pl.ds(start, chunk)
        span = pl.ds(start // COLS, chunk // COLS)
        values = (
            product(slab.at[0], start, chunk, taps[1]) + part[layer, 0, here, :],
            product(slab.at[0], start, chunk, taps[0])
            + product(slab.at[1], start, chunk, taps[1])
            + part[layer, 1, here, :],
        )
        for t, value in enumerate(values):
            if final:
                held = [x[0, t, here, :], x[1, t, here, : channels - LANES]]
                value = value + jnp.concatenate(held, axis=1)
                shape = (chunk // COLS, COLS, channels)
                y[t, span] = value.reshape(shape).astype(jnp.bfloat16)
                continue
            if residual is not None:
                value = value + residual[t, span].astype(jnp.float32).reshape(chunk, channels)
            main, other = halves(value)
            y[0, t, here, :] = main
            y[1, t, here, :] = twice(other)
            folded = value.reshape(chunk // COLS, COLS, channels)
            sum_rows = sum_rows + jnp.sum(folded, axis=0)
            square_rows = square_rows + jnp.sum(folded * folded, axis=0)
    if not final:
        both = jnp.concatenate(
            [
                jnp.sum(sum_rows, axis=0, keepdims=True),
                jnp.sum(square_rows, axis=0, keepdims=True),
            ],
            axis=0,
        )
        sums[...] = jnp.broadcast_to(both[None], sums.shape)
        for i in range(2):
            for t in range(frames):
                first[i, t] = y[i, t, pl.ds(0, rows, stride=COLS), :]
                last[i, t] = y[i, t, pl.ds(COLS - 1, rows, stride=COLS), :]
    copy.wait()


def scratch(frames, rows):
    return [
        pltpu.VMEM((2, 2, frames, rows, LANES), jnp.float32),
        pltpu.VMEM((frames, SLABS, rows * COLS + 16, LANES), jnp.bfloat16),
    ]


def local(video_span, caches, norm_gains, shifts, weights, biases):
    peers = lax.axis_size("lon")
    frames, rows, cols, channels = video_span.shape
    layers = caches.shape[0]
    places = rows * cols
    entries = frames * places * peers * (channels // GROUPS)
    up = [(i, (i + 1) % peers) for i in range(peers)]
    down = [(j, i) for i, j in up]
    chunk = 240

    def around(first, last):
        return lax.ppermute(last, "lon", up), lax.ppermute(first, "lon", down)

    def gathered(sums):
        return lax.all_to_all(sums, "lon", 0, 0)

    source = video_span.astype(jnp.float32)
    sums = jnp.stack([jnp.sum(source, axis=(0, 1, 2)), jnp.sum(source * source, axis=(0, 1, 2))])
    stats = gathered(jnp.broadcast_to(sums[None], (peers,) + sums.shape))
    before, after = around(video_span[:, :, 0], video_span[:, :, -1])
    cache_before, cache_after = around(caches[:, :, :, 0], caches[:, :, :, -1])
    part = pl.pallas_call(
        functools.partial(cached_kernel, chunk),
        out_shape=jax.ShapeDtypeStruct((layers, frames, places, channels), jnp.float32),
        in_specs=[VMEM] * 5,
        out_specs=VMEM,
        scratch_shapes=scratch(frames, rows),
        name="cached",
    )(caches, cache_before, cache_after, weights, biases)

    x = video_span
    carried = None
    for layer in range(layers):
        final = layer == layers - 1
        operands = [x, before, after, stats, norm_gains, shifts, weights, part]
        specs = [VMEM] * 8
        aliases = {}
        if layer == 1:
            operands.append(video_span)
            specs.append(VMEM)
        if layer > 0:
            aliases = {len(operands): 1}
            operands.append(carried)
            specs.append(ANY)
        state = jax.ShapeDtypeStruct((2, frames, places, LANES), jnp.float32)
        if final:
            state = jax.ShapeDtypeStruct(video_span.shape, jnp.bfloat16)
        outs = [state, jax.ShapeDtypeStruct(caches.shape, jnp.bfloat16)]
        out_specs = [VMEM, ANY]
        if not final:
            edge = jax.ShapeDtypeStruct((2, frames, rows, LANES), jnp.float32)
            outs += [jax.ShapeDtypeStruct((peers, 2, channels), jnp.float32), edge, edge]
            out_specs += [VMEM] * 3
        results = pl.pallas_call(
            functools.partial(active_kernel, layer, chunk, entries, final),
            out_shape=outs,
            in_specs=specs,
            out_specs=out_specs,
            scratch_shapes=scratch(frames, rows)
            + [pltpu.VMEM(video_span.shape, jnp.bfloat16), pltpu.SemaphoreType.DMA(())],
            input_output_aliases=aliases,
            name="active",
        )(*operands)
        x, carried = results[:2]
        if not final:
            stats = gathered(results[2])
            before, after = around(results[3], results[4])
    return x, carried


def solution(mesh):
    return jax.shard_map(
        local,
        mesh=mesh,
        in_specs=(
            P(None, "clips", "lon", None),
            P(None, None, "clips", "lon", None),
            P(),
            P(),
            P(),
            P(),
        ),
        out_specs=(P(None, "clips", "lon", None), P(None, None, "clips", "lon", None)),
        check_vma=False,
    )
```

profile of v0, /device:TPU:0, one launch (start us, length us, event | category | flops | bytes accessed | tf_op | source)
XLA Modules:
  0.0 115.9 jit_solution(8210294043965944418)
XLA Ops:
  0.6 1.8 %fusion.2 = (bf16[2,90,1,192]{3,2,1,0:T(2,128)(2,1)S(1)}, bf16[2,90,1,192]{3,2,1,0:T(2,128)(2,1)S(1)}) fusion(bf16[2,90,8,192]{3,2,1,0:T(8,128)(2,1)} %refs_8_.1), kind=kLoop, calls=%fused_computation.9 | loop fusion | bytes 276480 | tf_op jit(solution)/shard_map/slice | solution.py:276
  2.4 0.0 copy-start
  2.4 0.5 collective-permute-start
  3.0 5.1 %collective-permute-start.1 = (bf16[2,90,192]{2,1,0:T(8,128)(2,1)S(1)}, bf16[2,90,192]{2,1,0:T(8,128)(2,1)S(1)}, u32[]{:S(2)}, u32[]{:S(2)}) collective-permute-start(bf16[2,90,192]{2,1,0:T(8,128)(2,1)S(1)} %bitcast.17), channel_id=1, source_target_pairs={{1,0},{2,1},{3,2},{4,3},{5,4},{6,5},{7,6},{8,7},{9,8},{10,9},{11,1... | collective-permute-start | bytes 207368 | tf_op jit(solution)/shard_map/ppermute | solution.py:268
  8.0 3.1 %fusion.1 = (bf16[3,2,90,1,192]{4,3,2,1,0:T(2,128)(2,1)S(1)}, bf16[3,2,90,1,192]{4,3,2,1,0:T(2,128)(2,1)S(1)}) fusion(bf16[3,2,90,8,192]{4,3,2,1,0:T(8,128)(2,1)} %cache.1), kind=kLoop, calls=%fused_computation.8 | loop fusion | bytes 829440 | tf_op jit(solution)/shard_map/slice | solution.py:277
  11.2 0.1 collective-permute-start.2
  11.4 4.5 %collective-permute-start.3 = (bf16[3,2,90,192]{3,2,1,0:T(8,128)(2,1)S(1)}, bf16[3,2,90,192]{3,2,1,0:T(8,128)(2,1)S(1)}, u32[]{:S(2)}, u32[]{:S(2)}) collective-permute-start(bf16[3,2,90,192]{3,2,1,0:T(8,128)(2,1)S(1)} %bitcast.15), channel_id=1, source_target_pairs={{1,0},{2,1},{3,2},{4,3},{5,4},{6,5},{7,6},{8,7},{9,8},{10,9},{11,1... | collective-permute-start | bytes 622088 | tf_op jit(solution)/shard_map/ppermute | solution.py:268
  15.8 0.0 copy-done
  15.8 0.3 convert_reduce_fusion
  16.1 0.6 broadcast_in_dim.2
  16.7 3.5 %all-to-all-start = ((f32[16,2,192]{2,1,0:T(2,128)}), f32[16,2,192]{2,1,0:T(2,128)S(1)}, u32[]{:S(2)}, u32[]{:S(2)}) async-start(f32[16,2,192]{2,1,0:T(2,128)} %broadcast_in_dim.2), calls=%async_computation | async-start | bytes 65536 | tf_op jit(solution)/shard_map/all_to_all | solution.py:271
  20.3 10.2 %copy.15.weight.refs_6_ = bf16[3,5184,192]{2,1,0:T(8,128)(2,1)} copy(bf16[3,5184,192]{1,2,0:T(8,128)(2,1)} %param.10) | data formatting | bytes 11943936 | tf_op args[4]
  30.4 0.0 collective-permute-done.2.before
  30.4 0.0 copy-start.1
  30.4 0.0 collective-permute-done.3.after
  30.4 0.7 copy-done.1
  31.1 0.0 copy-start.2
  31.1 0.7 copy-done.2
  31.9 19.2 %cached.1.refs_7_ = f32[3,2,720,192]{3,2,1,0:T(8,128)} custom-call(bf16[3,2,90,8,192]{4,3,2,1,0:T(8,128)(2,1)} %cache.1, bf16[3,2,90,192]{3,2,1,0:T(8,128)(2,1)} %copy-done.1, bf16[3,2,90,192]{3,2,1,0:T(8,128)(2,1)} %copy-done.2, bf16[3,5184,192]{2,1,0:T(8,128)(2,1)} %copy.15.weight.refs_6_, f32[3,192]{1,0:T(4,128)} %bias.1), custom_call_target="tpu_custom_call" | custom-call | tf_op jit(solution)/shard_map/cached/pallas_call | solution.py:278
  51.1 0.0 all-to-all-done.refs_3_
  51.1 0.0 copy-start.7
  51.1 0.0 collective-permute-done.refs_1_
  51.1 0.0 copy-start.8
  51.1 0.0 collective-permute-done.1.refs_2_
  51.1 0.6 copy-done.7
  51.7 0.1 copy-done.8
  51.8 0.0 copy-start.9
  51.8 0.6 copy-done.9
  52.4 11.4 %active.3 = (f32[2,2,720,128]{3,2,1,0:T(8,128)}, bf16[3,2,90,8,192]{4,3,2,1,0:T(8,128)(2,1)}, f32[16,2,192]{2,1,0:T(2,128)}, f32[2,2,90,128]{3,2,1,0:T(8,128)}, f32[2,2,90,128]{3,2,1,0:T(8,128)}) custom-call(bf16[2,90,8,192]{3,2,1,0:T(8,128)(2,1)} %refs_8_.1, bf16[2,90,192]{2,1,0:T(8,128)(2,1)} %copy-done.8, bf16[2,90,192]{2,1,0:T(8,128)(2,1)} %copy-done.9, ...), custom_call_target="tpu_custom_call" | custom-call | tf_op jit(solution)/shard_map/active/pallas_call | solution.py:310
  63.8 0.3 collective-permute-start.4
  64.1 4.2 %collective-permute-start.5 = (f32[2,2,90,128]{3,2,1,0:T(8,128)}, f32[2,2,90,128]{3,2,1,0:T(8,128)S(1)}, u32[]{:S(2)}, u32[]{:S(2)}) collective-permute-start(f32[2,2,90,128]{3,2,1,0:T(8,128)} %get-tuple-element.14), channel_id=1, source_target_pairs={{1,0},{2,1},{3,2},{4,3},{5,4},{6,5},{7,6},{8,7},{9,8},{10,9},{11,1... | collective-permute-start | bytes 552968 | tf_op jit(solution)/shard_map/ppermute | solution.py:268
  68.3 10.7 %all_to_all.15.refs_3_ = f32[16,2,192]{2,1,0:T(2,128)} all-to-all(f32[16,2,192]{2,1,0:T(2,128)} %get-tuple-element.15), channel_id=1, replica_groups=mesh['clips'=2,'lon'=16] {'lon'}, dimensions={0} | all-to-all | bytes 49152 | tf_op jit(solution)/shard_map/all_to_all | solution.py:271
  78.9 0.0 collective-permute-done.4.refs_1_
  78.9 0.0 copy-start.3
  78.9 0.0 collective-permute-done.5.refs_2_
  79.0 0.0 copy-start.5
  79.0 0.6 copy-done.3
  79.6 0.1 copy-done.5
  79.7 10.4 %active.4 = (f32[2,2,720,128]{3,2,1,0:T(8,128)}, bf16[3,2,90,8,192]{4,3,2,1,0:T(8,128)(2,1)}, f32[16,2,192]{2,1,0:T(2,128)}, f32[2,2,90,128]{3,2,1,0:T(8,128)}, f32[2,2,90,128]{3,2,1,0:T(8,128)}) custom-call(f32[2,2,720,128]{3,2,1,0:T(8,128)} %get-tuple-element.12.refs_0_, f32[2,2,90,128]{3,2,1,0:T(8,128)} %copy-done.3, ...), custom_call_target="tpu_custom_call", output_to_operand_aliasing={{1}: (9, {})} | custom-call | tf_op jit(solution)/shard_map/active/pallas_call | solution.py:310
  90.1 0.1 collective-permute-start.6
  90.2 4.4 %collective-permute-start.7 = (f32[2,2,90,128]{3,2,1,0:T(8,128)}, f32[2,2,90,128]{3,2,1,0:T(8,128)S(1)}, u32[]{:S(2)}, u32[]{:S(2)}) collective-permute-start(f32[2,2,90,128]{3,2,1,0:T(8,128)} %get-tuple-element.19), channel_id=1, source_target_pairs={{1,0},{2,1},{3,2},{4,3},{5,4},{6,5},{7,6},{8,7},{9,8},{10,9},{11,1... | collective-permute-start | bytes 552968 | tf_op jit(solution)/shard_map/ppermute | solution.py:268
  94.6 10.7 %all_to_all.16.refs_3_ = f32[16,2,192]{2,1,0:T(2,128)} all-to-all(f32[16,2,192]{2,1,0:T(2,128)} %get-tuple-element.20), channel_id=1, replica_groups=mesh['clips'=2,'lon'=16] {'lon'}, dimensions={0} | all-to-all | bytes 49152 | tf_op jit(solution)/shard_map/all_to_all | solution.py:271
  105.3 0.0 collective-permute-done.6.refs_1_
  105.3 0.0 collective-permute-done.7.refs_2_
  105.3 0.0 copy-start.6
  105.3 0.7 copy-done.4
  106.0 0.1 copy-done.6
  106.1 9.7 %active.5 = (bf16[2,90,8,192]{3,2,1,0:T(8,128)(2,1)}, bf16[3,2,90,8,192]{4,3,2,1,0:T(8,128)(2,1)}) custom-call(f32[2,2,720,128]{3,2,1,0:T(8,128)} %get-tuple-element.17.refs_0_, f32[2,2,90,128]{3,2,1,0:T(8,128)} %copy-done.4, f32[2,2,90,128]{3,2,1,0:T(8,128)} %copy-done.6, f32[16,2,192]{2,1,0:T(2,128)} %all_to_all.16.refs_3_, ...), custom_call_target="tpu_custom_call", output_to_operand_aliasing={{1}: (8, {})} | custom-call | tf_op jit(solution)/shard_map/active/pallas_call | solution.py:310
  (6 shorter events, 0.1 us)
Async XLA Ops:
  2.4 13.5 %copy-start = (bf16[2,90,8,192]{3,2,1,0:T(8,128)(2,1)S(1)}, bf16[2,90,8,192]{3,2,1,0:T(8,128)(2,1)}, u32[]{:S(2)}) copy-start(bf16[2,90,8,192]{3,2,1,0:T(8,128)(2,1)} %refs_8_.1) | copy-start | bytes 1658884
  2.4 48.7 %collective-permute-start = (bf16[2,90,192]{2,1,0:T(8,128)(2,1)S(1)}, bf16[2,90,192]{2,1,0:T(8,128)(2,1)S(1)}, u32[]{:S(2)}, u32[]{:S(2)}) collective-permute-start(bf16[2,90,192]{2,1,0:T(8,128)(2,1)S(1)} %bitcast.16), channel_id=1, source_target_pairs={{0,1},{1,2},{2,3},{3,4},{4,5},{5,6},{6,7},{7,8},{8,9},{9,10},{10,1... | collective-permute-start | bytes 207368 | tf_op jit(solution)/shard_map/ppermute | solution.py:268
  3.0 48.1 %collective-permute-start.1 = (bf16[2,90,192]{2,1,0:T(8,128)(2,1)S(1)}, bf16[2,90,192]{2,1,0:T(8,128)(2,1)S(1)}, u32[]{:S(2)}, u32[]{:S(2)}) collective-permute-start(bf16[2,90,192]{2,1,0:T(8,128)(2,1)S(1)} %bitcast.17), channel_id=1, source_target_pairs={{1,0},{2,1},{3,2},{4,3},{5,4},{6,5},{7,6},{8,7},{9,8},{10,9},{11,1... | collective-permute-start | bytes 207368 | tf_op jit(solution)/shard_map/ppermute | solution.py:268
  11.2 19.2 %collective-permute-start.2 = (bf16[3,2,90,192]{3,2,1,0:T(8,128)(2,1)S(1)}, bf16[3,2,90,192]{3,2,1,0:T(8,128)(2,1)S(1)}, u32[]{:S(2)}, u32[]{:S(2)}) collective-permute-start(bf16[3,2,90,192]{3,2,1,0:T(8,128)(2,1)S(1)} %bitcast.14), channel_id=1, source_target_pairs={{0,1},{1,2},{2,3},{3,4},{4,5},{5,6},{6,7},{7,8},{8,9},{9,10},{10,1... | collective-permute-start | bytes 622088 | tf_op jit(solution)/shard_map/ppermute | solution.py:268
  11.4 19.1 %collective-permute-start.3 = (bf16[3,2,90,192]{3,2,1,0:T(8,128)(2,1)S(1)}, bf16[3,2,90,192]{3,2,1,0:T(8,128)(2,1)S(1)}, u32[]{:S(2)}, u32[]{:S(2)}) collective-permute-start(bf16[3,2,90,192]{3,2,1,0:T(8,128)(2,1)S(1)} %bitcast.15), channel_id=1, source_target_pairs={{1,0},{2,1},{3,2},{4,3},{5,4},{6,5},{7,6},{8,7},{9,8},{10,9},{11,1... | collective-permute-start | bytes 622088 | tf_op jit(solution)/shard_map/ppermute | solution.py:268
  16.7 34.4 %all-to-all-start = ((f32[16,2,192]{2,1,0:T(2,128)}), f32[16,2,192]{2,1,0:T(2,128)S(1)}, u32[]{:S(2)}, u32[]{:S(2)}) async-start(f32[16,2,192]{2,1,0:T(2,128)} %broadcast_in_dim.2), calls=%async_computation | async-start | bytes 65536 | tf_op jit(solution)/shard_map/all_to_all | solution.py:271
  30.4 0.7 copy-start.1
  31.1 0.7 copy-start.2
  51.1 0.6 copy-start.7
  51.1 0.6 copy-start.8
  51.8 0.6 copy-start.9
  63.8 15.2 %collective-permute-start.4 = (f32[2,2,90,128]{3,2,1,0:T(8,128)}, f32[2,2,90,128]{3,2,1,0:T(8,128)S(1)}, u32[]{:S(2)}, u32[]{:S(2)}) collective-permute-start(f32[2,2,90,128]{3,2,1,0:T(8,128)} %get-tuple-element.13), channel_id=1, source_target_pairs={{0,1},{1,2},{2,3},{3,4},{4,5},{5,6},{6,7},{7,8},{8,9},{9,10},{10,1... | collective-permute-start | bytes 552968 | tf_op jit(solution)/shard_map/ppermute | solution.py:268
  64.1 14.8 %collective-permute-start.5 = (f32[2,2,90,128]{3,2,1,0:T(8,128)}, f32[2,2,90,128]{3,2,1,0:T(8,128)S(1)}, u32[]{:S(2)}, u32[]{:S(2)}) collective-permute-start(f32[2,2,90,128]{3,2,1,0:T(8,128)} %get-tuple-element.14), channel_id=1, source_target_pairs={{1,0},{2,1},{3,2},{4,3},{5,4},{6,5},{7,6},{8,7},{9,8},{10,9},{11,1... | collective-permute-start | bytes 552968 | tf_op jit(solution)/shard_map/ppermute | solution.py:268
  78.9 0.7 copy-start.3
  79.0 0.7 copy-start.5
  90.1 15.2 %collective-permute-start.6 = (f32[2,2,90,128]{3,2,1,0:T(8,128)}, f32[2,2,90,128]{3,2,1,0:T(8,128)S(1)}, u32[]{:S(2)}, u32[]{:S(2)}) collective-permute-start(f32[2,2,90,128]{3,2,1,0:T(8,128)} %get-tuple-element.18), channel_id=1, source_target_pairs={{0,1},{1,2},{2,3},{3,4},{4,5},{5,6},{6,7},{7,8},{8,9},{9,10},{10,1... | collective-permute-start | bytes 552968 | tf_op jit(solution)/shard_map/ppermute | solution.py:268
  90.2 15.1 %collective-permute-start.7 = (f32[2,2,90,128]{3,2,1,0:T(8,128)}, f32[2,2,90,128]{3,2,1,0:T(8,128)S(1)}, u32[]{:S(2)}, u32[]{:S(2)}) collective-permute-start(f32[2,2,90,128]{3,2,1,0:T(8,128)} %get-tuple-element.19), channel_id=1, source_target_pairs={{1,0},{2,1},{3,2},{4,3},{5,4},{6,5},{7,6},{8,7},{9,8},{10,9},{11,1... | collective-permute-start | bytes 552968 | tf_op jit(solution)/shard_map/ppermute | solution.py:268
  105.3 0.7 copy-start.4
  105.3 0.8 copy-start.6
where the time goes:
time: 116 us
  Pallas kernels  50.7 us (44%)
  starting transfers between devices  22.6 us (19%)
  blocking collectives  21.4 us (18%)
  local copies, waits for them, and re-layouts  20 us (17%)
    pallas_call x3, Pallas kernels, local(): pl.pallas_call(functools.partial(active_kernel, layer, chunk, entries, fi...  31.5 us
    all_to_all x2, blocking collectives, gathered(): return lax.all_to_all(sums, 'lon', 0, 0)  21.4 us
    pallas_call x1, Pallas kernels, local(): pl.pallas_call(functools.partial(cached_kernel, chunk), out_shape=jax.Sha...  19.2 us
    ppermute x8, starting transfers between devices, around(): return (lax.ppermute(last, 'lon', up), lax.ppermute(first, 'lon', down))  19.1 us
    unnamed x25, local copies, waits for them, and re-layouts  14.5 us
    all_to_all x1, starting transfers between devices, gathered(): return lax.all_to_all(sums, 'lon', 0, 0)  3.5 us
    slice x1, local copies, waits for them, and re-layouts, local(): cache_before, cache_after = around(caches[:, :, :, 0], caches[:, :, :, -1])  3.15 us
  transfers between devices with their start and end apart: 9, of which 0 were waited for; matrix products, arithmetic and copies ran while one was open for 12% of the time, Pallas kernels for 17%

commit v1 on v0

--- a/solution.py
+++ b/solution.py
@@ -87,26 +87,38 @@
     return jnp.concatenate(tiles, axis=1)
 
 
-def tap_rows(weight, layer, tap_t, channels):
+def tap_lanes(weight, tap_t, channels):
     def at(q, r, start, size):
-        return weight[layer, pl.ds(((tap_t * 3 + q) * 3 + r) * channels + start, size), :]
+        return weight[:, pl.ds(((tap_t * 3 + q) * 3 + r) * channels + start, size)]
 
     half = LANES // 2
     tiles = [at(q, r, 0, LANES) for q in range(3) for r in range(3)]
     for q in range(3):
         tiles += [at(q, 0, LANES, half), at(q, 1, LANES, half)]
     tiles += [at(0, 2, LANES, half), at(2, 2, LANES, half), at(1, 2, LANES, half)]
-    tiles.append(jnp.zeros((half, weight.shape[2]), weight.dtype))
-    return jnp.concatenate(tiles, axis=0)
+    tiles.append(jnp.zeros((weight.shape[0], half), weight.dtype))
+    return jnp.concatenate(tiles, axis=1)
 
 
 def product(slab, start, size, weight):
-    return jnp.dot(slab_rows(slab, start, size), weight, preferred_element_type=jnp.float32)
-
-
-def cached_kernel(chunk, cache, before, after, weight, bias, out, edges, slab):
+    return lax.dot_general(
+        slab_rows(slab, start, size),
+        weight,
+        (((1,), (1,)), ((), ())),
+        preferred_element_type=jnp.float32,
+    )
+
+
+def cached_kernel(chunk, cache, before, after, weights, bias, out, edges, slab, weight, sem):
     layers, frames, rows, cols, channels = cache.shape
+    fetch = [
+        pltpu.make_async_copy(weights.at[layer], weight.at[layer % 2], sem.at[layer % 2])
+        for layer in range(layers)
+    ]
+    fetch[0].start()
     for layer in range(layers):
+        if layer + 1 < layers:
+            fetch[layer + 1].start()
         for frame in range(frames):
             for side, ref in enumerate((before, after)):
                 value = ref[layer, frame].astype(jnp.float32)
@@ -121,7 +133,8 @@
                 return [edges[side, part, frame, pl.ds(h, COLS, stride=0), :] for side in (0, 1)]
 
             build_slabs(rows, row_of, edge_of, slab.at[frame])
-        taps = [tap_rows(weight, layer, p, channels) for p in range(2)]
+        fetch[layer].wait()
+        taps = [tap_lanes(weight.at[layer % 2], p, channels) for p in range(2)]
         for i in range(rows * cols // chunk):
             start = i * chunk
             here = pl.ds(start, chunk)
@@ -140,7 +153,7 @@
 
 
 def active_kernel(layer, chunk, entries, final, *refs):
-    x, before, after, stats, gain, shift, weight, part = refs[:8]
+    x, before, after, stats, gain, shift, weights, parts = refs[:8]
     rest = refs[8:]
     residual = None
     if layer == 1:
@@ -148,12 +161,18 @@
     if layer > 0:
         _, *rest = rest
     if final:
-        y, carried, edges, slab, kept, sem = rest
+        y, carried, edges, slab, weight, part, kept, sem = rest
     else:
-        y, carried, sums, first, last, edges, slab, kept, sem = rest
+        y, carried, sums, first, last, edges, slab, weight, part, kept, sem = rest
     frames, rows, cols, channels = kept.shape
     places = rows * cols
     members = channels // GROUPS
+    fetch = [
+        pltpu.make_async_copy(weights.at[layer], weight, sem.at[0]),
+        pltpu.make_async_copy(parts.at[layer], part, sem.at[1]),
+    ]
+    for one in fetch:
+        one.start()
 
     total = jnp.sum(stats[...], axis=0)
     own = lax.broadcasted_iota(jnp.int32, (channels, channels), 0) // members
@@ -201,9 +220,11 @@
             return [edges[side, part, frame, pl.ds(h, COLS, stride=0), :] for side in (0, 1)]
 
         build_slabs(rows, row_of, edge_of, slab.at[frame])
-    copy = pltpu.make_async_copy(kept, carried.at[layer], sem)
+    copy = pltpu.make_async_copy(kept, carried.at[layer], sem.at[2])
     copy.start()
-    taps = [tap_rows(weight, layer, p, channels) for p in (1, 2)]
+    for one in fetch:
+        one.wait()
+    taps = [tap_lanes(weight, p, channels) for p in (1, 2)]
     sum_rows = jnp.zeros((COLS, channels), jnp.float32)
     square_rows = jnp.zeros((COLS, channels), jnp.float32)
     for i in range(places // chunk):
@@ -211,10 +232,10 @@
         here = pl.ds(start, chunk)
         span = pl.ds(start // COLS, chunk // COLS)
         values = (
-            product(slab.at[0], start, chunk, taps[1]) + part[layer, 0, here, :],
+            product(slab.at[0], start, chunk, taps[1]) + part[0, here, :],
             product(slab.at[0], start, chunk, taps[0])
             + product(slab.at[1], start, chunk, taps[1])
-            + part[layer, 1, here, :],
+            + part[1, here, :],
         )
         for t, value in enumerate(values):
             if final:
@@ -270,6 +291,7 @@
     def gathered(sums):
         return lax.all_to_all(sums, "lon", 0, 0)
 
+    turned = jnp.swapaxes(weights, 1, 2)
     source = video_span.astype(jnp.float32)
     sums = jnp.stack([jnp.sum(source, axis=(0, 1, 2)), jnp.sum(source * source, axis=(0, 1, 2))])
     stats = gathered(jnp.broadcast_to(sums[None], (peers,) + sums.shape))
@@ -278,18 +300,23 @@
     part = pl.pallas_call(
         functools.partial(cached_kernel, chunk),
         out_shape=jax.ShapeDtypeStruct((layers, frames, places, channels), jnp.float32),
-        in_specs=[VMEM] * 5,
+        in_specs=[VMEM, VMEM, VMEM, ANY, VMEM],
         out_specs=VMEM,
-        scratch_shapes=scratch(frames, rows),
+        scratch_shapes=scratch(frames, rows)
+        + [
+            pltpu.VMEM((2, channels, weights.shape[1]), weights.dtype),
+            pltpu.SemaphoreType.DMA((2,)),
+        ],
+        compiler_params=pltpu.CompilerParams(vmem_limit_bytes=28 << 20),
         name="cached",
-    )(caches, cache_before, cache_after, weights, biases)
+    )(caches, cache_before, cache_after, turned, biases)
 
     x = video_span
     carried = None
     for layer in range(layers):
         final = layer == layers - 1
-        operands = [x, before, after, stats, norm_gains, shifts, weights, part]
-        specs = [VMEM] * 8
+        operands = [x, before, after, stats, norm_gains, shifts, turned, part]
+        specs = [VMEM] * 6 + [ANY] * 2
         aliases = {}
         if layer == 1:
             operands.append(video_span)
@@ -313,7 +340,13 @@
             in_specs=specs,
             out_specs=out_specs,
             scratch_shapes=scratch(frames, rows)
-            + [pltpu.VMEM(video_span.shape, jnp.bfloat16), pltpu.SemaphoreType.DMA(())],
+            + [
+                pltpu.VMEM((channels, weights.shape[1]), weights.dtype),
+                pltpu.VMEM(part.shape[1:], jnp.float32),
+                pltpu.VMEM(video_span.shape, jnp.bfloat16),
+                pltpu.SemaphoreType.DMA((3,)),
+            ],
+            compiler_params=pltpu.CompilerParams(vmem_limit_bytes=28 << 20),
             input_output_aliases=aliases,
             name="active",
         )(*operands)

time: 116 us -> 93 us (0.80)
  Pallas kernels: 50.7 us -> 31.4 us
  blocking collectives: 21.4 us -> 18.8 us
  local copies, waits for them, and re-layouts: 20 us -> 18 us
    pallas_call x3, Pallas kernels: 31.5 us -> 16.7 us  [local(): pl.pallas_call(functools.partial(active_kernel, layer, chunk, entries, fi...]
    pallas_call x1, Pallas kernels: 19.2 us -> 14.7 us  [local(): pl.pallas_call(functools.partial(cached_kernel, chunk), out_shape=jax.Sha...]
    all_to_all x2, blocking collectives: 21.4 us -> 18.8 us  [gathered(): return lax.all_to_all(sums, 'lon', 0, 0)]
    unnamed x25 -> x22, local copies, waits for them, and re-layouts: 14.5 us -> 12.5 us
  transfers between devices with their start and end apart: 9 -> 9, of which waited for: 0 -> 0; matrix products, arithmetic and copies ran while one was open for 12% -> 7% of each run, Pallas kernels for 17% -> 16%
where the time goes in v1:
time: 93 us; the launch traced here: 92.5 us
  Pallas kernels  31.4 us (34%)
  starting transfers between devices  23 us (25%)
  blocking collectives  18.8 us (20%)
  local copies, waits for them, and re-layouts  18 us (19%)
  between operations  0.93 us (1%)
    ppermute x8, starting transfers between devices, around(): return (lax.ppermute(last, 'lon', up), lax.ppermute(first, 'lon', down))  18.9 us
    all_to_all x2, blocking collectives, gathered(): return lax.all_to_all(sums, 'lon', 0, 0)  18.8 us
    pallas_call x3, Pallas kernels, local(): pl.pallas_call(functools.partial(active_kernel, layer, chunk, entries, fi...  16.7 us
    pallas_call x1, Pallas kernels, local(): pl.pallas_call(functools.partial(cached_kernel, chunk), out_shape=jax.Sha...  14.7 us
    unnamed x22, local copies, waits for them, and re-layouts  12.5 us
    all_to_all x1, starting transfers between devices, gathered(): return lax.all_to_all(sums, 'lon', 0, 0)  4.13 us
    slice x1, local copies, waits for them, and re-layouts, local(): cache_before, cache_after = around(caches[:, :, :, 0], caches[:, :, :, -1])  3.21 us
  transfers between devices with their start and end apart: 9, of which 0 were waited for; matrix products, arithmetic and copies ran while one was open for 7% of the time, Pallas kernels for 16%

profile of v1, /device:TPU:0, one launch (start us, length us, event | category | flops | bytes accessed | tf_op | source)
XLA Modules:
  0.0 92.5 jit_solution(6757133891803111054)
XLA Ops:
  0.6 1.7 %fusion.2 = (bf16[2,90,1,192]{3,2,1,0:T(2,128)(2,1)S(1)}, bf16[2,90,1,192]{3,2,1,0:T(2,128)(2,1)S(1)}) fusion(bf16[2,90,8,192]{3,2,1,0:T(8,128)(2,1)} %refs_8_.1), kind=kLoop, calls=%fused_computation.9 | loop fusion | bytes 276480 | tf_op jit(solution)/shard_map/slice | solution.py:298
  2.3 0.0 copy-start.4
  2.3 0.6 copy.25
  3.0 0.5 collective-permute-start
  3.5 0.6 copy.24
  4.1 0.0 copy-start.5
  4.1 5.0 %collective-permute-start.1 = (bf16[2,90,192]{2,1,0:T(8,128)(2,1)}, bf16[2,90,192]{2,1,0:T(8,128)(2,1)}, u32[]{:S(2)}, u32[]{:S(2)}) collective-permute-start(bf16[2,90,192]{2,1,0:T(8,128)(2,1)} %bitcast.13), channel_id=1, source_target_pairs={{1,0},{2,1},{3,2},{4,3},{5,4},{6,5},{7,6},{8,7},{9,8},{10,9},{11,1... | collective-permute-start | bytes 207368 | tf_op jit(solution)/shard_map/ppermute | solution.py:289
  9.1 3.2 %fusion.1 = (bf16[3,2,90,1,192]{4,3,2,1,0:T(2,128)(2,1)S(1)}, bf16[3,2,90,1,192]{4,3,2,1,0:T(2,128)(2,1)S(1)}) fusion(bf16[3,2,90,8,192]{4,3,2,1,0:T(8,128)(2,1)} %cache.1), kind=kLoop, calls=%fused_computation.8 | loop fusion | bytes 829440 | tf_op jit(solution)/shard_map/slice | solution.py:299
  12.3 0.8 copy.23
  13.1 0.0 collective-permute-start.2
  13.1 0.8 copy.22
  13.8 4.4 %collective-permute-start.3 = (bf16[3,2,90,192]{3,2,1,0:T(8,128)(2,1)}, bf16[3,2,90,192]{3,2,1,0:T(8,128)(2,1)S(1)}, u32[]{:S(2)}, u32[]{:S(2)}) collective-permute-start(bf16[3,2,90,192]{3,2,1,0:T(8,128)(2,1)} %bitcast.11), channel_id=1, source_target_pairs={{1,0},{2,1},{3,2},{4,3},{5,4},{6,5},{7,6},{8,7},{9,8},{10,9},{11,1... | collective-permute-start | bytes 622088 | tf_op jit(solution)/shard_map/ppermute | solution.py:289
  18.3 0.0 copy-done.4
  18.3 0.3 convert_reduce_fusion
  18.6 0.6 broadcast_in_dim.2
  19.2 4.1 %all-to-all-start = ((f32[16,2,192]{2,1,0:T(2,128)}), f32[16,2,192]{2,1,0:T(2,128)}, u32[]{:S(2)}, u32[]{:S(2)}) async-start(f32[16,2,192]{2,1,0:T(2,128)} %broadcast_in_dim.2), calls=%async_computation | async-start | bytes 65536 | tf_op jit(solution)/shard_map/all_to_all | solution.py:292
  23.3 0.0 collective-permute-done.2.before
  23.3 0.0 collective-permute-done.3.after
  23.3 0.0 copy-done.5
  23.4 0.0 copy-done.8
  23.4 0.0 copy-start
  23.4 2.7 %copy-done = bf16[3,5184,192]{1,2,0:T(8,128)(2,1)S(1)} copy-done((bf16[3,5184,192]{1,2,0:T(8,128)(2,1)S(1)}, bf16[3,5184,192]{1,2,0:T(8,128)(2,1)}, u32[]{:S(2)}) %copy-start) | copy-done | bytes 5971992
  26.1 0.0 copy-start.6
  26.1 0.0 copy-start.7
  26.1 14.7 %cached.1.refs_7_ = f32[3,2,720,192]{3,2,1,0:T(8,128)S(1)} custom-call(bf16[3,2,90,8,192]{4,3,2,1,0:T(8,128)(2,1)S(1)} %copy-done.5, bf16[3,2,90,192]{3,2,1,0:T(8,128)(2,1)S(1)} %collective-permute-done.2.before, bf16[3,2,90,192]{3,2,1,0:T(8,128)(2,1)S(1)} %collective-permute-done.3.after, bf16[3,192,5184]{2,1,0:T(8,128)(2,1)S(1)} %bitcast.15, ...), custom_call_target="tpu_custom_call" | custom-call | tf_op jit(solution)/shard_map/cached/pallas_call | solution.py:300
  40.8 0.0 copy-start.2
  40.8 2.0 %copy-done.2 = f32[3,2,720,192]{3,2,1,0:T(8,128)} copy-done((f32[3,2,720,192]{3,2,1,0:T(8,128)}, f32[3,2,720,192]{3,2,1,0:T(8,128)S(1)}, u32[]{:S(2)}) %copy-start.2) | copy-done | bytes 3317784
  42.8 0.0 all-to-all-done.refs_3_
  42.8 0.0 collective-permute-done.refs_1_
  42.8 0.0 collective-permute-done.1.refs_2_
  42.8 0.0 copy-done.6
  42.8 0.0 copy-done.7
  42.8 0.0 copy-start.1
  42.9 2.7 %copy-done.1 = bf16[3,5184,192]{1,2,0:T(8,128)(2,1)S(1)} copy-done((bf16[3,5184,192]{1,2,0:T(8,128)(2,1)S(1)}, bf16[3,5184,192]{1,2,0:T(8,128)(2,1)}, u32[]{:S(2)}) %copy-start.1) | copy-done | bytes 5971992
  45.6 2.3 %copy-done.3 = f32[3,2,720,192]{3,2,1,0:T(8,128)S(1)} copy-done((f32[3,2,720,192]{3,2,1,0:T(8,128)S(1)}, f32[3,2,720,192]{3,2,1,0:T(8,128)}, u32[]{:S(2)}) %copy-start.3) | copy-done | bytes 3317784
  47.8 6.9 %active.3 = (f32[2,2,720,128]{3,2,1,0:T(8,128)S(1)}, bf16[3,2,90,8,192]{4,3,2,1,0:T(8,128)(2,1)}, f32[16,2,192]{2,1,0:T(2,128)S(1)}, f32[2,2,90,128]{3,2,1,0:T(8,128)S(1)}, f32[2,2,90,128]{3,2,1,0:T(8,128)S(1)}) custom-call(bf16[2,90,8,192]{3,2,1,0:T(8,128)(2,1)S(1)} %copy-done.4, bf16[2,90,192]{2,1,0:T(8,128)(2,1)} %collective-permute-done.refs_1_, ...), custom_call_target="tpu_custom_call" | custom-call | tf_op jit(solution)/shard_map/active/pallas_call | solution.py:337
  54.7 0.3 collective-permute-start.4
  55.0 4.2 %collective-permute-start.5 = (f32[2,2,90,128]{3,2,1,0:T(8,128)S(1)}, f32[2,2,90,128]{3,2,1,0:T(8,128)S(1)}, u32[]{:S(2)}, u32[]{:S(2)}) collective-permute-start(f32[2,2,90,128]{3,2,1,0:T(8,128)S(1)} %get-tuple-element.14), channel_id=1, source_target_pairs={{1,0},{2,1},{3,2},{4,3},{5,4},{6,5},{7,6},{8,7},{9,8},{10,9},{11,1... | collective-permute-start | bytes 552968 | tf_op jit(solution)/shard_map/ppermute | solution.py:289
  59.2 9.6 %all_to_all.15.refs_3_ = f32[16,2,192]{2,1,0:T(2,128)S(1)} all-to-all(f32[16,2,192]{2,1,0:T(2,128)S(1)} %get-tuple-element.15), channel_id=1, replica_groups=mesh['clips'=2,'lon'=16] {'lon'}, dimensions={0} | all-to-all | bytes 49152 | tf_op jit(solution)/shard_map/all_to_all | solution.py:292
  68.9 0.0 collective-permute-done.4.refs_1_
  68.9 0.0 collective-permute-done.5.refs_2_
  68.9 4.5 %active.4 = (f32[2,2,720,128]{3,2,1,0:T(8,128)S(1)}, bf16[3,2,90,8,192]{4,3,2,1,0:T(8,128)(2,1)}, f32[16,2,192]{2,1,0:T(2,128)S(1)}, f32[2,2,90,128]{3,2,1,0:T(8,128)S(1)}, f32[2,2,90,128]{3,2,1,0:T(8,128)S(1)}) custom-call(f32[2,2,720,128]{3,2,1,0:T(8,128)S(1)} %get-tuple-element.12.refs_0_, ...), custom_call_target="tpu_custom_call", output_to_operand_aliasing={{1}: (9, {})} | custom-call | tf_op jit(solution)/shard_map/active/pallas_call | solution.py:337
  73.4 0.1 collective-permute-start.6
  73.5 4.4 %collective-permute-start.7 = (f32[2,2,90,128]{3,2,1,0:T(8,128)S(1)}, f32[2,2,90,128]{3,2,1,0:T(8,128)S(1)}, u32[]{:S(2)}, u32[]{:S(2)}) collective-permute-start(f32[2,2,90,128]{3,2,1,0:T(8,128)S(1)} %get-tuple-element.19), channel_id=1, source_target_pairs={{1,0},{2,1},{3,2},{4,3},{5,4},{6,5},{7,6},{8,7},{9,8},{10,9},{11,1... | collective-permute-start | bytes 552968 | tf_op jit(solution)/shard_map/ppermute | solution.py:289
  77.9 9.2 %all_to_all.16.refs_3_ = f32[16,2,192]{2,1,0:T(2,128)S(1)} all-to-all(f32[16,2,192]{2,1,0:T(2,128)S(1)} %get-tuple-element.20), channel_id=1, replica_groups=mesh['clips'=2,'lon'=16] {'lon'}, dimensions={0} | all-to-all | bytes 49152 | tf_op jit(solution)/shard_map/all_to_all | solution.py:292
  87.1 0.0 collective-permute-done.6.refs_1_
  87.1 0.0 collective-permute-done.7.refs_2_
  87.1 5.3 %active.5 = (bf16[2,90,8,192]{3,2,1,0:T(8,128)(2,1)}, bf16[3,2,90,8,192]{4,3,2,1,0:T(8,128)(2,1)}) custom-call(f32[2,2,720,128]{3,2,1,0:T(8,128)S(1)} %get-tuple-element.17.refs_0_, f32[2,2,90,128]{3,2,1,0:T(8,128)S(1)} %collective-permute-done.6.refs_1_, f32[2,2,90,128]{3,2,1,0:T(8,128)S(1)} %collective-permute-done.7.refs_2_, ...), custom_call_target="tpu_custom_call", output_to_operand_aliasing={{1}: (8, {})} | custom-call | tf_op jit(solution)/shard_map/active/pallas_call | solution.py:337
  (3 shorter events, 0.0 us)
Async XLA Ops:
  2.3 16.0 %copy-start.4 = (bf16[2,90,8,192]{3,2,1,0:T(8,128)(2,1)S(1)}, bf16[2,90,8,192]{3,2,1,0:T(8,128)(2,1)}, u32[]{:S(2)}) copy-start(bf16[2,90,8,192]{3,2,1,0:T(8,128)(2,1)} %refs_8_.1) | copy-start | bytes 1658884
  3.0 39.8 %collective-permute-start = (bf16[2,90,192]{2,1,0:T(8,128)(2,1)}, bf16[2,90,192]{2,1,0:T(8,128)(2,1)}, u32[]{:S(2)}, u32[]{:S(2)}) collective-permute-start(bf16[2,90,192]{2,1,0:T(8,128)(2,1)} %bitcast.14), channel_id=1, source_target_pairs={{0,1},{1,2},{2,3},{3,4},{4,5},{5,6},{6,7},{7,8},{8,9},{9,10},{10,1... | collective-permute-start | bytes 207368 | tf_op jit(solution)/shard_map/ppermute | solution.py:289
  4.1 19.2 %copy-start.5 = (bf16[3,2,90,8,192]{4,3,2,1,0:T(8,128)(2,1)S(1)}, bf16[3,2,90,8,192]{4,3,2,1,0:T(8,128)(2,1)}, u32[]{:S(2)}) copy-start(bf16[3,2,90,8,192]{4,3,2,1,0:T(8,128)(2,1)} %cache.1) | copy-start | bytes 4976644
  4.1 19.2 %copy-start.8 = (f32[3,192]{1,0:T(4,128)S(1)}, f32[3,192]{1,0:T(4,128)}, u32[]{:S(2)}) copy-start(f32[3,192]{1,0:T(4,128)} %bias.1) | copy-start | bytes 6916
  4.1 38.7 %collective-permute-start.1 = (bf16[2,90,192]{2,1,0:T(8,128)(2,1)}, bf16[2,90,192]{2,1,0:T(8,128)(2,1)}, u32[]{:S(2)}, u32[]{:S(2)}) collective-permute-start(bf16[2,90,192]{2,1,0:T(8,128)(2,1)} %bitcast.13), channel_id=1, source_target_pairs={{1,0},{2,1},{3,2},{4,3},{5,4},{6,5},{7,6},{8,7},{9,8},{10,9},{11,1... | collective-permute-start | bytes 207368 | tf_op jit(solution)/shard_map/ppermute | solution.py:289
  13.1 10.3 %collective-permute-start.2 = (bf16[3,2,90,192]{3,2,1,0:T(8,128)(2,1)}, bf16[3,2,90,192]{3,2,1,0:T(8,128)(2,1)S(1)}, u32[]{:S(2)}, u32[]{:S(2)}) collective-permute-start(bf16[3,2,90,192]{3,2,1,0:T(8,128)(2,1)} %bitcast.12), channel_id=1, source_target_pairs={{0,1},{1,2},{2,3},{3,4},{4,5},{5,6},{6,7},{7,8},{8,9},{9,10},{10,1... | collective-permute-start | bytes 622088 | tf_op jit(solution)/shard_map/ppermute | solution.py:289
  13.8 9.5 %collective-permute-start.3 = (bf16[3,2,90,192]{3,2,1,0:T(8,128)(2,1)}, bf16[3,2,90,192]{3,2,1,0:T(8,128)(2,1)S(1)}, u32[]{:S(2)}, u32[]{:S(2)}) collective-permute-start(bf16[3,2,90,192]{3,2,1,0:T(8,128)(2,1)} %bitcast.11), channel_id=1, source_target_pairs={{1,0},{2,1},{3,2},{4,3},{5,4},{6,5},{7,6},{8,7},{9,8},{10,9},{11,1... | collective-permute-start | bytes 622088 | tf_op jit(solution)/shard_map/ppermute | solution.py:289
  19.2 23.6 %all-to-all-start = ((f32[16,2,192]{2,1,0:T(2,128)}), f32[16,2,192]{2,1,0:T(2,128)}, u32[]{:S(2)}, u32[]{:S(2)}) async-start(f32[16,2,192]{2,1,0:T(2,128)} %broadcast_in_dim.2), calls=%async_computation | async-start | bytes 65536 | tf_op jit(solution)/shard_map/all_to_all | solution.py:292
  23.4 2.7 %copy-start = (bf16[3,5184,192]{1,2,0:T(8,128)(2,1)S(1)}, bf16[3,5184,192]{1,2,0:T(8,128)(2,1)}, u32[]{:S(2)}) copy-start(bf16[3,5184,192]{1,2,0:T(8,128)(2,1)} %param.10) | copy-start | bytes 17915908
  26.1 16.7 %copy-start.6 = (f32[3,192]{1,0:T(4,128)S(1)}, f32[3,192]{1,0:T(4,128)}, u32[]{:S(2)}) copy-start(f32[3,192]{1,0:T(4,128)} %refs_4_.5) | copy-start | bytes 6916
  26.1 16.8 %copy-start.7 = (f32[3,192]{1,0:T(4,128)S(1)}, f32[3,192]{1,0:T(4,128)}, u32[]{:S(2)}) copy-start(f32[3,192]{1,0:T(4,128)} %refs_5_.5) | copy-start | bytes 6916
  40.8 2.0 %copy-start.2 = (f32[3,2,720,192]{3,2,1,0:T(8,128)}, f32[3,2,720,192]{3,2,1,0:T(8,128)S(1)}, u32[]{:S(2)}) copy-start(f32[3,2,720,192]{3,2,1,0:T(8,128)S(1)} %cached.1.refs_7_) | copy-start | bytes 9953284
  42.8 2.7 %copy-start.1 = (bf16[3,5184,192]{1,2,0:T(8,128)(2,1)S(1)}, bf16[3,5184,192]{1,2,0:T(8,128)(2,1)}, u32[]{:S(2)}) copy-start(bf16[3,5184,192]{1,2,0:T(8,128)(2,1)} %param.10) | copy-start | bytes 17915908
  45.6 2.3 %copy-start.3 = (f32[3,2,720,192]{3,2,1,0:T(8,128)S(1)}, f32[3,2,720,192]{3,2,1,0:T(8,128)}, u32[]{:S(2)}) copy-start(f32[3,2,720,192]{3,2,1,0:T(8,128)} %copy-done.2) | copy-start | bytes 9953284
  54.7 14.1 %collective-permute-start.4 = (f32[2,2,90,128]{3,2,1,0:T(8,128)S(1)}, f32[2,2,90,128]{3,2,1,0:T(8,128)S(1)}, u32[]{:S(2)}, u32[]{:S(2)}) collective-permute-start(f32[2,2,90,128]{3,2,1,0:T(8,128)S(1)} %get-tuple-element.13), channel_id=1, source_target_pairs={{0,1},{1,2},{2,3},{3,4},{4,5},{5,6},{6,7},{7,8},{8,9},{9,10},{10,1... | collective-permute-start | bytes 552968 | tf_op jit(solution)/shard_map/ppermute | solution.py:289
  55.0 13.9 %collective-permute-start.5 = (f32[2,2,90,128]{3,2,1,0:T(8,128)S(1)}, f32[2,2,90,128]{3,2,1,0:T(8,128)S(1)}, u32[]{:S(2)}, u32[]{:S(2)}) collective-permute-start(f32[2,2,90,128]{3,2,1,0:T(8,128)S(1)} %get-tuple-element.14), channel_id=1, source_target_pairs={{1,0},{2,1},{3,2},{4,3},{5,4},{6,5},{7,6},{8,7},{9,8},{10,9},{11,1... | collective-permute-start | bytes 552968 | tf_op jit(solution)/shard_map/ppermute | solution.py:289
  73.4 13.7 %collective-permute-start.6 = (f32[2,2,90,128]{3,2,1,0:T(8,128)S(1)}, f32[2,2,90,128]{3,2,1,0:T(8,128)S(1)}, u32[]{:S(2)}, u32[]{:S(2)}) collective-permute-start(f32[2,2,90,128]{3,2,1,0:T(8,128)S(1)} %get-tuple-element.18), channel_id=1, source_target_pairs={{0,1},{1,2},{2,3},{3,4},{4,5},{5,6},{6,7},{7,8},{8,9},{9,10},{10,1... | collective-permute-start | bytes 552968 | tf_op jit(solution)/shard_map/ppermute | solution.py:289
  73.5 13.6 %collective-permute-start.7 = (f32[2,2,90,128]{3,2,1,0:T(8,128)S(1)}, f32[2,2,90,128]{3,2,1,0:T(8,128)S(1)}, u32[]{:S(2)}, u32[]{:S(2)}) collective-permute-start(f32[2,2,90,128]{3,2,1,0:T(8,128)S(1)} %get-tuple-element.19), channel_id=1, source_target_pairs={{1,0},{2,1},{3,2},{4,3},{5,4},{6,5},{7,6},{8,7},{9,8},{10,9},{11,1... | collective-permute-start | bytes 552968 | tf_op jit(solution)/shard_map/ppermute | solution.py:289

commit v2 on v0

--- a/solution.py
+++ b/solution.py
@@ -13,7 +13,7 @@
 COLS = 8
 SLABS = 10
 VMEM = pl.BlockSpec(memory_space=pltpu.VMEM)
-ANY = pl.BlockSpec(memory_space=pl.ANY)
+HBM = pl.BlockSpec(memory_space=pltpu.HBM)
 
 
 def silu(u):
@@ -87,52 +87,103 @@
     return jnp.concatenate(tiles, axis=1)
 
 
-def tap_rows(weight, layer, tap_t, channels):
+def tap_lanes(weight, origin, channels):
     def at(q, r, start, size):
-        return weight[layer, pl.ds(((tap_t * 3 + q) * 3 + r) * channels + start, size), :]
+        return weight[:, pl.ds(origin + (q * 3 + r) * channels + start, size)]
 
     half = LANES // 2
     tiles = [at(q, r, 0, LANES) for q in range(3) for r in range(3)]
     for q in range(3):
         tiles += [at(q, 0, LANES, half), at(q, 1, LANES, half)]
     tiles += [at(0, 2, LANES, half), at(2, 2, LANES, half), at(1, 2, LANES, half)]
-    tiles.append(jnp.zeros((half, weight.shape[2]), weight.dtype))
-    return jnp.concatenate(tiles, axis=0)
+    tiles.append(jnp.zeros((weight.shape[0], half), weight.dtype))
+    return jnp.concatenate(tiles, axis=1)
 
 
 def product(slab, start, size, weight):
-    return jnp.dot(slab_rows(slab, start, size), weight, preferred_element_type=jnp.float32)
-
-
-def cached_kernel(chunk, cache, before, after, weight, bias, out, edges, slab):
-    layers, frames, rows, cols, channels = cache.shape
+    return lax.dot_general(
+        slab_rows(slab, start, size),
+        weight,
+        (((1,), (1,)), ((), ())),
+        preferred_element_type=jnp.float32,
+    )
+
+
+def begin_kernel(video, caches, sums, first, last, wide, held, sem):
+    layers, frames, rows, cols, channels = caches.shape
+    copies = [pltpu.make_async_copy(video, held.at[0], sem.at[0])]
     for layer in range(layers):
+        copies.append(
+            pltpu.make_async_copy(caches.at[layer], held.at[layer + 1], sem.at[layer + 1])
+        )
+    for copy in copies:
+        copy.start()
+    half = channels - LANES
+    total = [jnp.zeros((COLS, LANES), jnp.float32), jnp.zeros((COLS, half), jnp.float32)]
+    square = list(total)
+    for group, copy in enumerate(copies):
+        copy.wait()
         for frame in range(frames):
-            for side, ref in enumerate((before, after)):
-                value = ref[layer, frame].astype(jnp.float32)
-                edges[side, 0, frame] = value[:, :LANES]
-                edges[side, 1, frame] = twice(value[:, LANES:])
-
-            def row_of(h, frame=frame):
-                value = cache[layer, frame, h].astype(jnp.float32)
-                return value[:, :LANES], twice(value[:, LANES:])
-
-            def edge_of(h, part, frame=frame):
-                return [edges[side, part, frame, pl.ds(h, COLS, stride=0), :] for side in (0, 1)]
-
-            build_slabs(rows, row_of, edge_of, slab.at[frame])
-        taps = [tap_rows(weight, layer, p, channels) for p in range(2)]
-        for i in range(rows * cols // chunk):
-            start = i * chunk
-            here = pl.ds(start, chunk)
-            out[layer, 0, here, :] = (
-                product(slab.at[0], start, chunk, taps[0])
-                + product(slab.at[1], start, chunk, taps[1])
-                + bias[layer : layer + 1, :]
-            )
-            out[layer, 1, here, :] = (
-                product(slab.at[1], start, chunk, taps[0]) + bias[layer : layer + 1, :]
-            )
+            value = held[group, frame].astype(jnp.float32)
+            parts = halves(value)
+            if group == 0:
+                for i in range(2):
+                    total[i] = total[i] + jnp.sum(parts[i], axis=0)
+                    square[i] = square[i] + jnp.sum(parts[i] * parts[i], axis=0)
+            wide[0] = parts[0].reshape(rows * cols, LANES)
+            wide[1, :, :half] = parts[1].reshape(rows * cols, half)
+            for out, column in ((first, 0), (last, cols - 1)):
+                found = [wide[i, pl.ds(column, rows, stride=cols), :] for i in range(2)]
+                edge = jnp.concatenate([found[0], found[1][:, :half]], axis=1)
+                out[group * frames + frame] = edge.astype(jnp.bfloat16)
+    both = [
+        jnp.concatenate([jnp.sum(v, axis=0, keepdims=True) for v in pieces], axis=1)
+        for pieces in (total, square)
+    ]
+    sums[...] = jnp.broadcast_to(jnp.concatenate(both, axis=0)[None], sums.shape)
+
+
+def cached_kernel(layer, chunk, caches, before, after, weights, bias, out, *scratches):
+    edges, slab, cache, brims, weight, sem = scratches
+    _, frames, rows, cols, channels = caches.shape
+    where = pl.ds((layer + 1) * frames, frames)
+    begun = [pltpu.make_async_copy(caches.at[layer], cache, sem.at[0])]
+    for side, ref in enumerate((before, after)):
+        begun.append(pltpu.make_async_copy(ref.at[where], brims.at[side], sem.at[side + 1]))
+    fetch = pltpu.make_async_copy(
+        weights.at[layer, :, pl.ds(0, weight.shape[1])], weight, sem.at[3]
+    )
+    for copy in begun:
+        copy.start()
+    fetch.start()
+    for copy in begun:
+        copy.wait()
+    for frame in range(frames):
+        for side in range(2):
+            value = brims[side, frame].astype(jnp.float32)
+            edges[side, 0, frame] = value[:, :LANES]
+            edges[side, 1, frame] = twice(value[:, LANES:])
+
+        def row_of(h, frame=frame):
+            value = cache[frame, h].astype(jnp.float32)
+            return value[:, :LANES], twice(value[:, LANES:])
+
+        def edge_of(h, part, frame=frame):
+            return [edges[side, part, frame, pl.ds(h, COLS, stride=0), :] for side in (0, 1)]
+
+        build_slabs(rows, row_of, edge_of, slab.at[frame])
+    fetch.wait()
+    taps = [tap_lanes(weight, p * 9 * channels, channels) for p in range(2)]
+    constant = bias[layer : layer + 1, :]
+    for i in range(rows * cols // chunk):
+        start = i * chunk
+        here = pl.ds(start, chunk)
+        out[0, here, :] = (
+            product(slab.at[0], start, chunk, taps[0])
+            + product(slab.at[1], start, chunk, taps[1])
+            + constant
+        )
+        out[1, here, :] = product(slab.at[1], start, chunk, taps[0]) + constant
 
 
 def halves(value):
@@ -140,7 +191,7 @@
 
 
 def active_kernel(layer, chunk, entries, final, *refs):
-    x, before, after, stats, gain, shift, weight, part = refs[:8]
+    x, before, after, stats, gain, shift, weights, part = refs[:8]
     rest = refs[8:]
     residual = None
     if layer == 1:
@@ -148,12 +199,20 @@
     if layer > 0:
         _, *rest = rest
     if final:
-        y, carried, edges, slab, kept, sem = rest
+        y, carried, edges, slab, kept, held, weight, sem = rest
     else:
-        y, carried, sums, first, last, edges, slab, kept, sem = rest
+        y, carried, sums, first, last, edges, slab, kept, held, weight, sem = rest
     frames, rows, cols, channels = kept.shape
     places = rows * cols
     members = channels // GROUPS
+    skipped = weights.shape[2] - weight.shape[1]
+    fetch = pltpu.make_async_copy(
+        weights.at[layer, :, pl.ds(skipped, weight.shape[1])], weight, sem.at[1]
+    )
+    fetch.start()
+    if residual is not None:
+        source = pltpu.make_async_copy(residual, held, sem.at[2])
+        source.start()
 
     total = jnp.sum(stats[...], axis=0)
     own = lax.broadcasted_iota(jnp.int32, (channels, channels), 0) // members
@@ -201,9 +260,12 @@
             return [edges[side, part, frame, pl.ds(h, COLS, stride=0), :] for side in (0, 1)]
 
         build_slabs(rows, row_of, edge_of, slab.at[frame])
-    copy = pltpu.make_async_copy(kept, carried.at[layer], sem)
+    copy = pltpu.make_async_copy(kept, carried.at[layer], sem.at[0])
     copy.start()
-    taps = [tap_rows(weight, layer, p, channels) for p in (1, 2)]
+    fetch.wait()
+    if residual is not None:
+        source.wait()
+    taps = [tap_lanes(weight, p * 9 * channels - skipped, channels) for p in (1, 2)]
     sum_rows = jnp.zeros((COLS, channels), jnp.float32)
     square_rows = jnp.zeros((COLS, channels), jnp.float32)
     for i in range(places // chunk):
@@ -211,10 +273,10 @@
         here = pl.ds(start, chunk)
         span = pl.ds(start // COLS, chunk // COLS)
         values = (
-            product(slab.at[0], start, chunk, taps[1]) + part[layer, 0, here, :],
+            product(slab.at[0], start, chunk, taps[1]) + part[0, here, :],
             product(slab.at[0], start, chunk, taps[0])
             + product(slab.at[1], start, chunk, taps[1])
-            + part[layer, 1, here, :],
+            + part[1, here, :],
         )
         for t, value in enumerate(values):
             if final:
@@ -224,7 +286,7 @@
                 y[t, span] = value.reshape(shape).astype(jnp.bfloat16)
                 continue
             if residual is not None:
-                value = value + residual[t, span].astype(jnp.float32).reshape(chunk, channels)
+                value = value + held[t, span].astype(jnp.float32).reshape(chunk, channels)
             main, other = halves(value)
             y[0, t, here, :] = main
             y[1, t, here, :] = twice(other)
@@ -263,6 +325,7 @@
     up = [(i, (i + 1) % peers) for i in range(peers)]
     down = [(j, i) for i, j in up]
     chunk = 240
+    skipped = 9 * channels // LANES * LANES
 
     def around(first, last):
         return lax.ppermute(last, "lon", up), lax.ppermute(first, "lon", down)
@@ -270,42 +333,70 @@
     def gathered(sums):
         return lax.all_to_all(sums, "lon", 0, 0)
 
-    source = video_span.astype(jnp.float32)
-    sums = jnp.stack([jnp.sum(source, axis=(0, 1, 2)), jnp.sum(source * source, axis=(0, 1, 2))])
-    stats = gathered(jnp.broadcast_to(sums[None], (peers,) + sums.shape))
-    before, after = around(video_span[:, :, 0], video_span[:, :, -1])
-    cache_before, cache_after = around(caches[:, :, :, 0], caches[:, :, :, -1])
-    part = pl.pallas_call(
-        functools.partial(cached_kernel, chunk),
-        out_shape=jax.ShapeDtypeStruct((layers, frames, places, channels), jnp.float32),
-        in_specs=[VMEM] * 5,
-        out_specs=VMEM,
-        scratch_shapes=scratch(frames, rows),
-        name="cached",
-    )(caches, cache_before, cache_after, weights, biases)
+    def in_hbm(value):
+        return pltpu.with_memory_space_constraint(value, pltpu.HBM)
+
+    turned = in_hbm(jnp.swapaxes(weights, 1, 2))
+    caches, video = in_hbm(caches), in_hbm(video_span)
+    spread = jax.ShapeDtypeStruct((peers, 2, channels), jnp.float32)
+    brim = jax.ShapeDtypeStruct(((layers + 1) * frames, rows, channels), jnp.bfloat16)
+    sums, first, last = pl.pallas_call(
+        begin_kernel,
+        out_shape=[spread, brim, brim],
+        in_specs=[HBM, HBM],
+        out_specs=[VMEM] * 3,
+        scratch_shapes=[
+            pltpu.VMEM((2, places, LANES), jnp.float32),
+            pltpu.VMEM((layers + 1,) + video_span.shape, jnp.bfloat16),
+            pltpu.SemaphoreType.DMA((layers + 1,)),
+        ],
+        compiler_params=pltpu.CompilerParams(vmem_limit_bytes=24 << 20),
+        name="begin",
+    )(video, caches)
+    before, after = around(first, last)
+    brims = [in_hbm(before), in_hbm(after)]
+    stats = gathered(sums)
+
+    def cached_part(layer):
+        return pl.pallas_call(
+            functools.partial(cached_kernel, layer, chunk),
+            out_shape=jax.ShapeDtypeStruct((frames, places, channels), jnp.float32),
+            in_specs=[HBM, HBM, HBM, HBM, VMEM],
+            out_specs=VMEM,
+            scratch_shapes=scratch(frames, rows)
+            + [
+                pltpu.VMEM(video_span.shape, jnp.bfloat16),
+                pltpu.VMEM((2, frames, rows, channels), jnp.bfloat16),
+                pltpu.VMEM((channels, 18 * channels), weights.dtype),
+                pltpu.SemaphoreType.DMA((4,)),
+            ],
+            compiler_params=pltpu.CompilerParams(vmem_limit_bytes=24 << 20),
+            name="cached",
+        )(caches, *brims, turned, biases)
 
     x = video_span
     carried = None
     for layer in range(layers):
         final = layer == layers - 1
-        operands = [x, before, after, stats, norm_gains, shifts, weights, part]
-        specs = [VMEM] * 8
+        operands = [x, before, after, stats, norm_gains, shifts, turned]
+        operands.append(cached_part(layer))
+        specs = [VMEM] * 6 + [HBM, VMEM]
         aliases = {}
         if layer == 1:
-            operands.append(video_span)
-            specs.append(VMEM)
+            operands.append(video)
+            specs.append(HBM)
         if layer > 0:
             aliases = {len(operands): 1}
             operands.append(carried)
-            specs.append(ANY)
+            specs.append(HBM)
         state = jax.ShapeDtypeStruct((2, frames, places, LANES), jnp.float32)
         if final:
             state = jax.ShapeDtypeStruct(video_span.shape, jnp.bfloat16)
         outs = [state, jax.ShapeDtypeStruct(caches.shape, jnp.bfloat16)]
-        out_specs = [VMEM, ANY]
+        out_specs = [VMEM, HBM]
         if not final:
             edge = jax.ShapeDtypeStruct((2, frames, rows, LANES), jnp.float32)
-            outs += [jax.ShapeDtypeStruct((peers, 2, channels), jnp.float32), edge, edge]
+            outs += [spread, edge, edge]
             out_specs += [VMEM] * 3
         results = pl.pallas_call(
             functools.partial(active_kernel, layer, chunk, entries, final),
@@ -313,7 +404,13 @@
             in_specs=specs,
             out_specs=out_specs,
             scratch_shapes=scratch(frames, rows)
-            + [pltpu.VMEM(video_span.shape, jnp.bfloat16), pltpu.SemaphoreType.DMA(())],
+            + [
+                pltpu.VMEM(video_span.shape, jnp.bfloat16),
+                pltpu.VMEM(video_span.shape, jnp.bfloat16),
+                pltpu.VMEM((channels, 27 * channels - skipped), weights.dtype),
+                pltpu.SemaphoreType.DMA((3,)),
+            ],
+            compiler_params=pltpu.CompilerParams(vmem_limit_bytes=24 << 20),
             input_output_aliases=aliases,
             name="active",
         )(*operands)

time: 116 us -> 73 us (0.63)
  blocking collectives: 21.4 us -> 0 us
  Pallas kernels: 50.7 us -> 35.3 us
  local copies, waits for them, and re-layouts: 20 us -> 5.33 us
  starting transfers between devices: 22.6 us -> 27.2 us
  waiting for transfers between devices: 0.02 us -> 3.67 us
    all_to_all x2 -> x0, blocking collectives: 21.4 us -> none  [gathered(): return lax.all_to_all(sums, 'lon', 0, 0)]
    pallas_call x3, Pallas kernels: 31.5 us -> 15.6 us  [local(): pl.pallas_call(functools.partial(active_kernel, layer, chunk, entries, fi...]
    unnamed x25 -> x20, local copies, waits for them, and re-layouts: 14.5 us -> 5.33 us
    all_to_all x1 -> x3, starting transfers between devices: 3.5 us -> 12.5 us  [gathered(): return lax.all_to_all(sums, 'lon', 0, 0)]
    slice x2 -> x0, local copies, waits for them, and re-layouts: 4.91 us -> none  [the longest x1 3.15 us: local(): cache_before, cache_after = around(caches[:, :, :, 0], caches[:, :, :, -1])]
    ppermute x8 -> x6, starting transfers between devices: 19.1 us -> 14.7 us  [around(): return (lax.ppermute(last, 'lon', up), lax.ppermute(first, 'lon', down))]
    ppermute x8 -> x6, waiting for transfers between devices: 0.02 us -> 1.94 us  [around(): return (lax.ppermute(last, 'lon', up), lax.ppermute(first, 'lon', down))]
    all_to_all x1 -> x3, waiting for transfers between devices: 0.01 us -> 1.74 us  [gathered(): return lax.all_to_all(sums, 'lon', 0, 0)]
  transfers between devices with their start and end apart: 9 -> 9, of which waited for: 0 -> 4; matrix products, arithmetic and copies ran while one was open for 12% -> 0% of each run, Pallas kernels for 17% -> 23%
where the time goes in v2:
time: 73 us; the launch traced here: 72.5 us
  Pallas kernels  35.3 us (48%)
  starting transfers between devices  27.2 us (37%)
  local copies, waits for them, and re-layouts  5.33 us (7%)
  waiting for transfers between devices  3.67 us (5%)
  between operations  0.94 us (1%)
    pallas_call x3, Pallas kernels, cached_part(): pl.pallas_call(functools.partial(cached_kernel, layer, chunk), out_shape=...  17 us
    pallas_call x3, Pallas kernels, local(): pl.pallas_call(functools.partial(active_kernel, layer, chunk, entries, fi...  15.6 us
    ppermute x6, starting transfers between devices, around(): return (lax.ppermute(last, 'lon', up), lax.ppermute(first, 'lon', down))  14.7 us
    all_to_all x3, starting transfers between devices, gathered(): return lax.all_to_all(sums, 'lon', 0, 0)  12.5 us
    unnamed x20, local copies, waits for them, and re-layouts  5.33 us
    pallas_call x1, Pallas kernels, local(): pl.pallas_call(begin_kernel, out_shape=[spread, brim, brim], in_specs=[HB...  2.71 us
    ppermute x6, waiting for transfers between devices, around(): return (lax.ppermute(last, 'lon', up), lax.ppermute(first, 'lon', down))  1.94 us
    all_to_all x3, waiting for transfers between devices, gathered(): return lax.all_to_all(sums, 'lon', 0, 0)  1.74 us
  transfers between devices with their start and end apart: 9, of which 4 were waited for; matrix products, arithmetic and copies ran while one was open for 0% of the time, Pallas kernels for 23%

profile of v2, /device:TPU:0, one launch (start us, length us, event | category | flops | bytes accessed | tf_op | source)
XLA Modules:
  0.0 72.5 jit_solution(5574809281878528912)
XLA Ops:
  0.6 0.0 copy-start.9
  0.6 2.7 %begin.1 = (f32[16,2,192]{2,1,0:T(2,128)}, bf16[8,90,192]{2,1,0:T(8,128)(2,1)S(1)}, bf16[8,90,192]{2,1,0:T(8,128)(2,1)S(1)}) custom-call(bf16[2,90,8,192]{3,2,1,0:T(8,128)(2,1)} %refs_8_.1, bf16[3,2,90,8,192]{4,3,2,1,0:T(8,128)(2,1)} %caches.7), custom_call_target="tpu_custom_call" | custom-call | tf_op jit(solution)/shard_map/begin/pallas_call | solution.py:343
  3.4 0.5 collective-permute-start
  3.9 5.0 %collective-permute-start.1 = (bf16[8,90,192]{2,1,0:T(8,128)(2,1)S(1)}, bf16[8,90,192]{2,1,0:T(8,128)(2,1)S(1)}, u32[]{:S(2)}, u32[]{:S(2)}) collective-permute-start(bf16[8,90,192]{2,1,0:T(8,128)(2,1)S(1)} %get-tuple-element.16), channel_id=1, source_target_pairs={{1,0},{2,1},{3,2},{4,3},{5,4},{6,5},{7,6},{8,7},{9,8},{10,9},{11,1... | collective-permute-start | bytes 829448 | tf_op jit(solution)/shard_map/ppermute | solution.py:331
  9.0 3.6 %all-to-all-start = ((f32[16,2,192]{2,1,0:T(2,128)}), f32[16,2,192]{2,1,0:T(2,128)S(1)}, u32[]{:S(2)}, u32[]{:S(2)}) async-start(f32[16,2,192]{2,1,0:T(2,128)} %get-tuple-element.17), calls=%async_computation | async-start | bytes 65536 | tf_op jit(solution)/shard_map/all_to_all | solution.py:334
  12.6 1.9 %collective-permute-done.before.refs_1_ = bf16[8,90,192]{2,1,0:T(8,128)(2,1)S(1)} collective-permute-done((bf16[8,90,192]{2,1,0:T(8,128)(2,1)S(1)}, bf16[8,90,192]{2,1,0:T(8,128)(2,1)S(1)}, u32[]{:S(2)}, u32[]{:S(2)}) %collective-permute-start) | collective-permute-done | bytes 276512 | tf_op jit(solution)/shard_map/ppermute | solution.py:331
  14.4 0.0 copy-start.1
  14.4 0.1 collective-permute-done.1.after.refs_2_
  14.5 0.0 copy-start.3
  14.5 0.7 copy-done.1
  15.2 0.1 copy-done.3
  15.3 0.0 copy-done.9
  15.3 0.0 copy-start
  15.3 0.0 copy-start.7
  15.3 0.0 copy-start.8
  15.3 5.7 %cached.3.refs_7_ = f32[2,720,192]{2,1,0:T(8,128)S(1)} custom-call(bf16[3,2,90,8,192]{4,3,2,1,0:T(8,128)(2,1)} %caches.7, bf16[8,90,192]{2,1,0:T(8,128)(2,1)} %copy-done.1, bf16[8,90,192]{2,1,0:T(8,128)(2,1)} %copy-done.3, bf16[3,192,5184]{2,1,0:T(8,128)(2,1)} %bitcast.1, f32[3,192]{1,0:T(4,128)S(1)} %copy-done.9), custom_call_target="tpu_custom_call" | custom-call | tf_op jit(solution)/shard_map/cached/pallas_call | solution.py:361
  21.1 0.0 all-to-all-done.refs_3_
  21.1 0.0 copy-done
  21.1 0.0 copy-done.7
  21.1 0.0 copy-done.8
  21.1 0.0 copy-start.2
  21.1 1.0 %copy-done.2 = bf16[8,90,192]{2,1,0:T(8,128)(2,1)S(1)} copy-done((bf16[8,90,192]{2,1,0:T(8,128)(2,1)S(1)}, bf16[8,90,192]{2,1,0:T(8,128)(2,1)}, u32[]{:S(2)}) %copy-start.2) | copy-done | bytes 276504
  22.1 0.0 copy-start.4
  22.1 1.0 %copy-done.4 = bf16[8,90,192]{2,1,0:T(8,128)(2,1)S(1)} copy-done((bf16[8,90,192]{2,1,0:T(8,128)(2,1)S(1)}, bf16[8,90,192]{2,1,0:T(8,128)(2,1)}, u32[]{:S(2)}) %copy-start.4) | copy-done | bytes 276504
  23.1 6.1 %active.3 = (f32[2,2,720,128]{3,2,1,0:T(8,128)S(1)}, bf16[3,2,90,8,192]{4,3,2,1,0:T(8,128)(2,1)}, f32[16,2,192]{2,1,0:T(2,128)}, f32[2,2,90,128]{3,2,1,0:T(8,128)}, f32[2,2,90,128]{3,2,1,0:T(8,128)}) custom-call(bf16[2,90,8,192]{3,2,1,0:T(8,128)(2,1)S(1)} %copy-done, bf16[8,90,192]{2,1,0:T(8,128)(2,1)S(1)} %copy-done.2, bf16[8,90,192]{2,1,0:T(8,128)(2,1)S(1)} %copy-done.4, ...), custom_call_target="tpu_custom_call" | custom-call | tf_op jit(solution)/shard_map/active/pallas_call | solution.py:401
  29.2 0.0 copy-start.5
  29.2 1.1 %copy-done.5 = f32[2,2,720,128]{3,2,1,0:T(8,128)} copy-done((f32[2,2,720,128]{3,2,1,0:T(8,128)}, f32[2,2,720,128]{3,2,1,0:T(8,128)S(1)}, u32[]{:S(2)}) %copy-start.5) | copy-done | bytes 1474584
  30.3 3.9 %collective-permute-start.2 = (f32[2,2,90,128]{3,2,1,0:T(8,128)}, f32[2,2,90,128]{3,2,1,0:T(8,128)S(1)}, u32[]{:S(2)}, u32[]{:S(2)}) collective-permute-start(f32[2,2,90,128]{3,2,1,0:T(8,128)} %get-tuple-element.19), channel_id=1, source_target_pairs={{0,1},{1,2},{2,3},{3,4},{4,5},{5,6},{6,7},{7,8},{8,9},{9,10},{10,1... | collective-permute-start | bytes 552968 | tf_op jit(solution)/shard_map/ppermute | solution.py:331
  34.2 0.7 %collective-permute-start.3 = (f32[2,2,90,128]{3,2,1,0:T(8,128)}, f32[2,2,90,128]{3,2,1,0:T(8,128)S(1)}, u32[]{:S(2)}, u32[]{:S(2)}) collective-permute-start(f32[2,2,90,128]{3,2,1,0:T(8,128)} %get-tuple-element.20), channel_id=1, source_target_pairs={{1,0},{2,1},{3,2},{4,3},{5,4},{6,5},{7,6},{8,7},{9,8},{10,9},{11,1... | collective-permute-start | bytes 552968 | tf_op jit(solution)/shard_map/ppermute | solution.py:331
  34.9 5.2 %all-to-all-start.1 = ((f32[16,2,192]{2,1,0:T(2,128)}), f32[16,2,192]{2,1,0:T(2,128)S(1)}, u32[]{:S(2)}, u32[]{:S(2)}) async-start(f32[16,2,192]{2,1,0:T(2,128)} %get-tuple-element.21), calls=%async_computation.1 | async-start | bytes 65536 | tf_op jit(solution)/shard_map/all_to_all | solution.py:334
  40.2 5.7 %cached.4.refs_7_ = f32[2,720,192]{2,1,0:T(8,128)S(1)} custom-call(bf16[3,2,90,8,192]{4,3,2,1,0:T(8,128)(2,1)} %caches.7, bf16[8,90,192]{2,1,0:T(8,128)(2,1)} %copy-done.1, bf16[8,90,192]{2,1,0:T(8,128)(2,1)} %copy-done.3, bf16[3,192,5184]{2,1,0:T(8,128)(2,1)} %bitcast.3, f32[3,192]{1,0:T(4,128)S(1)} %copy-done.9), custom_call_target="tpu_custom_call" | custom-call | tf_op jit(solution)/shard_map/cached/pallas_call | solution.py:361
  45.9 1.0 %all-to-all-done.1.refs_3_ = f32[16,2,192]{2,1,0:T(2,128)S(1)} async-done(((f32[16,2,192]{2,1,0:T(2,128)}), f32[16,2,192]{2,1,0:T(2,128)S(1)}, u32[]{:S(2)}, u32[]{:S(2)}) %all-to-all-start.1) | async-done | bytes 24608 | tf_op jit(solution)/shard_map/all_to_all | solution.py:334
  46.8 0.0 collective-permute-done.2.refs_1_
  46.8 0.0 collective-permute-done.3.refs_2_
  46.8 0.0 copy-start.6
  46.8 1.4 %copy-done.6 = f32[2,2,720,128]{3,2,1,0:T(8,128)S(1)} copy-done((f32[2,2,720,128]{3,2,1,0:T(8,128)S(1)}, f32[2,2,720,128]{3,2,1,0:T(8,128)}, u32[]{:S(2)}) %copy-start.6) | copy-done | bytes 1474584
  48.2 4.9 %active.4 = (f32[2,2,720,128]{3,2,1,0:T(8,128)S(1)}, bf16[3,2,90,8,192]{4,3,2,1,0:T(8,128)(2,1)}, f32[16,2,192]{2,1,0:T(2,128)}, f32[2,2,90,128]{3,2,1,0:T(8,128)}, f32[2,2,90,128]{3,2,1,0:T(8,128)}) custom-call(f32[2,2,720,128]{3,2,1,0:T(8,128)S(1)} %copy-done.6, ...), custom_call_target="tpu_custom_call", output_to_operand_aliasing={{1}: (9, {})} | custom-call | tf_op jit(solution)/shard_map/active/pallas_call | solution.py:401
  53.1 0.1 collective-permute-start.4
  53.2 4.4 %collective-permute-start.5 = (f32[2,2,90,128]{3,2,1,0:T(8,128)}, f32[2,2,90,128]{3,2,1,0:T(8,128)S(1)}, u32[]{:S(2)}, u32[]{:S(2)}) collective-permute-start(f32[2,2,90,128]{3,2,1,0:T(8,128)} %get-tuple-element.25), channel_id=1, source_target_pairs={{1,0},{2,1},{3,2},{4,3},{5,4},{6,5},{7,6},{8,7},{9,8},{10,9},{11,1... | collective-permute-start | bytes 552968 | tf_op jit(solution)/shard_map/ppermute | solution.py:331
  57.6 3.7 %all-to-all-start.2 = ((f32[16,2,192]{2,1,0:T(2,128)}), f32[16,2,192]{2,1,0:T(2,128)S(1)}, u32[]{:S(2)}, u32[]{:S(2)}) async-start(f32[16,2,192]{2,1,0:T(2,128)} %get-tuple-element.26), calls=%async_computation.2 | async-start | bytes 65536 | tf_op jit(solution)/shard_map/all_to_all | solution.py:334
  61.3 5.6 %cached.5.refs_7_ = f32[2,720,192]{2,1,0:T(8,128)S(1)} custom-call(bf16[3,2,90,8,192]{4,3,2,1,0:T(8,128)(2,1)} %caches.7, bf16[8,90,192]{2,1,0:T(8,128)(2,1)} %copy-done.1, bf16[8,90,192]{2,1,0:T(8,128)(2,1)} %copy-done.3, bf16[3,192,5184]{2,1,0:T(8,128)(2,1)} %bitcast.5, f32[3,192]{1,0:T(4,128)S(1)} %copy-done.9), custom_call_target="tpu_custom_call" | custom-call | tf_op jit(solution)/shard_map/cached/pallas_call | solution.py:361
  67.0 0.8 %all-to-all-done.2.refs_3_ = f32[16,2,192]{2,1,0:T(2,128)S(1)} async-done(((f32[16,2,192]{2,1,0:T(2,128)}), f32[16,2,192]{2,1,0:T(2,128)S(1)}, u32[]{:S(2)}, u32[]{:S(2)}) %all-to-all-start.2) | async-done | bytes 24608 | tf_op jit(solution)/shard_map/all_to_all | solution.py:334
  67.7 0.0 collective-permute-done.4.refs_1_
  67.7 0.0 collective-permute-done.5.refs_2_
  67.7 4.6 %active.5 = (bf16[2,90,8,192]{3,2,1,0:T(8,128)(2,1)}, bf16[3,2,90,8,192]{4,3,2,1,0:T(8,128)(2,1)}) custom-call(f32[2,2,720,128]{3,2,1,0:T(8,128)S(1)} %get-tuple-element.23.refs_0_, f32[2,2,90,128]{3,2,1,0:T(8,128)S(1)} %collective-permute-done.4.refs_1_, f32[2,2,90,128]{3,2,1,0:T(8,128)S(1)} %collective-permute-done.5.refs_2_, ...), custom_call_target="tpu_custom_call", output_to_operand_aliasing={{1}: (8, {})} | custom-call | tf_op jit(solution)/shard_map/active/pallas_call | solution.py:401
Async XLA Ops:
  0.6 14.7 %copy-start.9 = (f32[3,192]{1,0:T(4,128)S(1)}, f32[3,192]{1,0:T(4,128)}, u32[]{:S(2)}) copy-start(f32[3,192]{1,0:T(4,128)} %bias.5) | copy-start | bytes 6916
  3.4 11.1 %collective-permute-start = (bf16[8,90,192]{2,1,0:T(8,128)(2,1)S(1)}, bf16[8,90,192]{2,1,0:T(8,128)(2,1)S(1)}, u32[]{:S(2)}, u32[]{:S(2)}) collective-permute-start(bf16[8,90,192]{2,1,0:T(8,128)(2,1)S(1)} %get-tuple-element.15), channel_id=1, source_target_pairs={{0,1},{1,2},{2,3},{3,4},{4,5},{5,6},{6,7},{7,8},{8,9},{9,10},{10,1... | collective-permute-start | bytes 829448 | tf_op jit(solution)/shard_map/ppermute | solution.py:331
  3.9 10.6 %collective-permute-start.1 = (bf16[8,90,192]{2,1,0:T(8,128)(2,1)S(1)}, bf16[8,90,192]{2,1,0:T(8,128)(2,1)S(1)}, u32[]{:S(2)}, u32[]{:S(2)}) collective-permute-start(bf16[8,90,192]{2,1,0:T(8,128)(2,1)S(1)} %get-tuple-element.16), channel_id=1, source_target_pairs={{1,0},{2,1},{3,2},{4,3},{5,4},{6,5},{7,6},{8,7},{9,8},{10,9},{11,1... | collective-permute-start | bytes 829448 | tf_op jit(solution)/shard_map/ppermute | solution.py:331
  9.0 12.1 %all-to-all-start = ((f32[16,2,192]{2,1,0:T(2,128)}), f32[16,2,192]{2,1,0:T(2,128)S(1)}, u32[]{:S(2)}, u32[]{:S(2)}) async-start(f32[16,2,192]{2,1,0:T(2,128)} %get-tuple-element.17), calls=%async_computation | async-start | bytes 65536 | tf_op jit(solution)/shard_map/all_to_all | solution.py:334
  14.4 0.7 %copy-start.1 = (bf16[8,90,192]{2,1,0:T(8,128)(2,1)}, bf16[8,90,192]{2,1,0:T(8,128)(2,1)S(1)}, u32[]{:S(2)}) copy-start(bf16[8,90,192]{2,1,0:T(8,128)(2,1)S(1)} %collective-permute-done.before.refs_1_) | copy-start | bytes 829444
  14.5 0.8 %copy-start.3 = (bf16[8,90,192]{2,1,0:T(8,128)(2,1)}, bf16[8,90,192]{2,1,0:T(8,128)(2,1)S(1)}, u32[]{:S(2)}) copy-start(bf16[8,90,192]{2,1,0:T(8,128)(2,1)S(1)} %collective-permute-done.1.after.refs_2_) | copy-start | bytes 829444
  15.3 5.7 %copy-start = (bf16[2,90,8,192]{3,2,1,0:T(8,128)(2,1)S(1)}, bf16[2,90,8,192]{3,2,1,0:T(8,128)(2,1)}, u32[]{:S(2)}) copy-start(bf16[2,90,8,192]{3,2,1,0:T(8,128)(2,1)} %refs_8_.1) | copy-start | bytes 1658884
  15.3 5.8 %copy-start.7 = (f32[3,192]{1,0:T(4,128)S(1)}, f32[3,192]{1,0:T(4,128)}, u32[]{:S(2)}) copy-start(f32[3,192]{1,0:T(4,128)} %refs_4_.5) | copy-start | bytes 6916
  15.3 5.8 %copy-start.8 = (f32[3,192]{1,0:T(4,128)S(1)}, f32[3,192]{1,0:T(4,128)}, u32[]{:S(2)}) copy-start(f32[3,192]{1,0:T(4,128)} %refs_5_.5) | copy-start | bytes 6916
  21.1 1.0 %copy-start.2 = (bf16[8,90,192]{2,1,0:T(8,128)(2,1)S(1)}, bf16[8,90,192]{2,1,0:T(8,128)(2,1)}, u32[]{:S(2)}) copy-start(bf16[8,90,192]{2,1,0:T(8,128)(2,1)} %copy-done.1) | copy-start | bytes 829444
  22.1 1.0 %copy-start.4 = (bf16[8,90,192]{2,1,0:T(8,128)(2,1)S(1)}, bf16[8,90,192]{2,1,0:T(8,128)(2,1)}, u32[]{:S(2)}) copy-start(bf16[8,90,192]{2,1,0:T(8,128)(2,1)} %copy-done.3) | copy-start | bytes 829444
  29.2 1.1 %copy-start.5 = (f32[2,2,720,128]{3,2,1,0:T(8,128)}, f32[2,2,720,128]{3,2,1,0:T(8,128)S(1)}, u32[]{:S(2)}) copy-start(f32[2,2,720,128]{3,2,1,0:T(8,128)S(1)} %get-tuple-element.18.refs_0_) | copy-start | bytes 4423684
  30.3 16.5 %collective-permute-start.2 = (f32[2,2,90,128]{3,2,1,0:T(8,128)}, f32[2,2,90,128]{3,2,1,0:T(8,128)S(1)}, u32[]{:S(2)}, u32[]{:S(2)}) collective-permute-start(f32[2,2,90,128]{3,2,1,0:T(8,128)} %get-tuple-element.19), channel_id=1, source_target_pairs={{0,1},{1,2},{2,3},{3,4},{4,5},{5,6},{6,7},{7,8},{8,9},{9,10},{10,1... | collective-permute-start | bytes 552968 | tf_op jit(solution)/shard_map/ppermute | solution.py:331
  34.2 12.6 %collective-permute-start.3 = (f32[2,2,90,128]{3,2,1,0:T(8,128)}, f32[2,2,90,128]{3,2,1,0:T(8,128)S(1)}, u32[]{:S(2)}, u32[]{:S(2)}) collective-permute-start(f32[2,2,90,128]{3,2,1,0:T(8,128)} %get-tuple-element.20), channel_id=1, source_target_pairs={{1,0},{2,1},{3,2},{4,3},{5,4},{6,5},{7,6},{8,7},{9,8},{10,9},{11,1... | collective-permute-start | bytes 552968 | tf_op jit(solution)/shard_map/ppermute | solution.py:331
  34.9 11.9 %all-to-all-start.1 = ((f32[16,2,192]{2,1,0:T(2,128)}), f32[16,2,192]{2,1,0:T(2,128)S(1)}, u32[]{:S(2)}, u32[]{:S(2)}) async-start(f32[16,2,192]{2,1,0:T(2,128)} %get-tuple-element.21), calls=%async_computation.1 | async-start | bytes 65536 | tf_op jit(solution)/shard_map/all_to_all | solution.py:334
  46.8 1.4 %copy-start.6 = (f32[2,2,720,128]{3,2,1,0:T(8,128)S(1)}, f32[2,2,720,128]{3,2,1,0:T(8,128)}, u32[]{:S(2)}) copy-start(f32[2,2,720,128]{3,2,1,0:T(8,128)} %copy-done.5) | copy-start | bytes 4423684
  53.1 14.6 %collective-permute-start.4 = (f32[2,2,90,128]{3,2,1,0:T(8,128)}, f32[2,2,90,128]{3,2,1,0:T(8,128)S(1)}, u32[]{:S(2)}, u32[]{:S(2)}) collective-permute-start(f32[2,2,90,128]{3,2,1,0:T(8,128)} %get-tuple-element.24), channel_id=1, source_target_pairs={{0,1},{1,2},{2,3},{3,4},{4,5},{5,6},{6,7},{7,8},{8,9},{9,10},{10,1... | collective-permute-start | bytes 552968 | tf_op jit(solution)/shard_map/ppermute | solution.py:331
  53.2 14.5 %collective-permute-start.5 = (f32[2,2,90,128]{3,2,1,0:T(8,128)}, f32[2,2,90,128]{3,2,1,0:T(8,128)S(1)}, u32[]{:S(2)}, u32[]{:S(2)}) collective-permute-start(f32[2,2,90,128]{3,2,1,0:T(8,128)} %get-tuple-element.25), channel_id=1, source_target_pairs={{1,0},{2,1},{3,2},{4,3},{5,4},{6,5},{7,6},{8,7},{9,8},{10,9},{11,1... | collective-permute-start | bytes 552968 | tf_op jit(solution)/shard_map/ppermute | solution.py:331
  57.6 10.1 %all-to-all-start.2 = ((f32[16,2,192]{2,1,0:T(2,128)}), f32[16,2,192]{2,1,0:T(2,128)S(1)}, u32[]{:S(2)}, u32[]{:S(2)}) async-start(f32[16,2,192]{2,1,0:T(2,128)} %get-tuple-element.26), calls=%async_computation.2 | async-start | bytes 65536 | tf_op jit(solution)/shard_map/all_to_all | solution.py:334

commit v3 on v2

--- a/solution.py
+++ b/solution.py
@@ -2,6 +2,7 @@
 
 import jax
 import jax.numpy as jnp
+import numpy as np
 from jax import lax
 from jax.experimental import pallas as pl
 from jax.experimental.pallas import tpu as pltpu
@@ -12,12 +13,13 @@
 LANES = 128
 COLS = 8
 SLABS = 10
+STEPS = 12
 VMEM = pl.BlockSpec(memory_space=pltpu.VMEM)
 HBM = pl.BlockSpec(memory_space=pltpu.HBM)
 
 
-def silu(u):
-    return u * (0.5 + 0.5 * jnp.tanh(0.5 * u))
+def silu_of_twice(u):
+    return u + u * jnp.tanh(u)
 
 
 def twice(v):
@@ -28,7 +30,7 @@
     return jnp.concatenate([a, b], axis=0).astype(jnp.bfloat16)
 
 
-def build_slabs(rows, row_of, edge_of, slab):
+def build_slabs(rows, row_of, edge_of, slab, steps):
     lane = lax.broadcasted_iota(jnp.int32, (COLS, LANES), 1)
     low = lane < LANES // 2
     column = lax.broadcasted_iota(jnp.int32, (COLS, LANES), 0)
@@ -62,19 +64,29 @@
         put(6, k, pair(one[3], two[3]))
         put(7, k, pair(before[3], one[3]))
         put(9, k, pair(one[4], two[4]))
-
         if older is not None:
             put(8, k - 1, pair(jnp.where(low, oldest, before[4]), jnp.where(low, older, one[4])))
-
         return two, one[4], before[4]
 
     count = rows // 2
-    begun = step(0, ((zero,) * 5, None, None))
-    before, older, oldest = lax.fori_loop(1, count, step, begun, unroll=4)
+    carry = step(0, ((zero,) * 5, None, None))
+    if steps:
+        for k in range(1, count):
+            carry = step(k, carry)
+            if k % steps == 0:
+                yield
+    else:
+        carry = lax.fori_loop(1, count, step, carry, unroll=4)
+    before, older, oldest = carry
     for r in range(3):
         put(3 + r, count, pair(before[r], zero))
     put(7, count, pair(before[3], zero))
     put(8, count - 1, pair(jnp.where(low, oldest, before[4]), jnp.where(low, older, zero)))
+
+
+def drain(pieces):
+    for _ in pieces:
+        pass
 
 
 def slab_rows(slab, start, size):
@@ -144,7 +156,7 @@
 
 
 def cached_kernel(layer, chunk, caches, before, after, weights, bias, out, *scratches):
-    edges, slab, cache, brims, weight, sem = scratches
+    edges, *slabs, cache, brims, weight, sem = scratches
     _, frames, rows, cols, channels = caches.shape
     where = pl.ds((layer + 1) * frames, frames)
     begun = [pltpu.make_async_copy(caches.at[layer], cache, sem.at[0])]
@@ -158,6 +170,7 @@
     fetch.start()
     for copy in begun:
         copy.wait()
+    pieces = []
     for frame in range(frames):
         for side in range(2):
             value = brims[side, frame].astype(jnp.float32)
@@ -171,78 +184,95 @@
         def edge_of(h, part, frame=frame):
             return [edges[side, part, frame, pl.ds(h, COLS, stride=0), :] for side in (0, 1)]
 
-        build_slabs(rows, row_of, edge_of, slab.at[frame])
+        steps = STEPS if frame else None
+        pieces.append(build_slabs(rows, row_of, edge_of, slabs[frame], steps))
+    drain(pieces[0])
     fetch.wait()
     taps = [tap_lanes(weight, p * 9 * channels, channels) for p in range(2)]
     constant = bias[layer : layer + 1, :]
-    for i in range(rows * cols // chunk):
-        start = i * chunk
+    for start in range(0, rows * cols, chunk):
         here = pl.ds(start, chunk)
-        out[0, here, :] = (
-            product(slab.at[0], start, chunk, taps[0])
-            + product(slab.at[1], start, chunk, taps[1])
-            + constant
-        )
-        out[1, here, :] = product(slab.at[1], start, chunk, taps[0]) + constant
+        out[0, here, :] = product(slabs[0], start, chunk, taps[0]) + constant
+        next(pieces[1], None)
+    drain(pieces[1])
+    for start in range(0, rows * cols, chunk):
+        here = pl.ds(start, chunk)
+        out[0, here, :] += product(slabs[1], start, chunk, taps[1])
+        out[1, here, :] = product(slabs[1], start, chunk, taps[0]) + constant
 
 
 def halves(value):
     return value[..., :LANES], value[..., LANES:]
 
 
+def group_means(stats, same, entries):
+    total = jnp.sum(stats, axis=0)
+    high = total.astype(jnp.bfloat16)
+    left = total - high.astype(jnp.float32)
+    middle = left.astype(jnp.bfloat16)
+    low = (left - middle.astype(jnp.float32)).astype(jnp.bfloat16)
+    split = jnp.concatenate([high, middle, low], axis=0)
+    sums = jnp.dot(split, same, preferred_element_type=jnp.float32)
+    return (sums[0:2] + sums[2:4] + sums[4:6]) / entries
+
+
 def active_kernel(layer, chunk, entries, final, *refs):
-    x, before, after, stats, gain, shift, weights, part = refs[:8]
-    rest = refs[8:]
+    x, before, after, stats, gain, shift, weights, part, same = refs[:9]
+    rest = refs[9:]
     residual = None
     if layer == 1:
         residual, *rest = rest
     if layer > 0:
         _, *rest = rest
     if final:
-        y, carried, edges, slab, kept, held, weight, sem = rest
+        y, carried, *rest = rest
     else:
-        y, carried, sums, first, last, edges, slab, kept, held, weight, sem = rest
+        y, carried, sums, first, last, *rest = rest
+    edges, *slabs, kept, held, brims, partial, weight, sem = rest
     frames, rows, cols, channels = kept.shape
     places = rows * cols
-    members = channels // GROUPS
+    half = channels - LANES
     skipped = weights.shape[2] - weight.shape[1]
-    fetch = pltpu.make_async_copy(
-        weights.at[layer, :, pl.ds(skipped, weight.shape[1])], weight, sem.at[1]
-    )
-    fetch.start()
+    fetch = [
+        pltpu.make_async_copy(
+            weights.at[layer, :, pl.ds(skipped, weight.shape[1])], weight, sem.at[1]
+        )
+    ]
+    brim = []
+    if layer == 0:
+        for side, ref in enumerate((before, after)):
+            brim.append(
+                pltpu.make_async_copy(ref.at[pl.ds(0, frames)], brims.at[side], sem.at[3 + side])
+            )
     if residual is not None:
-        source = pltpu.make_async_copy(residual, held, sem.at[2])
-        source.start()
-
-    total = jnp.sum(stats[...], axis=0)
-    own = lax.broadcasted_iota(jnp.int32, (channels, channels), 0) // members
-    other = lax.broadcasted_iota(jnp.int32, (channels, channels), 1) // members
-    same = jnp.where(own == other, 1.0, 0.0)
-    means = (
-        jnp.dot(
-            total, same, precision=lax.Precision.HIGHEST, preferred_element_type=jnp.float32
-        )
-        / entries
-    )
+        fetch.append(pltpu.make_async_copy(residual, held, sem.at[2]))
+    for copy in brim + fetch:
+        copy.start()
+
+    means = group_means(stats[...], same[...], entries)
     average = means[0:1]
     variance = means[1:2] - average * average
     scale = lax.rsqrt(variance + EPSILON) * gain[layer : layer + 1, :]
     offset = shift[layer : layer + 1, :] - average * scale
+    scale, offset = 0.5 * scale, 0.5 * offset
     scales = (scale[:, :LANES], twice(scale[:, LANES:]))
     offsets = (offset[:, :LANES], twice(offset[:, LANES:]))
 
-    def act(part, value):
-        return silu(value * scales[part] + offsets[part])
-
+    def act(index, value):
+        return silu_of_twice(value * scales[index] + offsets[index])
+
+    for copy in brim:
+        copy.wait()
+    pieces = []
     for frame in range(frames):
         for side, ref in enumerate((before, after)):
-            for part_index in range(2):
+            for index in range(2):
                 if layer:
-                    value = ref[part_index, frame]
+                    value = ref[index, frame].astype(jnp.float32)
                 else:
-                    value = halves(ref[frame].astype(jnp.float32))[part_index]
-                    value = twice(value) if part_index else value
-                edges[side, part_index, frame] = act(part_index, value)
+                    value = halves(brims[side, frame].astype(jnp.float32))[index]
+                    value = twice(value) if index else value
+                edges[side, index, frame] = act(index, value)
 
         def row_of(h, frame=frame):
             if layer:
@@ -252,68 +282,69 @@
                 main, other = halves(x[frame, h].astype(jnp.float32))
                 other = twice(other)
             main, other = act(0, main), act(1, other)
-            whole = jnp.concatenate([main, other[:, : channels - LANES]], axis=1)
+            whole = jnp.concatenate([main, other[:, :half]], axis=1)
             kept[frame, h] = whole.astype(jnp.bfloat16)
             return main, other
 
-        def edge_of(h, part, frame=frame):
-            return [edges[side, part, frame, pl.ds(h, COLS, stride=0), :] for side in (0, 1)]
-
-        build_slabs(rows, row_of, edge_of, slab.at[frame])
+        def edge_of(h, index, frame=frame):
+            return [edges[side, index, frame, pl.ds(h, COLS, stride=0), :] for side in (0, 1)]
+
+        steps = STEPS if frame else None
+        pieces.append(build_slabs(rows, row_of, edge_of, slabs[frame], steps))
+    drain(pieces[0])
+    for copy in fetch:
+        copy.wait()
+    taps = [tap_lanes(weight, p * 9 * channels - skipped, channels) for p in (1, 2)]
+    moments = [jnp.zeros((COLS, channels), jnp.float32)] * 2
+
+    def finish(t, start, value, moments):
+        here, span = pl.ds(start, chunk), pl.ds(start // COLS, chunk // COLS)
+        shape = (chunk // COLS, COLS, channels)
+        if final:
+            own = jnp.concatenate([x[0, t, here, :], x[1, t, here, :half]], axis=1)
+            y[t, span] = (value + own).reshape(shape).astype(jnp.bfloat16)
+            return moments
+        if residual is not None:
+            value = value + held[t, span].astype(jnp.float32).reshape(chunk, channels)
+        main, other = halves(value)
+        y[0, t, here, :] = main
+        y[1, t, here, :] = twice(other)
+        folded = value.reshape(shape)
+        return [
+            moments[0] + jnp.sum(folded, axis=0),
+            moments[1] + jnp.sum(folded * folded, axis=0),
+        ]
+
+    starts = range(0, places, chunk)
+    for start in starts:
+        here = pl.ds(start, chunk)
+        partial[here, :] = part[1, here, :] + product(slabs[0], start, chunk, taps[0])
+        next(pieces[1], None)
+    for start in starts:
+        value = product(slabs[0], start, chunk, taps[1]) + part[0, pl.ds(start, chunk), :]
+        next(pieces[1], None)
+        moments = finish(0, start, value, moments)
+    drain(pieces[1])
     copy = pltpu.make_async_copy(kept, carried.at[layer], sem.at[0])
     copy.start()
-    fetch.wait()
-    if residual is not None:
-        source.wait()
-    taps = [tap_lanes(weight, p * 9 * channels - skipped, channels) for p in (1, 2)]
-    sum_rows = jnp.zeros((COLS, channels), jnp.float32)
-    square_rows = jnp.zeros((COLS, channels), jnp.float32)
-    for i in range(places // chunk):
-        start = i * chunk
-        here = pl.ds(start, chunk)
-        span = pl.ds(start // COLS, chunk // COLS)
-        values = (
-            product(slab.at[0], start, chunk, taps[1]) + part[0, here, :],
-            product(slab.at[0], start, chunk, taps[0])
-            + product(slab.at[1], start, chunk, taps[1])
-            + part[1, here, :],
-        )
-        for t, value in enumerate(values):
-            if final:
-                held = [x[0, t, here, :], x[1, t, here, : channels - LANES]]
-                value = value + jnp.concatenate(held, axis=1)
-                shape = (chunk // COLS, COLS, channels)
-                y[t, span] = value.reshape(shape).astype(jnp.bfloat16)
-                continue
-            if residual is not None:
-                value = value + held[t, span].astype(jnp.float32).reshape(chunk, channels)
-            main, other = halves(value)
-            y[0, t, here, :] = main
-            y[1, t, here, :] = twice(other)
-            folded = value.reshape(chunk // COLS, COLS, channels)
-            sum_rows = sum_rows + jnp.sum(folded, axis=0)
-            square_rows = square_rows + jnp.sum(folded * folded, axis=0)
+    for start in starts:
+        value = product(slabs[1], start, chunk, taps[1]) + partial[pl.ds(start, chunk), :]
+        moments = finish(1, start, value, moments)
     if not final:
-        both = jnp.concatenate(
-            [
-                jnp.sum(sum_rows, axis=0, keepdims=True),
-                jnp.sum(square_rows, axis=0, keepdims=True),
-            ],
-            axis=0,
-        )
-        sums[...] = jnp.broadcast_to(both[None], sums.shape)
+        both = [jnp.sum(v, axis=0, keepdims=True) for v in moments]
+        sums[...] = jnp.broadcast_to(jnp.concatenate(both, axis=0)[None], sums.shape)
         for i in range(2):
             for t in range(frames):
-                first[i, t] = y[i, t, pl.ds(0, rows, stride=COLS), :]
-                last[i, t] = y[i, t, pl.ds(COLS - 1, rows, stride=COLS), :]
+                for out, column in ((first, 0), (last, cols - 1)):
+                    edge = y[i, t, pl.ds(column, rows, stride=cols), :]
+                    out[i, t] = edge.astype(jnp.bfloat16)
     copy.wait()
 
 
 def scratch(frames, rows):
     return [
         pltpu.VMEM((2, 2, frames, rows, LANES), jnp.float32),
-        pltpu.VMEM((frames, SLABS, rows * COLS + 16, LANES), jnp.bfloat16),
-    ]
+    ] + [pltpu.VMEM((SLABS, rows * COLS + 16, LANES), jnp.bfloat16)] * frames
 
 
 def local(video_span, caches, norm_gains, shifts, weights, biases):
@@ -324,7 +355,7 @@
     entries = frames * places * peers * (channels // GROUPS)
     up = [(i, (i + 1) % peers) for i in range(peers)]
     down = [(j, i) for i, j in up]
-    chunk = 240
+    chunk = 360
     skipped = 9 * channels // LANES * LANES
 
     def around(first, last):
@@ -353,8 +384,10 @@
         compiler_params=pltpu.CompilerParams(vmem_limit_bytes=24 << 20),
         name="begin",
     )(video, caches)
-    before, after = around(first, last)
-    brims = [in_hbm(before), in_hbm(after)]
+    brims = [in_hbm(brim) for brim in around(first, last)]
+    before, after = brims
+    members = channels // GROUPS
+    same = jnp.asarray(np.kron(np.eye(GROUPS), np.ones((members, members))), jnp.bfloat16)
     stats = gathered(sums)
 
     def cached_part(layer):
@@ -379,8 +412,10 @@
     for layer in range(layers):
         final = layer == layers - 1
         operands = [x, before, after, stats, norm_gains, shifts, turned]
-        operands.append(cached_part(layer))
-        specs = [VMEM] * 6 + [HBM, VMEM]
+        operands += [cached_part(layer), same]
+        specs = [VMEM] * 6 + [HBM, VMEM, VMEM]
+        if layer == 0:
+            specs[1:3] = [HBM, HBM]
         aliases = {}
         if layer == 1:
             operands.append(video)
@@ -395,7 +430,7 @@
         outs = [state, jax.ShapeDtypeStruct(caches.shape, jnp.bfloat16)]
         out_specs = [VMEM, HBM]
         if not final:
-            edge = jax.ShapeDtypeStruct((2, frames, rows, LANES), jnp.float32)
+            edge = jax.ShapeDtypeStruct((2, frames, rows, LANES), jnp.bfloat16)
             outs += [spread, edge, edge]
             out_specs += [VMEM] * 3
         results = pl.pallas_call(
@@ -407,8 +442,10 @@
             + [
                 pltpu.VMEM(video_span.shape, jnp.bfloat16),
                 pltpu.VMEM(video_span.shape, jnp.bfloat16),
+                pltpu.VMEM((2, frames, rows, channels), jnp.bfloat16),
+                pltpu.VMEM((places, channels), jnp.float32),
                 pltpu.VMEM((channels, 27 * channels - skipped), weights.dtype),
-                pltpu.SemaphoreType.DMA((3,)),
+                pltpu.SemaphoreType.DMA((5,)),
             ],
             compiler_params=pltpu.CompilerParams(vmem_limit_bytes=24 << 20),
             input_output_aliases=aliases,

time: 73 us -> 71.2 us (0.975)
  Pallas kernels: 35.3 us -> 32.7 us
  waiting for transfers between devices: 3.67 us -> 5.82 us
  local copies, waits for them, and re-layouts: 5.33 us -> 3.96 us
    pallas_call x3, Pallas kernels: 17 us -> 13.8 us  [cached_part(): pl.pallas_call(functools.partial(cached_kernel, layer, chunk), out_shape=...]
    all_to_all x3, waiting for transfers between devices: 1.74 us -> 3.88 us  [gathered(): return lax.all_to_all(sums, 'lon', 0, 0)]
    unnamed x20 -> x18, local copies, waits for them, and re-layouts: 5.33 us -> 3.96 us
  transfers between devices with their start and end apart: 9 -> 9, of which waited for: 4 -> 4; matrix products, arithmetic and copies ran while one was open for 0% -> 0% of each run, Pallas kernels for 23% -> 20%
where the time goes in v3:
time: 71.2 us; the launch traced here: 70.7 us
  Pallas kernels  32.7 us (46%)
  starting transfers between devices  27.2 us (38%)
  waiting for transfers between devices  5.82 us (8%)
  local copies, waits for them, and re-layouts  3.96 us (6%)
  between operations  0.95 us (1%)
    pallas_call x3, Pallas kernels, local(): pl.pallas_call(functools.partial(active_kernel, layer, chunk, entries, fi...  16.2 us
    ppermute x6, starting transfers between devices, around(): return (lax.ppermute(last, 'lon', up), lax.ppermute(first, 'lon', down))  14.5 us
    pallas_call x3, Pallas kernels, cached_part(): pl.pallas_call(functools.partial(cached_kernel, layer, chunk), out_shape=...  13.8 us
    all_to_all x3, starting transfers between devices, gathered(): return lax.all_to_all(sums, 'lon', 0, 0)  12.7 us
    unnamed x18, local copies, waits for them, and re-layouts  3.96 us
    all_to_all x3, waiting for transfers between devices, gathered(): return lax.all_to_all(sums, 'lon', 0, 0)  3.88 us
    pallas_call x1, Pallas kernels, local(): pl.pallas_call(begin_kernel, out_shape=[spread, brim, brim], in_specs=[HB...  2.71 us
    ppermute x6, waiting for transfers between devices, around(): return (lax.ppermute(last, 'lon', up), lax.ppermute(first, 'lon', down))  1.94 us
  transfers between devices with their start and end apart: 9, of which 4 were waited for; matrix products, arithmetic and copies ran while one was open for 0% of the time, Pallas kernels for 20%

profile of v3, /device:TPU:0, one launch (start us, length us, event | category | flops | bytes accessed | tf_op | source)
XLA Modules:
  0.0 70.7 jit_solution(16818951123358611271)
XLA Ops:
  0.6 0.0 copy-start.6
  0.6 2.7 %begin.1 = (f32[16,2,192]{2,1,0:T(2,128)}, bf16[8,90,192]{2,1,0:T(8,128)(2,1)S(1)}, bf16[8,90,192]{2,1,0:T(8,128)(2,1)S(1)}) custom-call(bf16[2,90,8,192]{3,2,1,0:T(8,128)(2,1)} %refs_9_.1, bf16[3,2,90,8,192]{4,3,2,1,0:T(8,128)(2,1)} %caches.7), custom_call_target="tpu_custom_call" | custom-call | tf_op jit(solution)/shard_map/begin/pallas_call | solution.py:374
  3.4 0.5 collective-permute-start
  3.9 5.0 %collective-permute-start.1 = (bf16[8,90,192]{2,1,0:T(8,128)(2,1)S(1)}, bf16[8,90,192]{2,1,0:T(8,128)(2,1)S(1)}, u32[]{:S(2)}, u32[]{:S(2)}) collective-permute-start(bf16[8,90,192]{2,1,0:T(8,128)(2,1)S(1)} %get-tuple-element.16), channel_id=1, source_target_pairs={{1,0},{2,1},{3,2},{4,3},{5,4},{6,5},{7,6},{8,7},{9,8},{10,9},{11,1... | collective-permute-start | bytes 829448 | tf_op jit(solution)/shard_map/ppermute | solution.py:362
  9.0 3.6 %all-to-all-start = ((f32[16,2,192]{2,1,0:T(2,128)}), f32[16,2,192]{2,1,0:T(2,128)S(1)}, u32[]{:S(2)}, u32[]{:S(2)}) async-start(f32[16,2,192]{2,1,0:T(2,128)} %get-tuple-element.17), calls=%async_computation | async-start | bytes 65536 | tf_op jit(solution)/shard_map/all_to_all | solution.py:365
  12.6 1.9 %collective-permute-done.before.refs_1_ = bf16[8,90,192]{2,1,0:T(8,128)(2,1)S(1)} collective-permute-done((bf16[8,90,192]{2,1,0:T(8,128)(2,1)S(1)}, bf16[8,90,192]{2,1,0:T(8,128)(2,1)S(1)}, u32[]{:S(2)}, u32[]{:S(2)}) %collective-permute-start) | collective-permute-done | bytes 276512 | tf_op jit(solution)/shard_map/ppermute | solution.py:362
  14.4 0.0 copy-start.7
  14.4 0.1 collective-permute-done.1.after.refs_2_
  14.5 0.7 copy-done.7
  15.2 0.0 copy-start.8
  15.2 0.7 %copy-done.8 = bf16[8,90,192]{2,1,0:T(8,128)(2,1)} copy-done((bf16[8,90,192]{2,1,0:T(8,128)(2,1)}, bf16[8,90,192]{2,1,0:T(8,128)(2,1)S(1)}, u32[]{:S(2)}) %copy-start.8) | copy-done | bytes 276504
  15.9 0.0 copy-done.6
  15.9 0.0 copy-start
  15.9 0.0 copy-start.3
  15.9 0.0 copy-start.4
  16.0 0.0 copy-start.5
  16.0 4.7 %cached.3.refs_7_ = f32[2,720,192]{2,1,0:T(8,128)S(1)} custom-call(bf16[3,2,90,8,192]{4,3,2,1,0:T(8,128)(2,1)} %caches.7, bf16[8,90,192]{2,1,0:T(8,128)(2,1)} %copy-done.7, bf16[8,90,192]{2,1,0:T(8,128)(2,1)} %copy-done.8, bf16[3,192,5184]{2,1,0:T(8,128)(2,1)} %bitcast.1, f32[3,192]{1,0:T(4,128)S(1)} %copy-done.6), custom_call_target="tpu_custom_call" | custom-call | tf_op jit(solution)/shard_map/cached/pallas_call | solution.py:394
  20.6 0.0 all-to-all-done.refs_3_
  20.6 0.0 copy-done
  20.6 0.0 copy-done.3
  20.7 0.0 copy-done.4
  20.7 0.0 copy-done.5
  20.7 5.6 %active.3 = (f32[2,2,720,128]{3,2,1,0:T(8,128)S(1)}, bf16[3,2,90,8,192]{4,3,2,1,0:T(8,128)(2,1)}, f32[16,2,192]{2,1,0:T(2,128)}, bf16[2,2,90,128]{3,2,1,0:T(8,128)(2,1)S(1)}, bf16[2,2,90,128]{3,2,1,0:T(8,128)(2,1)S(1)}) custom-call(bf16[2,90,8,192]{3,2,1,0:T(8,128)(2,1)S(1)} %copy-done, bf16[8,90,192]{2,1,0:T(8,128)(2,1)} %copy-done.7, ...), custom_call_target="tpu_custom_call" | custom-call | tf_op jit(solution)/shard_map/active/pallas_call | solution.py:436
  26.3 0.0 copy-start.1
  26.3 1.1 %copy-done.1 = f32[2,2,720,128]{3,2,1,0:T(8,128)} copy-done((f32[2,2,720,128]{3,2,1,0:T(8,128)}, f32[2,2,720,128]{3,2,1,0:T(8,128)S(1)}, u32[]{:S(2)}) %copy-start.1) | copy-done | bytes 1474584
  27.4 3.3 %collective-permute-start.2 = (bf16[2,2,90,128]{3,2,1,0:T(8,128)(2,1)S(1)}, bf16[2,2,90,128]{3,2,1,0:T(8,128)(2,1)S(1)}, u32[]{:S(2)}, u32[]{:S(2)}) collective-permute-start(bf16[2,2,90,128]{3,2,1,0:T(8,128)(2,1)S(1)} %get-tuple-element.19), channel_id=1, source_target_pairs={{0,1},{1,2},{2,3},{3,4},{4,5},{5,6},{6,7},{7,8},{8,9},{9,10},{10,1... | collective-permute-start | bytes 276488 | tf_op jit(solution)/shard_map/ppermute | solution.py:362
  30.7 1.2 %collective-permute-start.3 = (bf16[2,2,90,128]{3,2,1,0:T(8,128)(2,1)S(1)}, bf16[2,2,90,128]{3,2,1,0:T(8,128)(2,1)S(1)}, u32[]{:S(2)}, u32[]{:S(2)}) collective-permute-start(bf16[2,2,90,128]{3,2,1,0:T(8,128)(2,1)S(1)} %get-tuple-element.20), channel_id=1, source_target_pairs={{1,0},{2,1},{3,2},{4,3},{5,4},{6,5},{7,6},{8,7},{9,8},{10,9},{11,1... | collective-permute-start | bytes 276488 | tf_op jit(solution)/shard_map/ppermute | solution.py:362
  31.9 5.4 %all-to-all-start.1 = ((f32[16,2,192]{2,1,0:T(2,128)}), f32[16,2,192]{2,1,0:T(2,128)S(1)}, u32[]{:S(2)}, u32[]{:S(2)}) async-start(f32[16,2,192]{2,1,0:T(2,128)} %get-tuple-element.21), calls=%async_computation.1 | async-start | bytes 65536 | tf_op jit(solution)/shard_map/all_to_all | solution.py:365
  37.3 4.6 %cached.4.refs_7_ = f32[2,720,192]{2,1,0:T(8,128)S(1)} custom-call(bf16[3,2,90,8,192]{4,3,2,1,0:T(8,128)(2,1)} %caches.7, bf16[8,90,192]{2,1,0:T(8,128)(2,1)} %copy-done.7, bf16[8,90,192]{2,1,0:T(8,128)(2,1)} %copy-done.8, bf16[3,192,5184]{2,1,0:T(8,128)(2,1)} %bitcast.3, f32[3,192]{1,0:T(4,128)S(1)} %copy-done.6), custom_call_target="tpu_custom_call" | custom-call | tf_op jit(solution)/shard_map/cached/pallas_call | solution.py:394
  41.9 2.0 %all-to-all-done.1.refs_3_ = f32[16,2,192]{2,1,0:T(2,128)S(1)} async-done(((f32[16,2,192]{2,1,0:T(2,128)}), f32[16,2,192]{2,1,0:T(2,128)S(1)}, u32[]{:S(2)}, u32[]{:S(2)}) %all-to-all-start.1) | async-done | bytes 24608 | tf_op jit(solution)/shard_map/all_to_all | solution.py:365
  43.9 0.0 collective-permute-done.2.refs_1_
  43.9 0.0 collective-permute-done.3.refs_2_
  43.9 0.0 copy-start.2
  43.9 1.4 %copy-done.2 = f32[2,2,720,128]{3,2,1,0:T(8,128)S(1)} copy-done((f32[2,2,720,128]{3,2,1,0:T(8,128)S(1)}, f32[2,2,720,128]{3,2,1,0:T(8,128)}, u32[]{:S(2)}) %copy-start.2) | copy-done | bytes 1474584
  45.3 5.4 %active.4 = (f32[2,2,720,128]{3,2,1,0:T(8,128)S(1)}, bf16[3,2,90,8,192]{4,3,2,1,0:T(8,128)(2,1)}, f32[16,2,192]{2,1,0:T(2,128)}, bf16[2,2,90,128]{3,2,1,0:T(8,128)(2,1)S(1)}, bf16[2,2,90,128]{3,2,1,0:T(8,128)(2,1)S(1)}) custom-call(f32[2,2,720,128]{3,2,1,0:T(8,128)S(1)} %copy-done.2, ...), custom_call_target="tpu_custom_call", output_to_operand_aliasing={{1}: (10, {})} | custom-call | tf_op jit(solution)/shard_map/active/pallas_call | solution.py:436
  50.7 0.1 collective-permute-start.4
  50.8 4.4 %collective-permute-start.5 = (bf16[2,2,90,128]{3,2,1,0:T(8,128)(2,1)S(1)}, bf16[2,2,90,128]{3,2,1,0:T(8,128)(2,1)S(1)}, u32[]{:S(2)}, u32[]{:S(2)}) collective-permute-start(bf16[2,2,90,128]{3,2,1,0:T(8,128)(2,1)S(1)} %get-tuple-element.25), channel_id=1, source_target_pairs={{1,0},{2,1},{3,2},{4,3},{5,4},{6,5},{7,6},{8,7},{9,8},{10,9},{11,1... | collective-permute-start | bytes 276488 | tf_op jit(solution)/shard_map/ppermute | solution.py:362
  55.2 3.7 %all-to-all-start.2 = ((f32[16,2,192]{2,1,0:T(2,128)}), f32[16,2,192]{2,1,0:T(2,128)S(1)}, u32[]{:S(2)}, u32[]{:S(2)}) async-start(f32[16,2,192]{2,1,0:T(2,128)} %get-tuple-element.26), calls=%async_computation.2 | async-start | bytes 65536 | tf_op jit(solution)/shard_map/all_to_all | solution.py:365
  58.9 4.6 %cached.5.refs_7_ = f32[2,720,192]{2,1,0:T(8,128)S(1)} custom-call(bf16[3,2,90,8,192]{4,3,2,1,0:T(8,128)(2,1)} %caches.7, bf16[8,90,192]{2,1,0:T(8,128)(2,1)} %copy-done.7, bf16[8,90,192]{2,1,0:T(8,128)(2,1)} %copy-done.8, bf16[3,192,5184]{2,1,0:T(8,128)(2,1)} %bitcast.5, f32[3,192]{1,0:T(4,128)S(1)} %copy-done.6), custom_call_target="tpu_custom_call" | custom-call | tf_op jit(solution)/shard_map/cached/pallas_call | solution.py:394
  63.5 1.8 %all-to-all-done.2.refs_3_ = f32[16,2,192]{2,1,0:T(2,128)S(1)} async-done(((f32[16,2,192]{2,1,0:T(2,128)}), f32[16,2,192]{2,1,0:T(2,128)S(1)}, u32[]{:S(2)}, u32[]{:S(2)}) %all-to-all-start.2) | async-done | bytes 24608 | tf_op jit(solution)/shard_map/all_to_all | solution.py:365
  65.3 0.0 collective-permute-done.4.refs_1_
  65.3 0.0 collective-permute-done.5.refs_2_
  65.3 5.2 %active.5 = (bf16[2,90,8,192]{3,2,1,0:T(8,128)(2,1)}, bf16[3,2,90,8,192]{4,3,2,1,0:T(8,128)(2,1)}) custom-call(f32[2,2,720,128]{3,2,1,0:T(8,128)S(1)} %get-tuple-element.23.refs_0_, bf16[2,2,90,128]{3,2,1,0:T(8,128)(2,1)S(1)} %collective-permute-done.4.refs_1_, ...), custom_call_target="tpu_custom_call", output_to_operand_aliasing={{1}: (9, {})} | custom-call | tf_op jit(solution)/shard_map/active/pallas_call | solution.py:436
Async XLA Ops:
  0.6 15.3 %copy-start.6 = (f32[3,192]{1,0:T(4,128)S(1)}, f32[3,192]{1,0:T(4,128)}, u32[]{:S(2)}) copy-start(f32[3,192]{1,0:T(4,128)} %bias.5) | copy-start | bytes 6916
  3.4 11.1 %collective-permute-start = (bf16[8,90,192]{2,1,0:T(8,128)(2,1)S(1)}, bf16[8,90,192]{2,1,0:T(8,128)(2,1)S(1)}, u32[]{:S(2)}, u32[]{:S(2)}) collective-permute-start(bf16[8,90,192]{2,1,0:T(8,128)(2,1)S(1)} %get-tuple-element.15), channel_id=1, source_target_pairs={{0,1},{1,2},{2,3},{3,4},{4,5},{5,6},{6,7},{7,8},{8,9},{9,10},{10,1... | collective-permute-start | bytes 829448 | tf_op jit(solution)/shard_map/ppermute | solution.py:362
  3.9 10.6 %collective-permute-start.1 = (bf16[8,90,192]{2,1,0:T(8,128)(2,1)S(1)}, bf16[8,90,192]{2,1,0:T(8,128)(2,1)S(1)}, u32[]{:S(2)}, u32[]{:S(2)}) collective-permute-start(bf16[8,90,192]{2,1,0:T(8,128)(2,1)S(1)} %get-tuple-element.16), channel_id=1, source_target_pairs={{1,0},{2,1},{3,2},{4,3},{5,4},{6,5},{7,6},{8,7},{9,8},{10,9},{11,1... | collective-permute-start | bytes 829448 | tf_op jit(solution)/shard_map/ppermute | solution.py:362
  9.0 11.7 %all-to-all-start = ((f32[16,2,192]{2,1,0:T(2,128)}), f32[16,2,192]{2,1,0:T(2,128)S(1)}, u32[]{:S(2)}, u32[]{:S(2)}) async-start(f32[16,2,192]{2,1,0:T(2,128)} %get-tuple-element.17), calls=%async_computation | async-start | bytes 65536 | tf_op jit(solution)/shard_map/all_to_all | solution.py:365
  14.4 0.7 %copy-start.7 = (bf16[8,90,192]{2,1,0:T(8,128)(2,1)}, bf16[8,90,192]{2,1,0:T(8,128)(2,1)S(1)}, u32[]{:S(2)}) copy-start(bf16[8,90,192]{2,1,0:T(8,128)(2,1)S(1)} %collective-permute-done.before.refs_1_) | copy-start | bytes 829444
  15.2 0.7 %copy-start.8 = (bf16[8,90,192]{2,1,0:T(8,128)(2,1)}, bf16[8,90,192]{2,1,0:T(8,128)(2,1)S(1)}, u32[]{:S(2)}) copy-start(bf16[8,90,192]{2,1,0:T(8,128)(2,1)S(1)} %collective-permute-done.1.after.refs_2_) | copy-start | bytes 829444
  15.9 4.7 %copy-start = (bf16[2,90,8,192]{3,2,1,0:T(8,128)(2,1)S(1)}, bf16[2,90,8,192]{3,2,1,0:T(8,128)(2,1)}, u32[]{:S(2)}) copy-start(bf16[2,90,8,192]{3,2,1,0:T(8,128)(2,1)} %refs_9_.1) | copy-start | bytes 1658884
  15.9 4.7 %copy-start.3 = (bf16[192,192]{1,0:T(8,128)(2,1)S(1)}, bf16[192,192]{1,0:T(8,128)(2,1)}, u32[]{:S(2)}) copy-start(bf16[192,192]{1,0:T(8,128)(2,1)} %constant.2.clone.refs_8_) | copy-start | bytes 221188
  15.9 4.7 %copy-start.4 = (f32[3,192]{1,0:T(4,128)S(1)}, f32[3,192]{1,0:T(4,128)}, u32[]{:S(2)}) copy-start(f32[3,192]{1,0:T(4,128)} %refs_4_.5) | copy-start | bytes 6916
  16.0 4.7 %copy-start.5 = (f32[3,192]{1,0:T(4,128)S(1)}, f32[3,192]{1,0:T(4,128)}, u32[]{:S(2)}) copy-start(f32[3,192]{1,0:T(4,128)} %refs_5_.5) | copy-start | bytes 6916
  26.3 1.1 %copy-start.1 = (f32[2,2,720,128]{3,2,1,0:T(8,128)}, f32[2,2,720,128]{3,2,1,0:T(8,128)S(1)}, u32[]{:S(2)}) copy-start(f32[2,2,720,128]{3,2,1,0:T(8,128)S(1)} %get-tuple-element.18.refs_0_) | copy-start | bytes 4423684
  27.4 16.5 %collective-permute-start.2 = (bf16[2,2,90,128]{3,2,1,0:T(8,128)(2,1)S(1)}, bf16[2,2,90,128]{3,2,1,0:T(8,128)(2,1)S(1)}, u32[]{:S(2)}, u32[]{:S(2)}) collective-permute-start(bf16[2,2,90,128]{3,2,1,0:T(8,128)(2,1)S(1)} %get-tuple-element.19), channel_id=1, source_target_pairs={{0,1},{1,2},{2,3},{3,4},{4,5},{5,6},{6,7},{7,8},{8,9},{9,10},{10,1... | collective-permute-start | bytes 276488 | tf_op jit(solution)/shard_map/ppermute | solution.py:362
  30.7 13.2 %collective-permute-start.3 = (bf16[2,2,90,128]{3,2,1,0:T(8,128)(2,1)S(1)}, bf16[2,2,90,128]{3,2,1,0:T(8,128)(2,1)S(1)}, u32[]{:S(2)}, u32[]{:S(2)}) collective-permute-start(bf16[2,2,90,128]{3,2,1,0:T(8,128)(2,1)S(1)} %get-tuple-element.20), channel_id=1, source_target_pairs={{1,0},{2,1},{3,2},{4,3},{5,4},{6,5},{7,6},{8,7},{9,8},{10,9},{11,1... | collective-permute-start | bytes 276488 | tf_op jit(solution)/shard_map/ppermute | solution.py:362
  31.9 12.1 %all-to-all-start.1 = ((f32[16,2,192]{2,1,0:T(2,128)}), f32[16,2,192]{2,1,0:T(2,128)S(1)}, u32[]{:S(2)}, u32[]{:S(2)}) async-start(f32[16,2,192]{2,1,0:T(2,128)} %get-tuple-element.21), calls=%async_computation.1 | async-start | bytes 65536 | tf_op jit(solution)/shard_map/all_to_all | solution.py:365
  43.9 1.4 %copy-start.2 = (f32[2,2,720,128]{3,2,1,0:T(8,128)S(1)}, f32[2,2,720,128]{3,2,1,0:T(8,128)}, u32[]{:S(2)}) copy-start(f32[2,2,720,128]{3,2,1,0:T(8,128)} %copy-done.1) | copy-start | bytes 4423684
  50.7 14.6 %collective-permute-start.4 = (bf16[2,2,90,128]{3,2,1,0:T(8,128)(2,1)S(1)}, bf16[2,2,90,128]{3,2,1,0:T(8,128)(2,1)S(1)}, u32[]{:S(2)}, u32[]{:S(2)}) collective-permute-start(bf16[2,2,90,128]{3,2,1,0:T(8,128)(2,1)S(1)} %get-tuple-element.24), channel_id=1, source_target_pairs={{0,1},{1,2},{2,3},{3,4},{4,5},{5,6},{6,7},{7,8},{8,9},{9,10},{10,1... | collective-permute-start | bytes 276488 | tf_op jit(solution)/shard_map/ppermute | solution.py:362
  50.8 14.5 %collective-permute-start.5 = (bf16[2,2,90,128]{3,2,1,0:T(8,128)(2,1)S(1)}, bf16[2,2,90,128]{3,2,1,0:T(8,128)(2,1)S(1)}, u32[]{:S(2)}, u32[]{:S(2)}) collective-permute-start(bf16[2,2,90,128]{3,2,1,0:T(8,128)(2,1)S(1)} %get-tuple-element.25), channel_id=1, source_target_pairs={{1,0},{2,1},{3,2},{4,3},{5,4},{6,5},{7,6},{8,7},{9,8},{10,9},{11,1... | collective-permute-start | bytes 276488 | tf_op jit(solution)/shard_map/ppermute | solution.py:362
  55.2 10.1 %all-to-all-start.2 = ((f32[16,2,192]{2,1,0:T(2,128)}), f32[16,2,192]{2,1,0:T(2,128)S(1)}, u32[]{:S(2)}, u32[]{:S(2)}) async-start(f32[16,2,192]{2,1,0:T(2,128)} %get-tuple-element.26), calls=%async_computation.2 | async-start | bytes 65536 | tf_op jit(solution)/shard_map/all_to_all | solution.py:365

commit v4 on v3

v4 whole, which is shorter than its diff:
```python
import functools

import jax
import jax.numpy as jnp
import numpy as np
from jax import lax
from jax.experimental import pallas as pl
from jax.experimental.pallas import tpu as pltpu
from jax.sharding import PartitionSpec as P

GROUPS = 32
EPSILON = 1e-06
LANES = 128
HALF = LANES // 2
COLS = 8
SLABS = 10
UNROLL = 2
PLANES = 3
VMEM = pl.BlockSpec(memory_space=pltpu.VMEM)
HBM = pl.BlockSpec(memory_space=pltpu.HBM)


def silu_of_twice(u):
    return u + u * jnp.tanh(u)


def twice(v):
    return jnp.concatenate([v, v], axis=-1)


def halves(value):
    return value[..., :LANES], value[..., LANES:]


def planes(first, second):
    (a, b), (c, d) = halves(first), halves(second)
    return a, c, jnp.concatenate([b, d], axis=-1)


def pair(a, b):
    return jnp.concatenate([a, b], axis=0).astype(jnp.bfloat16)


def build_slabs(rows, row_of, edge_of, slabs, keep=None):
    lane = lax.broadcasted_iota(jnp.int32, (COLS, LANES), 1)
    low = lane < HALF
    column = lax.broadcasted_iota(jnp.int32, (COLS, LANES), 0)
    first, last = column == 0, column == COLS - 1
    zero = jnp.zeros((COLS, LANES), jnp.float32)

    def shifted(h):
        out = []
        for plane, value in enumerate(row_of(h)):
            left, right = edge_of(h, plane)
            out.append(
                (
                    jnp.where(first, left, pltpu.roll(value, 1, 0)),
                    value,
                    jnp.where(last, right, pltpu.roll(value, COLS - 1, 0)),
                )
            )
        rest = out[2]
        swapped = [pltpu.roll(v, HALF, 1) for v in rest]
        if keep is not None:
            keep(h, out[0][1], rest[1], out[1][1], swapped[1])
        mains = out[0] + out[1]
        packed = (jnp.where(low, rest[0], swapped[1]), jnp.where(low, swapped[0], rest[1]))
        return mains, packed, (rest[2], swapped[2])

    def put(frame, index, k, value):
        start = k * 16 if isinstance(k, int) else pl.multiple_of(k * 16, 16)
        slabs[frame][index, pl.ds(start, 16), :] = value

    def around(frame, upper, lower):
        return jnp.where(low, upper[frame], lower[1 - frame])

    def step(k, carry):
        before, older, oldest = carry
        one, two = shifted(2 * k), shifted(2 * k + 1)
        for frame in range(2):
            for r in range(3):
                put(frame, r, k, pair(one[0][3 * frame + r], two[0][3 * frame + r]))
                put(frame, 3 + r, k, pair(before[0][3 * frame + r], one[0][3 * frame + r]))
            put(frame, 6, k, pair(one[1][frame], two[1][frame]))
            put(frame, 7, k, pair(before[1][frame], one[1][frame]))
            put(frame, 9, k, pair(one[2][frame], two[2][frame]))
            if older is not None:
                upper = around(frame, oldest, before[2])
                put(frame, 8, k - 1, pair(upper, around(frame, older, one[2])))
        return two, one[2], before[2]

    count = rows // 2
    carry = step(0, (((zero,) * 6, (zero,) * 2, (zero,) * 2), None, None))
    before, older, oldest = lax.fori_loop(1, count, step, carry, unroll=UNROLL)
    for frame in range(2):
        for r in range(3):
            put(frame, 3 + r, count, pair(before[0][3 * frame + r], zero))
        put(frame, 7, count, pair(before[1][frame], zero))
        upper = around(frame, oldest, before[2])
        put(frame, 8, count - 1, pair(upper, around(frame, older, (zero, zero))))


def slab_rows(slab, start, size):
    def at(index, step=0):
        return slab[index, pl.ds(start + step, size), :]

    tiles = [at(3 + r) for r in range(3)] + [at(r) for r in range(3)]
    tiles += [at(3 + r, 16) for r in range(3)]
    return tiles + [at(7), at(6), at(7, 16), at(8), at(9)]


def tap_lanes(weight, origin, channels):
    def at(q, r, start, size):
        return weight[:, pl.ds(origin + (q * 3 + r) * channels + start, size)]

    tiles = [at(q, r, 0, LANES) for q in range(3) for r in range(3)]
    for q in range(3):
        tiles += [at(q, 0, LANES, HALF), at(q, 1, LANES, HALF)]
    tiles += [at(0, 2, LANES, HALF), at(2, 2, LANES, HALF), at(1, 2, LANES, HALF)]
    tiles.append(jnp.zeros((weight.shape[0], HALF), weight.dtype))
    return jnp.concatenate(tiles, axis=1)


def product(pairs, start, size):
    left = [tile for slab, _ in pairs for tile in slab_rows(slab, start, size)]
    right = [taps for _, taps in pairs]
    return lax.dot_general(
        jnp.concatenate(left, axis=1),
        jnp.concatenate(right, axis=1),
        (((1,), (1,)), ((), ())),
        preferred_element_type=jnp.float32,
    )


def put_planes(out, t, here, value):
    main, rest = halves(value)
    out[t, here, :] = main
    out[2, here, HALF * t : HALF * (t + 1)] = rest


def get_planes(held, t, here):
    rest = held[2, here, HALF * t : HALF * (t + 1)]
    return jnp.concatenate([held[t, here, :], rest], axis=1)


def begin_kernel(video, caches, sums, first, last, wide, held, sem):
    layers, frames, rows, cols, channels = caches.shape
    copies = [pltpu.make_async_copy(video, held.at[0], sem.at[0])]
    for layer in range(layers):
        copies.append(
            pltpu.make_async_copy(caches.at[layer], held.at[layer + 1], sem.at[layer + 1])
        )
    for copy in copies:
        copy.start()
    half = channels - LANES
    total = [jnp.zeros((COLS, LANES), jnp.float32), jnp.zeros((COLS, half), jnp.float32)]
    square = list(total)
    for group, copy in enumerate(copies):
        copy.wait()
        for frame in range(frames):
            value = held[group, frame].astype(jnp.float32)
            parts = halves(value)
            if group == 0:
                for i in range(2):
                    total[i] = total[i] + jnp.sum(parts[i], axis=0)
                    square[i] = square[i] + jnp.sum(parts[i] * parts[i], axis=0)
            wide[0] = parts[0].reshape(rows * cols, LANES)
            wide[1, :, :half] = parts[1].reshape(rows * cols, half)
            for out, column in ((first, 0), (last, cols - 1)):
                found = [wide[i, pl.ds(column, rows, stride=cols), :] for i in range(2)]
                edge = jnp.concatenate([found[0], found[1][:, :half]], axis=1)
                out[group * frames + frame] = edge.astype(jnp.bfloat16)
    both = [
        jnp.concatenate([jnp.sum(v, axis=0, keepdims=True) for v in pieces], axis=1)
        for pieces in (total, square)
    ]
    sums[...] = jnp.broadcast_to(jnp.concatenate(both, axis=0)[None], sums.shape)


def cached_kernel(layer, chunk, caches, before, after, weights, bias, out, ordered, *scratches):
    edges, *slabs, cache, weight, taps, sem = scratches
    _, frames, rows, cols, channels = caches.shape
    places = rows * cols
    begun = pltpu.make_async_copy(caches.at[layer], cache, sem.at[0])
    fetch = pltpu.make_async_copy(weights.at[layer], weight, sem.at[1])
    begun.start()
    fetch.start()
    begun.wait()
    origin = (layer + 1) * frames
    for side, ref in enumerate((before, after)):
        found = planes(*(ref[origin + frame].astype(jnp.float32) for frame in range(2)))
        for plane in range(PLANES):
            edges[side, plane] = found[plane]

    def row_of(h):
        return planes(*(cache[frame, h].astype(jnp.float32) for frame in range(2)))

    def edge_of(h, plane):
        return [edges[side, plane, pl.ds(h, COLS, stride=0), :] for side in (0, 1)]

    build_slabs(rows, row_of, edge_of, slabs)
    fetch.wait()
    for p in (1, 2, 0):
        taps[p] = tap_lanes(weight, p * 9 * channels, channels)
    store = pltpu.make_async_copy(taps.at[pl.ds(1, 2)], ordered, sem.at[2])
    store.start()
    constant = bias[layer : layer + 1, :]
    tables = [taps[p] for p in range(2)]
    for start in range(0, places, chunk):
        value = product([(slabs[1], tables[0])], start, chunk)
        put_planes(out, 1, pl.ds(start, chunk), value + constant)
    for start in range(0, places, chunk):
        value = product([(slabs[0], tables[0]), (slabs[1], tables[1])], start, chunk)
        put_planes(out, 0, pl.ds(start, chunk), value + constant)
    store.wait()


def group_means(stats, same, entries):
    total = jnp.sum(stats, axis=0)
    high = total.astype(jnp.bfloat16)
    left = total - high.astype(jnp.float32)
    middle = left.astype(jnp.bfloat16)
    low = (left - middle.astype(jnp.float32)).astype(jnp.bfloat16)
    split = jnp.concatenate([high, middle, low], axis=0)
    sums = jnp.dot(split, same, preferred_element_type=jnp.float32)
    return (sums[0:2] + sums[2:4] + sums[4:6]) / entries


def active_kernel(layer, chunk, entries, final, *refs):
    x, before, after, stats, gain, shift, ordered, part, same = refs[:9]
    rest = refs[9:]
    residual = None
    if layer == 1:
        residual, *rest = rest
    if layer > 0:
        _, *rest = rest
    if final:
        y, carried, *rest = rest
    else:
        y, carried, sums, first, last, *rest = rest
    edges, *slabs, kept, held, taps, sem = rest
    frames, rows, cols, channels = kept.shape
    places = rows * cols
    fetch = [pltpu.make_async_copy(ordered, taps, sem.at[1])]
    if residual is not None:
        fetch.append(pltpu.make_async_copy(residual, held, sem.at[2]))
    for copy in fetch:
        copy.start()

    means = group_means(stats[...], same[...], entries)
    average = means[0:1]
    variance = means[1:2] - average * average
    scale = lax.rsqrt(variance + EPSILON) * gain[layer : layer + 1, :]
    offset = shift[layer : layer + 1, :] - average * scale
    scale, offset = 0.5 * scale, 0.5 * offset
    scales = [scale[:, :LANES]] * 2 + [twice(scale[:, LANES:])]
    offsets = [offset[:, :LANES]] * 2 + [twice(offset[:, LANES:])]

    def act(values):
        return [silu_of_twice(v * a + b) for v, a, b in zip(values, scales, offsets)]

    for side, ref in enumerate((before, after)):
        if layer:
            values = [ref[plane].astype(jnp.float32) for plane in range(PLANES)]
        else:
            values = planes(*(ref[frame].astype(jnp.float32) for frame in range(2)))
        for plane, value in enumerate(act(values)):
            edges[side, plane] = value

    def row_of(h):
        if layer:
            start = h * COLS if isinstance(h, int) else pl.multiple_of(h * COLS, COLS)
            return act([x[plane, pl.ds(start, COLS), :] for plane in range(PLANES)])
        return act(planes(*(x[frame, h].astype(jnp.float32) for frame in range(2))))

    def edge_of(h, plane):
        return [edges[side, plane, pl.ds(h, COLS, stride=0), :] for side in (0, 1)]

    def keep(h, *values):
        for frame in range(2):
            main, other = values[2 * frame : 2 * frame + 2]
            whole = jnp.concatenate([main, other[:, : channels - LANES]], axis=1)
            kept[frame, h] = whole.astype(jnp.bfloat16)

    build_slabs(rows, row_of, edge_of, slabs, keep)
    copy = pltpu.make_async_copy(kept, carried.at[layer], sem.at[0])
    copy.start()
    for one in fetch:
        one.wait()
    tables = [taps[p] for p in range(2)]
    moments = [jnp.zeros((COLS, channels), jnp.float32)] * 2

    def finish(t, start, value, moments):
        here, span = pl.ds(start, chunk), pl.ds(start // COLS, chunk // COLS)
        shape = (chunk // COLS, COLS, channels)
        value = value + get_planes(part, t, here)
        if final:
            value = value + get_planes(x, t, here)
            y[t, span] = value.reshape(shape).astype(jnp.bfloat16)
            return moments
        if residual is not None:
            value = value + held[t, span].astype(jnp.float32).reshape(chunk, channels)
        put_planes(y, t, here, value)
        folded = value.reshape(shape)
        return [
            moments[0] + jnp.sum(folded, axis=0),
            moments[1] + jnp.sum(folded * folded, axis=0),
        ]

    starts = range(0, places, chunk)
    for start in starts:
        value = product([(slabs[0], tables[1])], start, chunk)
        moments = finish(0, start, value, moments)
    for start in starts:
        value = product([(slabs[0], tables[0]), (slabs[1], tables[1])], start, chunk)
        moments = finish(1, start, value, moments)
    if not final:
        both = [jnp.sum(v, axis=0, keepdims=True) for v in moments]
        sums[...] = jnp.broadcast_to(jnp.concatenate(both, axis=0)[None], sums.shape)
        for plane in range(PLANES):
            for out, column in ((first, 0), (last, cols - 1)):
                edge = y[plane, pl.ds(column, rows, stride=cols), :]
                out[plane] = edge.astype(jnp.bfloat16)
    copy.wait()


def scratch(frames, rows):
    slab = pltpu.VMEM((SLABS, rows * COLS + 16, LANES), jnp.bfloat16)
    return [pltpu.VMEM((2, PLANES, rows, LANES), jnp.float32)] + [slab] * frames


def local(video_span, caches, norm_gains, shifts, weights, biases):
    peers = lax.axis_size("lon")
    frames, rows, cols, channels = video_span.shape
    layers = caches.shape[0]
    places = rows * cols
    entries = frames * places * peers * (channels // GROUPS)
    up = [(i, (i + 1) % peers) for i in range(peers)]
    down = [(j, i) for i, j in up]
    chunk = 720
    tiles = 14 * LANES

    def around(first, last):
        return lax.ppermute(last, "lon", up), lax.ppermute(first, "lon", down)

    def gathered(sums):
        return lax.all_to_all(sums, "lon", 0, 0)

    def in_hbm(value):
        return pltpu.with_memory_space_constraint(value, pltpu.HBM)

    turned = in_hbm(jnp.swapaxes(weights, 1, 2))
    caches, video = in_hbm(caches), in_hbm(video_span)
    spread = jax.ShapeDtypeStruct((peers, 2, channels), jnp.float32)
    brim = jax.ShapeDtypeStruct(((layers + 1) * frames, rows, channels), jnp.bfloat16)
    sums, first, last = pl.pallas_call(
        begin_kernel,
        out_shape=[spread, brim, brim],
        in_specs=[HBM, HBM],
        out_specs=[VMEM] * 3,
        scratch_shapes=[
            pltpu.VMEM((2, places, LANES), jnp.float32),
            pltpu.VMEM((layers + 1,) + video_span.shape, jnp.bfloat16),
            pltpu.SemaphoreType.DMA((layers + 1,)),
        ],
        compiler_params=pltpu.CompilerParams(vmem_limit_bytes=24 << 20),
        name="begin",
    )(video, caches)
    brims = around(first, last)
    before, after = brims
    members = channels // GROUPS
    same = jnp.asarray(np.kron(np.eye(GROUPS), np.ones((members, members))), jnp.bfloat16)
    stats = gathered(sums)

    def cached_part(layer):
        return pl.pallas_call(
            functools.partial(cached_kernel, layer, chunk),
            out_shape=[
                jax.ShapeDtypeStruct((PLANES, places, LANES), jnp.float32),
                jax.ShapeDtypeStruct((2, channels, tiles), weights.dtype),
            ],
            in_specs=[HBM, VMEM, VMEM, HBM, VMEM],
            out_specs=[VMEM, HBM],
            scratch_shapes=scratch(frames, rows)
            + [
                pltpu.VMEM(video_span.shape, jnp.bfloat16),
                pltpu.VMEM((channels, weights.shape[1]), weights.dtype),
                pltpu.VMEM((3, channels, tiles), weights.dtype),
                pltpu.SemaphoreType.DMA((3,)),
            ],
            compiler_params=pltpu.CompilerParams(vmem_limit_bytes=24 << 20),
            name="cached",
        )(caches, *brims, turned, biases)

    x = video_span
    carried = None
    for layer in range(layers):
        final = layer == layers - 1
        part, ordered = cached_part(layer)
        operands = [x, before, after, stats, norm_gains, shifts, in_hbm(ordered), part, same]
        specs = [VMEM] * 6 + [HBM, VMEM, VMEM]
        aliases = {}
        if layer == 1:
            operands.append(video)
            specs.append(HBM)
        if layer > 0:
            aliases = {len(operands): 1}
            operands.append(carried)
            specs.append(HBM)
        state = jax.ShapeDtypeStruct((PLANES, places, LANES), jnp.float32)
        if final:
            state = jax.ShapeDtypeStruct(video_span.shape, jnp.bfloat16)
        outs = [state, jax.ShapeDtypeStruct(caches.shape, jnp.bfloat16)]
        out_specs = [VMEM, HBM]
        if not final:
            edge = jax.ShapeDtypeStruct((PLANES, rows, LANES), jnp.bfloat16)
            outs += [spread, edge, edge]
            out_specs += [VMEM] * 3
        results = pl.pallas_call(
            functools.partial(active_kernel, layer, chunk, entries, final),
            out_shape=outs,
            in_specs=specs,
            out_specs=out_specs,
            scratch_shapes=scratch(frames, rows)
            + [
                pltpu.VMEM(video_span.shape, jnp.bfloat16),
                pltpu.VMEM(video_span.shape, jnp.bfloat16),
                pltpu.VMEM((2, channels, tiles), weights.dtype),
                pltpu.SemaphoreType.DMA((3,)),
            ],
            compiler_params=pltpu.CompilerParams(vmem_limit_bytes=24 << 20),
            input_output_aliases=aliases,
            name="active",
        )(*operands)
        x, carried = results[:2]
        if not final:
            stats = gathered(results[2])
            before, after = around(results[3], results[4])
    return x, carried


def solution(mesh):
    return jax.shard_map(
        local,
        mesh=mesh,
        in_specs=(
            P(None, "clips", "lon", None),
            P(None, None, "clips", "lon", None),
            P(),
            P(),
            P(),
            P(),
        ),
        out_specs=(P(None, "clips", "lon", None), P(None, None, "clips", "lon", None)),
        check_vma=False,
    )
```

time: 71.2 us -> 84.2 us (1.18)
  Pallas kernels: 32.7 us -> 43.7 us
  local copies, waits for them, and re-layouts: 3.96 us -> 9.99 us
  waiting for transfers between devices: 5.82 us -> 1.95 us
    pallas_call x3, Pallas kernels: 13.8 us -> 23 us  [cached_part(): pl.pallas_call(functools.partial(cached_kernel, layer, chunk), out_shape=...]
    unnamed x18 -> x28, local copies, waits for them, and re-layouts: 3.96 us -> 9.99 us
    all_to_all x3, waiting for transfers between devices: 3.88 us -> 0.01 us  [gathered(): return lax.all_to_all(sums, 'lon', 0, 0)]
    pallas_call x3, Pallas kernels: 16.2 us -> 17.9 us  [local(): pl.pallas_call(functools.partial(active_kernel, layer, chunk, entries, fi...]
  transfers between devices with their start and end apart: 9 -> 9, of which waited for: 4 -> 2; matrix products, arithmetic and copies ran while one was open for 0% -> 0% of each run, Pallas kernels for 20% -> 27%
where the time goes in v4:
time: 84.2 us; the launch traced here: 83.8 us
  Pallas kernels  43.7 us (52%)
  starting transfers between devices  27.2 us (32%)
  local copies, waits for them, and re-layouts  9.99 us (12%)
  waiting for transfers between devices  1.95 us (2%)
  between operations  0.97 us (1%)
    pallas_call x3, Pallas kernels, cached_part(): pl.pallas_call(functools.partial(cached_kernel, layer, chunk), out_shape=...  23 us
    pallas_call x3, Pallas kernels, local(): pl.pallas_call(functools.partial(active_kernel, layer, chunk, entries, fi...  17.9 us
    ppermute x6, starting transfers between devices, around(): return (lax.ppermute(last, 'lon', up), lax.ppermute(first, 'lon', down))  14.8 us
    all_to_all x3, starting transfers between devices, gathered(): return lax.all_to_all(sums, 'lon', 0, 0)  12.4 us
    unnamed x28, local copies, waits for them, and re-layouts  9.99 us
    pallas_call x1, Pallas kernels, local(): pl.pallas_call(begin_kernel, out_shape=[spread, brim, brim], in_specs=[HB...  2.71 us
    ppermute x6, waiting for transfers between devices, around(): return (lax.ppermute(last, 'lon', up), lax.ppermute(first, 'lon', down))  1.94 us
  transfers between devices with their start and end apart: 9, of which 2 were waited for; matrix products, arithmetic and copies ran while one was open for 0% of the time, Pallas kernels for 27%

profile of v4, /device:TPU:0, one launch (start us, length us, event | category | flops | bytes accessed | tf_op | source)
XLA Modules:
  0.0 83.8 jit_solution(15007080490506041744)
XLA Ops:
  0.6 0.0 copy-start.11
  0.6 2.7 %begin.1 = (f32[16,2,192]{2,1,0:T(2,128)}, bf16[8,90,192]{2,1,0:T(8,128)(2,1)S(1)}, bf16[8,90,192]{2,1,0:T(8,128)(2,1)S(1)}) custom-call(bf16[2,90,8,192]{3,2,1,0:T(8,128)(2,1)} %refs_9_.1, bf16[3,2,90,8,192]{4,3,2,1,0:T(8,128)(2,1)} %caches.7), custom_call_target="tpu_custom_call" | custom-call | tf_op jit(solution)/shard_map/begin/pallas_call | solution.py:356
  3.4 0.5 collective-permute-start
  3.9 5.0 %collective-permute-start.1 = (bf16[8,90,192]{2,1,0:T(8,128)(2,1)S(1)}, bf16[8,90,192]{2,1,0:T(8,128)(2,1)S(1)}, u32[]{:S(2)}, u32[]{:S(2)}) collective-permute-start(bf16[8,90,192]{2,1,0:T(8,128)(2,1)S(1)} %get-tuple-element.22), channel_id=1, source_target_pairs={{1,0},{2,1},{3,2},{4,3},{5,4},{6,5},{7,6},{8,7},{9,8},{10,9},{11,1... | collective-permute-start | bytes 829448 | tf_op jit(solution)/shard_map/ppermute | solution.py:344
  9.0 3.6 %all-to-all-start = ((f32[16,2,192]{2,1,0:T(2,128)}), f32[16,2,192]{2,1,0:T(2,128)S(1)}, u32[]{:S(2)}, u32[]{:S(2)}) async-start(f32[16,2,192]{2,1,0:T(2,128)} %get-tuple-element.23), calls=%async_computation | async-start | bytes 65536 | tf_op jit(solution)/shard_map/all_to_all | solution.py:347
  12.6 1.9 %collective-permute-done.before.refs_1_ = bf16[8,90,192]{2,1,0:T(8,128)(2,1)S(1)} collective-permute-done((bf16[8,90,192]{2,1,0:T(8,128)(2,1)S(1)}, bf16[8,90,192]{2,1,0:T(8,128)(2,1)S(1)}, u32[]{:S(2)}, u32[]{:S(2)}) %collective-permute-start) | collective-permute-done | bytes 276512 | tf_op jit(solution)/shard_map/ppermute | solution.py:344
  14.4 0.1 collective-permute-done.1.after.refs_2_
  14.5 0.0 copy-done.11
  14.5 0.0 copy-start
  14.5 0.0 copy-start.13
  14.5 7.7 %cached.3 = (f32[3,720,128]{2,1,0:T(8,128)S(1)}, bf16[2,192,1792]{2,1,0:T(8,128)(2,1)S(1)}) custom-call(bf16[3,2,90,8,192]{4,3,2,1,0:T(8,128)(2,1)} %caches.7, bf16[8,90,192]{2,1,0:T(8,128)(2,1)S(1)} %collective-permute-done.before.refs_1_, bf16[8,90,192]{2,1,0:T(8,128)(2,1)S(1)} %collective-permute-done.1.after.refs_2_, bf16[3,192,5184]{2,1,0:T(8,128)(2,1)} %bitcast.1, ...), custom_call_target="tpu_custom_call" | custom-call | tf_op jit(solution)/shard_map/cached/pallas_call | solution.py:376
  22.3 0.0 copy-start.3
  22.3 1.1 %copy-done.3 = bf16[2,192,1792]{2,1,0:T(8,128)(2,1)} copy-done((bf16[2,192,1792]{2,1,0:T(8,128)(2,1)}, bf16[2,192,1792]{2,1,0:T(8,128)(2,1)S(1)}, u32[]{:S(2)}) %copy-start.3) | copy-done | bytes 1376280
  23.4 0.0 all-to-all-done.refs_3_
  23.4 0.0 copy-done
  23.4 0.0 copy-done.10
  23.4 0.0 copy-done.12
  23.4 0.0 copy-done.13
  23.4 6.9 %active.3 = (f32[3,720,128]{2,1,0:T(8,128)S(1)}, bf16[3,2,90,8,192]{4,3,2,1,0:T(8,128)(2,1)}, f32[16,2,192]{2,1,0:T(2,128)}, bf16[3,90,128]{2,1,0:T(8,128)(2,1)S(1)}, bf16[3,90,128]{2,1,0:T(8,128)(2,1)S(1)}) custom-call(bf16[2,90,8,192]{3,2,1,0:T(8,128)(2,1)S(1)} %copy-done, bf16[8,90,192]{2,1,0:T(8,128)(2,1)S(1)} %collective-permute-done.before.refs_1_, ...), custom_call_target="tpu_custom_call" | custom-call | tf_op jit(solution)/shard_map/active/pallas_call | solution.py:419
  30.3 0.0 copy-start.4
  30.3 1.0 %copy-done.4 = f32[3,720,128]{2,1,0:T(8,128)} copy-done((f32[3,720,128]{2,1,0:T(8,128)}, f32[3,720,128]{2,1,0:T(8,128)S(1)}, u32[]{:S(2)}) %copy-start.4) | copy-done | bytes 1105944
  31.3 3.9 %collective-permute-start.2 = (bf16[3,90,128]{2,1,0:T(8,128)(2,1)S(1)}, bf16[3,90,128]{2,1,0:T(8,128)(2,1)S(1)}, u32[]{:S(2)}, u32[]{:S(2)}) collective-permute-start(bf16[3,90,128]{2,1,0:T(8,128)(2,1)S(1)} %get-tuple-element.27), channel_id=1, source_target_pairs={{0,1},{1,2},{2,3},{3,4},{4,5},{5,6},{6,7},{7,8},{8,9},{9,10},{10,1... | collective-permute-start | bytes 207368 | tf_op jit(solution)/shard_map/ppermute | solution.py:344
  35.3 0.7 collective-permute-start.3
  36.0 5.1 %all-to-all-start.1 = ((f32[16,2,192]{2,1,0:T(2,128)}), f32[16,2,192]{2,1,0:T(2,128)S(1)}, u32[]{:S(2)}, u32[]{:S(2)}) async-start(f32[16,2,192]{2,1,0:T(2,128)} %get-tuple-element.29), calls=%async_computation.1 | async-start | bytes 65536 | tf_op jit(solution)/shard_map/all_to_all | solution.py:347
  41.1 7.7 %cached.4 = (f32[3,720,128]{2,1,0:T(8,128)S(1)}, bf16[2,192,1792]{2,1,0:T(8,128)(2,1)S(1)}) custom-call(bf16[3,2,90,8,192]{4,3,2,1,0:T(8,128)(2,1)} %caches.7, bf16[8,90,192]{2,1,0:T(8,128)(2,1)S(1)} %collective-permute-done.before.refs_1_, bf16[8,90,192]{2,1,0:T(8,128)(2,1)S(1)} %collective-permute-done.1.after.refs_2_, bf16[3,192,5184]{2,1,0:T(8,128)(2,1)} %bitcast.2, ...), custom_call_target="tpu_custom_call" | custom-call | tf_op jit(solution)/shard_map/cached/pallas_call | solution.py:376
  48.8 0.0 copy-start.1
  48.8 1.1 %copy-done.1 = bf16[2,192,1792]{2,1,0:T(8,128)(2,1)} copy-done((bf16[2,192,1792]{2,1,0:T(8,128)(2,1)}, bf16[2,192,1792]{2,1,0:T(8,128)(2,1)S(1)}, u32[]{:S(2)}) %copy-start.1) | copy-done | bytes 1376280
  49.9 1.0 %copy-done.6 = f32[3,720,128]{2,1,0:T(8,128)} copy-done((f32[3,720,128]{2,1,0:T(8,128)}, f32[3,720,128]{2,1,0:T(8,128)S(1)}, u32[]{:S(2)}) %copy-start.6) | copy-done | bytes 1105944
  50.9 0.0 all-to-all-done.1.refs_3_
  50.9 0.0 collective-permute-done.2.refs_1_
  50.9 0.0 collective-permute-done.3.refs_2_
  50.9 0.0 copy-start.5
  50.9 1.2 %copy-done.5 = f32[3,720,128]{2,1,0:T(8,128)S(1)} copy-done((f32[3,720,128]{2,1,0:T(8,128)S(1)}, f32[3,720,128]{2,1,0:T(8,128)}, u32[]{:S(2)}) %copy-start.5) | copy-done | bytes 1105944
  52.1 1.2 %copy-done.7 = f32[3,720,128]{2,1,0:T(8,128)S(1)} copy-done((f32[3,720,128]{2,1,0:T(8,128)S(1)}, f32[3,720,128]{2,1,0:T(8,128)}, u32[]{:S(2)}) %copy-start.7) | copy-done | bytes 1105944
  53.4 5.4 %active.4 = (f32[3,720,128]{2,1,0:T(8,128)S(1)}, bf16[3,2,90,8,192]{4,3,2,1,0:T(8,128)(2,1)}, f32[16,2,192]{2,1,0:T(2,128)}, bf16[3,90,128]{2,1,0:T(8,128)(2,1)S(1)}, bf16[3,90,128]{2,1,0:T(8,128)(2,1)S(1)}) custom-call(f32[3,720,128]{2,1,0:T(8,128)S(1)} %copy-done.5, ...), custom_call_target="tpu_custom_call", output_to_operand_aliasing={{1}: (10, {})} | custom-call | tf_op jit(solution)/shard_map/active/pallas_call | solution.py:419
  58.8 0.5 collective-permute-start.4
  59.3 4.0 %collective-permute-start.5 = (bf16[3,90,128]{2,1,0:T(8,128)(2,1)S(1)}, bf16[3,90,128]{2,1,0:T(8,128)(2,1)S(1)}, u32[]{:S(2)}, u32[]{:S(2)}) collective-permute-start(bf16[3,90,128]{2,1,0:T(8,128)(2,1)S(1)} %get-tuple-element.35), channel_id=1, source_target_pairs={{1,0},{2,1},{3,2},{4,3},{5,4},{6,5},{7,6},{8,7},{9,8},{10,9},{11,1... | collective-permute-start | bytes 207368 | tf_op jit(solution)/shard_map/ppermute | solution.py:344
  63.3 3.7 %all-to-all-start.2 = ((f32[16,2,192]{2,1,0:T(2,128)}), f32[16,2,192]{2,1,0:T(2,128)S(1)}, u32[]{:S(2)}, u32[]{:S(2)}) async-start(f32[16,2,192]{2,1,0:T(2,128)} %get-tuple-element.36), calls=%async_computation.2 | async-start | bytes 65536 | tf_op jit(solution)/shard_map/all_to_all | solution.py:347
  67.0 7.7 %cached.5 = (f32[3,720,128]{2,1,0:T(8,128)S(1)}, bf16[2,192,1792]{2,1,0:T(8,128)(2,1)S(1)}) custom-call(bf16[3,2,90,8,192]{4,3,2,1,0:T(8,128)(2,1)} %caches.7, bf16[8,90,192]{2,1,0:T(8,128)(2,1)S(1)} %collective-permute-done.before.refs_1_, bf16[8,90,192]{2,1,0:T(8,128)(2,1)S(1)} %collective-permute-done.1.after.refs_2_, bf16[3,192,5184]{2,1,0:T(8,128)(2,1)} %bitcast.3, ...), custom_call_target="tpu_custom_call" | custom-call | tf_op jit(solution)/shard_map/cached/pallas_call | solution.py:376
  74.7 0.0 copy-start.2
  74.7 1.1 %copy-done.2 = bf16[2,192,1792]{2,1,0:T(8,128)(2,1)} copy-done((bf16[2,192,1792]{2,1,0:T(8,128)(2,1)}, bf16[2,192,1792]{2,1,0:T(8,128)(2,1)S(1)}, u32[]{:S(2)}) %copy-start.2) | copy-done | bytes 1376280
  75.8 1.0 %copy-done.8 = f32[3,720,128]{2,1,0:T(8,128)} copy-done((f32[3,720,128]{2,1,0:T(8,128)}, f32[3,720,128]{2,1,0:T(8,128)S(1)}, u32[]{:S(2)}) %copy-start.8) | copy-done | bytes 1105944
  76.8 0.0 all-to-all-done.2.refs_3_
  76.8 0.0 collective-permute-done.4.refs_1_
  76.8 0.0 collective-permute-done.5.refs_2_
  76.8 0.0 copy-start.9
  76.8 1.2 %copy-done.9 = f32[3,720,128]{2,1,0:T(8,128)S(1)} copy-done((f32[3,720,128]{2,1,0:T(8,128)S(1)}, f32[3,720,128]{2,1,0:T(8,128)}, u32[]{:S(2)}) %copy-start.9) | copy-done | bytes 1105944
  78.0 5.6 %active.5 = (bf16[2,90,8,192]{3,2,1,0:T(8,128)(2,1)}, bf16[3,2,90,8,192]{4,3,2,1,0:T(8,128)(2,1)}) custom-call(f32[3,720,128]{2,1,0:T(8,128)S(1)} %get-tuple-element.33.refs_0_, bf16[3,90,128]{2,1,0:T(8,128)(2,1)S(1)} %collective-permute-done.4.refs_1_, bf16[3,90,128]{2,1,0:T(8,128)(2,1)S(1)} %collective-permute-done.5.refs_2_, ...), custom_call_target="tpu_custom_call", output_to_operand_aliasing={{1}: (9, {})} | custom-call | tf_op jit(solution)/shard_map/active/pallas_call | solution.py:419
  (5 shorter events, 0.0 us)
Async XLA Ops:
  0.6 13.9 %copy-start.11 = (f32[3,192]{1,0:T(4,128)S(1)}, f32[3,192]{1,0:T(4,128)}, u32[]{:S(2)}) copy-start(f32[3,192]{1,0:T(4,128)} %bias.5) | copy-start | bytes 6916
  3.4 11.1 %collective-permute-start = (bf16[8,90,192]{2,1,0:T(8,128)(2,1)S(1)}, bf16[8,90,192]{2,1,0:T(8,128)(2,1)S(1)}, u32[]{:S(2)}, u32[]{:S(2)}) collective-permute-start(bf16[8,90,192]{2,1,0:T(8,128)(2,1)S(1)} %get-tuple-element.21), channel_id=1, source_target_pairs={{0,1},{1,2},{2,3},{3,4},{4,5},{5,6},{6,7},{7,8},{8,9},{9,10},{10,1... | collective-permute-start | bytes 829448 | tf_op jit(solution)/shard_map/ppermute | solution.py:344
  3.9 10.6 %collective-permute-start.1 = (bf16[8,90,192]{2,1,0:T(8,128)(2,1)S(1)}, bf16[8,90,192]{2,1,0:T(8,128)(2,1)S(1)}, u32[]{:S(2)}, u32[]{:S(2)}) collective-permute-start(bf16[8,90,192]{2,1,0:T(8,128)(2,1)S(1)} %get-tuple-element.22), channel_id=1, source_target_pairs={{1,0},{2,1},{3,2},{4,3},{5,4},{6,5},{7,6},{8,7},{9,8},{10,9},{11,1... | collective-permute-start | bytes 829448 | tf_op jit(solution)/shard_map/ppermute | solution.py:344
  9.0 14.4 %all-to-all-start = ((f32[16,2,192]{2,1,0:T(2,128)}), f32[16,2,192]{2,1,0:T(2,128)S(1)}, u32[]{:S(2)}, u32[]{:S(2)}) async-start(f32[16,2,192]{2,1,0:T(2,128)} %get-tuple-element.23), calls=%async_computation | async-start | bytes 65536 | tf_op jit(solution)/shard_map/all_to_all | solution.py:347
  14.5 8.9 %copy-start = (bf16[2,90,8,192]{3,2,1,0:T(8,128)(2,1)S(1)}, bf16[2,90,8,192]{3,2,1,0:T(8,128)(2,1)}, u32[]{:S(2)}) copy-start(bf16[2,90,8,192]{3,2,1,0:T(8,128)(2,1)} %refs_9_.1) | copy-start | bytes 1658884
  14.5 8.9 %copy-start.10 = (bf16[192,192]{1,0:T(8,128)(2,1)S(1)}, bf16[192,192]{1,0:T(8,128)(2,1)}, u32[]{:S(2)}) copy-start(bf16[192,192]{1,0:T(8,128)(2,1)} %constant.2.clone.refs_8_) | copy-start | bytes 221188
  14.5 8.9 %copy-start.12 = (f32[3,192]{1,0:T(4,128)S(1)}, f32[3,192]{1,0:T(4,128)}, u32[]{:S(2)}) copy-start(f32[3,192]{1,0:T(4,128)} %refs_4_.5) | copy-start | bytes 6916
  14.5 8.9 %copy-start.13 = (f32[3,192]{1,0:T(4,128)S(1)}, f32[3,192]{1,0:T(4,128)}, u32[]{:S(2)}) copy-start(f32[3,192]{1,0:T(4,128)} %refs_5_.5) | copy-start | bytes 6916
  22.3 1.1 %copy-start.3 = (bf16[2,192,1792]{2,1,0:T(8,128)(2,1)}, bf16[2,192,1792]{2,1,0:T(8,128)(2,1)S(1)}, u32[]{:S(2)}) copy-start(bf16[2,192,1792]{2,1,0:T(8,128)(2,1)S(1)} %get-tuple-element.24.refs_6_) | copy-start | bytes 4128772
  30.3 1.0 %copy-start.4 = (f32[3,720,128]{2,1,0:T(8,128)}, f32[3,720,128]{2,1,0:T(8,128)S(1)}, u32[]{:S(2)}) copy-start(f32[3,720,128]{2,1,0:T(8,128)S(1)} %get-tuple-element.26.refs_0_) | copy-start | bytes 3317764
  31.3 19.6 %collective-permute-start.2 = (bf16[3,90,128]{2,1,0:T(8,128)(2,1)S(1)}, bf16[3,90,128]{2,1,0:T(8,128)(2,1)S(1)}, u32[]{:S(2)}, u32[]{:S(2)}) collective-permute-start(bf16[3,90,128]{2,1,0:T(8,128)(2,1)S(1)} %get-tuple-element.27), channel_id=1, source_target_pairs={{0,1},{1,2},{2,3},{3,4},{4,5},{5,6},{6,7},{7,8},{8,9},{9,10},{10,1... | collective-permute-start | bytes 207368 | tf_op jit(solution)/shard_map/ppermute | solution.py:344
  35.3 15.6 %collective-permute-start.3 = (bf16[3,90,128]{2,1,0:T(8,128)(2,1)S(1)}, bf16[3,90,128]{2,1,0:T(8,128)(2,1)S(1)}, u32[]{:S(2)}, u32[]{:S(2)}) collective-permute-start(bf16[3,90,128]{2,1,0:T(8,128)(2,1)S(1)} %get-tuple-element.28), channel_id=1, source_target_pairs={{1,0},{2,1},{3,2},{4,3},{5,4},{6,5},{7,6},{8,7},{9,8},{10,9},{11,1... | collective-permute-start | bytes 207368 | tf_op jit(solution)/shard_map/ppermute | solution.py:344
  36.0 14.9 %all-to-all-start.1 = ((f32[16,2,192]{2,1,0:T(2,128)}), f32[16,2,192]{2,1,0:T(2,128)S(1)}, u32[]{:S(2)}, u32[]{:S(2)}) async-start(f32[16,2,192]{2,1,0:T(2,128)} %get-tuple-element.29), calls=%async_computation.1 | async-start | bytes 65536 | tf_op jit(solution)/shard_map/all_to_all | solution.py:347
  48.8 1.1 %copy-start.1 = (bf16[2,192,1792]{2,1,0:T(8,128)(2,1)}, bf16[2,192,1792]{2,1,0:T(8,128)(2,1)S(1)}, u32[]{:S(2)}) copy-start(bf16[2,192,1792]{2,1,0:T(8,128)(2,1)S(1)} %get-tuple-element.30.refs_6_) | copy-start | bytes 4128772
  49.9 1.0 %copy-start.6 = (f32[3,720,128]{2,1,0:T(8,128)}, f32[3,720,128]{2,1,0:T(8,128)S(1)}, u32[]{:S(2)}) copy-start(f32[3,720,128]{2,1,0:T(8,128)S(1)} %get-tuple-element.31.refs_7_) | copy-start | bytes 3317764
  50.9 1.2 %copy-start.5 = (f32[3,720,128]{2,1,0:T(8,128)S(1)}, f32[3,720,128]{2,1,0:T(8,128)}, u32[]{:S(2)}) copy-start(f32[3,720,128]{2,1,0:T(8,128)} %copy-done.4) | copy-start | bytes 3317764
  52.1 1.2 %copy-start.7 = (f32[3,720,128]{2,1,0:T(8,128)S(1)}, f32[3,720,128]{2,1,0:T(8,128)}, u32[]{:S(2)}) copy-start(f32[3,720,128]{2,1,0:T(8,128)} %copy-done.6) | copy-start | bytes 3317764
  58.8 17.9 %collective-permute-start.4 = (bf16[3,90,128]{2,1,0:T(8,128)(2,1)S(1)}, bf16[3,90,128]{2,1,0:T(8,128)(2,1)S(1)}, u32[]{:S(2)}, u32[]{:S(2)}) collective-permute-start(bf16[3,90,128]{2,1,0:T(8,128)(2,1)S(1)} %get-tuple-element.34), channel_id=1, source_target_pairs={{0,1},{1,2},{2,3},{3,4},{4,5},{5,6},{6,7},{7,8},{8,9},{9,10},{10,1... | collective-permute-start | bytes 207368 | tf_op jit(solution)/shard_map/ppermute | solution.py:344
  59.3 17.5 %collective-permute-start.5 = (bf16[3,90,128]{2,1,0:T(8,128)(2,1)S(1)}, bf16[3,90,128]{2,1,0:T(8,128)(2,1)S(1)}, u32[]{:S(2)}, u32[]{:S(2)}) collective-permute-start(bf16[3,90,128]{2,1,0:T(8,128)(2,1)S(1)} %get-tuple-element.35), channel_id=1, source_target_pairs={{1,0},{2,1},{3,2},{4,3},{5,4},{6,5},{7,6},{8,7},{9,8},{10,9},{11,1... | collective-permute-start | bytes 207368 | tf_op jit(solution)/shard_map/ppermute | solution.py:344
  63.3 13.4 %all-to-all-start.2 = ((f32[16,2,192]{2,1,0:T(2,128)}), f32[16,2,192]{2,1,0:T(2,128)S(1)}, u32[]{:S(2)}, u32[]{:S(2)}) async-start(f32[16,2,192]{2,1,0:T(2,128)} %get-tuple-element.36), calls=%async_computation.2 | async-start | bytes 65536 | tf_op jit(solution)/shard_map/all_to_all | solution.py:347
  74.7 1.1 %copy-start.2 = (bf16[2,192,1792]{2,1,0:T(8,128)(2,1)}, bf16[2,192,1792]{2,1,0:T(8,128)(2,1)S(1)}, u32[]{:S(2)}) copy-start(bf16[2,192,1792]{2,1,0:T(8,128)(2,1)S(1)} %get-tuple-element.37.refs_6_) | copy-start | bytes 4128772
  75.8 1.0 %copy-start.8 = (f32[3,720,128]{2,1,0:T(8,128)}, f32[3,720,128]{2,1,0:T(8,128)S(1)}, u32[]{:S(2)}) copy-start(f32[3,720,128]{2,1,0:T(8,128)S(1)} %get-tuple-element.38.refs_7_) | copy-start | bytes 3317764
  76.8 1.2 %copy-start.9 = (f32[3,720,128]{2,1,0:T(8,128)S(1)}, f32[3,720,128]{2,1,0:T(8,128)}, u32[]{:S(2)}) copy-start(f32[3,720,128]{2,1,0:T(8,128)} %copy-done.8) | copy-start | bytes 3317764

commit v5 on v4

--- a/solution.py
+++ b/solution.py
@@ -14,7 +14,7 @@
 HALF = LANES // 2
 COLS = 8
 SLABS = 10
-UNROLL = 2
+UNROLL = 11
 PLANES = 3
 VMEM = pl.BlockSpec(memory_space=pltpu.VMEM)
 HBM = pl.BlockSpec(memory_space=pltpu.HBM)
@@ -143,16 +143,28 @@
     return jnp.concatenate([held[t, here, :], rest], axis=1)
 
 
-def begin_kernel(video, caches, sums, first, last, wide, held, sem):
+def group_sums(pieces, same):
+    total = jnp.concatenate([jnp.sum(v, axis=0, keepdims=True) for v in pieces], axis=0)
+    high = total.astype(jnp.bfloat16)
+    left = total - high.astype(jnp.float32)
+    middle = left.astype(jnp.bfloat16)
+    low = (left - middle.astype(jnp.float32)).astype(jnp.bfloat16)
+    split = jnp.concatenate([high, middle, low], axis=0)
+    sums = jnp.dot(split, same, preferred_element_type=jnp.float32)
+    return sums[0:2] + sums[2:4] + sums[4:6]
+
+
+def begin_kernel(video, caches, same, sums, first, last, wide, held, alike, sem):
     layers, frames, rows, cols, channels = caches.shape
     copies = [pltpu.make_async_copy(video, held.at[0], sem.at[0])]
     for layer in range(layers):
         copies.append(
             pltpu.make_async_copy(caches.at[layer], held.at[layer + 1], sem.at[layer + 1])
         )
-    for copy in copies:
+    fetch = pltpu.make_async_copy(same, alike, sem.at[layers + 1])
+    for copy in copies + [fetch]:
         copy.start()
-    half = channels - LANES
+    half, places = channels - LANES, rows * cols
     total = [jnp.zeros((COLS, LANES), jnp.float32), jnp.zeros((COLS, half), jnp.float32)]
     square = list(total)
     for group, copy in enumerate(copies):
@@ -164,33 +176,31 @@
                 for i in range(2):
                     total[i] = total[i] + jnp.sum(parts[i], axis=0)
                     square[i] = square[i] + jnp.sum(parts[i] * parts[i], axis=0)
-            wide[0] = parts[0].reshape(rows * cols, LANES)
-            wide[1, :, :half] = parts[1].reshape(rows * cols, half)
-            for out, column in ((first, 0), (last, cols - 1)):
-                found = [wide[i, pl.ds(column, rows, stride=cols), :] for i in range(2)]
-                edge = jnp.concatenate([found[0], found[1][:, :half]], axis=1)
-                out[group * frames + frame] = edge.astype(jnp.bfloat16)
-    both = [
-        jnp.concatenate([jnp.sum(v, axis=0, keepdims=True) for v in pieces], axis=1)
-        for pieces in (total, square)
-    ]
-    sums[...] = jnp.broadcast_to(jnp.concatenate(both, axis=0)[None], sums.shape)
-
-
-def cached_kernel(layer, chunk, caches, before, after, weights, bias, out, ordered, *scratches):
-    edges, *slabs, cache, weight, taps, sem = scratches
-    _, frames, rows, cols, channels = caches.shape
+            wide[frame] = parts[0].reshape(places, LANES)
+            wide[2, :, HALF * frame : HALF * (frame + 1)] = parts[1].reshape(places, half)
+        for out, column in ((first, 0), (last, cols - 1)):
+            for plane in range(PLANES):
+                edge = wide[plane, pl.ds(column, rows, stride=cols), :]
+                out[group * PLANES + plane] = edge.astype(jnp.bfloat16)
+    fetch.wait()
+    both = group_sums([jnp.concatenate(v, axis=1) for v in (total, square)], alike[...])
+    sums[...] = jnp.broadcast_to(both[None], sums.shape)
+
+
+def cached_kernel(layer, chunk, far, caches, before, after, weights, bias, *refs):
+    out, ordered, edges, *slabs, cache, weight, taps, sem = refs
+    if far:
+        away, out, *slabs = out, slabs[0], *slabs[1:]
+    _, _, rows, cols, channels = caches.shape
     places = rows * cols
     begun = pltpu.make_async_copy(caches.at[layer], cache, sem.at[0])
     fetch = pltpu.make_async_copy(weights.at[layer], weight, sem.at[1])
     begun.start()
     fetch.start()
     begun.wait()
-    origin = (layer + 1) * frames
     for side, ref in enumerate((before, after)):
-        found = planes(*(ref[origin + frame].astype(jnp.float32) for frame in range(2)))
         for plane in range(PLANES):
-            edges[side, plane] = found[plane]
+            edges[side, plane] = ref[(layer + 1) * PLANES + plane].astype(jnp.float32)
 
     def row_of(h):
         return planes(*(cache[frame, h].astype(jnp.float32) for frame in range(2)))
@@ -206,27 +216,19 @@
     store.start()
     constant = bias[layer : layer + 1, :]
     tables = [taps[p] for p in range(2)]
-    for start in range(0, places, chunk):
-        value = product([(slabs[1], tables[0])], start, chunk)
-        put_planes(out, 1, pl.ds(start, chunk), value + constant)
+    value = product([(slabs[1], tables[0])], 0, places)
+    put_planes(out, 1, pl.ds(0, places), value + constant)
     for start in range(0, places, chunk):
         value = product([(slabs[0], tables[0]), (slabs[1], tables[1])], start, chunk)
         put_planes(out, 0, pl.ds(start, chunk), value + constant)
+    if far:
+        leave = pltpu.make_async_copy(out, away, sem.at[3])
+        leave.start()
+        leave.wait()
     store.wait()
 
 
-def group_means(stats, same, entries):
-    total = jnp.sum(stats, axis=0)
-    high = total.astype(jnp.bfloat16)
-    left = total - high.astype(jnp.float32)
-    middle = left.astype(jnp.bfloat16)
-    low = (left - middle.astype(jnp.float32)).astype(jnp.bfloat16)
-    split = jnp.concatenate([high, middle, low], axis=0)
-    sums = jnp.dot(split, same, preferred_element_type=jnp.float32)
-    return (sums[0:2] + sums[2:4] + sums[4:6]) / entries
-
-
-def active_kernel(layer, chunk, entries, final, *refs):
+def active_kernel(layer, chunk, far, entries, final, *refs):
     x, before, after, stats, gain, shift, ordered, part, same = refs[:9]
     rest = refs[9:]
     residual = None
@@ -238,16 +240,23 @@
         y, carried, *rest = rest
     else:
         y, carried, sums, first, last, *rest = rest
-    edges, *slabs, kept, held, taps, sem = rest
+    edges, *slabs, kept, held, taps, alike, sem = rest
+    away = None
+    if far:
+        away, part, *slabs = part, *slabs
     frames, rows, cols, channels = kept.shape
     places = rows * cols
     fetch = [pltpu.make_async_copy(ordered, taps, sem.at[1])]
+    if not final:
+        fetch.append(pltpu.make_async_copy(same, alike, sem.at[4]))
+    if far:
+        fetch.append(pltpu.make_async_copy(away, part, sem.at[3]))
     if residual is not None:
         fetch.append(pltpu.make_async_copy(residual, held, sem.at[2]))
     for copy in fetch:
         copy.start()
 
-    means = group_means(stats[...], same[...], entries)
+    means = jnp.sum(stats[...], axis=0) / entries
     average = means[0:1]
     variance = means[1:2] - average * average
     scale = lax.rsqrt(variance + EPSILON) * gain[layer : layer + 1, :]
@@ -260,10 +269,7 @@
         return [silu_of_twice(v * a + b) for v, a, b in zip(values, scales, offsets)]
 
     for side, ref in enumerate((before, after)):
-        if layer:
-            values = [ref[plane].astype(jnp.float32) for plane in range(PLANES)]
-        else:
-            values = planes(*(ref[frame].astype(jnp.float32) for frame in range(2)))
+        values = [ref[plane].astype(jnp.float32) for plane in range(PLANES)]
         for plane, value in enumerate(act(values)):
             edges[side, plane] = value
 
@@ -290,16 +296,16 @@
     tables = [taps[p] for p in range(2)]
     moments = [jnp.zeros((COLS, channels), jnp.float32)] * 2
 
-    def finish(t, start, value, moments):
-        here, span = pl.ds(start, chunk), pl.ds(start // COLS, chunk // COLS)
-        shape = (chunk // COLS, COLS, channels)
+    def finish(t, start, size, value, moments):
+        here, span = pl.ds(start, size), pl.ds(start // COLS, size // COLS)
+        shape = (size // COLS, COLS, channels)
         value = value + get_planes(part, t, here)
         if final:
             value = value + get_planes(x, t, here)
             y[t, span] = value.reshape(shape).astype(jnp.bfloat16)
             return moments
         if residual is not None:
-            value = value + held[t, span].astype(jnp.float32).reshape(chunk, channels)
+            value = value + held[t, span].astype(jnp.float32).reshape(size, channels)
         put_planes(y, t, here, value)
         folded = value.reshape(shape)
         return [
@@ -307,16 +313,14 @@
             moments[1] + jnp.sum(folded * folded, axis=0),
         ]
 
-    starts = range(0, places, chunk)
-    for start in starts:
-        value = product([(slabs[0], tables[1])], start, chunk)
-        moments = finish(0, start, value, moments)
-    for start in starts:
+    value = product([(slabs[0], tables[1])], 0, places)
+    moments = finish(0, 0, places, value, moments)
+    for start in range(0, places, chunk):
         value = product([(slabs[0], tables[0]), (slabs[1], tables[1])], start, chunk)
-        moments = finish(1, start, value, moments)
+        moments = finish(1, start, chunk, value, moments)
     if not final:
-        both = [jnp.sum(v, axis=0, keepdims=True) for v in moments]
-        sums[...] = jnp.broadcast_to(jnp.concatenate(both, axis=0)[None], sums.shape)
+        both = group_sums(moments, alike[...])
+        sums[...] = jnp.broadcast_to(both[None], sums.shape)
         for plane in range(PLANES):
             for out, column in ((first, 0), (last, cols - 1)):
                 edge = y[plane, pl.ds(column, rows, stride=cols), :]
@@ -324,9 +328,9 @@
     copy.wait()
 
 
-def scratch(frames, rows):
+def scratch(frames, rows, room):
     slab = pltpu.VMEM((SLABS, rows * COLS + 16, LANES), jnp.bfloat16)
-    return [pltpu.VMEM((2, PLANES, rows, LANES), jnp.float32)] + [slab] * frames
+    return [pltpu.VMEM((2, PLANES, rows, LANES), jnp.float32)] + room + [slab] * frames
 
 
 def local(video_span, caches, norm_gains, shifts, weights, biases):
@@ -351,42 +355,48 @@
 
     turned = in_hbm(jnp.swapaxes(weights, 1, 2))
     caches, video = in_hbm(caches), in_hbm(video_span)
+    members = channels // GROUPS
+    alike = np.kron(np.eye(GROUPS), np.ones((members, members)))
+    same = in_hbm(jnp.asarray(alike, jnp.bfloat16))
     spread = jax.ShapeDtypeStruct((peers, 2, channels), jnp.float32)
-    brim = jax.ShapeDtypeStruct(((layers + 1) * frames, rows, channels), jnp.bfloat16)
+    brim = jax.ShapeDtypeStruct(((layers + 1) * PLANES, rows, LANES), jnp.bfloat16)
     sums, first, last = pl.pallas_call(
         begin_kernel,
         out_shape=[spread, brim, brim],
-        in_specs=[HBM, HBM],
+        in_specs=[HBM] * 3,
         out_specs=[VMEM] * 3,
         scratch_shapes=[
-            pltpu.VMEM((2, places, LANES), jnp.float32),
+            pltpu.VMEM((PLANES, places, LANES), jnp.float32),
             pltpu.VMEM((layers + 1,) + video_span.shape, jnp.bfloat16),
-            pltpu.SemaphoreType.DMA((layers + 1,)),
+            pltpu.VMEM(same.shape, same.dtype),
+            pltpu.SemaphoreType.DMA((layers + 2,)),
         ],
         compiler_params=pltpu.CompilerParams(vmem_limit_bytes=24 << 20),
         name="begin",
-    )(video, caches)
+    )(video, caches, same)
     brims = around(first, last)
     before, after = brims
-    members = channels // GROUPS
-    same = jnp.asarray(np.kron(np.eye(GROUPS), np.ones((members, members))), jnp.bfloat16)
     stats = gathered(sums)
 
-    def cached_part(layer):
+    def room(far):
+        return [pltpu.VMEM((PLANES, places, LANES), jnp.float32)] if far else []
+
+    def cached_part(layer, far):
+        planar = pltpu.HBM if far else jax.ShapeDtypeStruct
         return pl.pallas_call(
-            functools.partial(cached_kernel, layer, chunk),
+            functools.partial(cached_kernel, layer, chunk, far),
             out_shape=[
-                jax.ShapeDtypeStruct((PLANES, places, LANES), jnp.float32),
-                jax.ShapeDtypeStruct((2, channels, tiles), weights.dtype),
+                planar((PLANES, places, LANES), jnp.float32),
+                pltpu.HBM((2, channels, tiles), weights.dtype),
             ],
             in_specs=[HBM, VMEM, VMEM, HBM, VMEM],
-            out_specs=[VMEM, HBM],
-            scratch_shapes=scratch(frames, rows)
+            out_specs=[HBM if far else VMEM, HBM],
+            scratch_shapes=scratch(frames, rows, room(far))
             + [
                 pltpu.VMEM(video_span.shape, jnp.bfloat16),
                 pltpu.VMEM((channels, weights.shape[1]), weights.dtype),
                 pltpu.VMEM((3, channels, tiles), weights.dtype),
-                pltpu.SemaphoreType.DMA((3,)),
+                pltpu.SemaphoreType.DMA((4,)),
             ],
             compiler_params=pltpu.CompilerParams(vmem_limit_bytes=24 << 20),
             name="cached",
@@ -396,9 +406,12 @@
     carried = None
     for layer in range(layers):
         final = layer == layers - 1
-        part, ordered = cached_part(layer)
+        far = 0 < layer < layers - 1
+        part, ordered = cached_part(layer, far)
+        if far:
+            part = in_hbm(part)
         operands = [x, before, after, stats, norm_gains, shifts, in_hbm(ordered), part, same]
-        specs = [VMEM] * 6 + [HBM, VMEM, VMEM]
+        specs = [VMEM] * 6 + [HBM, HBM if far else VMEM, HBM]
         aliases = {}
         if layer == 1:
             operands.append(video)
@@ -417,16 +430,17 @@
             outs += [spread, edge, edge]
             out_specs += [VMEM] * 3
         results = pl.pallas_call(
-            functools.partial(active_kernel, layer, chunk, entries, final),
+            functools.partial(active_kernel, layer, chunk, far, entries, final),
             out_shape=outs,
             in_specs=specs,
             out_specs=out_specs,
-            scratch_shapes=scratch(frames, rows)
+            scratch_shapes=scratch(frames, rows, room(far))
             + [
                 pltpu.VMEM(video_span.shape, jnp.bfloat16),
                 pltpu.VMEM(video_span.shape, jnp.bfloat16),
                 pltpu.VMEM((2, channels, tiles), weights.dtype),
-                pltpu.SemaphoreType.DMA((3,)),
+                pltpu.VMEM(same.shape, same.dtype),
+                pltpu.SemaphoreType.DMA((5,)),
             ],
             compiler_params=pltpu.CompilerParams(vmem_limit_bytes=24 << 20),
             input_output_aliases=aliases,

time: 84.2 us -> 66.1 us (0.79)
  local copies, waits for them, and re-layouts: 9.99 us -> 1.39 us
  Pallas kernels: 43.7 us -> 36.4 us
  starting transfers between devices: 27.2 us -> 25.9 us
  waiting for transfers between devices: 1.95 us -> 0.94 us
    unnamed x28 -> x14, local copies, waits for them, and re-layouts: 9.99 us -> 1.39 us
    pallas_call x6, Pallas kernels: 41 us -> 33.6 us  [the longest x3 19.3 us: cached_part(): pl.pallas_call(functools.partial(cached_kernel, layer, chunk, far), out_s...]
    all_to_all x3, starting transfers between devices: 12.4 us -> 11.2 us  [gathered(): return lax.all_to_all(sums, 'lon', 0, 0)]
    ppermute x6, waiting for transfers between devices: 1.94 us -> 0.83 us  [around(): return (lax.ppermute(last, 'lon', up), lax.ppermute(first, 'lon', down))]
  transfers between devices with their start and end apart: 9 -> 9, of which waited for: 2 -> 2; matrix products, arithmetic and copies ran while one was open for 0% -> 0% of each run, Pallas kernels for 27% -> 29%
where the time goes in v5:
time: 66.1 us; the launch traced here: 65.6 us
  Pallas kernels  36.4 us (55%)
  starting transfers between devices  25.9 us (39%)
  local copies, waits for them, and re-layouts  1.39 us (2%)
  between operations  0.95 us (1%)
  waiting for transfers between devices  0.94 us (1%)
    pallas_call x3, Pallas kernels, cached_part(): pl.pallas_call(functools.partial(cached_kernel, layer, chunk, far), out_s...  19.3 us
    ppermute x6, starting transfers between devices, around(): return (lax.ppermute(last, 'lon', up), lax.ppermute(first, 'lon', down))  14.7 us
    pallas_call x3, Pallas kernels, local(): pl.pallas_call(functools.partial(active_kernel, layer, chunk, far, entrie...  14.2 us
    all_to_all x3, starting transfers between devices, gathered(): return lax.all_to_all(sums, 'lon', 0, 0)  11.2 us
    pallas_call x1, Pallas kernels, local(): pl.pallas_call(begin_kernel, out_shape=[spread, brim, brim], in_specs=[HB...  2.88 us
    unnamed x14, local copies, waits for them, and re-layouts  1.39 us
  transfers between devices with their start and end apart: 9, of which 2 were waited for; matrix products, arithmetic and copies ran while one was open for 0% of the time, Pallas kernels for 29%

profile of v5, /device:TPU:0, one launch (start us, length us, event | category | flops | bytes accessed | tf_op | source)
XLA Modules:
  0.0 65.6 jit_solution(11764028266389901256)
XLA Ops:
  0.6 0.0 copy-start.3
  0.6 2.9 %begin.1 = (f32[16,2,192]{2,1,0:T(2,128)}, bf16[12,90,128]{2,1,0:T(8,128)(2,1)S(1)}, bf16[12,90,128]{2,1,0:T(8,128)(2,1)S(1)}) custom-call(bf16[2,90,8,192]{3,2,1,0:T(8,128)(2,1)} %refs_9_.1, bf16[3,2,90,8,192]{4,3,2,1,0:T(8,128)(2,1)} %caches.7, bf16[192,192]{1,0:T(8,128)(2,1)} %constant.2.clone.same.refs_8_), custom_call_target="tpu_custom_call" | custom-call | tf_op jit(solution)/shard_map/begin/pallas_call | solution.py:363
  3.5 0.5 collective-permute-start
  4.1 5.0 %collective-permute-start.1 = (bf16[12,90,128]{2,1,0:T(8,128)(2,1)S(1)}, bf16[12,90,128]{2,1,0:T(8,128)(2,1)S(1)}, u32[]{:S(2)}, u32[]{:S(2)}) collective-permute-start(bf16[12,90,128]{2,1,0:T(8,128)(2,1)S(1)} %get-tuple-element.22), channel_id=1, source_target_pairs={{1,0},{2,1},{3,2},{4,3},{5,4},{6,5},{7,6},{8,7},{9,8},{10,9},{11,1... | collective-permute-start | bytes 829448 | tf_op jit(solution)/shard_map/ppermute | solution.py:348
  9.1 3.6 %all-to-all-start = ((f32[16,2,192]{2,1,0:T(2,128)}), f32[16,2,192]{2,1,0:T(2,128)S(1)}, u32[]{:S(2)}, u32[]{:S(2)}) async-start(f32[16,2,192]{2,1,0:T(2,128)} %get-tuple-element.23), calls=%async_computation | async-start | bytes 65536 | tf_op jit(solution)/shard_map/all_to_all | solution.py:351
  12.7 0.8 %collective-permute-done.before.refs_1_ = bf16[12,90,128]{2,1,0:T(8,128)(2,1)S(1)} collective-permute-done((bf16[12,90,128]{2,1,0:T(8,128)(2,1)S(1)}, bf16[12,90,128]{2,1,0:T(8,128)(2,1)S(1)}, u32[]{:S(2)}, u32[]{:S(2)}) %collective-permute-start) | collective-permute-done | bytes 276512 | tf_op jit(solution)/shard_map/ppermute | solution.py:348
  13.6 0.0 collective-permute-done.1.after.refs_2_
  13.6 0.0 copy-done.3
  13.6 0.0 copy-start
  13.6 0.0 copy-start.4
  13.6 0.0 copy-start.5
  13.6 6.4 %cached.3 = (f32[3,720,128]{2,1,0:T(8,128)S(1)}, bf16[2,192,1792]{2,1,0:T(8,128)(2,1)}) custom-call(bf16[3,2,90,8,192]{4,3,2,1,0:T(8,128)(2,1)} %caches.7, bf16[12,90,128]{2,1,0:T(8,128)(2,1)S(1)} %collective-permute-done.before.refs_1_, bf16[12,90,128]{2,1,0:T(8,128)(2,1)S(1)} %collective-permute-done.1.after.refs_2_, bf16[3,192,5184]{2,1,0:T(8,128)(2,1)} %bitcast.1, ...), custom_call_target="tpu_custom_call" | custom-call | tf_op jit(solution)/shard_map/cached/pallas_call | solution.py:386
  20.0 0.0 all-to-all-done.refs_3_
  20.0 0.0 copy-start.1
  20.0 0.6 copy-done.1
  20.6 0.0 copy-done
  20.6 0.0 copy-done.4
  20.6 0.0 copy-done.5
  20.6 0.0 copy-start.2
  20.6 0.8 %copy-done.2 = f32[16,2,192]{2,1,0:T(2,128)S(1)} copy-done((f32[16,2,192]{2,1,0:T(2,128)S(1)}, f32[16,2,192]{2,1,0:T(2,128)}, u32[]{:S(2)}) %copy-start.2) | copy-done | bytes 24600
  21.4 4.5 %active.3 = (f32[3,720,128]{2,1,0:T(8,128)S(1)}, bf16[3,2,90,8,192]{4,3,2,1,0:T(8,128)(2,1)}, f32[16,2,192]{2,1,0:T(2,128)S(1)}, bf16[3,90,128]{2,1,0:T(8,128)(2,1)}, bf16[3,90,128]{2,1,0:T(8,128)(2,1)}) custom-call(bf16[2,90,8,192]{3,2,1,0:T(8,128)(2,1)S(1)} %copy-done, bf16[12,90,128]{2,1,0:T(8,128)(2,1)S(1)} %collective-permute-done.before.refs_1_, ...), custom_call_target="tpu_custom_call" | custom-call | tf_op jit(solution)/shard_map/active/pallas_call | solution.py:432
  25.8 0.0 copy-start.6
  25.8 2.5 %collective-permute-start.2 = (bf16[3,90,128]{2,1,0:T(8,128)(2,1)}, bf16[3,90,128]{2,1,0:T(8,128)(2,1)S(1)}, u32[]{:S(2)}, u32[]{:S(2)}) collective-permute-start(bf16[3,90,128]{2,1,0:T(8,128)(2,1)} %get-tuple-element.27), channel_id=1, source_target_pairs={{0,1},{1,2},{2,3},{3,4},{4,5},{5,6},{6,7},{7,8},{8,9},{9,10},{10,1... | collective-permute-start | bytes 207368 | tf_op jit(solution)/shard_map/ppermute | solution.py:348
  28.4 2.1 %collective-permute-start.3 = (bf16[3,90,128]{2,1,0:T(8,128)(2,1)}, bf16[3,90,128]{2,1,0:T(8,128)(2,1)S(1)}, u32[]{:S(2)}, u32[]{:S(2)}) collective-permute-start(bf16[3,90,128]{2,1,0:T(8,128)(2,1)} %get-tuple-element.28), channel_id=1, source_target_pairs={{1,0},{2,1},{3,2},{4,3},{5,4},{6,5},{7,6},{8,7},{9,8},{10,9},{11,1... | collective-permute-start | bytes 207368 | tf_op jit(solution)/shard_map/ppermute | solution.py:348
  30.5 0.0 copy-done.6
  30.5 3.9 %all-to-all-start.1 = ((f32[16,2,192]{2,1,0:T(2,128)}), f32[16,2,192]{2,1,0:T(2,128)S(1)}, u32[]{:S(2)}, u32[]{:S(2)}) async-start(f32[16,2,192]{2,1,0:T(2,128)} %copy-done.6), calls=%async_computation.1 | async-start | bytes 65536 | tf_op jit(solution)/shard_map/all_to_all | solution.py:351
  34.4 6.7 %cached.4 = (f32[3,720,128]{2,1,0:T(8,128)}, bf16[2,192,1792]{2,1,0:T(8,128)(2,1)}) custom-call(bf16[3,2,90,8,192]{4,3,2,1,0:T(8,128)(2,1)} %caches.7, bf16[12,90,128]{2,1,0:T(8,128)(2,1)S(1)} %collective-permute-done.before.refs_1_, bf16[12,90,128]{2,1,0:T(8,128)(2,1)S(1)} %collective-permute-done.1.after.refs_2_, bf16[3,192,5184]{2,1,0:T(8,128)(2,1)} %bitcast.2, ...), custom_call_target="tpu_custom_call" | custom-call | tf_op jit(solution)/shard_map/cached/pallas_call | solution.py:386
  41.1 0.0 all-to-all-done.1.refs_3_
  41.1 0.0 collective-permute-done.2.refs_1_
  41.1 0.0 collective-permute-done.3.refs_2_
  41.1 5.3 %active.4 = (f32[3,720,128]{2,1,0:T(8,128)S(1)}, bf16[3,2,90,8,192]{4,3,2,1,0:T(8,128)(2,1)}, f32[16,2,192]{2,1,0:T(2,128)}, bf16[3,90,128]{2,1,0:T(8,128)(2,1)S(1)}, bf16[3,90,128]{2,1,0:T(8,128)(2,1)S(1)}) custom-call(f32[3,720,128]{2,1,0:T(8,128)S(1)} %get-tuple-element.26.refs_0_, ...), custom_call_target="tpu_custom_call", output_to_operand_aliasing={{1}: (10, {})} | custom-call | tf_op jit(solution)/shard_map/active/pallas_call | solution.py:432
  46.4 0.5 collective-permute-start.4
  46.9 4.0 %collective-permute-start.5 = (bf16[3,90,128]{2,1,0:T(8,128)(2,1)S(1)}, bf16[3,90,128]{2,1,0:T(8,128)(2,1)S(1)}, u32[]{:S(2)}, u32[]{:S(2)}) collective-permute-start(bf16[3,90,128]{2,1,0:T(8,128)(2,1)S(1)} %get-tuple-element.35), channel_id=1, source_target_pairs={{1,0},{2,1},{3,2},{4,3},{5,4},{6,5},{7,6},{8,7},{9,8},{10,9},{11,1... | collective-permute-start | bytes 207368 | tf_op jit(solution)/shard_map/ppermute | solution.py:348
  50.9 3.7 %all-to-all-start.2 = ((f32[16,2,192]{2,1,0:T(2,128)}), f32[16,2,192]{2,1,0:T(2,128)S(1)}, u32[]{:S(2)}, u32[]{:S(2)}) async-start(f32[16,2,192]{2,1,0:T(2,128)} %get-tuple-element.36), calls=%async_computation.2 | async-start | bytes 65536 | tf_op jit(solution)/shard_map/all_to_all | solution.py:351
  54.6 6.3 %cached.5 = (f32[3,720,128]{2,1,0:T(8,128)S(1)}, bf16[2,192,1792]{2,1,0:T(8,128)(2,1)}) custom-call(bf16[3,2,90,8,192]{4,3,2,1,0:T(8,128)(2,1)} %caches.7, bf16[12,90,128]{2,1,0:T(8,128)(2,1)S(1)} %collective-permute-done.before.refs_1_, bf16[12,90,128]{2,1,0:T(8,128)(2,1)S(1)} %collective-permute-done.1.after.refs_2_, bf16[3,192,5184]{2,1,0:T(8,128)(2,1)} %bitcast.3, ...), custom_call_target="tpu_custom_call" | custom-call | tf_op jit(solution)/shard_map/cached/pallas_call | solution.py:386
  60.9 0.1 all-to-all-done.2.refs_3_
  61.0 0.0 collective-permute-done.4.refs_1_
  61.0 0.0 collective-permute-done.5.refs_2_
  61.0 4.5 %active.5 = (bf16[2,90,8,192]{3,2,1,0:T(8,128)(2,1)}, bf16[3,2,90,8,192]{4,3,2,1,0:T(8,128)(2,1)}) custom-call(f32[3,720,128]{2,1,0:T(8,128)S(1)} %get-tuple-element.33.refs_0_, bf16[3,90,128]{2,1,0:T(8,128)(2,1)S(1)} %collective-permute-done.4.refs_1_, bf16[3,90,128]{2,1,0:T(8,128)(2,1)S(1)} %collective-permute-done.5.refs_2_, ...), custom_call_target="tpu_custom_call", output_to_operand_aliasing={{1}: (9, {})} | custom-call | tf_op jit(solution)/shard_map/active/pallas_call | solution.py:432
Async XLA Ops:
  0.6 12.9 %copy-start.3 = (f32[3,192]{1,0:T(4,128)S(1)}, f32[3,192]{1,0:T(4,128)}, u32[]{:S(2)}) copy-start(f32[3,192]{1,0:T(4,128)} %bias.5) | copy-start | bytes 6916
  3.5 10.0 %collective-permute-start = (bf16[12,90,128]{2,1,0:T(8,128)(2,1)S(1)}, bf16[12,90,128]{2,1,0:T(8,128)(2,1)S(1)}, u32[]{:S(2)}, u32[]{:S(2)}) collective-permute-start(bf16[12,90,128]{2,1,0:T(8,128)(2,1)S(1)} %get-tuple-element.21), channel_id=1, source_target_pairs={{0,1},{1,2},{2,3},{3,4},{4,5},{5,6},{6,7},{7,8},{8,9},{9,10},{10,1... | collective-permute-start | bytes 829448 | tf_op jit(solution)/shard_map/ppermute | solution.py:348
  4.1 9.5 %collective-permute-start.1 = (bf16[12,90,128]{2,1,0:T(8,128)(2,1)S(1)}, bf16[12,90,128]{2,1,0:T(8,128)(2,1)S(1)}, u32[]{:S(2)}, u32[]{:S(2)}) collective-permute-start(bf16[12,90,128]{2,1,0:T(8,128)(2,1)S(1)} %get-tuple-element.22), channel_id=1, source_target_pairs={{1,0},{2,1},{3,2},{4,3},{5,4},{6,5},{7,6},{8,7},{9,8},{10,9},{11,1... | collective-permute-start | bytes 829448 | tf_op jit(solution)/shard_map/ppermute | solution.py:348
  9.1 10.8 %all-to-all-start = ((f32[16,2,192]{2,1,0:T(2,128)}), f32[16,2,192]{2,1,0:T(2,128)S(1)}, u32[]{:S(2)}, u32[]{:S(2)}) async-start(f32[16,2,192]{2,1,0:T(2,128)} %get-tuple-element.23), calls=%async_computation | async-start | bytes 65536 | tf_op jit(solution)/shard_map/all_to_all | solution.py:351
  13.6 7.0 %copy-start = (bf16[2,90,8,192]{3,2,1,0:T(8,128)(2,1)S(1)}, bf16[2,90,8,192]{3,2,1,0:T(8,128)(2,1)}, u32[]{:S(2)}) copy-start(bf16[2,90,8,192]{3,2,1,0:T(8,128)(2,1)} %refs_9_.1) | copy-start | bytes 1658884
  13.6 7.0 %copy-start.4 = (f32[3,192]{1,0:T(4,128)S(1)}, f32[3,192]{1,0:T(4,128)}, u32[]{:S(2)}) copy-start(f32[3,192]{1,0:T(4,128)} %refs_4_.5) | copy-start | bytes 6916
  13.6 7.0 %copy-start.5 = (f32[3,192]{1,0:T(4,128)S(1)}, f32[3,192]{1,0:T(4,128)}, u32[]{:S(2)}) copy-start(f32[3,192]{1,0:T(4,128)} %refs_5_.5) | copy-start | bytes 6916
  20.0 0.6 copy-start.1
  20.6 0.8 %copy-start.2 = (f32[16,2,192]{2,1,0:T(2,128)S(1)}, f32[16,2,192]{2,1,0:T(2,128)}, u32[]{:S(2)}) copy-start(f32[16,2,192]{2,1,0:T(2,128)} %copy-done.1) | copy-start | bytes 73732
  25.8 4.6 %copy-start.6 = (f32[16,2,192]{2,1,0:T(2,128)}, f32[16,2,192]{2,1,0:T(2,128)S(1)}, u32[]{:S(2)}) copy-start(f32[16,2,192]{2,1,0:T(2,128)S(1)} %get-tuple-element.29) | copy-start | bytes 73732
  25.8 15.2 %collective-permute-start.2 = (bf16[3,90,128]{2,1,0:T(8,128)(2,1)}, bf16[3,90,128]{2,1,0:T(8,128)(2,1)S(1)}, u32[]{:S(2)}, u32[]{:S(2)}) collective-permute-start(bf16[3,90,128]{2,1,0:T(8,128)(2,1)} %get-tuple-element.27), channel_id=1, source_target_pairs={{0,1},{1,2},{2,3},{3,4},{4,5},{5,6},{6,7},{7,8},{8,9},{9,10},{10,1... | collective-permute-start | bytes 207368 | tf_op jit(solution)/shard_map/ppermute | solution.py:348
  28.4 12.7 %collective-permute-start.3 = (bf16[3,90,128]{2,1,0:T(8,128)(2,1)}, bf16[3,90,128]{2,1,0:T(8,128)(2,1)S(1)}, u32[]{:S(2)}, u32[]{:S(2)}) collective-permute-start(bf16[3,90,128]{2,1,0:T(8,128)(2,1)} %get-tuple-element.28), channel_id=1, source_target_pairs={{1,0},{2,1},{3,2},{4,3},{5,4},{6,5},{7,6},{8,7},{9,8},{10,9},{11,1... | collective-permute-start | bytes 207368 | tf_op jit(solution)/shard_map/ppermute | solution.py:348
  30.5 10.6 %all-to-all-start.1 = ((f32[16,2,192]{2,1,0:T(2,128)}), f32[16,2,192]{2,1,0:T(2,128)S(1)}, u32[]{:S(2)}, u32[]{:S(2)}) async-start(f32[16,2,192]{2,1,0:T(2,128)} %copy-done.6), calls=%async_computation.1 | async-start | bytes 65536 | tf_op jit(solution)/shard_map/all_to_all | solution.py:351
  46.4 14.6 %collective-permute-start.4 = (bf16[3,90,128]{2,1,0:T(8,128)(2,1)S(1)}, bf16[3,90,128]{2,1,0:T(8,128)(2,1)S(1)}, u32[]{:S(2)}, u32[]{:S(2)}) collective-permute-start(bf16[3,90,128]{2,1,0:T(8,128)(2,1)S(1)} %get-tuple-element.34), channel_id=1, source_target_pairs={{0,1},{1,2},{2,3},{3,4},{4,5},{5,6},{6,7},{7,8},{8,9},{9,10},{10,1... | collective-permute-start | bytes 207368 | tf_op jit(solution)/shard_map/ppermute | solution.py:348
  46.9 14.1 %collective-permute-start.5 = (bf16[3,90,128]{2,1,0:T(8,128)(2,1)S(1)}, bf16[3,90,128]{2,1,0:T(8,128)(2,1)S(1)}, u32[]{:S(2)}, u32[]{:S(2)}) collective-permute-start(bf16[3,90,128]{2,1,0:T(8,128)(2,1)S(1)} %get-tuple-element.35), channel_id=1, source_target_pairs={{1,0},{2,1},{3,2},{4,3},{5,4},{6,5},{7,6},{8,7},{9,8},{10,9},{11,1... | collective-permute-start | bytes 207368 | tf_op jit(solution)/shard_map/ppermute | solution.py:348
  50.9 10.1 %all-to-all-start.2 = ((f32[16,2,192]{2,1,0:T(2,128)}), f32[16,2,192]{2,1,0:T(2,128)S(1)}, u32[]{:S(2)}, u32[]{:S(2)}) async-start(f32[16,2,192]{2,1,0:T(2,128)} %get-tuple-element.36), calls=%async_computation.2 | async-start | bytes 65536 | tf_op jit(solution)/shard_map/all_to_all | solution.py:351

commit v6 on v5

--- a/solution.py
+++ b/solution.py
@@ -151,7 +151,9 @@
     low = (left - middle.astype(jnp.float32)).astype(jnp.bfloat16)
     split = jnp.concatenate([high, middle, low], axis=0)
     sums = jnp.dot(split, same, preferred_element_type=jnp.float32)
-    return sums[0:2] + sums[2:4] + sums[4:6]
+    sums = sums[0:2] + sums[2:4] + sums[4:6]
+    rest = twice(sums[:, LANES:])
+    return jnp.concatenate([sums[:, :LANES], rest, rest, rest], axis=0)
 
 
 def begin_kernel(video, caches, same, sums, first, last, wide, held, alike, sem):
@@ -257,13 +259,15 @@
         copy.start()
 
     means = jnp.sum(stats[...], axis=0) / entries
-    average = means[0:1]
-    variance = means[1:2] - average * average
-    scale = lax.rsqrt(variance + EPSILON) * gain[layer : layer + 1, :]
-    offset = shift[layer : layer + 1, :] - average * scale
-    scale, offset = 0.5 * scale, 0.5 * offset
-    scales = [scale[:, :LANES]] * 2 + [twice(scale[:, LANES:])]
-    offsets = [offset[:, :LANES]] * 2 + [twice(offset[:, LANES:])]
+    scales, offsets = [], []
+    for index, lift in enumerate((lambda v: v, twice)):
+        average = means[2 * index : 2 * index + 1]
+        variance = means[2 * index + 1 : 2 * index + 2] - average * average
+        scale = lax.rsqrt(variance + EPSILON) * lift(halves(gain[layer : layer + 1, :])[index])
+        offset = lift(halves(shift[layer : layer + 1, :])[index]) - average * scale
+        scales.append(0.5 * scale)
+        offsets.append(0.5 * offset)
+    scales, offsets = [[v[0], v[0], v[1]] for v in (scales, offsets)]
 
     def act(values):
         return [silu_of_twice(v * a + b) for v, a, b in zip(values, scales, offsets)]
@@ -358,7 +362,7 @@
     members = channels // GROUPS
     alike = np.kron(np.eye(GROUPS), np.ones((members, members)))
     same = in_hbm(jnp.asarray(alike, jnp.bfloat16))
-    spread = jax.ShapeDtypeStruct((peers, 2, channels), jnp.float32)
+    spread = jax.ShapeDtypeStruct((peers, COLS, LANES), jnp.float32)
     brim = jax.ShapeDtypeStruct(((layers + 1) * PLANES, rows, LANES), jnp.bfloat16)
     sums, first, last = pl.pallas_call(
         begin_kernel,

time: 66.1 us -> 70.3 us (1.064)
  starting transfers between devices: 25.9 us -> 28.5 us
  local copies, waits for them, and re-layouts: 1.39 us -> 3.37 us
    all_to_all x3, starting transfers between devices: 11.2 us -> 13.9 us  [gathered(): return lax.all_to_all(sums, 'lon', 0, 0)]
    unnamed x14 -> x18, local copies, waits for them, and re-layouts: 1.39 us -> 3.37 us
  transfers between devices with their start and end apart: 9 -> 9, of which waited for: 2 -> 1; matrix products, arithmetic and copies ran while one was open for 0% -> 0% of each run, Pallas kernels for 29% -> 28%
where the time goes in v6:
time: 70.3 us; the launch traced here: 69.8 us
  Pallas kernels  36.1 us (51%)
  starting transfers between devices  28.5 us (41%)
  local copies, waits for them, and re-layouts  3.37 us (5%)
  between operations  0.97 us (1%)
  waiting for transfers between devices  0.83 us (1%)
    pallas_call x3, Pallas kernels, cached_part(): pl.pallas_call(functools.partial(cached_kernel, layer, chunk, far), out_s...  19.3 us
    ppermute x6, starting transfers between devices, around(): return (lax.ppermute(last, 'lon', up), lax.ppermute(first, 'lon', down))  14.6 us
    all_to_all x3, starting transfers between devices, gathered(): return lax.all_to_all(sums, 'lon', 0, 0)  13.9 us
    pallas_call x3, Pallas kernels, local(): pl.pallas_call(functools.partial(active_kernel, layer, chunk, far, entrie...  13.8 us
    unnamed x18, local copies, waits for them, and re-layouts  3.37 us
    pallas_call x1, Pallas kernels, local(): pl.pallas_call(begin_kernel, out_shape=[spread, brim, brim], in_specs=[HB...  2.96 us
  transfers between devices with their start and end apart: 9, of which 1 were waited for; matrix products, arithmetic and copies ran while one was open for 0% of the time, Pallas kernels for 28%

profile of v6, /device:TPU:0, one launch (start us, length us, event | category | flops | bytes accessed | tf_op | source)
XLA Modules:
  0.0 69.8 jit_solution(17183340249024092939)
XLA Ops:
  0.6 0.0 copy-start.4
  0.6 3.0 %begin.1 = (f32[16,8,128]{2,1,0:T(8,128)}, bf16[12,90,128]{2,1,0:T(8,128)(2,1)S(1)}, bf16[12,90,128]{2,1,0:T(8,128)(2,1)S(1)}) custom-call(bf16[2,90,8,192]{3,2,1,0:T(8,128)(2,1)} %refs_9_.1, bf16[3,2,90,8,192]{4,3,2,1,0:T(8,128)(2,1)} %caches.7, bf16[192,192]{1,0:T(8,128)(2,1)} %constant.2.clone.same.refs_8_), custom_call_target="tpu_custom_call" | custom-call | tf_op jit(solution)/shard_map/begin/pallas_call | solution.py:367
  3.6 0.5 collective-permute-start
  4.2 5.0 %collective-permute-start.1 = (bf16[12,90,128]{2,1,0:T(8,128)(2,1)S(1)}, bf16[12,90,128]{2,1,0:T(8,128)(2,1)S(1)}, u32[]{:S(2)}, u32[]{:S(2)}) collective-permute-start(bf16[12,90,128]{2,1,0:T(8,128)(2,1)S(1)} %get-tuple-element.22), channel_id=1, source_target_pairs={{1,0},{2,1},{3,2},{4,3},{5,4},{6,5},{7,6},{8,7},{9,8},{10,9},{11,1... | collective-permute-start | bytes 829448 | tf_op jit(solution)/shard_map/ppermute | solution.py:352
  9.2 3.6 %all-to-all-start = ((f32[16,8,128]{2,1,0:T(8,128)}), f32[16,8,128]{2,1,0:T(8,128)S(1)}, u32[]{:S(2)}, u32[]{:S(2)}) async-start(f32[16,8,128]{2,1,0:T(8,128)} %get-tuple-element.23), calls=%async_computation | async-start | bytes 131072 | tf_op jit(solution)/shard_map/all_to_all | solution.py:355
  12.8 0.8 %collective-permute-done.before.refs_1_ = bf16[12,90,128]{2,1,0:T(8,128)(2,1)S(1)} collective-permute-done((bf16[12,90,128]{2,1,0:T(8,128)(2,1)S(1)}, bf16[12,90,128]{2,1,0:T(8,128)(2,1)S(1)}, u32[]{:S(2)}, u32[]{:S(2)}) %collective-permute-start) | collective-permute-done | bytes 276512 | tf_op jit(solution)/shard_map/ppermute | solution.py:352
  13.6 0.0 collective-permute-done.1.after.refs_2_
  13.6 0.0 copy-done.4
  13.7 0.0 copy-start
  13.7 0.0 copy-start.5
  13.7 0.0 copy-start.6
  13.7 6.4 %cached.3 = (f32[3,720,128]{2,1,0:T(8,128)S(1)}, bf16[2,192,1792]{2,1,0:T(8,128)(2,1)}) custom-call(bf16[3,2,90,8,192]{4,3,2,1,0:T(8,128)(2,1)} %caches.7, bf16[12,90,128]{2,1,0:T(8,128)(2,1)S(1)} %collective-permute-done.before.refs_1_, bf16[12,90,128]{2,1,0:T(8,128)(2,1)S(1)} %collective-permute-done.1.after.refs_2_, bf16[3,192,5184]{2,1,0:T(8,128)(2,1)} %bitcast.1, ...), custom_call_target="tpu_custom_call" | custom-call | tf_op jit(solution)/shard_map/cached/pallas_call | solution.py:390
  20.1 0.0 all-to-all-done.refs_3_
  20.1 0.0 copy-start.1
  20.1 0.6 copy-done.1
  20.7 0.0 copy-done
  20.7 0.0 copy-done.5
  20.7 0.0 copy-done.6
  20.7 0.0 copy-start.2
  20.7 0.8 %copy-done.2 = f32[16,8,128]{2,1,0:T(8,128)S(1)} copy-done((f32[16,8,128]{2,1,0:T(8,128)S(1)}, f32[16,8,128]{2,1,0:T(8,128)}, u32[]{:S(2)}) %copy-start.2) | copy-done | bytes 65560
  21.6 3.9 %active.3 = (f32[3,720,128]{2,1,0:T(8,128)S(1)}, bf16[3,2,90,8,192]{4,3,2,1,0:T(8,128)(2,1)}, f32[16,8,128]{2,1,0:T(8,128)S(1)}, bf16[3,90,128]{2,1,0:T(8,128)(2,1)S(1)}, bf16[3,90,128]{2,1,0:T(8,128)(2,1)S(1)}) custom-call(bf16[2,90,8,192]{3,2,1,0:T(8,128)(2,1)S(1)} %copy-done, bf16[12,90,128]{2,1,0:T(8,128)(2,1)S(1)} %collective-permute-done.before.refs_1_, ...), custom_call_target="tpu_custom_call" | custom-call | tf_op jit(solution)/shard_map/active/pallas_call | solution.py:436
  25.5 0.0 copy-start.3
  25.5 0.6 copy-done.3
  26.1 0.0 copy-start.7
  26.1 0.6 copy-done.7
  26.8 0.0 copy-start.8
  26.8 0.6 copy-done.8
  27.4 6.7 %all-to-all-start.1 = ((f32[16,8,128]{2,1,0:T(8,128)}), f32[16,8,128]{2,1,0:T(8,128)S(1)}, u32[]{:S(2)}, u32[]{:S(2)}) async-start(f32[16,8,128]{2,1,0:T(8,128)} %copy-done.3), calls=%async_computation.1 | async-start | bytes 131072 | tf_op jit(solution)/shard_map/all_to_all | solution.py:355
  34.2 0.4 collective-permute-start.2
  34.6 4.1 %collective-permute-start.3 = (bf16[3,90,128]{2,1,0:T(8,128)(2,1)}, bf16[3,90,128]{2,1,0:T(8,128)(2,1)S(1)}, u32[]{:S(2)}, u32[]{:S(2)}) collective-permute-start(bf16[3,90,128]{2,1,0:T(8,128)(2,1)} %copy-done.7), channel_id=1, source_target_pairs={{1,0},{2,1},{3,2},{4,3},{5,4},{6,5},{7,6},{8,7},{9,8},{10,9},{11,1... | collective-permute-start | bytes 207368 | tf_op jit(solution)/shard_map/ppermute | solution.py:352
  38.7 6.6 %cached.4 = (f32[3,720,128]{2,1,0:T(8,128)}, bf16[2,192,1792]{2,1,0:T(8,128)(2,1)}) custom-call(bf16[3,2,90,8,192]{4,3,2,1,0:T(8,128)(2,1)} %caches.7, bf16[12,90,128]{2,1,0:T(8,128)(2,1)S(1)} %collective-permute-done.before.refs_1_, bf16[12,90,128]{2,1,0:T(8,128)(2,1)S(1)} %collective-permute-done.1.after.refs_2_, bf16[3,192,5184]{2,1,0:T(8,128)(2,1)} %bitcast.2, ...), custom_call_target="tpu_custom_call" | custom-call | tf_op jit(solution)/shard_map/cached/pallas_call | solution.py:390
  45.3 0.0 collective-permute-done.2.refs_1_
  45.3 0.0 collective-permute-done.3.refs_2_
  45.3 0.0 all-to-all-done.1.refs_3_
  45.3 5.4 %active.4 = (f32[3,720,128]{2,1,0:T(8,128)S(1)}, bf16[3,2,90,8,192]{4,3,2,1,0:T(8,128)(2,1)}, f32[16,8,128]{2,1,0:T(8,128)}, bf16[3,90,128]{2,1,0:T(8,128)(2,1)S(1)}, bf16[3,90,128]{2,1,0:T(8,128)(2,1)S(1)}) custom-call(f32[3,720,128]{2,1,0:T(8,128)S(1)} %get-tuple-element.26.refs_0_, ...), custom_call_target="tpu_custom_call", output_to_operand_aliasing={{1}: (10, {})} | custom-call | tf_op jit(solution)/shard_map/active/pallas_call | solution.py:436
  50.7 3.5 %all-to-all-start.2 = ((f32[16,8,128]{2,1,0:T(8,128)}), f32[16,8,128]{2,1,0:T(8,128)S(1)}, u32[]{:S(2)}, u32[]{:S(2)}) async-start(f32[16,8,128]{2,1,0:T(8,128)} %get-tuple-element.36), calls=%async_computation.2 | async-start | bytes 131072 | tf_op jit(solution)/shard_map/all_to_all | solution.py:355
  54.3 0.3 collective-permute-start.4
  54.5 4.3 %collective-permute-start.5 = (bf16[3,90,128]{2,1,0:T(8,128)(2,1)S(1)}, bf16[3,90,128]{2,1,0:T(8,128)(2,1)S(1)}, u32[]{:S(2)}, u32[]{:S(2)}) collective-permute-start(bf16[3,90,128]{2,1,0:T(8,128)(2,1)S(1)} %get-tuple-element.35), channel_id=1, source_target_pairs={{1,0},{2,1},{3,2},{4,3},{5,4},{6,5},{7,6},{8,7},{9,8},{10,9},{11,1... | collective-permute-start | bytes 207368 | tf_op jit(solution)/shard_map/ppermute | solution.py:352
  58.8 6.3 %cached.5 = (f32[3,720,128]{2,1,0:T(8,128)S(1)}, bf16[2,192,1792]{2,1,0:T(8,128)(2,1)}) custom-call(bf16[3,2,90,8,192]{4,3,2,1,0:T(8,128)(2,1)} %caches.7, bf16[12,90,128]{2,1,0:T(8,128)(2,1)S(1)} %collective-permute-done.before.refs_1_, bf16[12,90,128]{2,1,0:T(8,128)(2,1)S(1)} %collective-permute-done.1.after.refs_2_, bf16[3,192,5184]{2,1,0:T(8,128)(2,1)} %bitcast.3, ...), custom_call_target="tpu_custom_call" | custom-call | tf_op jit(solution)/shard_map/cached/pallas_call | solution.py:390
  65.1 0.0 collective-permute-done.4.refs_1_
  65.1 0.0 collective-permute-done.5.refs_2_
  65.1 0.0 all-to-all-done.2.refs_3_
  65.2 4.5 %active.5 = (bf16[2,90,8,192]{3,2,1,0:T(8,128)(2,1)}, bf16[3,2,90,8,192]{4,3,2,1,0:T(8,128)(2,1)}) custom-call(f32[3,720,128]{2,1,0:T(8,128)S(1)} %get-tuple-element.33.refs_0_, bf16[3,90,128]{2,1,0:T(8,128)(2,1)S(1)} %collective-permute-done.4.refs_1_, bf16[3,90,128]{2,1,0:T(8,128)(2,1)S(1)} %collective-permute-done.5.refs_2_, ...), custom_call_target="tpu_custom_call", output_to_operand_aliasing={{1}: (9, {})} | custom-call | tf_op jit(solution)/shard_map/active/pallas_call | solution.py:436
Async XLA Ops:
  0.6 13.0 %copy-start.4 = (f32[3,192]{1,0:T(4,128)S(1)}, f32[3,192]{1,0:T(4,128)}, u32[]{:S(2)}) copy-start(f32[3,192]{1,0:T(4,128)} %bias.5) | copy-start | bytes 6916
  3.6 10.0 %collective-permute-start = (bf16[12,90,128]{2,1,0:T(8,128)(2,1)S(1)}, bf16[12,90,128]{2,1,0:T(8,128)(2,1)S(1)}, u32[]{:S(2)}, u32[]{:S(2)}) collective-permute-start(bf16[12,90,128]{2,1,0:T(8,128)(2,1)S(1)} %get-tuple-element.21), channel_id=1, source_target_pairs={{0,1},{1,2},{2,3},{3,4},{4,5},{5,6},{6,7},{7,8},{8,9},{9,10},{10,1... | collective-permute-start | bytes 829448 | tf_op jit(solution)/shard_map/ppermute | solution.py:352
  4.2 9.5 %collective-permute-start.1 = (bf16[12,90,128]{2,1,0:T(8,128)(2,1)S(1)}, bf16[12,90,128]{2,1,0:T(8,128)(2,1)S(1)}, u32[]{:S(2)}, u32[]{:S(2)}) collective-permute-start(bf16[12,90,128]{2,1,0:T(8,128)(2,1)S(1)} %get-tuple-element.22), channel_id=1, source_target_pairs={{1,0},{2,1},{3,2},{4,3},{5,4},{6,5},{7,6},{8,7},{9,8},{10,9},{11,1... | collective-permute-start | bytes 829448 | tf_op jit(solution)/shard_map/ppermute | solution.py:352
  9.2 10.9 %all-to-all-start = ((f32[16,8,128]{2,1,0:T(8,128)}), f32[16,8,128]{2,1,0:T(8,128)S(1)}, u32[]{:S(2)}, u32[]{:S(2)}) async-start(f32[16,8,128]{2,1,0:T(8,128)} %get-tuple-element.23), calls=%async_computation | async-start | bytes 131072 | tf_op jit(solution)/shard_map/all_to_all | solution.py:355
  13.7 7.1 %copy-start = (bf16[2,90,8,192]{3,2,1,0:T(8,128)(2,1)S(1)}, bf16[2,90,8,192]{3,2,1,0:T(8,128)(2,1)}, u32[]{:S(2)}) copy-start(bf16[2,90,8,192]{3,2,1,0:T(8,128)(2,1)} %refs_9_.1) | copy-start | bytes 1658884
  13.7 7.1 %copy-start.5 = (f32[3,192]{1,0:T(4,128)S(1)}, f32[3,192]{1,0:T(4,128)}, u32[]{:S(2)}) copy-start(f32[3,192]{1,0:T(4,128)} %refs_4_.5) | copy-start | bytes 6916
  13.7 7.0 %copy-start.6 = (f32[3,192]{1,0:T(4,128)S(1)}, f32[3,192]{1,0:T(4,128)}, u32[]{:S(2)}) copy-start(f32[3,192]{1,0:T(4,128)} %refs_5_.5) | copy-start | bytes 6916
  20.1 0.6 copy-start.1
  20.7 0.8 %copy-start.2 = (f32[16,8,128]{2,1,0:T(8,128)S(1)}, f32[16,8,128]{2,1,0:T(8,128)}, u32[]{:S(2)}) copy-start(f32[16,8,128]{2,1,0:T(8,128)} %copy-done.1) | copy-start | bytes 196612
  25.5 0.6 copy-start.3
  26.1 0.6 copy-start.7
  26.8 0.6 copy-start.8
  27.4 17.9 %all-to-all-start.1 = ((f32[16,8,128]{2,1,0:T(8,128)}), f32[16,8,128]{2,1,0:T(8,128)S(1)}, u32[]{:S(2)}, u32[]{:S(2)}) async-start(f32[16,8,128]{2,1,0:T(8,128)} %copy-done.3), calls=%async_computation.1 | async-start | bytes 131072 | tf_op jit(solution)/shard_map/all_to_all | solution.py:355
  34.2 11.1 %collective-permute-start.2 = (bf16[3,90,128]{2,1,0:T(8,128)(2,1)}, bf16[3,90,128]{2,1,0:T(8,128)(2,1)S(1)}, u32[]{:S(2)}, u32[]{:S(2)}) collective-permute-start(bf16[3,90,128]{2,1,0:T(8,128)(2,1)} %copy-done.8), channel_id=1, source_target_pairs={{0,1},{1,2},{2,3},{3,4},{4,5},{5,6},{6,7},{7,8},{8,9},{9,10},{10,1... | collective-permute-start | bytes 207368 | tf_op jit(solution)/shard_map/ppermute | solution.py:352
  34.6 10.7 %collective-permute-start.3 = (bf16[3,90,128]{2,1,0:T(8,128)(2,1)}, bf16[3,90,128]{2,1,0:T(8,128)(2,1)S(1)}, u32[]{:S(2)}, u32[]{:S(2)}) collective-permute-start(bf16[3,90,128]{2,1,0:T(8,128)(2,1)} %copy-done.7), channel_id=1, source_target_pairs={{1,0},{2,1},{3,2},{4,3},{5,4},{6,5},{7,6},{8,7},{9,8},{10,9},{11,1... | collective-permute-start | bytes 207368 | tf_op jit(solution)/shard_map/ppermute | solution.py:352
  50.7 14.4 %all-to-all-start.2 = ((f32[16,8,128]{2,1,0:T(8,128)}), f32[16,8,128]{2,1,0:T(8,128)S(1)}, u32[]{:S(2)}, u32[]{:S(2)}) async-start(f32[16,8,128]{2,1,0:T(8,128)} %get-tuple-element.36), calls=%async_computation.2 | async-start | bytes 131072 | tf_op jit(solution)/shard_map/all_to_all | solution.py:355
  54.3 10.9 %collective-permute-start.4 = (bf16[3,90,128]{2,1,0:T(8,128)(2,1)S(1)}, bf16[3,90,128]{2,1,0:T(8,128)(2,1)S(1)}, u32[]{:S(2)}, u32[]{:S(2)}) collective-permute-start(bf16[3,90,128]{2,1,0:T(8,128)(2,1)S(1)} %get-tuple-element.34), channel_id=1, source_target_pairs={{0,1},{1,2},{2,3},{3,4},{4,5},{5,6},{6,7},{7,8},{8,9},{9,10},{10,1... | collective-permute-start | bytes 207368 | tf_op jit(solution)/shard_map/ppermute | solution.py:352
  54.5 10.6 %collective-permute-start.5 = (bf16[3,90,128]{2,1,0:T(8,128)(2,1)S(1)}, bf16[3,90,128]{2,1,0:T(8,128)(2,1)S(1)}, u32[]{:S(2)}, u32[]{:S(2)}) collective-permute-start(bf16[3,90,128]{2,1,0:T(8,128)(2,1)S(1)} %get-tuple-element.35), channel_id=1, source_target_pairs={{1,0},{2,1},{3,2},{4,3},{5,4},{6,5},{7,6},{8,7},{9,8},{10,9},{11,1... | collective-permute-start | bytes 207368 | tf_op jit(solution)/shard_map/ppermute | solution.py:352

commit v7 on v5

--- a/solution.py
+++ b/solution.py
@@ -253,6 +253,9 @@
         fetch.append(pltpu.make_async_copy(away, part, sem.at[3]))
     if residual is not None:
         fetch.append(pltpu.make_async_copy(residual, held, sem.at[2]))
+    if not layer:
+        source = pltpu.make_async_copy(x, held, sem.at[2])
+        source.start()
     for copy in fetch:
         copy.start()
 
@@ -277,7 +280,7 @@
         if layer:
             start = h * COLS if isinstance(h, int) else pl.multiple_of(h * COLS, COLS)
             return act([x[plane, pl.ds(start, COLS), :] for plane in range(PLANES)])
-        return act(planes(*(x[frame, h].astype(jnp.float32) for frame in range(2))))
+        return act(planes(*(held[frame, h].astype(jnp.float32) for frame in range(2))))
 
     def edge_of(h, plane):
         return [edges[side, plane, pl.ds(h, COLS, stride=0), :] for side in (0, 1)]
@@ -288,6 +291,8 @@
             whole = jnp.concatenate([main, other[:, : channels - LANES]], axis=1)
             kept[frame, h] = whole.astype(jnp.bfloat16)
 
+    if not layer:
+        source.wait()
     build_slabs(rows, row_of, edge_of, slabs, keep)
     copy = pltpu.make_async_copy(kept, carried.at[layer], sem.at[0])
     copy.start()
@@ -402,7 +407,7 @@
             name="cached",
         )(caches, *brims, turned, biases)
 
-    x = video_span
+    x = video
     carried = None
     for layer in range(layers):
         final = layer == layers - 1
@@ -413,6 +418,8 @@
         operands = [x, before, after, stats, norm_gains, shifts, in_hbm(ordered), part, same]
         specs = [VMEM] * 6 + [HBM, HBM if far else VMEM, HBM]
         aliases = {}
+        if not layer:
+            specs[0] = HBM
         if layer == 1:
             operands.append(video)
             specs.append(HBM)

time: 66.1 us -> 65.6 us (level)
  local copies, waits for them, and re-layouts: 1.39 us -> 0.01 us
  Pallas kernels: 36.4 us -> 37.3 us
    unnamed x14 -> x6, local copies, waits for them, and re-layouts: 1.39 us -> 0.01 us
    pallas_call x3, Pallas kernels: 14.2 us -> 15.2 us  [local(): pl.pallas_call(functools.partial(active_kernel, layer, chunk, far, entrie...]
  transfers between devices with their start and end apart: 9 -> 9, of which waited for: 2 -> 2; matrix products, arithmetic and copies ran while one was open for 0% -> 0% of each run, Pallas kernels for 29% -> 30%
where the time goes in v7:
time: 65.6 us; the launch traced here: 65.1 us
  Pallas kernels  37.3 us (57%)
  starting transfers between devices  25.9 us (39%)
  waiting for transfers between devices  0.96 us (1%)
  between operations  0.93 us (1%)
    pallas_call x3, Pallas kernels, cached_part(): pl.pallas_call(functools.partial(cached_kernel, layer, chunk, far), out_s...  19.3 us
    pallas_call x3, Pallas kernels, local(): pl.pallas_call(functools.partial(active_kernel, layer, chunk, far, entrie...  15.2 us
    ppermute x6, starting transfers between devices, around(): return (lax.ppermute(last, 'lon', up), lax.ppermute(first, 'lon', down))  14.7 us
    all_to_all x3, starting transfers between devices, gathered(): return lax.all_to_all(sums, 'lon', 0, 0)  11.2 us
    pallas_call x1, Pallas kernels, local(): pl.pallas_call(begin_kernel, out_shape=[spread, brim, brim], in_specs=[HB...  2.88 us
  transfers between devices with their start and end apart: 9, of which 2 were waited for; matrix products, arithmetic and copies ran while one was open for 0% of the time, Pallas kernels for 30%

profile of v7, /device:TPU:0, one launch (start us, length us, event | category | flops | bytes accessed | tf_op | source)
XLA Modules:
  0.0 65.1 jit_solution(13123622686809359343)
XLA Ops:
  0.6 0.0 copy-start
  0.6 2.9 %begin.1 = (f32[16,2,192]{2,1,0:T(2,128)}, bf16[12,90,128]{2,1,0:T(8,128)(2,1)S(1)}, bf16[12,90,128]{2,1,0:T(8,128)(2,1)S(1)}) custom-call(bf16[2,90,8,192]{3,2,1,0:T(8,128)(2,1)} %refs_9_.1, bf16[3,2,90,8,192]{4,3,2,1,0:T(8,128)(2,1)} %caches.7, bf16[192,192]{1,0:T(8,128)(2,1)} %constant.2.clone.same.refs_8_), custom_call_target="tpu_custom_call" | custom-call | tf_op jit(solution)/shard_map/begin/pallas_call | solution.py:368
  3.5 0.5 collective-permute-start
  4.1 5.0 %collective-permute-start.1 = (bf16[12,90,128]{2,1,0:T(8,128)(2,1)S(1)}, bf16[12,90,128]{2,1,0:T(8,128)(2,1)S(1)}, u32[]{:S(2)}, u32[]{:S(2)}) collective-permute-start(bf16[12,90,128]{2,1,0:T(8,128)(2,1)S(1)} %get-tuple-element.22), channel_id=1, source_target_pairs={{1,0},{2,1},{3,2},{4,3},{5,4},{6,5},{7,6},{8,7},{9,8},{10,9},{11,1... | collective-permute-start | bytes 829448 | tf_op jit(solution)/shard_map/ppermute | solution.py:353
  9.1 3.6 %all-to-all-start = ((f32[16,2,192]{2,1,0:T(2,128)}), f32[16,2,192]{2,1,0:T(2,128)S(1)}, u32[]{:S(2)}, u32[]{:S(2)}) async-start(f32[16,2,192]{2,1,0:T(2,128)} %get-tuple-element.23), calls=%async_computation | async-start | bytes 65536 | tf_op jit(solution)/shard_map/all_to_all | solution.py:356
  12.7 0.8 %collective-permute-done.before.refs_1_ = bf16[12,90,128]{2,1,0:T(8,128)(2,1)S(1)} collective-permute-done((bf16[12,90,128]{2,1,0:T(8,128)(2,1)S(1)}, bf16[12,90,128]{2,1,0:T(8,128)(2,1)S(1)}, u32[]{:S(2)}, u32[]{:S(2)}) %collective-permute-start) | collective-permute-done | bytes 276512 | tf_op jit(solution)/shard_map/ppermute | solution.py:353
  13.6 0.0 collective-permute-done.1.after.refs_2_
  13.6 0.0 copy-done
  13.6 0.0 copy-start.1
  13.6 0.0 copy-start.2
  13.6 6.3 %cached.3 = (f32[3,720,128]{2,1,0:T(8,128)S(1)}, bf16[2,192,1792]{2,1,0:T(8,128)(2,1)}) custom-call(bf16[3,2,90,8,192]{4,3,2,1,0:T(8,128)(2,1)} %caches.7, bf16[12,90,128]{2,1,0:T(8,128)(2,1)S(1)} %collective-permute-done.before.refs_1_, bf16[12,90,128]{2,1,0:T(8,128)(2,1)S(1)} %collective-permute-done.1.after.refs_2_, bf16[3,192,5184]{2,1,0:T(8,128)(2,1)} %bitcast.1, ...), custom_call_target="tpu_custom_call" | custom-call | tf_op jit(solution)/shard_map/cached/pallas_call | solution.py:391
  19.9 0.0 all-to-all-done.refs_3_
  19.9 0.0 copy-done.1
  19.9 0.0 copy-done.2
  19.9 5.4 %active.3 = (f32[3,720,128]{2,1,0:T(8,128)S(1)}, bf16[3,2,90,8,192]{4,3,2,1,0:T(8,128)(2,1)}, f32[16,2,192]{2,1,0:T(2,128)}, bf16[3,90,128]{2,1,0:T(8,128)(2,1)S(1)}, bf16[3,90,128]{2,1,0:T(8,128)(2,1)S(1)}) custom-call(bf16[2,90,8,192]{3,2,1,0:T(8,128)(2,1)} %refs_9_.1, bf16[12,90,128]{2,1,0:T(8,128)(2,1)S(1)} %collective-permute-done.before.refs_1_, ...), custom_call_target="tpu_custom_call" | custom-call | tf_op jit(solution)/shard_map/active/pallas_call | solution.py:439
  25.3 2.5 %collective-permute-start.2 = (bf16[3,90,128]{2,1,0:T(8,128)(2,1)S(1)}, bf16[3,90,128]{2,1,0:T(8,128)(2,1)S(1)}, u32[]{:S(2)}, u32[]{:S(2)}) collective-permute-start(bf16[3,90,128]{2,1,0:T(8,128)(2,1)S(1)} %get-tuple-element.27), channel_id=1, source_target_pairs={{0,1},{1,2},{2,3},{3,4},{4,5},{5,6},{6,7},{7,8},{8,9},{9,10},{10,1... | collective-permute-start | bytes 207368 | tf_op jit(solution)/shard_map/ppermute | solution.py:353
  27.8 2.1 %collective-permute-start.3 = (bf16[3,90,128]{2,1,0:T(8,128)(2,1)S(1)}, bf16[3,90,128]{2,1,0:T(8,128)(2,1)S(1)}, u32[]{:S(2)}, u32[]{:S(2)}) collective-permute-start(bf16[3,90,128]{2,1,0:T(8,128)(2,1)S(1)} %get-tuple-element.28), channel_id=1, source_target_pairs={{1,0},{2,1},{3,2},{4,3},{5,4},{6,5},{7,6},{8,7},{9,8},{10,9},{11,1... | collective-permute-start | bytes 207368 | tf_op jit(solution)/shard_map/ppermute | solution.py:353
  29.9 3.9 %all-to-all-start.1 = ((f32[16,2,192]{2,1,0:T(2,128)}), f32[16,2,192]{2,1,0:T(2,128)S(1)}, u32[]{:S(2)}, u32[]{:S(2)}) async-start(f32[16,2,192]{2,1,0:T(2,128)} %get-tuple-element.29), calls=%async_computation.1 | async-start | bytes 65536 | tf_op jit(solution)/shard_map/all_to_all | solution.py:356
  33.9 6.7 %cached.4 = (f32[3,720,128]{2,1,0:T(8,128)}, bf16[2,192,1792]{2,1,0:T(8,128)(2,1)}) custom-call(bf16[3,2,90,8,192]{4,3,2,1,0:T(8,128)(2,1)} %caches.7, bf16[12,90,128]{2,1,0:T(8,128)(2,1)S(1)} %collective-permute-done.before.refs_1_, bf16[12,90,128]{2,1,0:T(8,128)(2,1)S(1)} %collective-permute-done.1.after.refs_2_, bf16[3,192,5184]{2,1,0:T(8,128)(2,1)} %bitcast.2, ...), custom_call_target="tpu_custom_call" | custom-call | tf_op jit(solution)/shard_map/cached/pallas_call | solution.py:391
  40.5 0.0 all-to-all-done.1.refs_3_
  40.5 0.0 collective-permute-done.2.refs_1_
  40.6 0.0 collective-permute-done.3.refs_2_
  40.6 5.3 %active.4 = (f32[3,720,128]{2,1,0:T(8,128)S(1)}, bf16[3,2,90,8,192]{4,3,2,1,0:T(8,128)(2,1)}, f32[16,2,192]{2,1,0:T(2,128)}, bf16[3,90,128]{2,1,0:T(8,128)(2,1)S(1)}, bf16[3,90,128]{2,1,0:T(8,128)(2,1)S(1)}) custom-call(f32[3,720,128]{2,1,0:T(8,128)S(1)} %get-tuple-element.26.refs_0_, ...), custom_call_target="tpu_custom_call", output_to_operand_aliasing={{1}: (10, {})} | custom-call | tf_op jit(solution)/shard_map/active/pallas_call | solution.py:439
  45.9 0.5 collective-permute-start.4
  46.3 4.0 %collective-permute-start.5 = (bf16[3,90,128]{2,1,0:T(8,128)(2,1)S(1)}, bf16[3,90,128]{2,1,0:T(8,128)(2,1)S(1)}, u32[]{:S(2)}, u32[]{:S(2)}) collective-permute-start(bf16[3,90,128]{2,1,0:T(8,128)(2,1)S(1)} %get-tuple-element.35), channel_id=1, source_target_pairs={{1,0},{2,1},{3,2},{4,3},{5,4},{6,5},{7,6},{8,7},{9,8},{10,9},{11,1... | collective-permute-start | bytes 207368 | tf_op jit(solution)/shard_map/ppermute | solution.py:353
  50.4 3.7 %all-to-all-start.2 = ((f32[16,2,192]{2,1,0:T(2,128)}), f32[16,2,192]{2,1,0:T(2,128)S(1)}, u32[]{:S(2)}, u32[]{:S(2)}) async-start(f32[16,2,192]{2,1,0:T(2,128)} %get-tuple-element.36), calls=%async_computation.2 | async-start | bytes 65536 | tf_op jit(solution)/shard_map/all_to_all | solution.py:356
  54.1 6.3 %cached.5 = (f32[3,720,128]{2,1,0:T(8,128)S(1)}, bf16[2,192,1792]{2,1,0:T(8,128)(2,1)}) custom-call(bf16[3,2,90,8,192]{4,3,2,1,0:T(8,128)(2,1)} %caches.7, bf16[12,90,128]{2,1,0:T(8,128)(2,1)S(1)} %collective-permute-done.before.refs_1_, bf16[12,90,128]{2,1,0:T(8,128)(2,1)S(1)} %collective-permute-done.1.after.refs_2_, bf16[3,192,5184]{2,1,0:T(8,128)(2,1)} %bitcast.3, ...), custom_call_target="tpu_custom_call" | custom-call | tf_op jit(solution)/shard_map/cached/pallas_call | solution.py:391
  60.4 0.1 all-to-all-done.2.refs_3_
  60.5 0.0 collective-permute-done.4.refs_1_
  60.5 0.0 collective-permute-done.5.refs_2_
  60.5 4.5 %active.5 = (bf16[2,90,8,192]{3,2,1,0:T(8,128)(2,1)}, bf16[3,2,90,8,192]{4,3,2,1,0:T(8,128)(2,1)}) custom-call(f32[3,720,128]{2,1,0:T(8,128)S(1)} %get-tuple-element.33.refs_0_, bf16[3,90,128]{2,1,0:T(8,128)(2,1)S(1)} %collective-permute-done.4.refs_1_, bf16[3,90,128]{2,1,0:T(8,128)(2,1)S(1)} %collective-permute-done.5.refs_2_, ...), custom_call_target="tpu_custom_call", output_to_operand_aliasing={{1}: (9, {})} | custom-call | tf_op jit(solution)/shard_map/active/pallas_call | solution.py:439
Async XLA Ops:
  0.6 12.9 %copy-start = (f32[3,192]{1,0:T(4,128)S(1)}, f32[3,192]{1,0:T(4,128)}, u32[]{:S(2)}) copy-start(f32[3,192]{1,0:T(4,128)} %bias.5) | copy-start | bytes 6916
  3.5 10.0 %collective-permute-start = (bf16[12,90,128]{2,1,0:T(8,128)(2,1)S(1)}, bf16[12,90,128]{2,1,0:T(8,128)(2,1)S(1)}, u32[]{:S(2)}, u32[]{:S(2)}) collective-permute-start(bf16[12,90,128]{2,1,0:T(8,128)(2,1)S(1)} %get-tuple-element.21), channel_id=1, source_target_pairs={{0,1},{1,2},{2,3},{3,4},{4,5},{5,6},{6,7},{7,8},{8,9},{9,10},{10,1... | collective-permute-start | bytes 829448 | tf_op jit(solution)/shard_map/ppermute | solution.py:353
  4.1 9.5 %collective-permute-start.1 = (bf16[12,90,128]{2,1,0:T(8,128)(2,1)S(1)}, bf16[12,90,128]{2,1,0:T(8,128)(2,1)S(1)}, u32[]{:S(2)}, u32[]{:S(2)}) collective-permute-start(bf16[12,90,128]{2,1,0:T(8,128)(2,1)S(1)} %get-tuple-element.22), channel_id=1, source_target_pairs={{1,0},{2,1},{3,2},{4,3},{5,4},{6,5},{7,6},{8,7},{9,8},{10,9},{11,1... | collective-permute-start | bytes 829448 | tf_op jit(solution)/shard_map/ppermute | solution.py:353
  9.1 10.8 %all-to-all-start = ((f32[16,2,192]{2,1,0:T(2,128)}), f32[16,2,192]{2,1,0:T(2,128)S(1)}, u32[]{:S(2)}, u32[]{:S(2)}) async-start(f32[16,2,192]{2,1,0:T(2,128)} %get-tuple-element.23), calls=%async_computation | async-start | bytes 65536 | tf_op jit(solution)/shard_map/all_to_all | solution.py:356
  13.6 6.3 %copy-start.1 = (f32[3,192]{1,0:T(4,128)S(1)}, f32[3,192]{1,0:T(4,128)}, u32[]{:S(2)}) copy-start(f32[3,192]{1,0:T(4,128)} %refs_4_.5) | copy-start | bytes 6916
  13.6 6.3 %copy-start.2 = (f32[3,192]{1,0:T(4,128)S(1)}, f32[3,192]{1,0:T(4,128)}, u32[]{:S(2)}) copy-start(f32[3,192]{1,0:T(4,128)} %refs_5_.5) | copy-start | bytes 6916
  25.3 15.2 %collective-permute-start.2 = (bf16[3,90,128]{2,1,0:T(8,128)(2,1)S(1)}, bf16[3,90,128]{2,1,0:T(8,128)(2,1)S(1)}, u32[]{:S(2)}, u32[]{:S(2)}) collective-permute-start(bf16[3,90,128]{2,1,0:T(8,128)(2,1)S(1)} %get-tuple-element.27), channel_id=1, source_target_pairs={{0,1},{1,2},{2,3},{3,4},{4,5},{5,6},{6,7},{7,8},{8,9},{9,10},{10,1... | collective-permute-start | bytes 207368 | tf_op jit(solution)/shard_map/ppermute | solution.py:353
  27.8 12.7 %collective-permute-start.3 = (bf16[3,90,128]{2,1,0:T(8,128)(2,1)S(1)}, bf16[3,90,128]{2,1,0:T(8,128)(2,1)S(1)}, u32[]{:S(2)}, u32[]{:S(2)}) collective-permute-start(bf16[3,90,128]{2,1,0:T(8,128)(2,1)S(1)} %get-tuple-element.28), channel_id=1, source_target_pairs={{1,0},{2,1},{3,2},{4,3},{5,4},{6,5},{7,6},{8,7},{9,8},{10,9},{11,1... | collective-permute-start | bytes 207368 | tf_op jit(solution)/shard_map/ppermute | solution.py:353
  29.9 10.6 %all-to-all-start.1 = ((f32[16,2,192]{2,1,0:T(2,128)}), f32[16,2,192]{2,1,0:T(2,128)S(1)}, u32[]{:S(2)}, u32[]{:S(2)}) async-start(f32[16,2,192]{2,1,0:T(2,128)} %get-tuple-element.29), calls=%async_computation.1 | async-start | bytes 65536 | tf_op jit(solution)/shard_map/all_to_all | solution.py:356
  45.9 14.6 %collective-permute-start.4 = (bf16[3,90,128]{2,1,0:T(8,128)(2,1)S(1)}, bf16[3,90,128]{2,1,0:T(8,128)(2,1)S(1)}, u32[]{:S(2)}, u32[]{:S(2)}) collective-permute-start(bf16[3,90,128]{2,1,0:T(8,128)(2,1)S(1)} %get-tuple-element.34), channel_id=1, source_target_pairs={{0,1},{1,2},{2,3},{3,4},{4,5},{5,6},{6,7},{7,8},{8,9},{9,10},{10,1... | collective-permute-start | bytes 207368 | tf_op jit(solution)/shard_map/ppermute | solution.py:353
  46.3 14.1 %collective-permute-start.5 = (bf16[3,90,128]{2,1,0:T(8,128)(2,1)S(1)}, bf16[3,90,128]{2,1,0:T(8,128)(2,1)S(1)}, u32[]{:S(2)}, u32[]{:S(2)}) collective-permute-start(bf16[3,90,128]{2,1,0:T(8,128)(2,1)S(1)} %get-tuple-element.35), channel_id=1, source_target_pairs={{1,0},{2,1},{3,2},{4,3},{5,4},{6,5},{7,6},{8,7},{9,8},{10,9},{11,1... | collective-permute-start | bytes 207368 | tf_op jit(solution)/shard_map/ppermute | solution.py:353
  50.4 10.1 %all-to-all-start.2 = ((f32[16,2,192]{2,1,0:T(2,128)}), f32[16,2,192]{2,1,0:T(2,128)S(1)}, u32[]{:S(2)}, u32[]{:S(2)}) async-start(f32[16,2,192]{2,1,0:T(2,128)} %get-tuple-element.36), calls=%async_computation.2 | async-start | bytes 65536 | tf_op jit(solution)/shard_map/all_to_all | solution.py:356

commit v8 on v5

--- a/solution.py
+++ b/solution.py
@@ -188,6 +188,11 @@
 
 
 def cached_kernel(layer, chunk, far, caches, before, after, weights, bias, *refs):
+    bring = None
+    if layer == 0:
+        video, out, ordered, near, *refs = refs
+        refs = [out, ordered, *refs]
+        bring = pltpu.make_async_copy(video, near, refs[-1].at[4])
     out, ordered, edges, *slabs, cache, weight, taps, sem = refs
     if far:
         away, out, *slabs = out, slabs[0], *slabs[1:]
@@ -197,6 +202,8 @@
     fetch = pltpu.make_async_copy(weights.at[layer], weight, sem.at[1])
     begun.start()
     fetch.start()
+    if bring is not None:
+        bring.start()
     begun.wait()
     for side, ref in enumerate((before, after)):
         for plane in range(PLANES):
@@ -226,6 +233,8 @@
         leave.start()
         leave.wait()
     store.wait()
+    if bring is not None:
+        bring.wait()
 
 
 def active_kernel(layer, chunk, far, entries, final, *refs):
@@ -388,26 +397,29 @@
             out_shape=[
                 planar((PLANES, places, LANES), jnp.float32),
                 pltpu.HBM((2, channels, tiles), weights.dtype),
-            ],
-            in_specs=[HBM, VMEM, VMEM, HBM, VMEM],
-            out_specs=[HBM if far else VMEM, HBM],
+            ]
+            + ([] if layer else [jax.ShapeDtypeStruct(video_span.shape, video_span.dtype)]),
+            in_specs=[HBM, VMEM, VMEM, HBM, VMEM] + ([] if layer else [HBM]),
+            out_specs=[HBM if far else VMEM, HBM] + ([] if layer else [VMEM]),
             scratch_shapes=scratch(frames, rows, room(far))
             + [
                 pltpu.VMEM(video_span.shape, jnp.bfloat16),
                 pltpu.VMEM((channels, weights.shape[1]), weights.dtype),
                 pltpu.VMEM((3, channels, tiles), weights.dtype),
-                pltpu.SemaphoreType.DMA((4,)),
+                pltpu.SemaphoreType.DMA((5,)),
             ],
             compiler_params=pltpu.CompilerParams(vmem_limit_bytes=24 << 20),
             name="cached",
-        )(caches, *brims, turned, biases)
-
-    x = video_span
+        )(caches, *brims, turned, biases, *([] if layer else [video]))
+
+    x = None
     carried = None
     for layer in range(layers):
         final = layer == layers - 1
-        far = 0 < layer < layers - 1
-        part, ordered = cached_part(layer, far)
+        far = layer < layers - 1
+        part, ordered, *near = cached_part(layer, far)
+        if near:
+            x = near[0]
         if far:
             part = in_hbm(part)
         operands = [x, before, after, stats, norm_gains, shifts, in_hbm(ordered), part, same]

time: 66.1 us -> 65.4 us (0.989)
  local copies, waits for them, and re-layouts: 1.39 us -> 0.01 us
  Pallas kernels: 36.4 us -> 37.1 us
    unnamed x14 -> x6, local copies, waits for them, and re-layouts: 1.39 us -> 0.01 us
  transfers between devices with their start and end apart: 9 -> 9, of which waited for: 2 -> 2; matrix products, arithmetic and copies ran while one was open for 0% -> 0% of each run, Pallas kernels for 29% -> 30%
where the time goes in v8:
time: 65.4 us; the launch traced here: 64.9 us
  Pallas kernels  37.1 us (57%)
  starting transfers between devices  25.9 us (40%)
  waiting for transfers between devices  0.95 us (1%)
  between operations  0.93 us (1%)
    pallas_call x3, Pallas kernels, cached_part(): pl.pallas_call(functools.partial(cached_kernel, layer, chunk, far), out_s...  19.7 us
    ppermute x6, starting transfers between devices, around(): return (lax.ppermute(last, 'lon', up), lax.ppermute(first, 'lon', down))  14.7 us
    pallas_call x3, Pallas kernels, local(): pl.pallas_call(functools.partial(active_kernel, layer, chunk, far, entrie...  14.6 us
    all_to_all x3, starting transfers between devices, gathered(): return lax.all_to_all(sums, 'lon', 0, 0)  11.2 us
    pallas_call x1, Pallas kernels, local(): pl.pallas_call(begin_kernel, out_shape=[spread, brim, brim], in_specs=[HB...  2.88 us
  transfers between devices with their start and end apart: 9, of which 2 were waited for; matrix products, arithmetic and copies ran while one was open for 0% of the time, Pallas kernels for 30%

profile of v8, /device:TPU:0, one launch (start us, length us, event | category | flops | bytes accessed | tf_op | source)
XLA Modules:
  0.0 64.9 jit_solution(9916336770613251553)
XLA Ops:
  0.6 0.0 copy-start
  0.6 2.9 %begin.1 = (f32[16,2,192]{2,1,0:T(2,128)}, bf16[12,90,128]{2,1,0:T(8,128)(2,1)S(1)}, bf16[12,90,128]{2,1,0:T(8,128)(2,1)S(1)}) custom-call(bf16[2,90,8,192]{3,2,1,0:T(8,128)(2,1)} %refs_9_.1, bf16[3,2,90,8,192]{4,3,2,1,0:T(8,128)(2,1)} %caches.7, bf16[192,192]{1,0:T(8,128)(2,1)} %constant.2.clone.same.refs_8_), custom_call_target="tpu_custom_call" | custom-call | tf_op jit(solution)/shard_map/begin/pallas_call | solution.py:372
  3.5 0.5 collective-permute-start
  4.1 5.0 %collective-permute-start.1 = (bf16[12,90,128]{2,1,0:T(8,128)(2,1)S(1)}, bf16[12,90,128]{2,1,0:T(8,128)(2,1)S(1)}, u32[]{:S(2)}, u32[]{:S(2)}) collective-permute-start(bf16[12,90,128]{2,1,0:T(8,128)(2,1)S(1)} %get-tuple-element.23), channel_id=1, source_target_pairs={{1,0},{2,1},{3,2},{4,3},{5,4},{6,5},{7,6},{8,7},{9,8},{10,9},{11,1... | collective-permute-start | bytes 829448 | tf_op jit(solution)/shard_map/ppermute | solution.py:357
  9.1 3.6 %all-to-all-start = ((f32[16,2,192]{2,1,0:T(2,128)}), f32[16,2,192]{2,1,0:T(2,128)S(1)}, u32[]{:S(2)}, u32[]{:S(2)}) async-start(f32[16,2,192]{2,1,0:T(2,128)} %get-tuple-element.25), calls=%async_computation | async-start | bytes 65536 | tf_op jit(solution)/shard_map/all_to_all | solution.py:360
  12.7 0.8 %collective-permute-done.before.refs_1_ = bf16[12,90,128]{2,1,0:T(8,128)(2,1)S(1)} collective-permute-done((bf16[12,90,128]{2,1,0:T(8,128)(2,1)S(1)}, bf16[12,90,128]{2,1,0:T(8,128)(2,1)S(1)}, u32[]{:S(2)}, u32[]{:S(2)}) %collective-permute-start) | collective-permute-done | bytes 276512 | tf_op jit(solution)/shard_map/ppermute | solution.py:357
  13.6 0.0 collective-permute-done.1.after.refs_2_
  13.6 0.0 copy-done
  13.6 0.0 copy-start.1
  13.6 0.0 copy-start.2
  13.6 6.7 %cached.3 = (f32[3,720,128]{2,1,0:T(8,128)}, bf16[2,192,1792]{2,1,0:T(8,128)(2,1)}, bf16[2,90,8,192]{3,2,1,0:T(8,128)(2,1)S(1)}) custom-call(bf16[3,2,90,8,192]{4,3,2,1,0:T(8,128)(2,1)} %caches.7, bf16[12,90,128]{2,1,0:T(8,128)(2,1)S(1)} %collective-permute-done.before.refs_1_, bf16[12,90,128]{2,1,0:T(8,128)(2,1)S(1)} %collective-permute-done.1.after.refs_2_, ...), custom_call_target="tpu_custom_call" | custom-call | tf_op jit(solution)/shard_map/cached/pallas_call | solution.py:395
  20.3 0.0 all-to-all-done.refs_3_
  20.3 0.0 copy-done.1
  20.3 0.0 copy-done.2
  20.3 4.8 %active.3 = (f32[3,720,128]{2,1,0:T(8,128)S(1)}, bf16[3,2,90,8,192]{4,3,2,1,0:T(8,128)(2,1)}, f32[16,2,192]{2,1,0:T(2,128)}, bf16[3,90,128]{2,1,0:T(8,128)(2,1)S(1)}, bf16[3,90,128]{2,1,0:T(8,128)(2,1)S(1)}) custom-call(bf16[2,90,8,192]{3,2,1,0:T(8,128)(2,1)S(1)} %get-tuple-element.24.refs_0_, bf16[12,90,128]{2,1,0:T(8,128)(2,1)S(1)} %collective-permute-done.before.refs_1_, ...), custom_call_target="tpu_custom_call" | custom-call | tf_op jit(solution)/shard_map/active/pallas_call | solution.py:444
  25.1 2.5 %collective-permute-start.2 = (bf16[3,90,128]{2,1,0:T(8,128)(2,1)S(1)}, bf16[3,90,128]{2,1,0:T(8,128)(2,1)S(1)}, u32[]{:S(2)}, u32[]{:S(2)}) collective-permute-start(bf16[3,90,128]{2,1,0:T(8,128)(2,1)S(1)} %get-tuple-element.29), channel_id=1, source_target_pairs={{0,1},{1,2},{2,3},{3,4},{4,5},{5,6},{6,7},{7,8},{8,9},{9,10},{10,1... | collective-permute-start | bytes 207368 | tf_op jit(solution)/shard_map/ppermute | solution.py:357
  27.6 2.1 %collective-permute-start.3 = (bf16[3,90,128]{2,1,0:T(8,128)(2,1)S(1)}, bf16[3,90,128]{2,1,0:T(8,128)(2,1)S(1)}, u32[]{:S(2)}, u32[]{:S(2)}) collective-permute-start(bf16[3,90,128]{2,1,0:T(8,128)(2,1)S(1)} %get-tuple-element.30), channel_id=1, source_target_pairs={{1,0},{2,1},{3,2},{4,3},{5,4},{6,5},{7,6},{8,7},{9,8},{10,9},{11,1... | collective-permute-start | bytes 207368 | tf_op jit(solution)/shard_map/ppermute | solution.py:357
  29.7 3.9 %all-to-all-start.1 = ((f32[16,2,192]{2,1,0:T(2,128)}), f32[16,2,192]{2,1,0:T(2,128)S(1)}, u32[]{:S(2)}, u32[]{:S(2)}) async-start(f32[16,2,192]{2,1,0:T(2,128)} %get-tuple-element.31), calls=%async_computation.1 | async-start | bytes 65536 | tf_op jit(solution)/shard_map/all_to_all | solution.py:360
  33.7 6.7 %cached.4 = (f32[3,720,128]{2,1,0:T(8,128)}, bf16[2,192,1792]{2,1,0:T(8,128)(2,1)}) custom-call(bf16[3,2,90,8,192]{4,3,2,1,0:T(8,128)(2,1)} %caches.7, bf16[12,90,128]{2,1,0:T(8,128)(2,1)S(1)} %collective-permute-done.before.refs_1_, bf16[12,90,128]{2,1,0:T(8,128)(2,1)S(1)} %collective-permute-done.1.after.refs_2_, bf16[3,192,5184]{2,1,0:T(8,128)(2,1)} %bitcast.2, ...), custom_call_target="tpu_custom_call" | custom-call | tf_op jit(solution)/shard_map/cached/pallas_call | solution.py:395
  40.4 0.0 all-to-all-done.1.refs_3_
  40.4 0.0 collective-permute-done.2.refs_1_
  40.4 0.0 collective-permute-done.3.refs_2_
  40.4 5.3 %active.4 = (f32[3,720,128]{2,1,0:T(8,128)S(1)}, bf16[3,2,90,8,192]{4,3,2,1,0:T(8,128)(2,1)}, f32[16,2,192]{2,1,0:T(2,128)}, bf16[3,90,128]{2,1,0:T(8,128)(2,1)S(1)}, bf16[3,90,128]{2,1,0:T(8,128)(2,1)S(1)}) custom-call(f32[3,720,128]{2,1,0:T(8,128)S(1)} %get-tuple-element.28.refs_0_, ...), custom_call_target="tpu_custom_call", output_to_operand_aliasing={{1}: (10, {})} | custom-call | tf_op jit(solution)/shard_map/active/pallas_call | solution.py:444
  45.7 0.5 collective-permute-start.4
  46.2 4.0 %collective-permute-start.5 = (bf16[3,90,128]{2,1,0:T(8,128)(2,1)S(1)}, bf16[3,90,128]{2,1,0:T(8,128)(2,1)S(1)}, u32[]{:S(2)}, u32[]{:S(2)}) collective-permute-start(bf16[3,90,128]{2,1,0:T(8,128)(2,1)S(1)} %get-tuple-element.37), channel_id=1, source_target_pairs={{1,0},{2,1},{3,2},{4,3},{5,4},{6,5},{7,6},{8,7},{9,8},{10,9},{11,1... | collective-permute-start | bytes 207368 | tf_op jit(solution)/shard_map/ppermute | solution.py:357
  50.2 3.7 %all-to-all-start.2 = ((f32[16,2,192]{2,1,0:T(2,128)}), f32[16,2,192]{2,1,0:T(2,128)S(1)}, u32[]{:S(2)}, u32[]{:S(2)}) async-start(f32[16,2,192]{2,1,0:T(2,128)} %get-tuple-element.38), calls=%async_computation.2 | async-start | bytes 65536 | tf_op jit(solution)/shard_map/all_to_all | solution.py:360
  53.9 6.3 %cached.5 = (f32[3,720,128]{2,1,0:T(8,128)S(1)}, bf16[2,192,1792]{2,1,0:T(8,128)(2,1)}) custom-call(bf16[3,2,90,8,192]{4,3,2,1,0:T(8,128)(2,1)} %caches.7, bf16[12,90,128]{2,1,0:T(8,128)(2,1)S(1)} %collective-permute-done.before.refs_1_, bf16[12,90,128]{2,1,0:T(8,128)(2,1)S(1)} %collective-permute-done.1.after.refs_2_, bf16[3,192,5184]{2,1,0:T(8,128)(2,1)} %bitcast.3, ...), custom_call_target="tpu_custom_call" | custom-call | tf_op jit(solution)/shard_map/cached/pallas_call | solution.py:395
  60.2 0.1 all-to-all-done.2.refs_3_
  60.3 0.0 collective-permute-done.4.refs_1_
  60.3 0.0 collective-permute-done.5.refs_2_
  60.3 4.5 %active.5 = (bf16[2,90,8,192]{3,2,1,0:T(8,128)(2,1)}, bf16[3,2,90,8,192]{4,3,2,1,0:T(8,128)(2,1)}) custom-call(f32[3,720,128]{2,1,0:T(8,128)S(1)} %get-tuple-element.35.refs_0_, bf16[3,90,128]{2,1,0:T(8,128)(2,1)S(1)} %collective-permute-done.4.refs_1_, bf16[3,90,128]{2,1,0:T(8,128)(2,1)S(1)} %collective-permute-done.5.refs_2_, ...), custom_call_target="tpu_custom_call", output_to_operand_aliasing={{1}: (9, {})} | custom-call | tf_op jit(solution)/shard_map/active/pallas_call | solution.py:444
Async XLA Ops:
  0.6 12.9 %copy-start = (f32[3,192]{1,0:T(4,128)S(1)}, f32[3,192]{1,0:T(4,128)}, u32[]{:S(2)}) copy-start(f32[3,192]{1,0:T(4,128)} %bias.5) | copy-start | bytes 6916
  3.5 10.0 %collective-permute-start = (bf16[12,90,128]{2,1,0:T(8,128)(2,1)S(1)}, bf16[12,90,128]{2,1,0:T(8,128)(2,1)S(1)}, u32[]{:S(2)}, u32[]{:S(2)}) collective-permute-start(bf16[12,90,128]{2,1,0:T(8,128)(2,1)S(1)} %get-tuple-element.22), channel_id=1, source_target_pairs={{0,1},{1,2},{2,3},{3,4},{4,5},{5,6},{6,7},{7,8},{8,9},{9,10},{10,1... | collective-permute-start | bytes 829448 | tf_op jit(solution)/shard_map/ppermute | solution.py:357
  4.1 9.5 %collective-permute-start.1 = (bf16[12,90,128]{2,1,0:T(8,128)(2,1)S(1)}, bf16[12,90,128]{2,1,0:T(8,128)(2,1)S(1)}, u32[]{:S(2)}, u32[]{:S(2)}) collective-permute-start(bf16[12,90,128]{2,1,0:T(8,128)(2,1)S(1)} %get-tuple-element.23), channel_id=1, source_target_pairs={{1,0},{2,1},{3,2},{4,3},{5,4},{6,5},{7,6},{8,7},{9,8},{10,9},{11,1... | collective-permute-start | bytes 829448 | tf_op jit(solution)/shard_map/ppermute | solution.py:357
  9.1 11.2 %all-to-all-start = ((f32[16,2,192]{2,1,0:T(2,128)}), f32[16,2,192]{2,1,0:T(2,128)S(1)}, u32[]{:S(2)}, u32[]{:S(2)}) async-start(f32[16,2,192]{2,1,0:T(2,128)} %get-tuple-element.25), calls=%async_computation | async-start | bytes 65536 | tf_op jit(solution)/shard_map/all_to_all | solution.py:360
  13.6 6.7 %copy-start.1 = (f32[3,192]{1,0:T(4,128)S(1)}, f32[3,192]{1,0:T(4,128)}, u32[]{:S(2)}) copy-start(f32[3,192]{1,0:T(4,128)} %refs_4_.5) | copy-start | bytes 6916
  13.6 6.7 %copy-start.2 = (f32[3,192]{1,0:T(4,128)S(1)}, f32[3,192]{1,0:T(4,128)}, u32[]{:S(2)}) copy-start(f32[3,192]{1,0:T(4,128)} %refs_5_.5) | copy-start | bytes 6916
  25.1 15.3 %collective-permute-start.2 = (bf16[3,90,128]{2,1,0:T(8,128)(2,1)S(1)}, bf16[3,90,128]{2,1,0:T(8,128)(2,1)S(1)}, u32[]{:S(2)}, u32[]{:S(2)}) collective-permute-start(bf16[3,90,128]{2,1,0:T(8,128)(2,1)S(1)} %get-tuple-element.29), channel_id=1, source_target_pairs={{0,1},{1,2},{2,3},{3,4},{4,5},{5,6},{6,7},{7,8},{8,9},{9,10},{10,1... | collective-permute-start | bytes 207368 | tf_op jit(solution)/shard_map/ppermute | solution.py:357
  27.6 12.7 %collective-permute-start.3 = (bf16[3,90,128]{2,1,0:T(8,128)(2,1)S(1)}, bf16[3,90,128]{2,1,0:T(8,128)(2,1)S(1)}, u32[]{:S(2)}, u32[]{:S(2)}) collective-permute-start(bf16[3,90,128]{2,1,0:T(8,128)(2,1)S(1)} %get-tuple-element.30), channel_id=1, source_target_pairs={{1,0},{2,1},{3,2},{4,3},{5,4},{6,5},{7,6},{8,7},{9,8},{10,9},{11,1... | collective-permute-start | bytes 207368 | tf_op jit(solution)/shard_map/ppermute | solution.py:357
  29.7 10.6 %all-to-all-start.1 = ((f32[16,2,192]{2,1,0:T(2,128)}), f32[16,2,192]{2,1,0:T(2,128)S(1)}, u32[]{:S(2)}, u32[]{:S(2)}) async-start(f32[16,2,192]{2,1,0:T(2,128)} %get-tuple-element.31), calls=%async_computation.1 | async-start | bytes 65536 | tf_op jit(solution)/shard_map/all_to_all | solution.py:360
  45.7 14.6 %collective-permute-start.4 = (bf16[3,90,128]{2,1,0:T(8,128)(2,1)S(1)}, bf16[3,90,128]{2,1,0:T(8,128)(2,1)S(1)}, u32[]{:S(2)}, u32[]{:S(2)}) collective-permute-start(bf16[3,90,128]{2,1,0:T(8,128)(2,1)S(1)} %get-tuple-element.36), channel_id=1, source_target_pairs={{0,1},{1,2},{2,3},{3,4},{4,5},{5,6},{6,7},{7,8},{8,9},{9,10},{10,1... | collective-permute-start | bytes 207368 | tf_op jit(solution)/shard_map/ppermute | solution.py:357
  46.2 14.1 %collective-permute-start.5 = (bf16[3,90,128]{2,1,0:T(8,128)(2,1)S(1)}, bf16[3,90,128]{2,1,0:T(8,128)(2,1)S(1)}, u32[]{:S(2)}, u32[]{:S(2)}) collective-permute-start(bf16[3,90,128]{2,1,0:T(8,128)(2,1)S(1)} %get-tuple-element.37), channel_id=1, source_target_pairs={{1,0},{2,1},{3,2},{4,3},{5,4},{6,5},{7,6},{8,7},{9,8},{10,9},{11,1... | collective-permute-start | bytes 207368 | tf_op jit(solution)/shard_map/ppermute | solution.py:357
  50.2 10.1 %all-to-all-start.2 = ((f32[16,2,192]{2,1,0:T(2,128)}), f32[16,2,192]{2,1,0:T(2,128)S(1)}, u32[]{:S(2)}, u32[]{:S(2)}) async-start(f32[16,2,192]{2,1,0:T(2,128)} %get-tuple-element.38), calls=%async_computation.2 | async-start | bytes 65536 | tf_op jit(solution)/shard_map/all_to_all | solution.py:360

commit v9 on v8

--- a/solution.py
+++ b/solution.py
@@ -154,13 +154,12 @@
     return sums[0:2] + sums[2:4] + sums[4:6]
 
 
-def begin_kernel(video, caches, same, sums, first, last, wide, held, alike, sem):
+def begin_kernel(video, caches, same, sums, first, last, near, wide, held, alike, sem):
     layers, frames, rows, cols, channels = caches.shape
     copies = [pltpu.make_async_copy(video, held.at[0], sem.at[0])]
     for layer in range(layers):
-        copies.append(
-            pltpu.make_async_copy(caches.at[layer], held.at[layer + 1], sem.at[layer + 1])
-        )
+        target = held.at[layer + 1] if layer else near
+        copies.append(pltpu.make_async_copy(caches.at[layer], target, sem.at[layer + 1]))
     fetch = pltpu.make_async_copy(same, alike, sem.at[layers + 1])
     for copy in copies + [fetch]:
         copy.start()
@@ -170,7 +169,7 @@
     for group, copy in enumerate(copies):
         copy.wait()
         for frame in range(frames):
-            value = held[group, frame].astype(jnp.float32)
+            value = (near[frame] if group == 1 else held[group, frame]).astype(jnp.float32)
             parts = halves(value)
             if group == 0:
                 for i in range(2):
@@ -187,24 +186,29 @@
     sums[...] = jnp.broadcast_to(both[None], sums.shape)
 
 
-def cached_kernel(layer, chunk, far, caches, before, after, weights, bias, *refs):
+def cached_kernel(layer, chunk, far, distant, cache, before, after, weights, bias, *refs):
     bring = None
     if layer == 0:
         video, out, ordered, near, *refs = refs
         refs = [out, ordered, *refs]
         bring = pltpu.make_async_copy(video, near, refs[-1].at[4])
-    out, ordered, edges, *slabs, cache, weight, taps, sem = refs
+    if distant:
+        caches, out, ordered, cache, *refs = cache, *refs
+        refs = [out, ordered, *refs]
+    out, ordered, edges, *slabs, weight, taps, sem = refs
     if far:
         away, out, *slabs = out, slabs[0], *slabs[1:]
-    _, _, rows, cols, channels = caches.shape
+    rows, cols, channels = cache.shape[-3:]
     places = rows * cols
-    begun = pltpu.make_async_copy(caches.at[layer], cache, sem.at[0])
     fetch = pltpu.make_async_copy(weights.at[layer], weight, sem.at[1])
-    begun.start()
+    if distant:
+        begun = pltpu.make_async_copy(caches.at[layer], cache, sem.at[0])
+        begun.start()
     fetch.start()
     if bring is not None:
         bring.start()
-    begun.wait()
+    if distant:
+        begun.wait()
     for side, ref in enumerate((before, after)):
         for plane in range(PLANES):
             edges[side, plane] = ref[(layer + 1) * PLANES + plane].astype(jnp.float32)
@@ -237,7 +241,7 @@
         bring.wait()
 
 
-def active_kernel(layer, chunk, far, entries, final, *refs):
+def active_kernel(layer, chunk, far, bring, entries, final, *refs):
     x, before, after, stats, gain, shift, ordered, part, same = refs[:9]
     rest = refs[9:]
     residual = None
@@ -248,21 +252,27 @@
     if final:
         y, carried, *rest = rest
     else:
+        if bring:
+            caches, *rest = rest
         y, carried, sums, first, last, *rest = rest
+        if bring:
+            near, *rest = rest
     edges, *slabs, kept, held, taps, alike, sem = rest
     away = None
     if far:
         away, part, *slabs = part, *slabs
     frames, rows, cols, channels = kept.shape
     places = rows * cols
-    fetch = [pltpu.make_async_copy(ordered, taps, sem.at[1])]
-    if not final:
-        fetch.append(pltpu.make_async_copy(same, alike, sem.at[4]))
+    fetch, late = [pltpu.make_async_copy(ordered, taps, sem.at[1])], []
     if far:
         fetch.append(pltpu.make_async_copy(away, part, sem.at[3]))
     if residual is not None:
         fetch.append(pltpu.make_async_copy(residual, held, sem.at[2]))
-    for copy in fetch:
+    if not final:
+        late.append(pltpu.make_async_copy(same, alike, sem.at[4]))
+    if bring:
+        late.append(pltpu.make_async_copy(caches.at[layer + 1], near, sem.at[5]))
+    for copy in fetch + late:
         copy.start()
 
     means = jnp.sum(stats[...], axis=0) / entries
@@ -328,6 +338,8 @@
         value = product([(slabs[0], tables[0]), (slabs[1], tables[1])], start, chunk)
         moments = finish(1, start, chunk, value, moments)
     if not final:
+        for one in late:
+            one.wait()
         both = group_sums(moments, alike[...])
         sums[...] = jnp.broadcast_to(both[None], sums.shape)
         for plane in range(PLANES):
@@ -369,11 +381,12 @@
     same = in_hbm(jnp.asarray(alike, jnp.bfloat16))
     spread = jax.ShapeDtypeStruct((peers, 2, channels), jnp.float32)
     brim = jax.ShapeDtypeStruct(((layers + 1) * PLANES, rows, LANES), jnp.bfloat16)
-    sums, first, last = pl.pallas_call(
+    block = jax.ShapeDtypeStruct(video_span.shape, video_span.dtype)
+    sums, first, last, cache = pl.pallas_call(
         begin_kernel,
-        out_shape=[spread, brim, brim],
+        out_shape=[spread, brim, brim, block],
         in_specs=[HBM] * 3,
-        out_specs=[VMEM] * 3,
+        out_specs=[VMEM] * 4,
         scratch_shapes=[
             pltpu.VMEM((PLANES, places, LANES), jnp.float32),
             pltpu.VMEM((layers + 1,) + video_span.shape, jnp.bfloat16),
@@ -390,34 +403,37 @@
     def room(far):
         return [pltpu.VMEM((PLANES, places, LANES), jnp.float32)] if far else []
 
-    def cached_part(layer, far):
+    def cached_part(layer, far, cache):
+        distant = cache is None
+        own = [pltpu.VMEM(video_span.shape, jnp.bfloat16)] if distant else []
         planar = pltpu.HBM if far else jax.ShapeDtypeStruct
         return pl.pallas_call(
-            functools.partial(cached_kernel, layer, chunk, far),
+            functools.partial(cached_kernel, layer, chunk, far, distant),
             out_shape=[
                 planar((PLANES, places, LANES), jnp.float32),
                 pltpu.HBM((2, channels, tiles), weights.dtype),
             ]
-            + ([] if layer else [jax.ShapeDtypeStruct(video_span.shape, video_span.dtype)]),
-            in_specs=[HBM, VMEM, VMEM, HBM, VMEM] + ([] if layer else [HBM]),
+            + ([] if layer else [block]),
+            in_specs=[HBM if distant else VMEM, VMEM, VMEM, HBM, VMEM]
+            + ([] if layer else [HBM]),
             out_specs=[HBM if far else VMEM, HBM] + ([] if layer else [VMEM]),
-            scratch_shapes=scratch(frames, rows, room(far))
+            scratch_shapes=own + scratch(frames, rows, room(far))
             + [
-                pltpu.VMEM(video_span.shape, jnp.bfloat16),
                 pltpu.VMEM((channels, weights.shape[1]), weights.dtype),
                 pltpu.VMEM((3, channels, tiles), weights.dtype),
                 pltpu.SemaphoreType.DMA((5,)),
             ],
             compiler_params=pltpu.CompilerParams(vmem_limit_bytes=24 << 20),
             name="cached",
-        )(caches, *brims, turned, biases, *([] if layer else [video]))
+        )(caches if distant else cache, *brims, turned, biases, *([] if layer else [video]))
 
     x = None
     carried = None
     for layer in range(layers):
         final = layer == layers - 1
         far = layer < layers - 1
-        part, ordered, *near = cached_part(layer, far)
+        bring = layer < layers - 2
+        part, ordered, *near = cached_part(layer, far, cache)
         if near:
             x = near[0]
         if far:
@@ -441,8 +457,13 @@
             edge = jax.ShapeDtypeStruct((PLANES, rows, LANES), jnp.bfloat16)
             outs += [spread, edge, edge]
             out_specs += [VMEM] * 3
+        if bring:
+            outs.append(block)
+            out_specs.append(VMEM)
+            operands.append(caches)
+            specs.append(HBM)
         results = pl.pallas_call(
-            functools.partial(active_kernel, layer, chunk, far, entries, final),
+            functools.partial(active_kernel, layer, chunk, far, bring, entries, final),
             out_shape=outs,
             in_specs=specs,
             out_specs=out_specs,
@@ -452,7 +473,7 @@
                 pltpu.VMEM(video_span.shape, jnp.bfloat16),
                 pltpu.VMEM((2, channels, tiles), weights.dtype),
                 pltpu.VMEM(same.shape, same.dtype),
-                pltpu.SemaphoreType.DMA((5,)),
+                pltpu.SemaphoreType.DMA((6,)),
             ],
             compiler_params=pltpu.CompilerParams(vmem_limit_bytes=24 << 20),
             input_output_aliases=aliases,
@@ -462,6 +483,7 @@
         if not final:
             stats = gathered(results[2])
             before, after = around(results[3], results[4])
+            cache = results[5] if bring else None
     return x, carried
 
 

time: 65.4 us -> 64.1 us (0.980)
  Pallas kernels: 37.1 us -> 34.8 us
  waiting for transfers between devices: 0.95 us -> 2.23 us
    pallas_call x7, Pallas kernels: 37.1 us -> 34.8 us  [the longest x3 17.4 us: cached_part(): pl.pallas_call(functools.partial(cached_kernel, layer, chunk, far, distan...]
    all_to_all x3, waiting for transfers between devices: 0.12 us -> 1.4 us  [gathered(): return lax.all_to_all(sums, 'lon', 0, 0)]
  transfers between devices with their start and end apart: 9 -> 9, of which waited for: 2 -> 4; matrix products, arithmetic and copies ran while one was open for 0% -> 0% of each run, Pallas kernels for 30% -> 27%
where the time goes in v9:
time: 64.1 us; the launch traced here: 63.7 us
  Pallas kernels  34.8 us (54%)
  starting transfers between devices  25.7 us (40%)
  waiting for transfers between devices  2.23 us (3%)
  between operations  0.9 us (1%)
    pallas_call x3, Pallas kernels, cached_part(): pl.pallas_call(functools.partial(cached_kernel, layer, chunk, far, distan...  17.4 us
    ppermute x6, starting transfers between devices, around(): return (lax.ppermute(last, 'lon', up), lax.ppermute(first, 'lon', down))  14.6 us
    pallas_call x3, Pallas kernels, local(): pl.pallas_call(functools.partial(active_kernel, layer, chunk, far, bring,...  14.5 us
    all_to_all x3, starting transfers between devices, gathered(): return lax.all_to_all(sums, 'lon', 0, 0)  11.1 us
    pallas_call x1, Pallas kernels, local(): pl.pallas_call(begin_kernel, out_shape=[spread, brim, brim, block], in_sp...  2.88 us
    all_to_all x3, waiting for transfers between devices, gathered(): return lax.all_to_all(sums, 'lon', 0, 0)  1.4 us
  transfers between devices with their start and end apart: 9, of which 4 were waited for; matrix products, arithmetic and copies ran while one was open for 0% of the time, Pallas kernels for 27%

profile of v9, /device:TPU:0, one launch (start us, length us, event | category | flops | bytes accessed | tf_op | source)
XLA Modules:
  0.0 63.7 jit_solution(4316203626435266532)
XLA Ops:
  0.6 0.0 copy-start
  0.6 2.9 %begin.1 = (f32[16,2,192]{2,1,0:T(2,128)}, bf16[12,90,128]{2,1,0:T(8,128)(2,1)S(1)}, bf16[12,90,128]{2,1,0:T(8,128)(2,1)S(1)}, bf16[2,90,8,192]{3,2,1,0:T(8,128)(2,1)S(1)}) custom-call(bf16[2,90,8,192]{3,2,1,0:T(8,128)(2,1)} %refs_9_.3, bf16[3,2,90,8,192]{4,3,2,1,0:T(8,128)(2,1)} %cache.1, bf16[192,192]{1,0:T(8,128)(2,1)} %constant.2.clone.same.refs_8_), custom_call_target="tpu_custom_call" | custom-call | tf_op jit(solution)/shard_map/begin/pallas_call | solution.py:385
  3.5 0.5 collective-permute-start
  4.1 5.0 %collective-permute-start.1 = (bf16[12,90,128]{2,1,0:T(8,128)(2,1)S(1)}, bf16[12,90,128]{2,1,0:T(8,128)(2,1)S(1)}, u32[]{:S(2)}, u32[]{:S(2)}) collective-permute-start(bf16[12,90,128]{2,1,0:T(8,128)(2,1)S(1)} %get-tuple-element.26), channel_id=1, source_target_pairs={{1,0},{2,1},{3,2},{4,3},{5,4},{6,5},{7,6},{8,7},{9,8},{10,9},{11,1... | collective-permute-start | bytes 829448 | tf_op jit(solution)/shard_map/ppermute | solution.py:369
  9.1 3.6 %all-to-all-start = ((f32[16,2,192]{2,1,0:T(2,128)}), f32[16,2,192]{2,1,0:T(2,128)S(1)}, u32[]{:S(2)}, u32[]{:S(2)}) async-start(f32[16,2,192]{2,1,0:T(2,128)} %get-tuple-element.28), calls=%async_computation | async-start | bytes 65536 | tf_op jit(solution)/shard_map/all_to_all | solution.py:372
  12.7 0.8 %collective-permute-done.before.refs_1_ = bf16[12,90,128]{2,1,0:T(8,128)(2,1)S(1)} collective-permute-done((bf16[12,90,128]{2,1,0:T(8,128)(2,1)S(1)}, bf16[12,90,128]{2,1,0:T(8,128)(2,1)S(1)}, u32[]{:S(2)}, u32[]{:S(2)}) %collective-permute-start) | collective-permute-done | bytes 276512 | tf_op jit(solution)/shard_map/ppermute | solution.py:369
  13.6 0.0 collective-permute-done.1.after.refs_2_
  13.6 0.0 copy-done
  13.6 0.0 copy-start.1
  13.6 0.0 copy-start.2
  13.6 5.6 %cached.3 = (f32[3,720,128]{2,1,0:T(8,128)}, bf16[2,192,1792]{2,1,0:T(8,128)(2,1)}, bf16[2,90,8,192]{3,2,1,0:T(8,128)(2,1)S(1)}) custom-call(bf16[2,90,8,192]{3,2,1,0:T(8,128)(2,1)S(1)} %get-tuple-element.24.cache, bf16[12,90,128]{2,1,0:T(8,128)(2,1)S(1)} %collective-permute-done.before.refs_1_, ...), custom_call_target="tpu_custom_call" | custom-call | tf_op jit(solution)/shard_map/cached/pallas_call | solution.py:410
  19.2 0.2 all-to-all-done.refs_3_
  19.4 0.0 copy-done.1
  19.4 0.0 copy-done.2
  19.4 4.8 %active.3 = (f32[3,720,128]{2,1,0:T(8,128)S(1)}, bf16[3,2,90,8,192]{4,3,2,1,0:T(8,128)(2,1)}, f32[16,2,192]{2,1,0:T(2,128)}, bf16[3,90,128]{2,1,0:T(8,128)(2,1)S...) custom-call(bf16[2,90,8,192]{3,2,1,0:T(8,128)(2,1)S(1)} %get-tuple-element.27.refs_0_, ...), custom_call_target="tpu_custom_call" | custom-call | tf_op jit(solution)/shard_map/active/pallas_call | solution.py:465
  24.2 2.3 %collective-permute-start.2 = (bf16[3,90,128]{2,1,0:T(8,128)(2,1)S(1)}, bf16[3,90,128]{2,1,0:T(8,128)(2,1)S(1)}, u32[]{:S(2)}, u32[]{:S(2)}) collective-permute-start(bf16[3,90,128]{2,1,0:T(8,128)(2,1)S(1)} %get-tuple-element.32), channel_id=1, source_target_pairs={{0,1},{1,2},{2,3},{3,4},{4,5},{5,6},{6,7},{7,8},{8,9},{9,10},{10,1... | collective-permute-start | bytes 207368 | tf_op jit(solution)/shard_map/ppermute | solution.py:369
  26.5 2.2 %collective-permute-start.3 = (bf16[3,90,128]{2,1,0:T(8,128)(2,1)S(1)}, bf16[3,90,128]{2,1,0:T(8,128)(2,1)S(1)}, u32[]{:S(2)}, u32[]{:S(2)}) collective-permute-start(bf16[3,90,128]{2,1,0:T(8,128)(2,1)S(1)} %get-tuple-element.33), channel_id=1, source_target_pairs={{1,0},{2,1},{3,2},{4,3},{5,4},{6,5},{7,6},{8,7},{9,8},{10,9},{11,1... | collective-permute-start | bytes 207368 | tf_op jit(solution)/shard_map/ppermute | solution.py:369
  28.7 3.9 %all-to-all-start.1 = ((f32[16,2,192]{2,1,0:T(2,128)}), f32[16,2,192]{2,1,0:T(2,128)S(1)}, u32[]{:S(2)}, u32[]{:S(2)}) async-start(f32[16,2,192]{2,1,0:T(2,128)} %get-tuple-element.34), calls=%async_computation.1 | async-start | bytes 65536 | tf_op jit(solution)/shard_map/all_to_all | solution.py:372
  32.5 5.6 %cached.4 = (f32[3,720,128]{2,1,0:T(8,128)}, bf16[2,192,1792]{2,1,0:T(8,128)(2,1)}) custom-call(bf16[2,90,8,192]{3,2,1,0:T(8,128)(2,1)S(1)} %get-tuple-element.35.cache, bf16[12,90,128]{2,1,0:T(8,128)(2,1)S(1)} %collective-permute-done.before.refs_1_, bf16[12,90,128]{2,1,0:T(8,128)(2,1)S(1)} %collective-permute-done.1.after.refs_2_, ...), custom_call_target="tpu_custom_call" | custom-call | tf_op jit(solution)/shard_map/cached/pallas_call | solution.py:410
  38.1 1.1 %all-to-all-done.1.refs_3_ = f32[16,2,192]{2,1,0:T(2,128)S(1)} async-done(((f32[16,2,192]{2,1,0:T(2,128)}), f32[16,2,192]{2,1,0:T(2,128)S(1)}, u32[]{:S(2)}, u32[]{:S(2)}) %all-to-all-start.1) | async-done | bytes 24608 | tf_op jit(solution)/shard_map/all_to_all | solution.py:372
  39.2 0.0 collective-permute-done.2.refs_1_
  39.2 0.0 collective-permute-done.3.refs_2_
  39.2 5.2 %active.4 = (f32[3,720,128]{2,1,0:T(8,128)S(1)}, bf16[3,2,90,8,192]{4,3,2,1,0:T(8,128)(2,1)}, f32[16,2,192]{2,1,0:T(2,128)}, bf16[3,90,128]{2,1,0:T(8,128)(2,1)S(1)}, bf16[3,90,128]{2,1,0:T(8,128)(2,1)S(1)}) custom-call(f32[3,720,128]{2,1,0:T(8,128)S(1)} %get-tuple-element.31.refs_0_, ...), custom_call_target="tpu_custom_call", output_to_operand_aliasing={{1}: (10, {})} | custom-call | tf_op jit(solution)/shard_map/active/pallas_call | solution.py:465
  44.4 0.1 collective-permute-start.4
  44.5 4.4 %collective-permute-start.5 = (bf16[3,90,128]{2,1,0:T(8,128)(2,1)S(1)}, bf16[3,90,128]{2,1,0:T(8,128)(2,1)S(1)}, u32[]{:S(2)}, u32[]{:S(2)}) collective-permute-start(bf16[3,90,128]{2,1,0:T(8,128)(2,1)S(1)} %get-tuple-element.41), channel_id=1, source_target_pairs={{1,0},{2,1},{3,2},{4,3},{5,4},{6,5},{7,6},{8,7},{9,8},{10,9},{11,1... | collective-permute-start | bytes 207368 | tf_op jit(solution)/shard_map/ppermute | solution.py:369
  48.9 3.7 %all-to-all-start.2 = ((f32[16,2,192]{2,1,0:T(2,128)}), f32[16,2,192]{2,1,0:T(2,128)S(1)}, u32[]{:S(2)}, u32[]{:S(2)}) async-start(f32[16,2,192]{2,1,0:T(2,128)} %get-tuple-element.42), calls=%async_computation.2 | async-start | bytes 65536 | tf_op jit(solution)/shard_map/all_to_all | solution.py:372
  52.6 6.3 %cached.5 = (f32[3,720,128]{2,1,0:T(8,128)S(1)}, bf16[2,192,1792]{2,1,0:T(8,128)(2,1)}) custom-call(bf16[3,2,90,8,192]{4,3,2,1,0:T(8,128)(2,1)} %cache.1, bf16[12,90,128]{2,1,0:T(8,128)(2,1)S(1)} %collective-permute-done.before.refs_1_, bf16[12,90,128]{2,1,0:T(8,128)(2,1)S(1)} %collective-permute-done.1.after.refs_2_, bf16[3,192,5184]{2,1,0:T(8,128)(2,1)} %bitcast.3, ...), custom_call_target="tpu_custom_call" | custom-call | tf_op jit(solution)/shard_map/cached/pallas_call | solution.py:410
  58.9 0.1 all-to-all-done.2.refs_3_
  59.0 0.0 collective-permute-done.4.refs_1_
  59.0 0.0 collective-permute-done.5.refs_2_
  59.0 4.5 %active.5 = (bf16[2,90,8,192]{3,2,1,0:T(8,128)(2,1)}, bf16[3,2,90,8,192]{4,3,2,1,0:T(8,128)(2,1)}) custom-call(f32[3,720,128]{2,1,0:T(8,128)S(1)} %get-tuple-element.39.refs_0_, bf16[3,90,128]{2,1,0:T(8,128)(2,1)S(1)} %collective-permute-done.4.refs_1_, bf16[3,90,128]{2,1,0:T(8,128)(2,1)S(1)} %collective-permute-done.5.refs_2_, ...), custom_call_target="tpu_custom_call", output_to_operand_aliasing={{1}: (9, {})} | custom-call | tf_op jit(solution)/shard_map/active/pallas_call | solution.py:465
Async XLA Ops:
  0.6 12.9 %copy-start = (f32[3,192]{1,0:T(4,128)S(1)}, f32[3,192]{1,0:T(4,128)}, u32[]{:S(2)}) copy-start(f32[3,192]{1,0:T(4,128)} %bias.5) | copy-start | bytes 6916
  3.5 10.0 %collective-permute-start = (bf16[12,90,128]{2,1,0:T(8,128)(2,1)S(1)}, bf16[12,90,128]{2,1,0:T(8,128)(2,1)S(1)}, u32[]{:S(2)}, u32[]{:S(2)}) collective-permute-start(bf16[12,90,128]{2,1,0:T(8,128)(2,1)S(1)} %get-tuple-element.25), channel_id=1, source_target_pairs={{0,1},{1,2},{2,3},{3,4},{4,5},{5,6},{6,7},{7,8},{8,9},{9,10},{10,1... | collective-permute-start | bytes 829448 | tf_op jit(solution)/shard_map/ppermute | solution.py:369
  4.1 9.5 %collective-permute-start.1 = (bf16[12,90,128]{2,1,0:T(8,128)(2,1)S(1)}, bf16[12,90,128]{2,1,0:T(8,128)(2,1)S(1)}, u32[]{:S(2)}, u32[]{:S(2)}) collective-permute-start(bf16[12,90,128]{2,1,0:T(8,128)(2,1)S(1)} %get-tuple-element.26), channel_id=1, source_target_pairs={{1,0},{2,1},{3,2},{4,3},{5,4},{6,5},{7,6},{8,7},{9,8},{10,9},{11,1... | collective-permute-start | bytes 829448 | tf_op jit(solution)/shard_map/ppermute | solution.py:369
  9.1 10.3 %all-to-all-start = ((f32[16,2,192]{2,1,0:T(2,128)}), f32[16,2,192]{2,1,0:T(2,128)S(1)}, u32[]{:S(2)}, u32[]{:S(2)}) async-start(f32[16,2,192]{2,1,0:T(2,128)} %get-tuple-element.28), calls=%async_computation | async-start | bytes 65536 | tf_op jit(solution)/shard_map/all_to_all | solution.py:372
  13.6 5.8 %copy-start.1 = (f32[3,192]{1,0:T(4,128)S(1)}, f32[3,192]{1,0:T(4,128)}, u32[]{:S(2)}) copy-start(f32[3,192]{1,0:T(4,128)} %refs_4_.5) | copy-start | bytes 6916
  13.6 5.8 %copy-start.2 = (f32[3,192]{1,0:T(4,128)S(1)}, f32[3,192]{1,0:T(4,128)}, u32[]{:S(2)}) copy-start(f32[3,192]{1,0:T(4,128)} %refs_5_.5) | copy-start | bytes 6916
  24.2 15.0 %collective-permute-start.2 = (bf16[3,90,128]{2,1,0:T(8,128)(2,1)S(1)}, bf16[3,90,128]{2,1,0:T(8,128)(2,1)S(1)}, u32[]{:S(2)}, u32[]{:S(2)}) collective-permute-start(bf16[3,90,128]{2,1,0:T(8,128)(2,1)S(1)} %get-tuple-element.32), channel_id=1, source_target_pairs={{0,1},{1,2},{2,3},{3,4},{4,5},{5,6},{6,7},{7,8},{8,9},{9,10},{10,1... | collective-permute-start | bytes 207368 | tf_op jit(solution)/shard_map/ppermute | solution.py:369
  26.5 12.7 %collective-permute-start.3 = (bf16[3,90,128]{2,1,0:T(8,128)(2,1)S(1)}, bf16[3,90,128]{2,1,0:T(8,128)(2,1)S(1)}, u32[]{:S(2)}, u32[]{:S(2)}) collective-permute-start(bf16[3,90,128]{2,1,0:T(8,128)(2,1)S(1)} %get-tuple-element.33), channel_id=1, source_target_pairs={{1,0},{2,1},{3,2},{4,3},{5,4},{6,5},{7,6},{8,7},{9,8},{10,9},{11,1... | collective-permute-start | bytes 207368 | tf_op jit(solution)/shard_map/ppermute | solution.py:369
  28.7 10.5 %all-to-all-start.1 = ((f32[16,2,192]{2,1,0:T(2,128)}), f32[16,2,192]{2,1,0:T(2,128)S(1)}, u32[]{:S(2)}, u32[]{:S(2)}) async-start(f32[16,2,192]{2,1,0:T(2,128)} %get-tuple-element.34), calls=%async_computation.1 | async-start | bytes 65536 | tf_op jit(solution)/shard_map/all_to_all | solution.py:372
  44.4 14.6 %collective-permute-start.4 = (bf16[3,90,128]{2,1,0:T(8,128)(2,1)S(1)}, bf16[3,90,128]{2,1,0:T(8,128)(2,1)S(1)}, u32[]{:S(2)}, u32[]{:S(2)}) collective-permute-start(bf16[3,90,128]{2,1,0:T(8,128)(2,1)S(1)} %get-tuple-element.40), channel_id=1, source_target_pairs={{0,1},{1,2},{2,3},{3,4},{4,5},{5,6},{6,7},{7,8},{8,9},{9,10},{10,1... | collective-permute-start | bytes 207368 | tf_op jit(solution)/shard_map/ppermute | solution.py:369
  44.5 14.5 %collective-permute-start.5 = (bf16[3,90,128]{2,1,0:T(8,128)(2,1)S(1)}, bf16[3,90,128]{2,1,0:T(8,128)(2,1)S(1)}, u32[]{:S(2)}, u32[]{:S(2)}) collective-permute-start(bf16[3,90,128]{2,1,0:T(8,128)(2,1)S(1)} %get-tuple-element.41), channel_id=1, source_target_pairs={{1,0},{2,1},{3,2},{4,3},{5,4},{6,5},{7,6},{8,7},{9,8},{10,9},{11,1... | collective-permute-start | bytes 207368 | tf_op jit(solution)/shard_map/ppermute | solution.py:369
  48.9 10.1 %all-to-all-start.2 = ((f32[16,2,192]{2,1,0:T(2,128)}), f32[16,2,192]{2,1,0:T(2,128)S(1)}, u32[]{:S(2)}, u32[]{:S(2)}) async-start(f32[16,2,192]{2,1,0:T(2,128)} %get-tuple-element.42), calls=%async_computation.2 | async-start | bytes 65536 | tf_op jit(solution)/shard_map/all_to_all | solution.py:372

commit v10 on v9

--- a/solution.py
+++ b/solution.py
@@ -188,13 +188,23 @@
 
 def cached_kernel(layer, chunk, far, distant, cache, before, after, weights, bias, *refs):
     bring = None
-    if layer == 0:
-        video, out, ordered, near, *refs = refs
+    if layer < 2:
+        video, out, ordered, *refs = refs
+        handed = [refs.pop(0) for _ in range(2 * layer)]
+        near, *refs = refs
         refs = [out, ordered, *refs]
         bring = pltpu.make_async_copy(video, near, refs[-1].at[4])
+    passed = []
+    if layer == 1:
+        later = pl.ds((layer + 2) * PLANES, handed[0].shape[0])
+        for side, ref in enumerate((before, after)):
+            passed.append(pltpu.make_async_copy(ref.at[later], handed[side], refs[-1].at[5 + side]))
     if distant:
-        caches, out, ordered, cache, *refs = cache, *refs
+        caches, out, ordered, cache, brims, *refs = cache, *refs
         refs = [out, ordered, *refs]
+        here = pl.ds((layer - 2) * PLANES, PLANES)
+        for side, ref in enumerate((before, after)):
+            passed.append(pltpu.make_async_copy(ref.at[here], brims.at[side], refs[-1].at[5 + side]))
     out, ordered, edges, *slabs, weight, taps, sem = refs
     if far:
         away, out, *slabs = out, slabs[0], *slabs[1:]
@@ -207,11 +217,17 @@
     fetch.start()
     if bring is not None:
         bring.start()
+    for copy in passed:
+        copy.start()
+    origin = (layer + 1) * PLANES
     if distant:
         begun.wait()
+        for copy in passed:
+            copy.wait()
+        before, after, origin, passed = brims.at[0], brims.at[1], 0, []
     for side, ref in enumerate((before, after)):
         for plane in range(PLANES):
-            edges[side, plane] = ref[(layer + 1) * PLANES + plane].astype(jnp.float32)
+            edges[side, plane] = ref[origin + plane].astype(jnp.float32)
 
     def row_of(h):
         return planes(*(cache[frame, h].astype(jnp.float32) for frame in range(2)))
@@ -221,32 +237,36 @@
 
     build_slabs(rows, row_of, edge_of, slabs)
     fetch.wait()
+    if layer == 1:
+        bring.wait()
     for p in (1, 2, 0):
         taps[p] = tap_lanes(weight, p * 9 * channels, channels)
     store = pltpu.make_async_copy(taps.at[pl.ds(1, 2)], ordered, sem.at[2])
     store.start()
     constant = bias[layer : layer + 1, :]
     tables = [taps[p] for p in range(2)]
-    value = product([(slabs[1], tables[0])], 0, places)
-    put_planes(out, 1, pl.ds(0, places), value + constant)
-    for start in range(0, places, chunk):
-        value = product([(slabs[0], tables[0]), (slabs[1], tables[1])], start, chunk)
-        put_planes(out, 0, pl.ds(start, chunk), value + constant)
+
+    def finish(t, value):
+        value = value + constant
+        if layer == 1:
+            value = value + near[t].astype(jnp.float32).reshape(places, channels)
+        put_planes(out, t, pl.ds(0, places), value)
+
+    finish(1, product([(slabs[1], tables[0])], 0, places))
+    finish(0, product([(slabs[0], tables[0]), (slabs[1], tables[1])], 0, places))
     if far:
         leave = pltpu.make_async_copy(out, away, sem.at[3])
         leave.start()
         leave.wait()
-    store.wait()
-    if bring is not None:
+    for copy in [store] + passed:
+        copy.wait()
+    if layer == 0:
         bring.wait()
 
 
 def active_kernel(layer, chunk, far, bring, entries, final, *refs):
     x, before, after, stats, gain, shift, ordered, part, same = refs[:9]
     rest = refs[9:]
-    residual = None
-    if layer == 1:
-        residual, *rest = rest
     if layer > 0:
         _, *rest = rest
     if final:
@@ -257,7 +277,7 @@
         y, carried, sums, first, last, *rest = rest
         if bring:
             near, *rest = rest
-    edges, *slabs, kept, held, taps, alike, sem = rest
+    edges, *slabs, kept, taps, alike, sem = rest
     away = None
     if far:
         away, part, *slabs = part, *slabs
@@ -266,8 +286,6 @@
     fetch, late = [pltpu.make_async_copy(ordered, taps, sem.at[1])], []
     if far:
         fetch.append(pltpu.make_async_copy(away, part, sem.at[3]))
-    if residual is not None:
-        fetch.append(pltpu.make_async_copy(residual, held, sem.at[2]))
     if not final:
         late.append(pltpu.make_async_copy(same, alike, sem.at[4]))
     if bring:
@@ -323,8 +341,6 @@
             value = value + get_planes(x, t, here)
             y[t, span] = value.reshape(shape).astype(jnp.bfloat16)
             return moments
-        if residual is not None:
-            value = value + held[t, span].astype(jnp.float32).reshape(size, channels)
         put_planes(y, t, here, value)
         folded = value.reshape(shape)
         return [
@@ -403,9 +419,14 @@
     def room(far):
         return [pltpu.VMEM((PLANES, places, LANES), jnp.float32)] if far else []
 
-    def cached_part(layer, far, cache):
+    def cached_part(layer, far, cache, brims):
         distant = cache is None
-        own = [pltpu.VMEM(video_span.shape, jnp.bfloat16)] if distant else []
+        own = [pltpu.VMEM(video_span.shape, jnp.bfloat16)] if distant or layer == 1 else []
+        if distant:
+            brims = [in_hbm(brim) for brim in brims]
+            own.append(pltpu.VMEM((2, PLANES, rows, LANES), jnp.bfloat16))
+        later = pltpu.HBM(((layers - 2) * PLANES, rows, LANES), jnp.bfloat16)
+        more = {0: [block], 1: [later] * 2}.get(layer, [])
         planar = pltpu.HBM if far else jax.ShapeDtypeStruct
         return pl.pallas_call(
             functools.partial(cached_kernel, layer, chunk, far, distant),
@@ -413,19 +434,19 @@
                 planar((PLANES, places, LANES), jnp.float32),
                 pltpu.HBM((2, channels, tiles), weights.dtype),
             ]
-            + ([] if layer else [block]),
-            in_specs=[HBM if distant else VMEM, VMEM, VMEM, HBM, VMEM]
-            + ([] if layer else [HBM]),
-            out_specs=[HBM if far else VMEM, HBM] + ([] if layer else [VMEM]),
+            + more,
+            in_specs=[HBM if distant else VMEM] * 3 + [HBM, VMEM]
+            + ([HBM] if layer < 2 else []),
+            out_specs=[HBM if far else VMEM, HBM] + [HBM if layer else VMEM] * len(more),
             scratch_shapes=own + scratch(frames, rows, room(far))
             + [
                 pltpu.VMEM((channels, weights.shape[1]), weights.dtype),
                 pltpu.VMEM((3, channels, tiles), weights.dtype),
-                pltpu.SemaphoreType.DMA((5,)),
+                pltpu.SemaphoreType.DMA((7,)),
             ],
             compiler_params=pltpu.CompilerParams(vmem_limit_bytes=24 << 20),
             name="cached",
-        )(caches if distant else cache, *brims, turned, biases, *([] if layer else [video]))
+        )(caches if distant else cache, *brims, turned, biases, *([video] if layer < 2 else []))
 
     x = None
     carried = None
@@ -433,17 +454,16 @@
         final = layer == layers - 1
         far = layer < layers - 1
         bring = layer < layers - 2
-        part, ordered, *near = cached_part(layer, far, cache)
-        if near:
-            x = near[0]
+        part, ordered, *more = cached_part(layer, far, cache, brims)
+        if layer == 0:
+            x = more[0]
+        elif more:
+            brims = more
         if far:
             part = in_hbm(part)
         operands = [x, before, after, stats, norm_gains, shifts, in_hbm(ordered), part, same]
         specs = [VMEM] * 6 + [HBM, HBM if far else VMEM, HBM]
         aliases = {}
-        if layer == 1:
-            operands.append(video)
-            specs.append(HBM)
         if layer > 0:
             aliases = {len(operands): 1}
             operands.append(carried)
@@ -470,7 +490,6 @@
             scratch_shapes=scratch(frames, rows, room(far))
             + [
                 pltpu.VMEM(video_span.shape, jnp.bfloat16),
-                pltpu.VMEM(video_span.shape, jnp.bfloat16),
                 pltpu.VMEM((2, channels, tiles), weights.dtype),
                 pltpu.VMEM(same.shape, same.dtype),
                 pltpu.SemaphoreType.DMA((6,)),

time: 64.1 us -> 64.2 us (level)
    pallas_call x3, Pallas kernels: 17.4 us -> 18.1 us  [cached_part(): pl.pallas_call(functools.partial(cached_kernel, layer, chunk, far, distan...]
  transfers between devices with their start and end apart: 9 -> 9, of which waited for: 4 -> 3; matrix products, arithmetic and copies ran while one was open for 0% -> 0% of each run, Pallas kernels for 27% -> 28%
where the time goes in v10:
time: 64.2 us; the launch traced here: 63.8 us
  Pallas kernels  35 us (55%)
  starting transfers between devices  25.7 us (40%)
  waiting for transfers between devices  2.09 us (3%)
  between operations  0.92 us (1%)
    pallas_call x3, Pallas kernels, cached_part(): pl.pallas_call(functools.partial(cached_kernel, layer, chunk, far, distan...  18.1 us
    ppermute x6, starting transfers between devices, around(): return (lax.ppermute(last, 'lon', up), lax.ppermute(first, 'lon', down))  14.6 us
    pallas_call x3, Pallas kernels, local(): pl.pallas_call(functools.partial(active_kernel, layer, chunk, far, bring,...  14.1 us
    all_to_all x3, starting transfers between devices, gathered(): return lax.all_to_all(sums, 'lon', 0, 0)  11.1 us
    pallas_call x1, Pallas kernels, local(): pl.pallas_call(begin_kernel, out_shape=[spread, brim, brim, block], in_sp...  2.88 us
  transfers between devices with their start and end apart: 9, of which 3 were waited for; matrix products, arithmetic and copies ran while one was open for 0% of the time, Pallas kernels for 28%

profile of v10, /device:TPU:0, one launch (start us, length us, event | category | flops | bytes accessed | tf_op | source)
XLA Modules:
  0.0 63.8 jit_solution(17740373478535725390)
XLA Ops:
  0.6 0.0 copy-start
  0.6 2.9 %begin.1 = (f32[16,2,192]{2,1,0:T(2,128)}, bf16[12,90,128]{2,1,0:T(8,128)(2,1)S(1)}, bf16[12,90,128]{2,1,0:T(8,128)(2,1)S(1)}, bf16[2,90,8,192]{3,2,1,0:T(8,128)(2,1)S(1)}) custom-call(bf16[2,90,8,192]{3,2,1,0:T(8,128)(2,1)} %refs_0_.3, bf16[3,2,90,8,192]{4,3,2,1,0:T(8,128)(2,1)} %cache.1, bf16[192,192]{1,0:T(8,128)(2,1)} %constant.2.clone.same.refs_8_), custom_call_target="tpu_custom_call" | custom-call | tf_op jit(solution)/shard_map/begin/pallas_call | solution.py:401
  3.5 0.5 collective-permute-start
  4.1 5.0 %collective-permute-start.1 = (bf16[12,90,128]{2,1,0:T(8,128)(2,1)S(1)}, bf16[12,90,128]{2,1,0:T(8,128)(2,1)S(1)}, u32[]{:S(2)}, u32[]{:S(2)}) collective-permute-start(bf16[12,90,128]{2,1,0:T(8,128)(2,1)S(1)} %get-tuple-element.28), channel_id=1, source_target_pairs={{1,0},{2,1},{3,2},{4,3},{5,4},{6,5},{7,6},{8,7},{9,8},{10,9},{11,1... | collective-permute-start | bytes 829448 | tf_op jit(solution)/shard_map/ppermute | solution.py:385
  9.1 3.6 %all-to-all-start = ((f32[16,2,192]{2,1,0:T(2,128)}), f32[16,2,192]{2,1,0:T(2,128)S(1)}, u32[]{:S(2)}, u32[]{:S(2)}) async-start(f32[16,2,192]{2,1,0:T(2,128)} %get-tuple-element.30), calls=%async_computation | async-start | bytes 65536 | tf_op jit(solution)/shard_map/all_to_all | solution.py:388
  12.7 0.8 %collective-permute-done.before.refs_1_ = bf16[12,90,128]{2,1,0:T(8,128)(2,1)S(1)} collective-permute-done((bf16[12,90,128]{2,1,0:T(8,128)(2,1)S(1)}, bf16[12,90,128]{2,1,0:T(8,128)(2,1)S(1)}, u32[]{:S(2)}, u32[]{:S(2)}) %collective-permute-start) | collective-permute-done | bytes 276512 | tf_op jit(solution)/shard_map/ppermute | solution.py:385
  13.6 0.0 collective-permute-done.1.after.refs_2_
  13.6 0.0 copy-done
  13.6 0.0 copy-start.1
  13.6 0.0 copy-start.2
  13.6 5.6 %cached.3 = (f32[3,720,128]{2,1,0:T(8,128)}, bf16[2,192,1792]{2,1,0:T(8,128)(2,1)}, bf16[2,90,8,192]{3,2,1,0:T(8,128)(2,1)S(1)}) custom-call(bf16[2,90,8,192]{3,2,1,0:T(8,128)(2,1)S(1)} %get-tuple-element.26.cache, bf16[12,90,128]{2,1,0:T(8,128)(2,1)S(1)} %collective-permute-done.before.refs_1_, ...), custom_call_target="tpu_custom_call" | custom-call | tf_op jit(solution)/shard_map/cached/pallas_call | solution.py:431
  19.2 0.2 all-to-all-done.refs_3_
  19.4 0.0 copy-done.1
  19.4 0.0 copy-done.2
  19.4 4.8 %active.3 = (f32[3,720,128]{2,1,0:T(8,128)S(1)}, bf16[3,2,90,8,192]{4,3,2,1,0:T(8,128)(2,1)}, f32[16,2,192]{2,1,0:T(2,128)}, bf16[3,90,128]{2,1,0:T(8,128)(2,1)S...) custom-call(bf16[2,90,8,192]{3,2,1,0:T(8,128)(2,1)S(1)} %get-tuple-element.29.refs_0_, ...), custom_call_target="tpu_custom_call" | custom-call | tf_op jit(solution)/shard_map/active/pallas_call | solution.py:485
  24.2 2.3 %collective-permute-start.2 = (bf16[3,90,128]{2,1,0:T(8,128)(2,1)S(1)}, bf16[3,90,128]{2,1,0:T(8,128)(2,1)S(1)}, u32[]{:S(2)}, u32[]{:S(2)}) collective-permute-start(bf16[3,90,128]{2,1,0:T(8,128)(2,1)S(1)} %get-tuple-element.34), channel_id=1, source_target_pairs={{0,1},{1,2},{2,3},{3,4},{4,5},{5,6},{6,7},{7,8},{8,9},{9,10},{10,1... | collective-permute-start | bytes 207368 | tf_op jit(solution)/shard_map/ppermute | solution.py:385
  26.5 2.2 %collective-permute-start.3 = (bf16[3,90,128]{2,1,0:T(8,128)(2,1)S(1)}, bf16[3,90,128]{2,1,0:T(8,128)(2,1)S(1)}, u32[]{:S(2)}, u32[]{:S(2)}) collective-permute-start(bf16[3,90,128]{2,1,0:T(8,128)(2,1)S(1)} %get-tuple-element.35), channel_id=1, source_target_pairs={{1,0},{2,1},{3,2},{4,3},{5,4},{6,5},{7,6},{8,7},{9,8},{10,9},{11,1... | collective-permute-start | bytes 207368 | tf_op jit(solution)/shard_map/ppermute | solution.py:385
  28.7 3.9 %all-to-all-start.1 = ((f32[16,2,192]{2,1,0:T(2,128)}), f32[16,2,192]{2,1,0:T(2,128)S(1)}, u32[]{:S(2)}, u32[]{:S(2)}) async-start(f32[16,2,192]{2,1,0:T(2,128)} %get-tuple-element.36), calls=%async_computation.1 | async-start | bytes 65536 | tf_op jit(solution)/shard_map/all_to_all | solution.py:388
  32.5 5.6 %cached.4 = (f32[3,720,128]{2,1,0:T(8,128)}, bf16[2,192,1792]{2,1,0:T(8,128)(2,1)}, bf16[3,90,128]{2,1,0:T(8,128)(2,1)}, bf16[3,90,128]{2,1,0:T(8,128)(2,1)}) custom-call(bf16[2,90,8,192]{3,2,1,0:T(8,128)(2,1)S(1)} %get-tuple-element.37.cache, bf16[12,90,128]{2,1,0:T(8,128)(2,1)S(1)} %collective-permute-done.before.refs_1_, ...), custom_call_target="tpu_custom_call" | custom-call | tf_op jit(solution)/shard_map/cached/pallas_call | solution.py:431
  38.1 1.0 %all-to-all-done.1.refs_3_ = f32[16,2,192]{2,1,0:T(2,128)S(1)} async-done(((f32[16,2,192]{2,1,0:T(2,128)}), f32[16,2,192]{2,1,0:T(2,128)S(1)}, u32[]{:S(2)}, u32[]{:S(2)}) %all-to-all-start.1) | async-done | bytes 24608 | tf_op jit(solution)/shard_map/all_to_all | solution.py:388
  39.2 0.0 collective-permute-done.2.refs_1_
  39.2 0.0 collective-permute-done.3.refs_2_
  39.2 4.8 %active.4 = (f32[3,720,128]{2,1,0:T(8,128)S(1)}, bf16[3,2,90,8,192]{4,3,2,1,0:T(8,128)(2,1)}, f32[16,2,192]{2,1,0:T(2,128)}, bf16[3,90,128]{2,1,0:T(8,128)(2,1)S(1)}, bf16[3,90,128]{2,1,0:T(8,128)(2,1)S(1)}) custom-call(f32[3,720,128]{2,1,0:T(8,128)S(1)} %get-tuple-element.33.refs_0_, ...), custom_call_target="tpu_custom_call", output_to_operand_aliasing={{1}: (9, {})} | custom-call | tf_op jit(solution)/shard_map/active/pallas_call | solution.py:485
  44.0 0.1 collective-permute-start.4
  44.0 4.4 %collective-permute-start.5 = (bf16[3,90,128]{2,1,0:T(8,128)(2,1)S(1)}, bf16[3,90,128]{2,1,0:T(8,128)(2,1)S(1)}, u32[]{:S(2)}, u32[]{:S(2)}) collective-permute-start(bf16[3,90,128]{2,1,0:T(8,128)(2,1)S(1)} %get-tuple-element.43), channel_id=1, source_target_pairs={{1,0},{2,1},{3,2},{4,3},{5,4},{6,5},{7,6},{8,7},{9,8},{10,9},{11,1... | collective-permute-start | bytes 207368 | tf_op jit(solution)/shard_map/ppermute | solution.py:385
  48.5 3.7 %all-to-all-start.2 = ((f32[16,2,192]{2,1,0:T(2,128)}), f32[16,2,192]{2,1,0:T(2,128)S(1)}, u32[]{:S(2)}, u32[]{:S(2)}) async-start(f32[16,2,192]{2,1,0:T(2,128)} %get-tuple-element.44), calls=%async_computation.2 | async-start | bytes 65536 | tf_op jit(solution)/shard_map/all_to_all | solution.py:388
  52.1 7.0 %cached.5 = (f32[3,720,128]{2,1,0:T(8,128)S(1)}, bf16[2,192,1792]{2,1,0:T(8,128)(2,1)}) custom-call(bf16[3,2,90,8,192]{4,3,2,1,0:T(8,128)(2,1)} %cache.1, bf16[3,90,128]{2,1,0:T(8,128)(2,1)} %get-tuple-element.45.before, bf16[3,90,128]{2,1,0:T(8,128)(2,1)} %get-tuple-element.46.after, bf16[3,192,5184]{2,1,0:T(8,128)(2,1)} %bitcast.3, f32[3,192]{1,0:T(4,128)S(1)} %copy-done), custom_call_target="tpu_custom_call" | custom-call | tf_op jit(solution)/shard_map/cached/pallas_call | solution.py:431
  59.1 0.0 all-to-all-done.2.refs_3_
  59.1 0.0 collective-permute-done.4.refs_1_
  59.1 0.0 collective-permute-done.5.refs_2_
  59.1 4.5 %active.5 = (bf16[2,90,8,192]{3,2,1,0:T(8,128)(2,1)}, bf16[3,2,90,8,192]{4,3,2,1,0:T(8,128)(2,1)}) custom-call(f32[3,720,128]{2,1,0:T(8,128)S(1)} %get-tuple-element.41.refs_0_, bf16[3,90,128]{2,1,0:T(8,128)(2,1)S(1)} %collective-permute-done.4.refs_1_, bf16[3,90,128]{2,1,0:T(8,128)(2,1)S(1)} %collective-permute-done.5.refs_2_, ...), custom_call_target="tpu_custom_call", output_to_operand_aliasing={{1}: (9, {})} | custom-call | tf_op jit(solution)/shard_map/active/pallas_call | solution.py:485
Async XLA Ops:
  0.6 12.9 %copy-start = (f32[3,192]{1,0:T(4,128)S(1)}, f32[3,192]{1,0:T(4,128)}, u32[]{:S(2)}) copy-start(f32[3,192]{1,0:T(4,128)} %bias.5) | copy-start | bytes 6916
  3.5 10.0 %collective-permute-start = (bf16[12,90,128]{2,1,0:T(8,128)(2,1)S(1)}, bf16[12,90,128]{2,1,0:T(8,128)(2,1)S(1)}, u32[]{:S(2)}, u32[]{:S(2)}) collective-permute-start(bf16[12,90,128]{2,1,0:T(8,128)(2,1)S(1)} %get-tuple-element.27), channel_id=1, source_target_pairs={{0,1},{1,2},{2,3},{3,4},{4,5},{5,6},{6,7},{7,8},{8,9},{9,10},{10,1... | collective-permute-start | bytes 829448 | tf_op jit(solution)/shard_map/ppermute | solution.py:385
  4.1 9.5 %collective-permute-start.1 = (bf16[12,90,128]{2,1,0:T(8,128)(2,1)S(1)}, bf16[12,90,128]{2,1,0:T(8,128)(2,1)S(1)}, u32[]{:S(2)}, u32[]{:S(2)}) collective-permute-start(bf16[12,90,128]{2,1,0:T(8,128)(2,1)S(1)} %get-tuple-element.28), channel_id=1, source_target_pairs={{1,0},{2,1},{3,2},{4,3},{5,4},{6,5},{7,6},{8,7},{9,8},{10,9},{11,1... | collective-permute-start | bytes 829448 | tf_op jit(solution)/shard_map/ppermute | solution.py:385
  9.1 10.3 %all-to-all-start = ((f32[16,2,192]{2,1,0:T(2,128)}), f32[16,2,192]{2,1,0:T(2,128)S(1)}, u32[]{:S(2)}, u32[]{:S(2)}) async-start(f32[16,2,192]{2,1,0:T(2,128)} %get-tuple-element.30), calls=%async_computation | async-start | bytes 65536 | tf_op jit(solution)/shard_map/all_to_all | solution.py:388
  13.6 5.8 %copy-start.1 = (f32[3,192]{1,0:T(4,128)S(1)}, f32[3,192]{1,0:T(4,128)}, u32[]{:S(2)}) copy-start(f32[3,192]{1,0:T(4,128)} %refs_4_.5) | copy-start | bytes 6916
  13.6 5.8 %copy-start.2 = (f32[3,192]{1,0:T(4,128)S(1)}, f32[3,192]{1,0:T(4,128)}, u32[]{:S(2)}) copy-start(f32[3,192]{1,0:T(4,128)} %refs_5_.5) | copy-start | bytes 6916
  24.2 15.0 %collective-permute-start.2 = (bf16[3,90,128]{2,1,0:T(8,128)(2,1)S(1)}, bf16[3,90,128]{2,1,0:T(8,128)(2,1)S(1)}, u32[]{:S(2)}, u32[]{:S(2)}) collective-permute-start(bf16[3,90,128]{2,1,0:T(8,128)(2,1)S(1)} %get-tuple-element.34), channel_id=1, source_target_pairs={{0,1},{1,2},{2,3},{3,4},{4,5},{5,6},{6,7},{7,8},{8,9},{9,10},{10,1... | collective-permute-start | bytes 207368 | tf_op jit(solution)/shard_map/ppermute | solution.py:385
  26.5 12.7 %collective-permute-start.3 = (bf16[3,90,128]{2,1,0:T(8,128)(2,1)S(1)}, bf16[3,90,128]{2,1,0:T(8,128)(2,1)S(1)}, u32[]{:S(2)}, u32[]{:S(2)}) collective-permute-start(bf16[3,90,128]{2,1,0:T(8,128)(2,1)S(1)} %get-tuple-element.35), channel_id=1, source_target_pairs={{1,0},{2,1},{3,2},{4,3},{5,4},{6,5},{7,6},{8,7},{9,8},{10,9},{11,1... | collective-permute-start | bytes 207368 | tf_op jit(solution)/shard_map/ppermute | solution.py:385
  28.7 10.5 %all-to-all-start.1 = ((f32[16,2,192]{2,1,0:T(2,128)}), f32[16,2,192]{2,1,0:T(2,128)S(1)}, u32[]{:S(2)}, u32[]{:S(2)}) async-start(f32[16,2,192]{2,1,0:T(2,128)} %get-tuple-element.36), calls=%async_computation.1 | async-start | bytes 65536 | tf_op jit(solution)/shard_map/all_to_all | solution.py:388
  44.0 15.2 %collective-permute-start.4 = (bf16[3,90,128]{2,1,0:T(8,128)(2,1)S(1)}, bf16[3,90,128]{2,1,0:T(8,128)(2,1)S(1)}, u32[]{:S(2)}, u32[]{:S(2)}) collective-permute-start(bf16[3,90,128]{2,1,0:T(8,128)(2,1)S(1)} %get-tuple-element.42), channel_id=1, source_target_pairs={{0,1},{1,2},{2,3},{3,4},{4,5},{5,6},{6,7},{7,8},{8,9},{9,10},{10,1... | collective-permute-start | bytes 207368 | tf_op jit(solution)/shard_map/ppermute | solution.py:385
  44.0 15.1 %collective-permute-start.5 = (bf16[3,90,128]{2,1,0:T(8,128)(2,1)S(1)}, bf16[3,90,128]{2,1,0:T(8,128)(2,1)S(1)}, u32[]{:S(2)}, u32[]{:S(2)}) collective-permute-start(bf16[3,90,128]{2,1,0:T(8,128)(2,1)S(1)} %get-tuple-element.43), channel_id=1, source_target_pairs={{1,0},{2,1},{3,2},{4,3},{5,4},{6,5},{7,6},{8,7},{9,8},{10,9},{11,1... | collective-permute-start | bytes 207368 | tf_op jit(solution)/shard_map/ppermute | solution.py:385
  48.5 10.6 %all-to-all-start.2 = ((f32[16,2,192]{2,1,0:T(2,128)}), f32[16,2,192]{2,1,0:T(2,128)S(1)}, u32[]{:S(2)}, u32[]{:S(2)}) async-start(f32[16,2,192]{2,1,0:T(2,128)} %get-tuple-element.44), calls=%async_computation.2 | async-start | bytes 65536 | tf_op jit(solution)/shard_map/all_to_all | solution.py:388

commit v11 on v10

--- a/solution.py
+++ b/solution.py
@@ -186,12 +186,14 @@
     sums[...] = jnp.broadcast_to(both[None], sums.shape)
 
 
-def cached_kernel(layer, chunk, far, distant, cache, before, after, weights, bias, *refs):
+def cached_kernel(layer, chunk, far, cache, before, after, weights, bias, *refs):
     bring = None
     if layer < 2:
         video, out, ordered, *refs = refs
         handed = [refs.pop(0) for _ in range(2 * layer)]
         near, *refs = refs
+        if layer == 1:
+            caches, cache, *refs = cache, *refs
         refs = [out, ordered, *refs]
         bring = pltpu.make_async_copy(video, near, refs[-1].at[4])
     passed = []
@@ -199,19 +201,13 @@
         later = pl.ds((layer + 2) * PLANES, handed[0].shape[0])
         for side, ref in enumerate((before, after)):
             passed.append(pltpu.make_async_copy(ref.at[later], handed[side], refs[-1].at[5 + side]))
-    if distant:
-        caches, out, ordered, cache, brims, *refs = cache, *refs
-        refs = [out, ordered, *refs]
-        here = pl.ds((layer - 2) * PLANES, PLANES)
-        for side, ref in enumerate((before, after)):
-            passed.append(pltpu.make_async_copy(ref.at[here], brims.at[side], refs[-1].at[5 + side]))
     out, ordered, edges, *slabs, weight, taps, sem = refs
     if far:
         away, out, *slabs = out, slabs[0], *slabs[1:]
     rows, cols, channels = cache.shape[-3:]
     places = rows * cols
     fetch = pltpu.make_async_copy(weights.at[layer], weight, sem.at[1])
-    if distant:
+    if layer == 1:
         begun = pltpu.make_async_copy(caches.at[layer], cache, sem.at[0])
         begun.start()
     fetch.start()
@@ -219,12 +215,7 @@
         bring.start()
     for copy in passed:
         copy.start()
-    origin = (layer + 1) * PLANES
-    if distant:
-        begun.wait()
-        for copy in passed:
-            copy.wait()
-        before, after, origin, passed = brims.at[0], brims.at[1], 0, []
+    origin = (layer + 1) * PLANES if layer < 2 else (layer - 2) * PLANES
     for side, ref in enumerate((before, after)):
         for plane in range(PLANES):
             edges[side, plane] = ref[origin + plane].astype(jnp.float32)
@@ -235,6 +226,8 @@
     def edge_of(h, plane):
         return [edges[side, plane, pl.ds(h, COLS, stride=0), :] for side in (0, 1)]
 
+    if layer == 1:
+        begun.wait()
     build_slabs(rows, row_of, edge_of, slabs)
     fetch.wait()
     if layer == 1:
@@ -420,22 +413,18 @@
         return [pltpu.VMEM((PLANES, places, LANES), jnp.float32)] if far else []
 
     def cached_part(layer, far, cache, brims):
-        distant = cache is None
-        own = [pltpu.VMEM(video_span.shape, jnp.bfloat16)] if distant or layer == 1 else []
-        if distant:
-            brims = [in_hbm(brim) for brim in brims]
-            own.append(pltpu.VMEM((2, PLANES, rows, LANES), jnp.bfloat16))
+        own = [pltpu.VMEM(video_span.shape, jnp.bfloat16)] * 2 if layer == 1 else []
         later = pltpu.HBM(((layers - 2) * PLANES, rows, LANES), jnp.bfloat16)
         more = {0: [block], 1: [later] * 2}.get(layer, [])
         planar = pltpu.HBM if far else jax.ShapeDtypeStruct
         return pl.pallas_call(
-            functools.partial(cached_kernel, layer, chunk, far, distant),
+            functools.partial(cached_kernel, layer, chunk, far),
             out_shape=[
                 planar((PLANES, places, LANES), jnp.float32),
                 pltpu.HBM((2, channels, tiles), weights.dtype),
             ]
             + more,
-            in_specs=[HBM if distant else VMEM] * 3 + [HBM, VMEM]
+            in_specs=[HBM if cache is None else VMEM, VMEM, VMEM, HBM, VMEM]
             + ([HBM] if layer < 2 else []),
             out_specs=[HBM if far else VMEM, HBM] + [HBM if layer else VMEM] * len(more),
             scratch_shapes=own + scratch(frames, rows, room(far))
@@ -446,14 +435,14 @@
             ],
             compiler_params=pltpu.CompilerParams(vmem_limit_bytes=24 << 20),
             name="cached",
-        )(caches if distant else cache, *brims, turned, biases, *([video] if layer < 2 else []))
+        )(caches if cache is None else cache, *brims, turned, biases, *([video] if layer < 2 else []))
 
     x = None
     carried = None
     for layer in range(layers):
         final = layer == layers - 1
         far = layer < layers - 1
-        bring = layer < layers - 2
+        bring = 0 < layer < layers - 1
         part, ordered, *more = cached_part(layer, far, cache, brims)
         if layer == 0:
             x = more[0]

time: 64.2 us -> 63.9 us (level)
  no operation moved by 1% of the time
where the time goes in v11:
time: 63.9 us; the launch traced here: 63.5 us
  Pallas kernels  34.6 us (54%)
  starting transfers between devices  25.7 us (40%)
  waiting for transfers between devices  2.24 us (4%)
  between operations  0.94 us (1%)
    pallas_call x3, Pallas kernels, cached_part(): pl.pallas_call(functools.partial(cached_kernel, layer, chunk, far), out_s...  17.5 us
    ppermute x6, starting transfers between devices, around(): return (lax.ppermute(last, 'lon', up), lax.ppermute(first, 'lon', down))  14.6 us
    pallas_call x3, Pallas kernels, local(): pl.pallas_call(functools.partial(active_kernel, layer, chunk, far, bring,...  14.2 us
    all_to_all x3, starting transfers between devices, gathered(): return lax.all_to_all(sums, 'lon', 0, 0)  11.1 us
    pallas_call x1, Pallas kernels, local(): pl.pallas_call(begin_kernel, out_shape=[spread, brim, brim, block], in_sp...  2.88 us
    all_to_all x3, waiting for transfers between devices, gathered(): return lax.all_to_all(sums, 'lon', 0, 0)  1.41 us
  transfers between devices with their start and end apart: 9, of which 3 were waited for; matrix products, arithmetic and copies ran while one was open for 0% of the time, Pallas kernels for 28%

profile of v11, /device:TPU:0, one launch (start us, length us, event | category | flops | bytes accessed | tf_op | source)
XLA Modules:
  0.0 63.5 jit_solution(1621641195018086063)
XLA Ops:
  0.6 0.0 copy-start.2
  0.6 2.9 %begin.1 = (f32[16,2,192]{2,1,0:T(2,128)}, bf16[12,90,128]{2,1,0:T(8,128)(2,1)S(1)}, bf16[12,90,128]{2,1,0:T(8,128)(2,1)S(1)}, bf16[2,90,8,192]{3,2,1,0:T(8,128)(2,1)S(1)}) custom-call(bf16[2,90,8,192]{3,2,1,0:T(8,128)(2,1)} %refs_0_.3, bf16[3,2,90,8,192]{4,3,2,1,0:T(8,128)(2,1)} %refs_10_.1, bf16[192,192]{1,0:T(8,128)(2,1)} %constant.2.clone.same.refs_8_), custom_call_target="tpu_custom_call" | custom-call | tf_op jit(solution)/shard_map/begin/pallas_call | solution.py:394
  3.5 0.5 collective-permute-start
  4.1 5.0 %collective-permute-start.1 = (bf16[12,90,128]{2,1,0:T(8,128)(2,1)S(1)}, bf16[12,90,128]{2,1,0:T(8,128)(2,1)S(1)}, u32[]{:S(2)}, u32[]{:S(2)}) collective-permute-start(bf16[12,90,128]{2,1,0:T(8,128)(2,1)S(1)} %get-tuple-element.28), channel_id=1, source_target_pairs={{1,0},{2,1},{3,2},{4,3},{5,4},{6,5},{7,6},{8,7},{9,8},{10,9},{11,1... | collective-permute-start | bytes 829448 | tf_op jit(solution)/shard_map/ppermute | solution.py:378
  9.1 3.6 %all-to-all-start = ((f32[16,2,192]{2,1,0:T(2,128)}), f32[16,2,192]{2,1,0:T(2,128)S(1)}, u32[]{:S(2)}, u32[]{:S(2)}) async-start(f32[16,2,192]{2,1,0:T(2,128)} %get-tuple-element.30), calls=%async_computation | async-start | bytes 65536 | tf_op jit(solution)/shard_map/all_to_all | solution.py:381
  12.7 0.8 %collective-permute-done.before.refs_1_ = bf16[12,90,128]{2,1,0:T(8,128)(2,1)S(1)} collective-permute-done((bf16[12,90,128]{2,1,0:T(8,128)(2,1)S(1)}, bf16[12,90,128]{2,1,0:T(8,128)(2,1)S(1)}, u32[]{:S(2)}, u32[]{:S(2)}) %collective-permute-start) | collective-permute-done | bytes 276512 | tf_op jit(solution)/shard_map/ppermute | solution.py:378
  13.6 0.0 collective-permute-done.1.after.refs_2_
  13.6 0.0 copy-done.2
  13.6 0.0 copy-start.3
  13.6 0.0 copy-start.4
  13.6 5.6 %cached.3 = (f32[3,720,128]{2,1,0:T(8,128)}, bf16[2,192,1792]{2,1,0:T(8,128)(2,1)}, bf16[2,90,8,192]{3,2,1,0:T(8,128)(2,1)S(1)}) custom-call(bf16[2,90,8,192]{3,2,1,0:T(8,128)(2,1)S(1)} %get-tuple-element.26.cache, bf16[12,90,128]{2,1,0:T(8,128)(2,1)S(1)} %collective-permute-done.before.refs_1_, ...), custom_call_target="tpu_custom_call" | custom-call | tf_op jit(solution)/shard_map/cached/pallas_call | solution.py:420
  19.2 0.2 all-to-all-done.refs_3_
  19.4 0.0 copy-done.3
  19.4 0.0 copy-done.4
  19.4 4.8 %active.3 = (f32[3,720,128]{2,1,0:T(8,128)S(1)}, bf16[3,2,90,8,192]{4,3,2,1,0:T(8,128)(2,1)}, f32[16,2,192]{2,1,0:T(2,128)}, bf16[3,90,128]{2,1,0:T(8,128)(2,1)S(1)}, bf16[3,90,128]{2,1,0:T(8,128)(2,1)S(1)}) custom-call(bf16[2,90,8,192]{3,2,1,0:T(8,128)(2,1)S(1)} %get-tuple-element.29.refs_0_, bf16[12,90,128]{2,1,0:T(8,128)(2,1)S(1)} %collective-permute-done.before.refs_1_, ...), custom_call_target="tpu_custom_call" | custom-call | tf_op jit(solution)/shard_map/active/pallas_call | solution.py:474
  24.2 2.3 %collective-permute-start.2 = (bf16[3,90,128]{2,1,0:T(8,128)(2,1)S(1)}, bf16[3,90,128]{2,1,0:T(8,128)(2,1)S(1)}, u32[]{:S(2)}, u32[]{:S(2)}) collective-permute-start(bf16[3,90,128]{2,1,0:T(8,128)(2,1)S(1)} %get-tuple-element.34), channel_id=1, source_target_pairs={{0,1},{1,2},{2,3},{3,4},{4,5},{5,6},{6,7},{7,8},{8,9},{9,10},{10,1... | collective-permute-start | bytes 207368 | tf_op jit(solution)/shard_map/ppermute | solution.py:378
  26.5 2.2 %collective-permute-start.3 = (bf16[3,90,128]{2,1,0:T(8,128)(2,1)S(1)}, bf16[3,90,128]{2,1,0:T(8,128)(2,1)S(1)}, u32[]{:S(2)}, u32[]{:S(2)}) collective-permute-start(bf16[3,90,128]{2,1,0:T(8,128)(2,1)S(1)} %get-tuple-element.35), channel_id=1, source_target_pairs={{1,0},{2,1},{3,2},{4,3},{5,4},{6,5},{7,6},{8,7},{9,8},{10,9},{11,1... | collective-permute-start | bytes 207368 | tf_op jit(solution)/shard_map/ppermute | solution.py:378
  28.7 3.8 %all-to-all-start.1 = ((f32[16,2,192]{2,1,0:T(2,128)}), f32[16,2,192]{2,1,0:T(2,128)S(1)}, u32[]{:S(2)}, u32[]{:S(2)}) async-start(f32[16,2,192]{2,1,0:T(2,128)} %get-tuple-element.36), calls=%async_computation.1 | async-start | bytes 65536 | tf_op jit(solution)/shard_map/all_to_all | solution.py:381
  32.5 6.7 %cached.4 = (f32[3,720,128]{2,1,0:T(8,128)}, bf16[2,192,1792]{2,1,0:T(8,128)(2,1)}, bf16[3,90,128]{2,1,0:T(8,128)(2,1)}, bf16[3,90,128]{2,1,0:T(8,128)(2,1)}) custom-call(bf16[3,2,90,8,192]{4,3,2,1,0:T(8,128)(2,1)} %refs_10_.1, bf16[12,90,128]{2,1,0:T(8,128)(2,1)S(1)} %collective-permute-done.before.refs_1_, ...), custom_call_target="tpu_custom_call" | custom-call | tf_op jit(solution)/shard_map/cached/pallas_call | solution.py:420
  39.3 0.0 all-to-all-done.1.refs_3_
  39.3 0.0 collective-permute-done.2.refs_1_
  39.3 0.0 collective-permute-done.3.refs_2_
  39.3 0.0 copy-start
  39.3 0.0 copy-start.1
  39.3 4.9 %active.4 = (f32[3,720,128]{2,1,0:T(8,128)S(1)}, bf16[3,2,90,8,192]{4,3,2,1,0:T(8,128)(2,1)}, f32[16,2,192]{2,1,0:T(2,128)}, bf16[3,90,128]{2,1,0:T(8,128)(2,1)S...) custom-call(f32[3,720,128]{2,1,0:T(8,128)S(1)} %get-tuple-element.33.re, ...), custom_call_target="tpu_custom_call", output_to_operand_aliasing={{1}: (9, {})} | custom-call | tf_op jit(solution)/shard_map/active/pallas_call | solution.py:474
  44.3 0.5 collective-permute-start.4
  44.7 4.0 %collective-permute-start.5 = (bf16[3,90,128]{2,1,0:T(8,128)(2,1)S(1)}, bf16[3,90,128]{2,1,0:T(8,128)(2,1)S(1)}, u32[]{:S(2)}, u32[]{:S(2)}) collective-permute-start(bf16[3,90,128]{2,1,0:T(8,128)(2,1)S(1)} %get-tuple-element.42), channel_id=1, source_target_pairs={{1,0},{2,1},{3,2},{4,3},{5,4},{6,5},{7,6},{8,7},{9,8},{10,9},{11,1... | collective-permute-start | bytes 207368 | tf_op jit(solution)/shard_map/ppermute | solution.py:378
  48.7 3.7 %all-to-all-start.2 = ((f32[16,2,192]{2,1,0:T(2,128)}), f32[16,2,192]{2,1,0:T(2,128)S(1)}, u32[]{:S(2)}, u32[]{:S(2)}) async-start(f32[16,2,192]{2,1,0:T(2,128)} %get-tuple-element.43), calls=%async_computation.2 | async-start | bytes 65536 | tf_op jit(solution)/shard_map/all_to_all | solution.py:381
  52.4 0.0 copy-done
  52.4 0.0 copy-done.1
  52.4 5.2 %cached.5 = (f32[3,720,128]{2,1,0:T(8,128)S(1)}, bf16[2,192,1792]{2,1,0:T(8,128)(2,1)}) custom-call(bf16[2,90,8,192]{3,2,1,0:T(8,128)(2,1)S(1)} %get-tuple-element.44.cache, bf16[3,90,128]{2,1,0:T(8,128)(2,1)S(1)} %copy-done, bf16[3,90,128]{2,1,0:T(8,128)(2,1)S(1)} %copy-done.1, bf16[3,192,5184]{2,1,0:T(8,128)(2,1)} %bitcast.3, f32[3,192]{1,0:T(4,128)S(1)} %copy-done.2), custom_call_target="tpu_custom_call" | custom-call | tf_op jit(solution)/shard_map/cached/pallas_call | solution.py:420
  57.6 1.2 %all-to-all-done.2.refs_3_ = f32[16,2,192]{2,1,0:T(2,128)S(1)} async-done(((f32[16,2,192]{2,1,0:T(2,128)}), f32[16,2,192]{2,1,0:T(2,128)S(1)}, u32[]{:S(2)}, u32[]{:S(2)}) %all-to-all-start.2) | async-done | bytes 24608 | tf_op jit(solution)/shard_map/all_to_all | solution.py:381
  58.8 0.0 collective-permute-done.4.refs_1_
  58.8 0.0 collective-permute-done.5.refs_2_
  58.8 4.5 %active.5 = (bf16[2,90,8,192]{3,2,1,0:T(8,128)(2,1)}, bf16[3,2,90,8,192]{4,3,2,1,0:T(8,128)(2,1)}) custom-call(f32[3,720,128]{2,1,0:T(8,128)S(1)} %get-tuple-element.40.refs_0_, bf16[3,90,128]{2,1,0:T(8,128)(2,1)S(1)} %collective-permute-done.4.refs_1_, bf16[3,90,128]{2,1,0:T(8,128)(2,1)S(1)} %collective-permute-done.5.refs_2_, ...), custom_call_target="tpu_custom_call", output_to_operand_aliasing={{1}: (9, {})} | custom-call | tf_op jit(solution)/shard_map/active/pallas_call | solution.py:474
Async XLA Ops:
  0.6 12.9 %copy-start.2 = (f32[3,192]{1,0:T(4,128)S(1)}, f32[3,192]{1,0:T(4,128)}, u32[]{:S(2)}) copy-start(f32[3,192]{1,0:T(4,128)} %bias.5) | copy-start | bytes 6916
  3.5 10.0 %collective-permute-start = (bf16[12,90,128]{2,1,0:T(8,128)(2,1)S(1)}, bf16[12,90,128]{2,1,0:T(8,128)(2,1)S(1)}, u32[]{:S(2)}, u32[]{:S(2)}) collective-permute-start(bf16[12,90,128]{2,1,0:T(8,128)(2,1)S(1)} %get-tuple-element.27), channel_id=1, source_target_pairs={{0,1},{1,2},{2,3},{3,4},{4,5},{5,6},{6,7},{7,8},{8,9},{9,10},{10,1... | collective-permute-start | bytes 829448 | tf_op jit(solution)/shard_map/ppermute | solution.py:378
  4.1 9.5 %collective-permute-start.1 = (bf16[12,90,128]{2,1,0:T(8,128)(2,1)S(1)}, bf16[12,90,128]{2,1,0:T(8,128)(2,1)S(1)}, u32[]{:S(2)}, u32[]{:S(2)}) collective-permute-start(bf16[12,90,128]{2,1,0:T(8,128)(2,1)S(1)} %get-tuple-element.28), channel_id=1, source_target_pairs={{1,0},{2,1},{3,2},{4,3},{5,4},{6,5},{7,6},{8,7},{9,8},{10,9},{11,1... | collective-permute-start | bytes 829448 | tf_op jit(solution)/shard_map/ppermute | solution.py:378
  9.1 10.3 %all-to-all-start = ((f32[16,2,192]{2,1,0:T(2,128)}), f32[16,2,192]{2,1,0:T(2,128)S(1)}, u32[]{:S(2)}, u32[]{:S(2)}) async-start(f32[16,2,192]{2,1,0:T(2,128)} %get-tuple-element.30), calls=%async_computation | async-start | bytes 65536 | tf_op jit(solution)/shard_map/all_to_all | solution.py:381
  13.6 5.8 %copy-start.3 = (f32[3,192]{1,0:T(4,128)S(1)}, f32[3,192]{1,0:T(4,128)}, u32[]{:S(2)}) copy-start(f32[3,192]{1,0:T(4,128)} %refs_4_.5) | copy-start | bytes 6916
  13.6 5.8 %copy-start.4 = (f32[3,192]{1,0:T(4,128)S(1)}, f32[3,192]{1,0:T(4,128)}, u32[]{:S(2)}) copy-start(f32[3,192]{1,0:T(4,128)} %refs_5_.5) | copy-start | bytes 6916
  24.2 15.1 %collective-permute-start.2 = (bf16[3,90,128]{2,1,0:T(8,128)(2,1)S(1)}, bf16[3,90,128]{2,1,0:T(8,128)(2,1)S(1)}, u32[]{:S(2)}, u32[]{:S(2)}) collective-permute-start(bf16[3,90,128]{2,1,0:T(8,128)(2,1)S(1)} %get-tuple-element.34), channel_id=1, source_target_pairs={{0,1},{1,2},{2,3},{3,4},{4,5},{5,6},{6,7},{7,8},{8,9},{9,10},{10,1... | collective-permute-start | bytes 207368 | tf_op jit(solution)/shard_map/ppermute | solution.py:378
  26.5 12.8 %collective-permute-start.3 = (bf16[3,90,128]{2,1,0:T(8,128)(2,1)S(1)}, bf16[3,90,128]{2,1,0:T(8,128)(2,1)S(1)}, u32[]{:S(2)}, u32[]{:S(2)}) collective-permute-start(bf16[3,90,128]{2,1,0:T(8,128)(2,1)S(1)} %get-tuple-element.35), channel_id=1, source_target_pairs={{1,0},{2,1},{3,2},{4,3},{5,4},{6,5},{7,6},{8,7},{9,8},{10,9},{11,1... | collective-permute-start | bytes 207368 | tf_op jit(solution)/shard_map/ppermute | solution.py:378
  28.7 10.6 %all-to-all-start.1 = ((f32[16,2,192]{2,1,0:T(2,128)}), f32[16,2,192]{2,1,0:T(2,128)S(1)}, u32[]{:S(2)}, u32[]{:S(2)}) async-start(f32[16,2,192]{2,1,0:T(2,128)} %get-tuple-element.36), calls=%async_computation.1 | async-start | bytes 65536 | tf_op jit(solution)/shard_map/all_to_all | solution.py:381
  39.3 13.1 %copy-start = (bf16[3,90,128]{2,1,0:T(8,128)(2,1)S(1)}, bf16[3,90,128]{2,1,0:T(8,128)(2,1)}, u32[]{:S(2)}) copy-start(bf16[3,90,128]{2,1,0:T(8,128)(2,1)} %get-tuple-element.45.before) | copy-start | bytes 207364
  39.3 13.1 %copy-start.1 = (bf16[3,90,128]{2,1,0:T(8,128)(2,1)S(1)}, bf16[3,90,128]{2,1,0:T(8,128)(2,1)}, u32[]{:S(2)}) copy-start(bf16[3,90,128]{2,1,0:T(8,128)(2,1)} %get-tuple-element.46.after) | copy-start | bytes 207364
  44.3 14.6 %collective-permute-start.4 = (bf16[3,90,128]{2,1,0:T(8,128)(2,1)S(1)}, bf16[3,90,128]{2,1,0:T(8,128)(2,1)S(1)}, u32[]{:S(2)}, u32[]{:S(2)}) collective-permute-start(bf16[3,90,128]{2,1,0:T(8,128)(2,1)S(1)} %get-tuple-element.41), channel_id=1, source_target_pairs={{0,1},{1,2},{2,3},{3,4},{4,5},{5,6},{6,7},{7,8},{8,9},{9,10},{10,1... | collective-permute-start | bytes 207368 | tf_op jit(solution)/shard_map/ppermute | solution.py:378
  44.7 14.1 %collective-permute-start.5 = (bf16[3,90,128]{2,1,0:T(8,128)(2,1)S(1)}, bf16[3,90,128]{2,1,0:T(8,128)(2,1)S(1)}, u32[]{:S(2)}, u32[]{:S(2)}) collective-permute-start(bf16[3,90,128]{2,1,0:T(8,128)(2,1)S(1)} %get-tuple-element.42), channel_id=1, source_target_pairs={{1,0},{2,1},{3,2},{4,3},{5,4},{6,5},{7,6},{8,7},{9,8},{10,9},{11,1... | collective-permute-start | bytes 207368 | tf_op jit(solution)/shard_map/ppermute | solution.py:378
  48.7 10.1 %all-to-all-start.2 = ((f32[16,2,192]{2,1,0:T(2,128)}), f32[16,2,192]{2,1,0:T(2,128)S(1)}, u32[]{:S(2)}, u32[]{:S(2)}) async-start(f32[16,2,192]{2,1,0:T(2,128)} %get-tuple-element.43), calls=%async_computation.2 | async-start | bytes 65536 | tf_op jit(solution)/shard_map/all_to_all | solution.py:381

commit v12 on v11

--- a/solution.py
+++ b/solution.py
@@ -154,7 +154,7 @@
     return sums[0:2] + sums[2:4] + sums[4:6]
 
 
-def begin_kernel(video, caches, same, sums, first, last, near, wide, held, alike, sem):
+def begin_kernel(video, caches, same, sums, first, last, near, state, wide, held, alike, sem):
     layers, frames, rows, cols, channels = caches.shape
     copies = [pltpu.make_async_copy(video, held.at[0], sem.at[0])]
     for layer in range(layers):
@@ -168,6 +168,7 @@
     square = list(total)
     for group, copy in enumerate(copies):
         copy.wait()
+        target = wide if group else state
         for frame in range(frames):
             value = (near[frame] if group == 1 else held[group, frame]).astype(jnp.float32)
             parts = halves(value)
@@ -175,11 +176,11 @@
                 for i in range(2):
                     total[i] = total[i] + jnp.sum(parts[i], axis=0)
                     square[i] = square[i] + jnp.sum(parts[i] * parts[i], axis=0)
-            wide[frame] = parts[0].reshape(places, LANES)
-            wide[2, :, HALF * frame : HALF * (frame + 1)] = parts[1].reshape(places, half)
+            target[frame] = parts[0].reshape(places, LANES)
+            target[2, :, HALF * frame : HALF * (frame + 1)] = parts[1].reshape(places, half)
         for out, column in ((first, 0), (last, cols - 1)):
             for plane in range(PLANES):
-                edge = wide[plane, pl.ds(column, rows, stride=cols), :]
+                edge = target[plane, pl.ds(column, rows, stride=cols), :]
                 out[group * PLANES + plane] = edge.astype(jnp.bfloat16)
     fetch.wait()
     both = group_sums([jnp.concatenate(v, axis=1) for v in (total, square)], alike[...])
@@ -188,15 +189,15 @@
 
 def cached_kernel(layer, chunk, far, cache, before, after, weights, bias, *refs):
     bring = None
-    if layer < 2:
-        video, out, ordered, *refs = refs
-        handed = [refs.pop(0) for _ in range(2 * layer)]
-        near, *refs = refs
-        if layer == 1:
-            caches, cache, *refs = cache, *refs
+    if layer == 1:
+        video, out, ordered, *handed = refs[:5]
+        near, *refs = refs[5:]
+        caches, cache, *refs = cache, *refs
         refs = [out, ordered, *refs]
         bring = pltpu.make_async_copy(video, near, refs[-1].at[4])
-    passed = []
+    passed, middle = [], None
+    if layer > 1:
+        middle, *refs = refs
     if layer == 1:
         later = pl.ds((layer + 2) * PLANES, handed[0].shape[0])
         for side, ref in enumerate((before, after)):
@@ -243,6 +244,8 @@
         value = value + constant
         if layer == 1:
             value = value + near[t].astype(jnp.float32).reshape(places, channels)
+        elif middle is not None:
+            value = value + get_planes(middle, t, pl.ds(0, places))
         put_planes(out, t, pl.ds(0, places), value)
 
     finish(1, product([(slabs[1], tables[0])], 0, places))
@@ -253,8 +256,6 @@
         leave.wait()
     for copy in [store] + passed:
         copy.wait()
-    if layer == 0:
-        bring.wait()
 
 
 def active_kernel(layer, chunk, far, bring, entries, final, *refs):
@@ -304,10 +305,8 @@
             edges[side, plane] = value
 
     def row_of(h):
-        if layer:
-            start = h * COLS if isinstance(h, int) else pl.multiple_of(h * COLS, COLS)
-            return act([x[plane, pl.ds(start, COLS), :] for plane in range(PLANES)])
-        return act(planes(*(x[frame, h].astype(jnp.float32) for frame in range(2))))
+        start = h * COLS if isinstance(h, int) else pl.multiple_of(h * COLS, COLS)
+        return act([x[plane, pl.ds(start, COLS), :] for plane in range(PLANES)])
 
     def edge_of(h, plane):
         return [edges[side, plane, pl.ds(h, COLS, stride=0), :] for side in (0, 1)]
@@ -331,7 +330,6 @@
         shape = (size // COLS, COLS, channels)
         value = value + get_planes(part, t, here)
         if final:
-            value = value + get_planes(x, t, here)
             y[t, span] = value.reshape(shape).astype(jnp.bfloat16)
             return moments
         put_planes(y, t, here, value)
@@ -391,11 +389,12 @@
     spread = jax.ShapeDtypeStruct((peers, 2, channels), jnp.float32)
     brim = jax.ShapeDtypeStruct(((layers + 1) * PLANES, rows, LANES), jnp.bfloat16)
     block = jax.ShapeDtypeStruct(video_span.shape, video_span.dtype)
-    sums, first, last, cache = pl.pallas_call(
+    planar = jax.ShapeDtypeStruct((PLANES, places, LANES), jnp.float32)
+    sums, first, last, cache, x = pl.pallas_call(
         begin_kernel,
-        out_shape=[spread, brim, brim, block],
+        out_shape=[spread, brim, brim, block, planar],
         in_specs=[HBM] * 3,
-        out_specs=[VMEM] * 4,
+        out_specs=[VMEM] * 5,
         scratch_shapes=[
             pltpu.VMEM((PLANES, places, LANES), jnp.float32),
             pltpu.VMEM((layers + 1,) + video_span.shape, jnp.bfloat16),
@@ -412,10 +411,11 @@
     def room(far):
         return [pltpu.VMEM((PLANES, places, LANES), jnp.float32)] if far else []
 
-    def cached_part(layer, far, cache, brims):
+    def cached_part(layer, far, cache, brims, x):
         own = [pltpu.VMEM(video_span.shape, jnp.bfloat16)] * 2 if layer == 1 else []
         later = pltpu.HBM(((layers - 2) * PLANES, rows, LANES), jnp.bfloat16)
-        more = {0: [block], 1: [later] * 2}.get(layer, [])
+        more = [later] * 2 if layer == 1 else []
+        extra = {0: [], 1: [video]}.get(layer, [x])
         planar = pltpu.HBM if far else jax.ShapeDtypeStruct
         return pl.pallas_call(
             functools.partial(cached_kernel, layer, chunk, far),
@@ -425,8 +425,8 @@
             ]
             + more,
             in_specs=[HBM if cache is None else VMEM, VMEM, VMEM, HBM, VMEM]
-            + ([HBM] if layer < 2 else []),
-            out_specs=[HBM if far else VMEM, HBM] + [HBM if layer else VMEM] * len(more),
+            + [HBM if layer < 2 else VMEM] * len(extra),
+            out_specs=[HBM if far else VMEM, HBM] + [HBM] * len(more),
             scratch_shapes=own + scratch(frames, rows, room(far))
             + [
                 pltpu.VMEM((channels, weights.shape[1]), weights.dtype),
@@ -435,18 +435,15 @@
             ],
             compiler_params=pltpu.CompilerParams(vmem_limit_bytes=24 << 20),
             name="cached",
-        )(caches if cache is None else cache, *brims, turned, biases, *([video] if layer < 2 else []))
-
-    x = None
+        )(caches if cache is None else cache, *brims, turned, biases, *extra)
+
     carried = None
     for layer in range(layers):
         final = layer == layers - 1
         far = layer < layers - 1
         bring = 0 < layer < layers - 1
-        part, ordered, *more = cached_part(layer, far, cache, brims)
-        if layer == 0:
-            x = more[0]
-        elif more:
+        part, ordered, *more = cached_part(layer, far, cache, brims, x)
+        if more:
             brims = more
         if far:
             part = in_hbm(part)

time: 63.9 us -> 64.6 us (1.011)
  local copies, waits for them, and re-layouts: 0.02 us -> 1.78 us
  waiting for transfers between devices: 2.24 us -> 1.05 us
    unnamed x10, local copies, waits for them, and re-layouts: 0.02 us -> 1.78 us
    all_to_all x3, waiting for transfers between devices: 1.41 us -> 0.22 us  [gathered(): return lax.all_to_all(sums, 'lon', 0, 0)]
  transfers between devices with their start and end apart: 9 -> 9, of which waited for: 3 -> 2; matrix products, arithmetic and copies ran while one was open for 0% -> 0% of each run, Pallas kernels for 28% -> 27%
where the time goes in v12:
time: 64.6 us; the launch traced here: 64.1 us
  Pallas kernels  34.7 us (54%)
  starting transfers between devices  25.7 us (40%)
  local copies, waits for them, and re-layouts  1.78 us (3%)
  waiting for transfers between devices  1.05 us (2%)
  between operations  0.94 us (1%)
    pallas_call x3, Pallas kernels, cached_part(): pl.pallas_call(functools.partial(cached_kernel, layer, chunk, far), out_s...  17.5 us
    ppermute x6, starting transfers between devices, around(): return (lax.ppermute(last, 'lon', up), lax.ppermute(first, 'lon', down))  14.6 us
    pallas_call x3, Pallas kernels, local(): pl.pallas_call(functools.partial(active_kernel, layer, chunk, far, bring,...  14.2 us
    all_to_all x3, starting transfers between devices, gathered(): return lax.all_to_all(sums, 'lon', 0, 0)  11.1 us
    pallas_call x1, Pallas kernels, local(): pl.pallas_call(begin_kernel, out_shape=[spread, brim, brim, block, planar...  2.88 us
    unnamed x10, local copies, waits for them, and re-layouts  1.78 us
  transfers between devices with their start and end apart: 9, of which 2 were waited for; matrix products, arithmetic and copies ran while one was open for 0% of the time, Pallas kernels for 27%

profile of v12, /device:TPU:0, one launch (start us, length us, event | category | flops | bytes accessed | tf_op | source)
XLA Modules:
  0.0 64.1 jit_solution(15807849261012317440)
XLA Ops:
  0.6 0.0 copy-start.2
  0.6 2.9 %begin.1 = (f32[16,2,192]{2,1,0:T(2,128)}, bf16[12,90,128]{2,1,0:T(8,128)(2,1)S(1)}, bf16[12,90,128]{2,1,0:T(8,128)(2,1)S(1)}, bf16[2,90,8,192]{3,2,1,0:T(8,128)(2,1)S(1)}, f32[3,720,128]{2,1,0:T(8,128)S(1)}) custom-call(bf16[2,90,8,192]{3,2,1,0:T(8,128)(2,1)} %refs_0_.1, bf16[3,2,90,8,192]{4,3,2,1,0:T(8,128)(2,1)} %refs_10_.1, ...), custom_call_target="tpu_custom_call" | custom-call | tf_op jit(solution)/shard_map/begin/pallas_call | solution.py:393
  3.5 0.5 collective-permute-start
  4.1 5.0 %collective-permute-start.1 = (bf16[12,90,128]{2,1,0:T(8,128)(2,1)S(1)}, bf16[12,90,128]{2,1,0:T(8,128)(2,1)S(1)}, u32[]{:S(2)}, u32[]{:S(2)}) collective-permute-start(bf16[12,90,128]{2,1,0:T(8,128)(2,1)S(1)} %get-tuple-element.28), channel_id=1, source_target_pairs={{1,0},{2,1},{3,2},{4,3},{5,4},{6,5},{7,6},{8,7},{9,8},{10,9},{11,1... | collective-permute-start | bytes 829448 | tf_op jit(solution)/shard_map/ppermute | solution.py:376
  9.1 3.6 %all-to-all-start = ((f32[16,2,192]{2,1,0:T(2,128)}), f32[16,2,192]{2,1,0:T(2,128)S(1)}, u32[]{:S(2)}, u32[]{:S(2)}) async-start(f32[16,2,192]{2,1,0:T(2,128)} %get-tuple-element.29), calls=%async_computation | async-start | bytes 65536 | tf_op jit(solution)/shard_map/all_to_all | solution.py:379
  12.7 0.8 %collective-permute-done.before.refs_1_ = bf16[12,90,128]{2,1,0:T(8,128)(2,1)S(1)} collective-permute-done((bf16[12,90,128]{2,1,0:T(8,128)(2,1)S(1)}, bf16[12,90,128]{2,1,0:T(8,128)(2,1)S(1)}, u32[]{:S(2)}, u32[]{:S(2)}) %collective-permute-start) | collective-permute-done | bytes 276512 | tf_op jit(solution)/shard_map/ppermute | solution.py:376
  13.6 0.0 collective-permute-done.1.after.refs_2_
  13.6 0.0 copy-done.2
  13.6 0.0 copy-start.3
  13.6 0.0 copy-start.4
  13.6 5.6 %cached.3 = (f32[3,720,128]{2,1,0:T(8,128)}, bf16[2,192,1792]{2,1,0:T(8,128)(2,1)}) custom-call(bf16[2,90,8,192]{3,2,1,0:T(8,128)(2,1)S(1)} %get-tuple-element.30.cache, bf16[12,90,128]{2,1,0:T(8,128)(2,1)S(1)} %collective-permute-done.before.refs_1_, bf16[12,90,128]{2,1,0:T(8,128)(2,1)S(1)} %collective-permute-done.1.after.refs_2_, ...), custom_call_target="tpu_custom_call" | custom-call | tf_op jit(solution)/shard_map/cached/pallas_call | solution.py:420
  19.2 0.2 all-to-all-done.refs_3_
  19.4 0.0 copy-done.3
  19.4 0.0 copy-done.4
  19.4 4.8 %active.3 = (f32[3,720,128]{2,1,0:T(8,128)S(1)}, bf16[3,2,90,8,192]{4,3,2,1,0:T(8,128)(2,1)}, f32[16,2,192]{2,1,0:T(2,128)}, bf16[3,90,128]{2,1,0:T(8,128)(2,1)S(1)}, bf16[3,90,128]{2,1,0:T(8,128)(2,1)S(1)}) custom-call(f32[3,720,128]{2,1,0:T(8,128)S(1)} %get-tuple-element.26.refs_0_, bf16[12,90,128]{2,1,0:T(8,128)(2,1)S(1)} %collective-permute-done.before.refs_1_, ...), custom_call_target="tpu_custom_call" | custom-call | tf_op jit(solution)/shard_map/active/pallas_call | solution.py:471
  24.2 2.3 %collective-permute-start.2 = (bf16[3,90,128]{2,1,0:T(8,128)(2,1)S(1)}, bf16[3,90,128]{2,1,0:T(8,128)(2,1)S(1)}, u32[]{:S(2)}, u32[]{:S(2)}) collective-permute-start(bf16[3,90,128]{2,1,0:T(8,128)(2,1)S(1)} %get-tuple-element.34), channel_id=1, source_target_pairs={{0,1},{1,2},{2,3},{3,4},{4,5},{5,6},{6,7},{7,8},{8,9},{9,10},{10,1... | collective-permute-start | bytes 207368 | tf_op jit(solution)/shard_map/ppermute | solution.py:376
  26.5 2.2 %collective-permute-start.3 = (bf16[3,90,128]{2,1,0:T(8,128)(2,1)S(1)}, bf16[3,90,128]{2,1,0:T(8,128)(2,1)S(1)}, u32[]{:S(2)}, u32[]{:S(2)}) collective-permute-start(bf16[3,90,128]{2,1,0:T(8,128)(2,1)S(1)} %get-tuple-element.35), channel_id=1, source_target_pairs={{1,0},{2,1},{3,2},{4,3},{5,4},{6,5},{7,6},{8,7},{9,8},{10,9},{11,1... | collective-permute-start | bytes 207368 | tf_op jit(solution)/shard_map/ppermute | solution.py:376
  28.7 3.9 %all-to-all-start.1 = ((f32[16,2,192]{2,1,0:T(2,128)}), f32[16,2,192]{2,1,0:T(2,128)S(1)}, u32[]{:S(2)}, u32[]{:S(2)}) async-start(f32[16,2,192]{2,1,0:T(2,128)} %get-tuple-element.36), calls=%async_computation.1 | async-start | bytes 65536 | tf_op jit(solution)/shard_map/all_to_all | solution.py:379
  32.5 6.8 %cached.4 = (f32[3,720,128]{2,1,0:T(8,128)}, bf16[2,192,1792]{2,1,0:T(8,128)(2,1)}, bf16[3,90,128]{2,1,0:T(8,128)(2,1)}, bf16[3,90,128]{2,1,0:T(8,128)(2,1)}) custom-call(bf16[3,2,90,8,192]{4,3,2,1,0:T(8,128)(2,1)} %refs_10_.1, bf16[12,90,128]{2,1,0:T(8,128)(2,1)S(1)} %collective-permute-done.before.refs_1_, ...), custom_call_target="tpu_custom_call" | custom-call | tf_op jit(solution)/shard_map/cached/pallas_call | solution.py:420
  39.3 0.0 all-to-all-done.1.refs_3_
  39.3 0.0 collective-permute-done.2.refs_1_
  39.3 0.0 collective-permute-done.3.refs_2_
  39.3 5.0 %active.4 = (f32[3,720,128]{2,1,0:T(8,128)S(1)}, bf16[3,2,90,8,192]{4,3,2,1,0:T(8,128)(2,1)}, f32[16,2,192]{2,1,0:T(2,128)}, bf16[3,90,128]{2,1,0:T(8,128)(2,1)}...) custom-call(f32[3,720,128]{2,1,0:T(8,128)S(1)} %get-tuple-element.33.refs_0_, ...), custom_call_target="tpu_custom_call", output_to_operand_aliasing={{1}: (9, {})} | custom-call | tf_op jit(solution)/shard_map/active/pallas_call | solution.py:471
  44.3 0.5 collective-permute-start.4
  44.8 4.0 %collective-permute-start.5 = (bf16[3,90,128]{2,1,0:T(8,128)(2,1)}, bf16[3,90,128]{2,1,0:T(8,128)(2,1)S(1)}, u32[]{:S(2)}, u32[]{:S(2)}) collective-permute-start(bf16[3,90,128]{2,1,0:T(8,128)(2,1)} %get-tuple-element.42), channel_id=1, source_target_pairs={{1,0},{2,1},{3,2},{4,3},{5,4},{6,5},{7,6},{8,7},{9,8},{10,9},{11,1... | collective-permute-start | bytes 207368 | tf_op jit(solution)/shard_map/ppermute | solution.py:376
  48.8 3.7 %all-to-all-start.2 = ((f32[16,2,192]{2,1,0:T(2,128)}), f32[16,2,192]{2,1,0:T(2,128)S(1)}, u32[]{:S(2)}, u32[]{:S(2)}) async-start(f32[16,2,192]{2,1,0:T(2,128)} %get-tuple-element.43), calls=%async_computation.2 | async-start | bytes 65536 | tf_op jit(solution)/shard_map/all_to_all | solution.py:379
  52.5 0.0 copy-start
  52.5 0.9 %copy-done = bf16[3,90,128]{2,1,0:T(8,128)(2,1)S(1)} copy-done((bf16[3,90,128]{2,1,0:T(8,128)(2,1)S(1)}, bf16[3,90,128]{2,1,0:T(8,128)(2,1)}, u32[]{:S(2)}) %copy-start) | copy-done | bytes 69144
  53.4 0.0 copy-start.1
  53.4 0.9 %copy-done.1 = bf16[3,90,128]{2,1,0:T(8,128)(2,1)S(1)} copy-done((bf16[3,90,128]{2,1,0:T(8,128)(2,1)S(1)}, bf16[3,90,128]{2,1,0:T(8,128)(2,1)}, u32[]{:S(2)}) %copy-start.1) | copy-done | bytes 69144
  54.3 5.2 %cached.5 = (f32[3,720,128]{2,1,0:T(8,128)S(1)}, bf16[2,192,1792]{2,1,0:T(8,128)(2,1)}) custom-call(bf16[2,90,8,192]{3,2,1,0:T(8,128)(2,1)S(1)} %get-tuple-element.44.cache, bf16[3,90,128]{2,1,0:T(8,128)(2,1)S(1)} %copy-done, bf16[3,90,128]{2,1,0:T(8,128)(2,1)S(1)} %copy-done.1, bf16[3,192,5184]{2,1,0:T(8,128)(2,1)} %bitcast.3, f32[3,192]{1,0:T(4,128)S(1)} %copy-done.2, ...), custom_call_target="tpu_custom_call" | custom-call | tf_op jit(solution)/shard_map/cached/pallas_call | solution.py:420
  59.5 0.0 all-to-all-done.2.refs_3_
  59.5 0.0 collective-permute-done.4.refs_1_
  59.5 0.0 collective-permute-done.5.refs_2_
  59.5 4.5 %active.5 = (bf16[2,90,8,192]{3,2,1,0:T(8,128)(2,1)}, bf16[3,2,90,8,192]{4,3,2,1,0:T(8,128)(2,1)}) custom-call(f32[3,720,128]{2,1,0:T(8,128)S(1)} %get-tuple-element.40.refs_0_, bf16[3,90,128]{2,1,0:T(8,128)(2,1)S(1)} %collective-permute-done.4.refs_1_, bf16[3,90,128]{2,1,0:T(8,128)(2,1)S(1)} %collective-permute-done.5.refs_2_, ...), custom_call_target="tpu_custom_call", output_to_operand_aliasing={{1}: (9, {})} | custom-call | tf_op jit(solution)/shard_map/active/pallas_call | solution.py:471
Async XLA Ops:
  0.6 12.9 %copy-start.2 = (f32[3,192]{1,0:T(4,128)S(1)}, f32[3,192]{1,0:T(4,128)}, u32[]{:S(2)}) copy-start(f32[3,192]{1,0:T(4,128)} %bias.5) | copy-start | bytes 6916
  3.5 10.0 %collective-permute-start = (bf16[12,90,128]{2,1,0:T(8,128)(2,1)S(1)}, bf16[12,90,128]{2,1,0:T(8,128)(2,1)S(1)}, u32[]{:S(2)}, u32[]{:S(2)}) collective-permute-start(bf16[12,90,128]{2,1,0:T(8,128)(2,1)S(1)} %get-tuple-element.27), channel_id=1, source_target_pairs={{0,1},{1,2},{2,3},{3,4},{4,5},{5,6},{6,7},{7,8},{8,9},{9,10},{10,1... | collective-permute-start | bytes 829448 | tf_op jit(solution)/shard_map/ppermute | solution.py:376
  4.1 9.5 %collective-permute-start.1 = (bf16[12,90,128]{2,1,0:T(8,128)(2,1)S(1)}, bf16[12,90,128]{2,1,0:T(8,128)(2,1)S(1)}, u32[]{:S(2)}, u32[]{:S(2)}) collective-permute-start(bf16[12,90,128]{2,1,0:T(8,128)(2,1)S(1)} %get-tuple-element.28), channel_id=1, source_target_pairs={{1,0},{2,1},{3,2},{4,3},{5,4},{6,5},{7,6},{8,7},{9,8},{10,9},{11,1... | collective-permute-start | bytes 829448 | tf_op jit(solution)/shard_map/ppermute | solution.py:376
  9.1 10.3 %all-to-all-start = ((f32[16,2,192]{2,1,0:T(2,128)}), f32[16,2,192]{2,1,0:T(2,128)S(1)}, u32[]{:S(2)}, u32[]{:S(2)}) async-start(f32[16,2,192]{2,1,0:T(2,128)} %get-tuple-element.29), calls=%async_computation | async-start | bytes 65536 | tf_op jit(solution)/shard_map/all_to_all | solution.py:379
  13.6 5.8 %copy-start.3 = (f32[3,192]{1,0:T(4,128)S(1)}, f32[3,192]{1,0:T(4,128)}, u32[]{:S(2)}) copy-start(f32[3,192]{1,0:T(4,128)} %refs_4_.5) | copy-start | bytes 6916
  13.6 5.8 %copy-start.4 = (f32[3,192]{1,0:T(4,128)S(1)}, f32[3,192]{1,0:T(4,128)}, u32[]{:S(2)}) copy-start(f32[3,192]{1,0:T(4,128)} %refs_5_.5) | copy-start | bytes 6916
  24.2 15.1 %collective-permute-start.2 = (bf16[3,90,128]{2,1,0:T(8,128)(2,1)S(1)}, bf16[3,90,128]{2,1,0:T(8,128)(2,1)S(1)}, u32[]{:S(2)}, u32[]{:S(2)}) collective-permute-start(bf16[3,90,128]{2,1,0:T(8,128)(2,1)S(1)} %get-tuple-element.34), channel_id=1, source_target_pairs={{0,1},{1,2},{2,3},{3,4},{4,5},{5,6},{6,7},{7,8},{8,9},{9,10},{10,1... | collective-permute-start | bytes 207368 | tf_op jit(solution)/shard_map/ppermute | solution.py:376
  26.5 12.8 %collective-permute-start.3 = (bf16[3,90,128]{2,1,0:T(8,128)(2,1)S(1)}, bf16[3,90,128]{2,1,0:T(8,128)(2,1)S(1)}, u32[]{:S(2)}, u32[]{:S(2)}) collective-permute-start(bf16[3,90,128]{2,1,0:T(8,128)(2,1)S(1)} %get-tuple-element.35), channel_id=1, source_target_pairs={{1,0},{2,1},{3,2},{4,3},{5,4},{6,5},{7,6},{8,7},{9,8},{10,9},{11,1... | collective-permute-start | bytes 207368 | tf_op jit(solution)/shard_map/ppermute | solution.py:376
  28.7 10.6 %all-to-all-start.1 = ((f32[16,2,192]{2,1,0:T(2,128)}), f32[16,2,192]{2,1,0:T(2,128)S(1)}, u32[]{:S(2)}, u32[]{:S(2)}) async-start(f32[16,2,192]{2,1,0:T(2,128)} %get-tuple-element.36), calls=%async_computation.1 | async-start | bytes 65536 | tf_op jit(solution)/shard_map/all_to_all | solution.py:379
  44.3 15.2 %collective-permute-start.4 = (bf16[3,90,128]{2,1,0:T(8,128)(2,1)}, bf16[3,90,128]{2,1,0:T(8,128)(2,1)S(1)}, u32[]{:S(2)}, u32[]{:S(2)}) collective-permute-start(bf16[3,90,128]{2,1,0:T(8,128)(2,1)} %get-tuple-element.41), channel_id=1, source_target_pairs={{0,1},{1,2},{2,3},{3,4},{4,5},{5,6},{6,7},{7,8},{8,9},{9,10},{10,1... | collective-permute-start | bytes 207368 | tf_op jit(solution)/shard_map/ppermute | solution.py:376
  44.8 14.7 %collective-permute-start.5 = (bf16[3,90,128]{2,1,0:T(8,128)(2,1)}, bf16[3,90,128]{2,1,0:T(8,128)(2,1)S(1)}, u32[]{:S(2)}, u32[]{:S(2)}) collective-permute-start(bf16[3,90,128]{2,1,0:T(8,128)(2,1)} %get-tuple-element.42), channel_id=1, source_target_pairs={{1,0},{2,1},{3,2},{4,3},{5,4},{6,5},{7,6},{8,7},{9,8},{10,9},{11,1... | collective-permute-start | bytes 207368 | tf_op jit(solution)/shard_map/ppermute | solution.py:376
  48.8 10.7 %all-to-all-start.2 = ((f32[16,2,192]{2,1,0:T(2,128)}), f32[16,2,192]{2,1,0:T(2,128)S(1)}, u32[]{:S(2)}, u32[]{:S(2)}) async-start(f32[16,2,192]{2,1,0:T(2,128)} %get-tuple-element.43), calls=%async_computation.2 | async-start | bytes 65536 | tf_op jit(solution)/shard_map/all_to_all | solution.py:379
  52.5 0.9 %copy-start = (bf16[3,90,128]{2,1,0:T(8,128)(2,1)S(1)}, bf16[3,90,128]{2,1,0:T(8,128)(2,1)}, u32[]{:S(2)}) copy-start(bf16[3,90,128]{2,1,0:T(8,128)(2,1)} %get-tuple-element.45.before) | copy-start | bytes 207364
  53.4 0.9 %copy-start.1 = (bf16[3,90,128]{2,1,0:T(8,128)(2,1)S(1)}, bf16[3,90,128]{2,1,0:T(8,128)(2,1)}, u32[]{:S(2)}) copy-start(bf16[3,90,128]{2,1,0:T(8,128)(2,1)} %get-tuple-element.46.after) | copy-start | bytes 207364

commit v13 on v11

--- a/solution.py
+++ b/solution.py
@@ -152,6 +152,17 @@
     split = jnp.concatenate([high, middle, low], axis=0)
     sums = jnp.dot(split, same, preferred_element_type=jnp.float32)
     return sums[0:2] + sums[2:4] + sums[4:6]
+
+
+def pieces(source, target, sem, first, cuts):
+    size = source.shape[1] // cuts
+    copies = []
+    for lead in range(source.shape[0]):
+        for cut in range(cuts):
+            at = (lead, pl.ds(cut * size, size))
+            own = sem.at[first + len(copies)]
+            copies.append(pltpu.make_async_copy(source.at[at], target.at[at], own))
+    return copies
 
 
 def begin_kernel(video, caches, same, sums, first, last, near, wide, held, alike, sem):
@@ -196,7 +207,9 @@
             caches, cache, *refs = cache, *refs
         refs = [out, ordered, *refs]
         bring = pltpu.make_async_copy(video, near, refs[-1].at[4])
-    passed = []
+    passed, middle = [], None
+    if layer > 1:
+        middle, *refs = refs
     if layer == 1:
         later = pl.ds((layer + 2) * PLANES, handed[0].shape[0])
         for side, ref in enumerate((before, after)):
@@ -208,8 +221,9 @@
     places = rows * cols
     fetch = pltpu.make_async_copy(weights.at[layer], weight, sem.at[1])
     if layer == 1:
-        begun = pltpu.make_async_copy(caches.at[layer], cache, sem.at[0])
-        begun.start()
+        begun = pieces(caches.at[layer], cache, sem, 12, 3)
+        for copy in begun:
+            copy.start()
     fetch.start()
     if bring is not None:
         bring.start()
@@ -227,7 +241,8 @@
         return [edges[side, plane, pl.ds(h, COLS, stride=0), :] for side in (0, 1)]
 
     if layer == 1:
-        begun.wait()
+        for copy in begun:
+            copy.wait()
     build_slabs(rows, row_of, edge_of, slabs)
     fetch.wait()
     if layer == 1:
@@ -243,14 +258,18 @@
         value = value + constant
         if layer == 1:
             value = value + near[t].astype(jnp.float32).reshape(places, channels)
+        elif middle is not None:
+            value = value + get_planes(middle, t, pl.ds(0, places))
         put_planes(out, t, pl.ds(0, places), value)
 
     finish(1, product([(slabs[1], tables[0])], 0, places))
     finish(0, product([(slabs[0], tables[0]), (slabs[1], tables[1])], 0, places))
     if far:
-        leave = pltpu.make_async_copy(out, away, sem.at[3])
-        leave.start()
-        leave.wait()
+        leave = pieces(out, away, sem, 8, 1)
+        for copy in leave:
+            copy.start()
+        for copy in leave:
+            copy.wait()
     for copy in [store] + passed:
         copy.wait()
     if layer == 0:
@@ -276,9 +295,9 @@
         away, part, *slabs = part, *slabs
     frames, rows, cols, channels = kept.shape
     places = rows * cols
-    fetch, late = [pltpu.make_async_copy(ordered, taps, sem.at[1])], []
+    fetch, late = pieces(ordered, taps, sem, 8, 4), []
     if far:
-        fetch.append(pltpu.make_async_copy(away, part, sem.at[3]))
+        fetch += pieces(away, part, sem, 16, 1)
     if not final:
         late.append(pltpu.make_async_copy(same, alike, sem.at[4]))
     if bring:
@@ -331,7 +350,6 @@
         shape = (size // COLS, COLS, channels)
         value = value + get_planes(part, t, here)
         if final:
-            value = value + get_planes(x, t, here)
             y[t, span] = value.reshape(shape).astype(jnp.bfloat16)
             return moments
         put_planes(y, t, here, value)
@@ -412,7 +430,7 @@
     def room(far):
         return [pltpu.VMEM((PLANES, places, LANES), jnp.float32)] if far else []
 
-    def cached_part(layer, far, cache, brims):
+    def cached_part(layer, far, cache, brims, x):
         own = [pltpu.VMEM(video_span.shape, jnp.bfloat16)] * 2 if layer == 1 else []
         later = pltpu.HBM(((layers - 2) * PLANES, rows, LANES), jnp.bfloat16)
         more = {0: [block], 1: [later] * 2}.get(layer, [])
@@ -425,17 +443,17 @@
             ]
             + more,
             in_specs=[HBM if cache is None else VMEM, VMEM, VMEM, HBM, VMEM]
-            + ([HBM] if layer < 2 else []),
+            + [HBM if layer < 2 else VMEM],
             out_specs=[HBM if far else VMEM, HBM] + [HBM if layer else VMEM] * len(more),
             scratch_shapes=own + scratch(frames, rows, room(far))
             + [
                 pltpu.VMEM((channels, weights.shape[1]), weights.dtype),
                 pltpu.VMEM((3, channels, tiles), weights.dtype),
-                pltpu.SemaphoreType.DMA((7,)),
+                pltpu.SemaphoreType.DMA((20,)),
             ],
             compiler_params=pltpu.CompilerParams(vmem_limit_bytes=24 << 20),
             name="cached",
-        )(caches if cache is None else cache, *brims, turned, biases, *([video] if layer < 2 else []))
+        )(caches if cache is None else cache, *brims, turned, biases, video if layer < 2 else x)
 
     x = None
     carried = None
@@ -443,7 +461,7 @@
         final = layer == layers - 1
         far = layer < layers - 1
         bring = 0 < layer < layers - 1
-        part, ordered, *more = cached_part(layer, far, cache, brims)
+        part, ordered, *more = cached_part(layer, far, cache, brims, x)
         if layer == 0:
             x = more[0]
         elif more:
@@ -481,7 +499,7 @@
                 pltpu.VMEM(video_span.shape, jnp.bfloat16),
                 pltpu.VMEM((2, channels, tiles), weights.dtype),
                 pltpu.VMEM(same.shape, same.dtype),
-                pltpu.SemaphoreType.DMA((6,)),
+                pltpu.SemaphoreType.DMA((20,)),
             ],
             compiler_params=pltpu.CompilerParams(vmem_limit_bytes=24 << 20),
             input_output_aliases=aliases,

time: 63.9 us -> 65.1 us (1.019)
  Pallas kernels: 34.6 us -> 35.9 us
    pallas_call x3, Pallas kernels: 14.2 us -> 15.1 us  [local(): pl.pallas_call(functools.partial(active_kernel, layer, chunk, far, bring,...]
where the time goes in v13:
time: 65.1 us; the launch traced here: 64.7 us
  Pallas kernels  35.9 us (55%)
  starting transfers between devices  25.8 us (40%)
  waiting for transfers between devices  1.99 us (3%)
  between operations  0.94 us (1%)
    pallas_call x3, Pallas kernels, cached_part(): pl.pallas_call(functools.partial(cached_kernel, layer, chunk, far), out_s...  18 us
    pallas_call x3, Pallas kernels, local(): pl.pallas_call(functools.partial(active_kernel, layer, chunk, far, bring,...  15.1 us
    ppermute x6, starting transfers between devices, around(): return (lax.ppermute(last, 'lon', up), lax.ppermute(first, 'lon', down))  14.6 us
    all_to_all x3, starting transfers between devices, gathered(): return lax.all_to_all(sums, 'lon', 0, 0)  11.2 us
    pallas_call x1, Pallas kernels, local(): pl.pallas_call(begin_kernel, out_shape=[spread, brim, brim, block], in_sp...  2.88 us
  transfers between devices with their start and end apart: 9, of which 3 were waited for; matrix products, arithmetic and copies ran while one was open for 0% of the time, Pallas kernels for 28%

profile of v13, /device:TPU:0, one launch (start us, length us, event | category | flops | bytes accessed | tf_op | source)
XLA Modules:
  0.0 64.7 jit_solution(7018302771924695605)
XLA Ops:
  0.6 0.0 copy-start.2
  0.6 2.9 %begin.1 = (f32[16,2,192]{2,1,0:T(2,128)}, bf16[12,90,128]{2,1,0:T(8,128)(2,1)S(1)}, bf16[12,90,128]{2,1,0:T(8,128)(2,1)S(1)}, bf16[2,90,8,192]{3,2,1,0:T(8,128)(2,1)S(1)}) custom-call(bf16[2,90,8,192]{3,2,1,0:T(8,128)(2,1)} %refs_0_.3, bf16[3,2,90,8,192]{4,3,2,1,0:T(8,128)(2,1)} %refs_10_.1, bf16[192,192]{1,0:T(8,128)(2,1)} %constant.2.clone.same.refs_8_), custom_call_target="tpu_custom_call" | custom-call | tf_op jit(solution)/shard_map/begin/pallas_call | solution.py:412
  3.5 0.5 collective-permute-start
  4.1 5.0 %collective-permute-start.1 = (bf16[12,90,128]{2,1,0:T(8,128)(2,1)S(1)}, bf16[12,90,128]{2,1,0:T(8,128)(2,1)S(1)}, u32[]{:S(2)}, u32[]{:S(2)}) collective-permute-start(bf16[12,90,128]{2,1,0:T(8,128)(2,1)S(1)} %get-tuple-element.28), channel_id=1, source_target_pairs={{1,0},{2,1},{3,2},{4,3},{5,4},{6,5},{7,6},{8,7},{9,8},{10,9},{11,1... | collective-permute-start | bytes 829448 | tf_op jit(solution)/shard_map/ppermute | solution.py:396
  9.1 3.6 %all-to-all-start = ((f32[16,2,192]{2,1,0:T(2,128)}), f32[16,2,192]{2,1,0:T(2,128)S(1)}, u32[]{:S(2)}, u32[]{:S(2)}) async-start(f32[16,2,192]{2,1,0:T(2,128)} %get-tuple-element.30), calls=%async_computation | async-start | bytes 65536 | tf_op jit(solution)/shard_map/all_to_all | solution.py:399
  12.7 0.8 %collective-permute-done.before.refs_1_ = bf16[12,90,128]{2,1,0:T(8,128)(2,1)S(1)} collective-permute-done((bf16[12,90,128]{2,1,0:T(8,128)(2,1)S(1)}, bf16[12,90,128]{2,1,0:T(8,128)(2,1)S(1)}, u32[]{:S(2)}, u32[]{:S(2)}) %collective-permute-start) | collective-permute-done | bytes 276512 | tf_op jit(solution)/shard_map/ppermute | solution.py:396
  13.6 0.0 collective-permute-done.1.after.refs_2_
  13.6 0.0 copy-done.2
  13.6 0.0 copy-start.3
  13.6 0.0 copy-start.4
  13.6 5.7 %cached.3 = (f32[3,720,128]{2,1,0:T(8,128)}, bf16[2,192,1792]{2,1,0:T(8,128)(2,1)}, bf16[2,90,8,192]{3,2,1,0:T(8,128)(2,1)S(1)}) custom-call(bf16[2,90,8,192]{3,2,1,0:T(8,128)(2,1)S(1)} %get-tuple-element.26.cache, bf16[12,90,128]{2,1,0:T(8,128)(2,1)S(1)} %collective-permute-done.before.refs_1_, ...), custom_call_target="tpu_custom_call" | custom-call | tf_op jit(solution)/shard_map/cached/pallas_call | solution.py:438
  19.3 0.1 all-to-all-done.refs_3_
  19.4 0.0 copy-done.3
  19.4 0.0 copy-done.4
  19.4 5.0 %active.3 = (f32[3,720,128]{2,1,0:T(8,128)S(1)}, bf16[3,2,90,8,192]{4,3,2,1,0:T(8,128)(2,1)}, f32[16,2,192]{2,1,0:T(2,128)}, bf16[3,90,128]{2,1,0:T(8,128)(2,1)S(1)}, bf16[3,90,128]{2,1,0:T(8,128)(2,1)S(1)}) custom-call(bf16[2,90,8,192]{3,2,1,0:T(8,128)(2,1)S(1)} %get-tuple-element.29.refs_0_, bf16[12,90,128]{2,1,0:T(8,128)(2,1)S(1)} %collective-permute-done.before.refs_1_, ...), custom_call_target="tpu_custom_call" | custom-call | tf_op jit(solution)/shard_map/active/pallas_call | solution.py:492
  24.4 2.4 %collective-permute-start.2 = (bf16[3,90,128]{2,1,0:T(8,128)(2,1)S(1)}, bf16[3,90,128]{2,1,0:T(8,128)(2,1)S(1)}, u32[]{:S(2)}, u32[]{:S(2)}) collective-permute-start(bf16[3,90,128]{2,1,0:T(8,128)(2,1)S(1)} %get-tuple-element.34), channel_id=1, source_target_pairs={{0,1},{1,2},{2,3},{3,4},{4,5},{5,6},{6,7},{7,8},{8,9},{9,10},{10,1... | collective-permute-start | bytes 207368 | tf_op jit(solution)/shard_map/ppermute | solution.py:396
  26.9 2.1 %collective-permute-start.3 = (bf16[3,90,128]{2,1,0:T(8,128)(2,1)S(1)}, bf16[3,90,128]{2,1,0:T(8,128)(2,1)S(1)}, u32[]{:S(2)}, u32[]{:S(2)}) collective-permute-start(bf16[3,90,128]{2,1,0:T(8,128)(2,1)S(1)} %get-tuple-element.35), channel_id=1, source_target_pairs={{1,0},{2,1},{3,2},{4,3},{5,4},{6,5},{7,6},{8,7},{9,8},{10,9},{11,1... | collective-permute-start | bytes 207368 | tf_op jit(solution)/shard_map/ppermute | solution.py:396
  28.9 3.9 %all-to-all-start.1 = ((f32[16,2,192]{2,1,0:T(2,128)}), f32[16,2,192]{2,1,0:T(2,128)S(1)}, u32[]{:S(2)}, u32[]{:S(2)}) async-start(f32[16,2,192]{2,1,0:T(2,128)} %get-tuple-element.36), calls=%async_computation.1 | async-start | bytes 65536 | tf_op jit(solution)/shard_map/all_to_all | solution.py:399
  32.9 6.9 %cached.4 = (f32[3,720,128]{2,1,0:T(8,128)}, bf16[2,192,1792]{2,1,0:T(8,128)(2,1)}, bf16[3,90,128]{2,1,0:T(8,128)(2,1)}, bf16[3,90,128]{2,1,0:T(8,128)(2,1)}) custom-call(bf16[3,2,90,8,192]{4,3,2,1,0:T(8,128)(2,1)} %refs_10_.1, bf16[12,90,128]{2,1,0:T(8,128)(2,1)S(1)} %collective-permute-done.before.refs_1_, ...), custom_call_target="tpu_custom_call" | custom-call | tf_op jit(solution)/shard_map/cached/pallas_call | solution.py:438
  39.8 0.0 all-to-all-done.1.refs_3_
  39.9 0.0 collective-permute-done.2.refs_1_
  39.9 0.0 collective-permute-done.3.refs_2_
  39.9 0.0 copy-start
  39.9 0.0 copy-start.1
  39.9 5.3 %active.4 = (f32[3,720,128]{2,1,0:T(8,128)S(1)}, bf16[3,2,90,8,192]{4,3,2,1,0:T(8,128)(2,1)}, f32[16,2,192]{2,1,0:T(2,128)}, bf16[3,90,128]{2,1,0:T(8,128)(2,1)S...) custom-call(f32[3,720,128]{2,1,0:T(8,128)S(1)} %get-tuple-element.33.re, ...), custom_call_target="tpu_custom_call", output_to_operand_aliasing={{1}: (9, {})} | custom-call | tf_op jit(solution)/shard_map/active/pallas_call | solution.py:492
  45.2 0.5 collective-permute-start.4
  45.7 4.0 %collective-permute-start.5 = (bf16[3,90,128]{2,1,0:T(8,128)(2,1)S(1)}, bf16[3,90,128]{2,1,0:T(8,128)(2,1)S(1)}, u32[]{:S(2)}, u32[]{:S(2)}) collective-permute-start(bf16[3,90,128]{2,1,0:T(8,128)(2,1)S(1)} %get-tuple-element.42), channel_id=1, source_target_pairs={{1,0},{2,1},{3,2},{4,3},{5,4},{6,5},{7,6},{8,7},{9,8},{10,9},{11,1... | collective-permute-start | bytes 207368 | tf_op jit(solution)/shard_map/ppermute | solution.py:396
  49.7 3.7 %all-to-all-start.2 = ((f32[16,2,192]{2,1,0:T(2,128)}), f32[16,2,192]{2,1,0:T(2,128)S(1)}, u32[]{:S(2)}, u32[]{:S(2)}) async-start(f32[16,2,192]{2,1,0:T(2,128)} %get-tuple-element.43), calls=%async_computation.2 | async-start | bytes 65536 | tf_op jit(solution)/shard_map/all_to_all | solution.py:399
  53.4 0.0 copy-done
  53.4 0.0 copy-done.1
  53.4 5.3 %cached.5 = (f32[3,720,128]{2,1,0:T(8,128)S(1)}, bf16[2,192,1792]{2,1,0:T(8,128)(2,1)}) custom-call(bf16[2,90,8,192]{3,2,1,0:T(8,128)(2,1)S(1)} %get-tuple-element.44.cache, bf16[3,90,128]{2,1,0:T(8,128)(2,1)S(1)} %copy-done, bf16[3,90,128]{2,1,0:T(8,128)(2,1)S(1)} %copy-done.1, bf16[3,192,5184]{2,1,0:T(8,128)(2,1)} %bitcast.3, f32[3,192]{1,0:T(4,128)S(1)} %copy-done.2, ...), custom_call_target="tpu_custom_call" | custom-call | tf_op jit(solution)/shard_map/cached/pallas_call | solution.py:438
  58.8 1.1 %all-to-all-done.2.refs_3_ = f32[16,2,192]{2,1,0:T(2,128)S(1)} async-done(((f32[16,2,192]{2,1,0:T(2,128)}), f32[16,2,192]{2,1,0:T(2,128)S(1)}, u32[]{:S(2)}, u32[]{:S(2)}) %all-to-all-start.2) | async-done | bytes 24608 | tf_op jit(solution)/shard_map/all_to_all | solution.py:399
  59.8 0.0 collective-permute-done.4.refs_1_
  59.8 0.0 collective-permute-done.5.refs_2_
  59.8 4.7 %active.5 = (bf16[2,90,8,192]{3,2,1,0:T(8,128)(2,1)}, bf16[3,2,90,8,192]{4,3,2,1,0:T(8,128)(2,1)}) custom-call(f32[3,720,128]{2,1,0:T(8,128)S(1)} %get-tuple-element.40.refs_0_, bf16[3,90,128]{2,1,0:T(8,128)(2,1)S(1)} %collective-permute-done.4.refs_1_, bf16[3,90,128]{2,1,0:T(8,128)(2,1)S(1)} %collective-permute-done.5.refs_2_, ...), custom_call_target="tpu_custom_call", output_to_operand_aliasing={{1}: (9, {})} | custom-call | tf_op jit(solution)/shard_map/active/pallas_call | solution.py:492
Async XLA Ops:
  0.6 12.9 %copy-start.2 = (f32[3,192]{1,0:T(4,128)S(1)}, f32[3,192]{1,0:T(4,128)}, u32[]{:S(2)}) copy-start(f32[3,192]{1,0:T(4,128)} %bias.5) | copy-start | bytes 6916
  3.5 10.0 %collective-permute-start = (bf16[12,90,128]{2,1,0:T(8,128)(2,1)S(1)}, bf16[12,90,128]{2,1,0:T(8,128)(2,1)S(1)}, u32[]{:S(2)}, u32[]{:S(2)}) collective-permute-start(bf16[12,90,128]{2,1,0:T(8,128)(2,1)S(1)} %get-tuple-element.27), channel_id=1, source_target_pairs={{0,1},{1,2},{2,3},{3,4},{4,5},{5,6},{6,7},{7,8},{8,9},{9,10},{10,1... | collective-permute-start | bytes 829448 | tf_op jit(solution)/shard_map/ppermute | solution.py:396
  4.1 9.5 %collective-permute-start.1 = (bf16[12,90,128]{2,1,0:T(8,128)(2,1)S(1)}, bf16[12,90,128]{2,1,0:T(8,128)(2,1)S(1)}, u32[]{:S(2)}, u32[]{:S(2)}) collective-permute-start(bf16[12,90,128]{2,1,0:T(8,128)(2,1)S(1)} %get-tuple-element.28), channel_id=1, source_target_pairs={{1,0},{2,1},{3,2},{4,3},{5,4},{6,5},{7,6},{8,7},{9,8},{10,9},{11,1... | collective-permute-start | bytes 829448 | tf_op jit(solution)/shard_map/ppermute | solution.py:396
  9.1 10.3 %all-to-all-start = ((f32[16,2,192]{2,1,0:T(2,128)}), f32[16,2,192]{2,1,0:T(2,128)S(1)}, u32[]{:S(2)}, u32[]{:S(2)}) async-start(f32[16,2,192]{2,1,0:T(2,128)} %get-tuple-element.30), calls=%async_computation | async-start | bytes 65536 | tf_op jit(solution)/shard_map/all_to_all | solution.py:399
  13.6 5.8 %copy-start.3 = (f32[3,192]{1,0:T(4,128)S(1)}, f32[3,192]{1,0:T(4,128)}, u32[]{:S(2)}) copy-start(f32[3,192]{1,0:T(4,128)} %refs_4_.5) | copy-start | bytes 6916
  13.6 5.8 %copy-start.4 = (f32[3,192]{1,0:T(4,128)S(1)}, f32[3,192]{1,0:T(4,128)}, u32[]{:S(2)}) copy-start(f32[3,192]{1,0:T(4,128)} %refs_5_.5) | copy-start | bytes 6916
  24.4 15.4 %collective-permute-start.2 = (bf16[3,90,128]{2,1,0:T(8,128)(2,1)S(1)}, bf16[3,90,128]{2,1,0:T(8,128)(2,1)S(1)}, u32[]{:S(2)}, u32[]{:S(2)}) collective-permute-start(bf16[3,90,128]{2,1,0:T(8,128)(2,1)S(1)} %get-tuple-element.34), channel_id=1, source_target_pairs={{0,1},{1,2},{2,3},{3,4},{4,5},{5,6},{6,7},{7,8},{8,9},{9,10},{10,1... | collective-permute-start | bytes 207368 | tf_op jit(solution)/shard_map/ppermute | solution.py:396
  26.9 13.0 %collective-permute-start.3 = (bf16[3,90,128]{2,1,0:T(8,128)(2,1)S(1)}, bf16[3,90,128]{2,1,0:T(8,128)(2,1)S(1)}, u32[]{:S(2)}, u32[]{:S(2)}) collective-permute-start(bf16[3,90,128]{2,1,0:T(8,128)(2,1)S(1)} %get-tuple-element.35), channel_id=1, source_target_pairs={{1,0},{2,1},{3,2},{4,3},{5,4},{6,5},{7,6},{8,7},{9,8},{10,9},{11,1... | collective-permute-start | bytes 207368 | tf_op jit(solution)/shard_map/ppermute | solution.py:396
  28.9 10.9 %all-to-all-start.1 = ((f32[16,2,192]{2,1,0:T(2,128)}), f32[16,2,192]{2,1,0:T(2,128)S(1)}, u32[]{:S(2)}, u32[]{:S(2)}) async-start(f32[16,2,192]{2,1,0:T(2,128)} %get-tuple-element.36), calls=%async_computation.1 | async-start | bytes 65536 | tf_op jit(solution)/shard_map/all_to_all | solution.py:399
  39.9 13.5 %copy-start = (bf16[3,90,128]{2,1,0:T(8,128)(2,1)S(1)}, bf16[3,90,128]{2,1,0:T(8,128)(2,1)}, u32[]{:S(2)}) copy-start(bf16[3,90,128]{2,1,0:T(8,128)(2,1)} %get-tuple-element.45.before) | copy-start | bytes 207364
  39.9 13.5 %copy-start.1 = (bf16[3,90,128]{2,1,0:T(8,128)(2,1)S(1)}, bf16[3,90,128]{2,1,0:T(8,128)(2,1)}, u32[]{:S(2)}) copy-start(bf16[3,90,128]{2,1,0:T(8,128)(2,1)} %get-tuple-element.46.after) | copy-start | bytes 207364
  45.2 14.6 %collective-permute-start.4 = (bf16[3,90,128]{2,1,0:T(8,128)(2,1)S(1)}, bf16[3,90,128]{2,1,0:T(8,128)(2,1)S(1)}, u32[]{:S(2)}, u32[]{:S(2)}) collective-permute-start(bf16[3,90,128]{2,1,0:T(8,128)(2,1)S(1)} %get-tuple-element.41), channel_id=1, source_target_pairs={{0,1},{1,2},{2,3},{3,4},{4,5},{5,6},{6,7},{7,8},{8,9},{9,10},{10,1... | collective-permute-start | bytes 207368 | tf_op jit(solution)/shard_map/ppermute | solution.py:396
  45.7 14.1 %collective-permute-start.5 = (bf16[3,90,128]{2,1,0:T(8,128)(2,1)S(1)}, bf16[3,90,128]{2,1,0:T(8,128)(2,1)S(1)}, u32[]{:S(2)}, u32[]{:S(2)}) collective-permute-start(bf16[3,90,128]{2,1,0:T(8,128)(2,1)S(1)} %get-tuple-element.42), channel_id=1, source_target_pairs={{1,0},{2,1},{3,2},{4,3},{5,4},{6,5},{7,6},{8,7},{9,8},{10,9},{11,1... | collective-permute-start | bytes 207368 | tf_op jit(solution)/shard_map/ppermute | solution.py:396
  49.7 10.1 %all-to-all-start.2 = ((f32[16,2,192]{2,1,0:T(2,128)}), f32[16,2,192]{2,1,0:T(2,128)S(1)}, u32[]{:S(2)}, u32[]{:S(2)}) async-start(f32[16,2,192]{2,1,0:T(2,128)} %get-tuple-element.43), calls=%async_computation.2 | async-start | bytes 65536 | tf_op jit(solution)/shard_map/all_to_all | solution.py:399

commit v14 on v11

--- a/solution.py
+++ b/solution.py
@@ -283,7 +283,7 @@
         late.append(pltpu.make_async_copy(same, alike, sem.at[4]))
     if bring:
         late.append(pltpu.make_async_copy(caches.at[layer + 1], near, sem.at[5]))
-    for copy in fetch + late:
+    for copy in fetch:
         copy.start()
 
     means = jnp.sum(stats[...], axis=0) / entries
@@ -323,6 +323,8 @@
     copy.start()
     for one in fetch:
         one.wait()
+    for one in late:
+        one.start()
     tables = [taps[p] for p in range(2)]
     moments = [jnp.zeros((COLS, channels), jnp.float32)] * 2
 

time: 63.9 us -> 63.9 us (level)
  no operation moved by 1% of the time
where the time goes in v14:
time: 63.9 us; the launch traced here: 63.5 us
  Pallas kernels  34.6 us (54%)
  starting transfers between devices  25.7 us (40%)
  waiting for transfers between devices  2.24 us (4%)
  between operations  0.94 us (1%)
    pallas_call x3, Pallas kernels, cached_part(): pl.pallas_call(functools.partial(cached_kernel, layer, chunk, far), out_s...  17.5 us
    ppermute x6, starting transfers between devices, around(): return (lax.ppermute(last, 'lon', up), lax.ppermute(first, 'lon', down))  14.6 us
    pallas_call x3, Pallas kernels, local(): pl.pallas_call(functools.partial(active_kernel, layer, chunk, far, bring,...  14.2 us
    all_to_all x3, starting transfers between devices, gathered(): return lax.all_to_all(sums, 'lon', 0, 0)  11.1 us
    pallas_call x1, Pallas kernels, local(): pl.pallas_call(begin_kernel, out_shape=[spread, brim, brim, block], in_sp...  2.88 us
    all_to_all x3, waiting for transfers between devices, gathered(): return lax.all_to_all(sums, 'lon', 0, 0)  1.41 us
  transfers between devices with their start and end apart: 9, of which 3 were waited for; matrix products, arithmetic and copies ran while one was open for 0% of the time, Pallas kernels for 28%

profile of v14, /device:TPU:0, one launch (start us, length us, event | category | flops | bytes accessed | tf_op | source)
XLA Modules:
  0.0 63.5 jit_solution(11653219006194837911)
XLA Ops:
  0.6 0.0 copy-start.2
  0.6 2.9 %begin.1 = (f32[16,2,192]{2,1,0:T(2,128)}, bf16[12,90,128]{2,1,0:T(8,128)(2,1)S(1)}, bf16[12,90,128]{2,1,0:T(8,128)(2,1)S(1)}, bf16[2,90,8,192]{3,2,1,0:T(8,128)(2,1)S(1)}) custom-call(bf16[2,90,8,192]{3,2,1,0:T(8,128)(2,1)} %refs_0_.3, bf16[3,2,90,8,192]{4,3,2,1,0:T(8,128)(2,1)} %refs_10_.1, bf16[192,192]{1,0:T(8,128)(2,1)} %constant.2.clone.same.refs_8_), custom_call_target="tpu_custom_call" | custom-call | tf_op jit(solution)/shard_map/begin/pallas_call | solution.py:396
  3.5 0.5 collective-permute-start
  4.1 5.0 %collective-permute-start.1 = (bf16[12,90,128]{2,1,0:T(8,128)(2,1)S(1)}, bf16[12,90,128]{2,1,0:T(8,128)(2,1)S(1)}, u32[]{:S(2)}, u32[]{:S(2)}) collective-permute-start(bf16[12,90,128]{2,1,0:T(8,128)(2,1)S(1)} %get-tuple-element.28), channel_id=1, source_target_pairs={{1,0},{2,1},{3,2},{4,3},{5,4},{6,5},{7,6},{8,7},{9,8},{10,9},{11,1... | collective-permute-start | bytes 829448 | tf_op jit(solution)/shard_map/ppermute | solution.py:380
  9.1 3.6 %all-to-all-start = ((f32[16,2,192]{2,1,0:T(2,128)}), f32[16,2,192]{2,1,0:T(2,128)S(1)}, u32[]{:S(2)}, u32[]{:S(2)}) async-start(f32[16,2,192]{2,1,0:T(2,128)} %get-tuple-element.30), calls=%async_computation | async-start | bytes 65536 | tf_op jit(solution)/shard_map/all_to_all | solution.py:383
  12.7 0.8 %collective-permute-done.before.refs_1_ = bf16[12,90,128]{2,1,0:T(8,128)(2,1)S(1)} collective-permute-done((bf16[12,90,128]{2,1,0:T(8,128)(2,1)S(1)}, bf16[12,90,128]{2,1,0:T(8,128)(2,1)S(1)}, u32[]{:S(2)}, u32[]{:S(2)}) %collective-permute-start) | collective-permute-done | bytes 276512 | tf_op jit(solution)/shard_map/ppermute | solution.py:380
  13.6 0.0 collective-permute-done.1.after.refs_2_
  13.6 0.0 copy-done.2
  13.6 0.0 copy-start.3
  13.6 0.0 copy-start.4
  13.6 5.6 %cached.3 = (f32[3,720,128]{2,1,0:T(8,128)}, bf16[2,192,1792]{2,1,0:T(8,128)(2,1)}, bf16[2,90,8,192]{3,2,1,0:T(8,128)(2,1)S(1)}) custom-call(bf16[2,90,8,192]{3,2,1,0:T(8,128)(2,1)S(1)} %get-tuple-element.26.cache, bf16[12,90,128]{2,1,0:T(8,128)(2,1)S(1)} %collective-permute-done.before.refs_1_, ...), custom_call_target="tpu_custom_call" | custom-call | tf_op jit(solution)/shard_map/cached/pallas_call | solution.py:422
  19.2 0.2 all-to-all-done.refs_3_
  19.4 0.0 copy-done.3
  19.4 0.0 copy-done.4
  19.4 4.8 %active.3 = (f32[3,720,128]{2,1,0:T(8,128)S(1)}, bf16[3,2,90,8,192]{4,3,2,1,0:T(8,128)(2,1)}, f32[16,2,192]{2,1,0:T(2,128)}, bf16[3,90,128]{2,1,0:T(8,128)(2,1)S(1)}, bf16[3,90,128]{2,1,0:T(8,128)(2,1)S(1)}) custom-call(bf16[2,90,8,192]{3,2,1,0:T(8,128)(2,1)S(1)} %get-tuple-element.29.refs_0_, bf16[12,90,128]{2,1,0:T(8,128)(2,1)S(1)} %collective-permute-done.before.refs_1_, ...), custom_call_target="tpu_custom_call" | custom-call | tf_op jit(solution)/shard_map/active/pallas_call | solution.py:476
  24.2 2.3 %collective-permute-start.2 = (bf16[3,90,128]{2,1,0:T(8,128)(2,1)S(1)}, bf16[3,90,128]{2,1,0:T(8,128)(2,1)S(1)}, u32[]{:S(2)}, u32[]{:S(2)}) collective-permute-start(bf16[3,90,128]{2,1,0:T(8,128)(2,1)S(1)} %get-tuple-element.34), channel_id=1, source_target_pairs={{0,1},{1,2},{2,3},{3,4},{4,5},{5,6},{6,7},{7,8},{8,9},{9,10},{10,1... | collective-permute-start | bytes 207368 | tf_op jit(solution)/shard_map/ppermute | solution.py:380
  26.5 2.2 %collective-permute-start.3 = (bf16[3,90,128]{2,1,0:T(8,128)(2,1)S(1)}, bf16[3,90,128]{2,1,0:T(8,128)(2,1)S(1)}, u32[]{:S(2)}, u32[]{:S(2)}) collective-permute-start(bf16[3,90,128]{2,1,0:T(8,128)(2,1)S(1)} %get-tuple-element.35), channel_id=1, source_target_pairs={{1,0},{2,1},{3,2},{4,3},{5,4},{6,5},{7,6},{8,7},{9,8},{10,9},{11,1... | collective-permute-start | bytes 207368 | tf_op jit(solution)/shard_map/ppermute | solution.py:380
  28.7 3.8 %all-to-all-start.1 = ((f32[16,2,192]{2,1,0:T(2,128)}), f32[16,2,192]{2,1,0:T(2,128)S(1)}, u32[]{:S(2)}, u32[]{:S(2)}) async-start(f32[16,2,192]{2,1,0:T(2,128)} %get-tuple-element.36), calls=%async_computation.1 | async-start | bytes 65536 | tf_op jit(solution)/shard_map/all_to_all | solution.py:383
  32.5 6.7 %cached.4 = (f32[3,720,128]{2,1,0:T(8,128)}, bf16[2,192,1792]{2,1,0:T(8,128)(2,1)}, bf16[3,90,128]{2,1,0:T(8,128)(2,1)}, bf16[3,90,128]{2,1,0:T(8,128)(2,1)}) custom-call(bf16[3,2,90,8,192]{4,3,2,1,0:T(8,128)(2,1)} %refs_10_.1, bf16[12,90,128]{2,1,0:T(8,128)(2,1)S(1)} %collective-permute-done.before.refs_1_, ...), custom_call_target="tpu_custom_call" | custom-call | tf_op jit(solution)/shard_map/cached/pallas_call | solution.py:422
  39.3 0.0 all-to-all-done.1.refs_3_
  39.3 0.0 collective-permute-done.2.refs_1_
  39.3 0.0 collective-permute-done.3.refs_2_
  39.3 0.0 copy-start
  39.3 0.0 copy-start.1
  39.3 4.9 %active.4 = (f32[3,720,128]{2,1,0:T(8,128)S(1)}, bf16[3,2,90,8,192]{4,3,2,1,0:T(8,128)(2,1)}, f32[16,2,192]{2,1,0:T(2,128)}, bf16[3,90,128]{2,1,0:T(8,128)(2,1)S...) custom-call(f32[3,720,128]{2,1,0:T(8,128)S(1)} %get-tuple-element.33.re, ...), custom_call_target="tpu_custom_call", output_to_operand_aliasing={{1}: (9, {})} | custom-call | tf_op jit(solution)/shard_map/active/pallas_call | solution.py:476
  44.3 0.5 collective-permute-start.4
  44.7 4.0 %collective-permute-start.5 = (bf16[3,90,128]{2,1,0:T(8,128)(2,1)S(1)}, bf16[3,90,128]{2,1,0:T(8,128)(2,1)S(1)}, u32[]{:S(2)}, u32[]{:S(2)}) collective-permute-start(bf16[3,90,128]{2,1,0:T(8,128)(2,1)S(1)} %get-tuple-element.42), channel_id=1, source_target_pairs={{1,0},{2,1},{3,2},{4,3},{5,4},{6,5},{7,6},{8,7},{9,8},{10,9},{11,1... | collective-permute-start | bytes 207368 | tf_op jit(solution)/shard_map/ppermute | solution.py:380
  48.7 3.7 %all-to-all-start.2 = ((f32[16,2,192]{2,1,0:T(2,128)}), f32[16,2,192]{2,1,0:T(2,128)S(1)}, u32[]{:S(2)}, u32[]{:S(2)}) async-start(f32[16,2,192]{2,1,0:T(2,128)} %get-tuple-element.43), calls=%async_computation.2 | async-start | bytes 65536 | tf_op jit(solution)/shard_map/all_to_all | solution.py:383
  52.4 0.0 copy-done
  52.4 0.0 copy-done.1
  52.4 5.2 %cached.5 = (f32[3,720,128]{2,1,0:T(8,128)S(1)}, bf16[2,192,1792]{2,1,0:T(8,128)(2,1)}) custom-call(bf16[2,90,8,192]{3,2,1,0:T(8,128)(2,1)S(1)} %get-tuple-element.44.cache, bf16[3,90,128]{2,1,0:T(8,128)(2,1)S(1)} %copy-done, bf16[3,90,128]{2,1,0:T(8,128)(2,1)S(1)} %copy-done.1, bf16[3,192,5184]{2,1,0:T(8,128)(2,1)} %bitcast.3, f32[3,192]{1,0:T(4,128)S(1)} %copy-done.2), custom_call_target="tpu_custom_call" | custom-call | tf_op jit(solution)/shard_map/cached/pallas_call | solution.py:422
  57.6 1.2 %all-to-all-done.2.refs_3_ = f32[16,2,192]{2,1,0:T(2,128)S(1)} async-done(((f32[16,2,192]{2,1,0:T(2,128)}), f32[16,2,192]{2,1,0:T(2,128)S(1)}, u32[]{:S(2)}, u32[]{:S(2)}) %all-to-all-start.2) | async-done | bytes 24608 | tf_op jit(solution)/shard_map/all_to_all | solution.py:383
  58.8 0.0 collective-permute-done.4.refs_1_
  58.8 0.0 collective-permute-done.5.refs_2_
  58.8 4.5 %active.5 = (bf16[2,90,8,192]{3,2,1,0:T(8,128)(2,1)}, bf16[3,2,90,8,192]{4,3,2,1,0:T(8,128)(2,1)}) custom-call(f32[3,720,128]{2,1,0:T(8,128)S(1)} %get-tuple-element.40.refs_0_, bf16[3,90,128]{2,1,0:T(8,128)(2,1)S(1)} %collective-permute-done.4.refs_1_, bf16[3,90,128]{2,1,0:T(8,128)(2,1)S(1)} %collective-permute-done.5.refs_2_, ...), custom_call_target="tpu_custom_call", output_to_operand_aliasing={{1}: (9, {})} | custom-call | tf_op jit(solution)/shard_map/active/pallas_call | solution.py:476
Async XLA Ops:
  0.6 12.9 %copy-start.2 = (f32[3,192]{1,0:T(4,128)S(1)}, f32[3,192]{1,0:T(4,128)}, u32[]{:S(2)}) copy-start(f32[3,192]{1,0:T(4,128)} %bias.5) | copy-start | bytes 6916
  3.5 10.0 %collective-permute-start = (bf16[12,90,128]{2,1,0:T(8,128)(2,1)S(1)}, bf16[12,90,128]{2,1,0:T(8,128)(2,1)S(1)}, u32[]{:S(2)}, u32[]{:S(2)}) collective-permute-start(bf16[12,90,128]{2,1,0:T(8,128)(2,1)S(1)} %get-tuple-element.27), channel_id=1, source_target_pairs={{0,1},{1,2},{2,3},{3,4},{4,5},{5,6},{6,7},{7,8},{8,9},{9,10},{10,1... | collective-permute-start | bytes 829448 | tf_op jit(solution)/shard_map/ppermute | solution.py:380
  4.1 9.5 %collective-permute-start.1 = (bf16[12,90,128]{2,1,0:T(8,128)(2,1)S(1)}, bf16[12,90,128]{2,1,0:T(8,128)(2,1)S(1)}, u32[]{:S(2)}, u32[]{:S(2)}) collective-permute-start(bf16[12,90,128]{2,1,0:T(8,128)(2,1)S(1)} %get-tuple-element.28), channel_id=1, source_target_pairs={{1,0},{2,1},{3,2},{4,3},{5,4},{6,5},{7,6},{8,7},{9,8},{10,9},{11,1... | collective-permute-start | bytes 829448 | tf_op jit(solution)/shard_map/ppermute | solution.py:380
  9.1 10.3 %all-to-all-start = ((f32[16,2,192]{2,1,0:T(2,128)}), f32[16,2,192]{2,1,0:T(2,128)S(1)}, u32[]{:S(2)}, u32[]{:S(2)}) async-start(f32[16,2,192]{2,1,0:T(2,128)} %get-tuple-element.30), calls=%async_computation | async-start | bytes 65536 | tf_op jit(solution)/shard_map/all_to_all | solution.py:383
  13.6 5.8 %copy-start.3 = (f32[3,192]{1,0:T(4,128)S(1)}, f32[3,192]{1,0:T(4,128)}, u32[]{:S(2)}) copy-start(f32[3,192]{1,0:T(4,128)} %refs_4_.5) | copy-start | bytes 6916
  13.6 5.8 %copy-start.4 = (f32[3,192]{1,0:T(4,128)S(1)}, f32[3,192]{1,0:T(4,128)}, u32[]{:S(2)}) copy-start(f32[3,192]{1,0:T(4,128)} %refs_5_.5) | copy-start | bytes 6916
  24.2 15.1 %collective-permute-start.2 = (bf16[3,90,128]{2,1,0:T(8,128)(2,1)S(1)}, bf16[3,90,128]{2,1,0:T(8,128)(2,1)S(1)}, u32[]{:S(2)}, u32[]{:S(2)}) collective-permute-start(bf16[3,90,128]{2,1,0:T(8,128)(2,1)S(1)} %get-tuple-element.34), channel_id=1, source_target_pairs={{0,1},{1,2},{2,3},{3,4},{4,5},{5,6},{6,7},{7,8},{8,9},{9,10},{10,1... | collective-permute-start | bytes 207368 | tf_op jit(solution)/shard_map/ppermute | solution.py:380
  26.5 12.8 %collective-permute-start.3 = (bf16[3,90,128]{2,1,0:T(8,128)(2,1)S(1)}, bf16[3,90,128]{2,1,0:T(8,128)(2,1)S(1)}, u32[]{:S(2)}, u32[]{:S(2)}) collective-permute-start(bf16[3,90,128]{2,1,0:T(8,128)(2,1)S(1)} %get-tuple-element.35), channel_id=1, source_target_pairs={{1,0},{2,1},{3,2},{4,3},{5,4},{6,5},{7,6},{8,7},{9,8},{10,9},{11,1... | collective-permute-start | bytes 207368 | tf_op jit(solution)/shard_map/ppermute | solution.py:380
  28.7 10.6 %all-to-all-start.1 = ((f32[16,2,192]{2,1,0:T(2,128)}), f32[16,2,192]{2,1,0:T(2,128)S(1)}, u32[]{:S(2)}, u32[]{:S(2)}) async-start(f32[16,2,192]{2,1,0:T(2,128)} %get-tuple-element.36), calls=%async_computation.1 | async-start | bytes 65536 | tf_op jit(solution)/shard_map/all_to_all | solution.py:383
  39.3 13.1 %copy-start = (bf16[3,90,128]{2,1,0:T(8,128)(2,1)S(1)}, bf16[3,90,128]{2,1,0:T(8,128)(2,1)}, u32[]{:S(2)}) copy-start(bf16[3,90,128]{2,1,0:T(8,128)(2,1)} %get-tuple-element.45.before) | copy-start | bytes 207364
  39.3 13.1 %copy-start.1 = (bf16[3,90,128]{2,1,0:T(8,128)(2,1)S(1)}, bf16[3,90,128]{2,1,0:T(8,128)(2,1)}, u32[]{:S(2)}) copy-start(bf16[3,90,128]{2,1,0:T(8,128)(2,1)} %get-tuple-element.46.after) | copy-start | bytes 207364
  44.3 14.6 %collective-permute-start.4 = (bf16[3,90,128]{2,1,0:T(8,128)(2,1)S(1)}, bf16[3,90,128]{2,1,0:T(8,128)(2,1)S(1)}, u32[]{:S(2)}, u32[]{:S(2)}) collective-permute-start(bf16[3,90,128]{2,1,0:T(8,128)(2,1)S(1)} %get-tuple-element.41), channel_id=1, source_target_pairs={{0,1},{1,2},{2,3},{3,4},{4,5},{5,6},{6,7},{7,8},{8,9},{9,10},{10,1... | collective-permute-start | bytes 207368 | tf_op jit(solution)/shard_map/ppermute | solution.py:380
  44.7 14.1 %collective-permute-start.5 = (bf16[3,90,128]{2,1,0:T(8,128)(2,1)S(1)}, bf16[3,90,128]{2,1,0:T(8,128)(2,1)S(1)}, u32[]{:S(2)}, u32[]{:S(2)}) collective-permute-start(bf16[3,90,128]{2,1,0:T(8,128)(2,1)S(1)} %get-tuple-element.42), channel_id=1, source_target_pairs={{1,0},{2,1},{3,2},{4,3},{5,4},{6,5},{7,6},{8,7},{9,8},{10,9},{11,1... | collective-permute-start | bytes 207368 | tf_op jit(solution)/shard_map/ppermute | solution.py:380
  48.7 10.1 %all-to-all-start.2 = ((f32[16,2,192]{2,1,0:T(2,128)}), f32[16,2,192]{2,1,0:T(2,128)S(1)}, u32[]{:S(2)}, u32[]{:S(2)}) async-start(f32[16,2,192]{2,1,0:T(2,128)} %get-tuple-element.43), calls=%async_computation.2 | async-start | bytes 65536 | tf_op jit(solution)/shard_map/all_to_all | solution.py:383
